TPU v7x, 32 devices: a whole 2x2x4 slice. The times are simulated.
32 devices in a mesh: ctx: 16 (over z, x, core), ws: 2 (over y).
Axes of the slice: x: 2, y: 2, z: 4, core: 2. Of those that a mesh axis runs over, the one named last changes fastest.
Arguments:
- tokens: bfloat16 [2, 2048, 960], P('ws', 'ctx'), may hold values from -6 to 6
- cotangent: bfloat16 [2, 2048, 960], P('ws', 'ctx'), may hold values from -6 to 6
- w_query: bfloat16 [960, 960], P('ws'), may hold values from -0.1875 to 0.1875
- key_weight: bfloat16 [960, 320], P('ws'), may hold values from -0.1875 to 0.1875
- value_weight: bfloat16 [960, 320], P('ws'), may hold values from -0.1875 to 0.1875
- w_out: bfloat16 [960, 960], P('ws'), may hold values from -3.5 to 3.5
- w_gate: bfloat16 [960, 2560], P('ws'), may hold values from -0.1875 to 0.1875
- w_up: bfloat16 [960, 2560], P('ws'), may hold values from -0.1875 to 0.1875
- w_down: bfloat16 [2560, 960], P('ws'), may hold values from -0.125 to 0.125
- gain_attn: bfloat16 [960], P('ws'), may hold values from 0.5 to 1.5
- gain_ffn: bfloat16 [960], P('ws'), may hold values from 0.5 to 1.5
- block_order: int32 [32], replicated, may hold values from 0 to 31, each once
- sel_mid: int32 [2, 1536], P('ws'), may hold values from 0 to 127, as said below
- live_mid: int32 [2, 1536], P('ws'), may hold values from 0 to 1, as said below
- sel_last: int32 [2, 1024], P('ws'), may hold values from 0 to 127, as said below
- live_last: int32 [2, 1024], P('ws'), may hold values from 0 to 1, as said below
Outputs:
- output: bfloat16 [2, 2048, 960], P('ws', 'ctx')
- grad_tokens: float32 [2, 2048, 960], P('ws', 'ctx')
- query_weight_gradient: float32 [960, 960], P('ws')
- grad_key: float32 [960, 320], P('ws')
- grad_value: float32 [960, 320], P('ws')
- grad_out: float32 [960, 960], P('ws')
- grad_gate: float32 [960, 2560], P('ws')
- grad_up: float32 [960, 2560], P('ws')
- grad_down: float32 [2560, 960], P('ws')
- grad_gain_attn: float32 [960], P('ws')
- grad_gain_ffn: float32 [960], P('ws')
Inputs may be any that keep to these rules, and one draw needn't show every extreme that they name: `sel_mid`: within a group each device's run of 96 slots names distinct local rows of that device. `live_mid`: in each device's run the live slots come first; every device has at least half of its 96 slots live and one device of each group has all live. `sel_last`: each device's run of 64 slots equals the first 64 slots of its run in sel_mid. `live_last`: in each device's run the live slots come first, are also live at step two, number at least half of 64; one device of each group has all live.
All inputs are finite; a program needn't handle non-finite values.
Results may differ from a plain program's by a relative error of at most 0.04.
Values may be sent and summed in bfloat16 or wider, within the bound.
No kernel may reach another device: no remote copies, remote signals or barrier semaphores. Data moves between devices by JAX's collectives and lax.ppermute only.
A program may use at most 320 MiB of HBM per device.

v0:
```python
import jax
import jax.numpy as jnp
from jax import lax
from jax.sharding import PartitionSpec as P

QUERY_HEADS = 15
KEY_VALUE_HEADS = 5
HEAD_SIZE = 64
BLK = 64
CONT = 1024


EPSILON = 1e-05
ROPE_BASE = 10000.0
MASK_FLOOR = -1e30


def normed_rows(values):
    inverse = lax.rsqrt(jnp.mean(values * values, axis=-1, keepdims=True) + EPSILON)
    return (values * inverse, inverse)


def norm_back(grad_in, normed, inverse, gain):
    scaled = grad_in * gain
    return inverse * (scaled - normed * jnp.mean(scaled * normed, axis=-1, keepdims=True))


def rotary_tables(token_positions):
    half_size = HEAD_SIZE // 2
    frequency = ROPE_BASE ** (-jnp.arange(half_size, dtype=jnp.float32) / half_size)
    angles = token_positions.astype(jnp.float32)[:, None] * frequency[None, :]
    return (jnp.cos(angles)[:, None, :], jnp.sin(angles)[:, None, :])


def turn_ahead(values, angle_tables, head_count):
    cosine, sine_part = angle_tables
    total_row_count = values.shape[0]
    shaped = values.reshape(total_row_count, head_count, HEAD_SIZE)
    half_size = HEAD_SIZE // 2
    front = shaped[..., :half_size]
    behind = shaped[..., half_size:]
    turned = jnp.concatenate(
        [front * cosine - behind * sine_part, behind * cosine + front * sine_part], axis=-1
    )
    return turned.reshape(total_row_count, head_count * HEAD_SIZE)


def rotate_backward(values, angle_tables, head_count):
    cosine, sine_part = angle_tables
    total_row_count = values.shape[0]
    shaped = values.reshape(total_row_count, head_count, HEAD_SIZE)
    half_size = HEAD_SIZE // 2
    front = shaped[..., :half_size]
    behind = shaped[..., half_size:]
    turned = jnp.concatenate(
        [front * cosine + behind * sine_part, behind * cosine - front * sine_part], axis=-1
    )
    return turned.reshape(total_row_count, head_count * HEAD_SIZE)


def segment_of(token_positions, prompt):
    return jnp.where(token_positions < prompt, 0, 1 + (token_positions - prompt) // CONT)


def visible(query_places, key_places, key_live, prompt):
    query_seg = segment_of(query_places, prompt)
    key_seg = segment_of(key_places, prompt)
    earlier = key_places[None, :] <= query_places[:, None]
    shared = (key_seg[None, :] == 0) | (key_seg[None, :] == query_seg[:, None])
    itself = key_places[None, :] == query_places[:, None]
    return earlier & shared & ((key_live[None, :] > 0) | itself)


def block_size(total_row_count, upper_limit):
    block_length = total_row_count
    while block_length > upper_limit and block_length % 2 == 0:
        block_length = block_length // 2
    return block_length


def key_layout(every_key, every_value, key_places, key_live):
    key_grand_total = every_key.shape[0]
    block_length = block_size(key_grand_total, 1024)
    block_count = key_grand_total // block_length
    return (
        every_key.reshape(block_count, block_length, KEY_VALUE_HEADS, HEAD_SIZE),
        every_value.reshape(block_count, block_length, KEY_VALUE_HEADS, HEAD_SIZE),
        key_places.reshape(block_count, block_length),
        key_live.reshape(block_count, block_length),
    )


def masked_scores(query_head_rows, key_part, place_part, live_part, query_places, prompt):
    attention_score_scale = HEAD_SIZE ** (-0.5)
    scores = (
        jnp.einsum("qhgd,khd->hgqk", query_head_rows, key_part, preferred_element_type=jnp.float32)
        * attention_score_scale
    )
    allowed = visible(query_places, place_part, live_part, prompt)[None, None]
    return (jnp.where(allowed, scores, MASK_FLOOR), allowed)


def attend(query_matrix, every_key, every_value, query_places, key_places, key_live, prompt):
    total_row_count = query_matrix.shape[0]
    queries_per_group = QUERY_HEADS // KEY_VALUE_HEADS
    query_head_rows = query_matrix.reshape(
        total_row_count, KEY_VALUE_HEADS, queries_per_group, HEAD_SIZE
    )
    layout = key_layout(every_key, every_value, key_places, key_live)

    def sweep(running, pieces):
        row_top, row_mass, rounded_sum, rest_sum = running
        key_part, value_part, place_part, live_part = pieces
        scores, allowed = masked_scores(
            query_head_rows, key_part, place_part, live_part, query_places, prompt
        )
        new_top = jnp.maximum(row_top, jnp.max(scores, axis=-1))
        factor = jnp.exp(row_top - new_top)
        prob_rows = jnp.where(allowed, jnp.exp(scores - new_top[..., None]), 0.0)
        prob_low = prob_rows.astype(jnp.bfloat16)
        prob_rest = (prob_rows - prob_low.astype(jnp.float32)).astype(jnp.bfloat16)
        rounded_sum = rounded_sum * factor[..., None] + jnp.einsum(
            "hgqk,khd->hgqd", prob_low, value_part, preferred_element_type=jnp.float32
        )
        rest_sum = rest_sum * factor[..., None] + jnp.einsum(
            "hgqk,khd->hgqd", prob_rest, value_part, preferred_element_type=jnp.float32
        )
        row_mass = row_mass * factor + jnp.sum(prob_rows, axis=-1)
        return ((new_top, row_mass, rounded_sum, rest_sum), None)

    zero_output = jnp.zeros(
        (KEY_VALUE_HEADS, queries_per_group, total_row_count, HEAD_SIZE), jnp.float32
    )
    initial_state = (
        jnp.full((KEY_VALUE_HEADS, queries_per_group, total_row_count), MASK_FLOOR, jnp.float32),
        jnp.zeros((KEY_VALUE_HEADS, queries_per_group, total_row_count), jnp.float32),
        zero_output,
        zero_output,
    )
    (row_top, row_mass, rounded_sum, rest_sum), unused = lax.scan(sweep, initial_state, layout)
    log_mass = row_top + jnp.log(row_mass)
    inverse_mass = (1.0 / row_mass)[..., None]
    mixed_low = (
        (rounded_sum * inverse_mass)
        .transpose(2, 0, 1, 3)
        .reshape(total_row_count, QUERY_HEADS * HEAD_SIZE)
        .astype(jnp.bfloat16)
    )
    exact_output = (
        ((rounded_sum + rest_sum) * inverse_mass)
        .transpose(2, 0, 1, 3)
        .reshape(total_row_count, QUERY_HEADS * HEAD_SIZE)
    )
    return (mixed_low, exact_output, log_mass)


def attend_back(
    query_matrix,
    every_key,
    every_value,
    query_places,
    key_places,
    key_live,
    prompt,
    log_mass,
    mixed_gradient,
    exact_output,
):
    total_row_count = query_matrix.shape[0]
    key_grand_total = every_key.shape[0]
    queries_per_group = QUERY_HEADS // KEY_VALUE_HEADS
    attention_score_scale = HEAD_SIZE ** (-0.5)
    query_head_rows = query_matrix.reshape(
        total_row_count, KEY_VALUE_HEADS, queries_per_group, HEAD_SIZE
    )
    head_gradient = mixed_gradient.reshape(
        total_row_count, KEY_VALUE_HEADS, queries_per_group, HEAD_SIZE
    )
    row_delta = jnp.sum(
        head_gradient.astype(jnp.float32)
        * exact_output.reshape(total_row_count, KEY_VALUE_HEADS, queries_per_group, HEAD_SIZE),
        axis=-1,
    ).transpose(1, 2, 0)
    layout = key_layout(every_key, every_value, key_places, key_live)

    def sweep_back(running, pieces):
        key_part, value_part, place_part, live_part = pieces
        scores, allowed = masked_scores(
            query_head_rows, key_part, place_part, live_part, query_places, prompt
        )
        prob_rows = jnp.where(allowed, jnp.exp(scores - log_mass[..., None]), 0.0)
        grad_probs = jnp.einsum(
            "qhgd,khd->hgqk", head_gradient, value_part, preferred_element_type=jnp.float32
        )
        grad_scores = (prob_rows * (grad_probs - row_delta[..., None])).astype(jnp.bfloat16)
        running = running + jnp.einsum(
            "hgqk,khd->qhgd", grad_scores, key_part, preferred_element_type=jnp.float32
        )
        prob_low = prob_rows.astype(jnp.bfloat16)
        key_gradient = jnp.einsum(
            "hgqk,qhgd->khd", grad_scores, query_head_rows, preferred_element_type=jnp.float32
        )
        value_gradient = jnp.einsum(
            "hgqk,qhgd->khd", prob_low, head_gradient, preferred_element_type=jnp.float32
        )
        return (running, (key_gradient, value_gradient))

    initial_state = jnp.zeros(
        (total_row_count, KEY_VALUE_HEADS, queries_per_group, HEAD_SIZE), jnp.float32
    )
    query_weight_gradient, key_terms = lax.scan(sweep_back, initial_state, layout)
    query_weight_gradient = (
        query_weight_gradient.reshape(total_row_count, QUERY_HEADS * HEAD_SIZE)
        * attention_score_scale
    )
    key_gradients, value_gradients = key_terms
    return (
        query_weight_gradient,
        key_gradients.reshape(key_grand_total, KEY_VALUE_HEADS * HEAD_SIZE) * attention_score_scale,
        value_gradients.reshape(key_grand_total, KEY_VALUE_HEADS * HEAD_SIZE),
        row_delta,
    )


def on_device(
    tokens,
    cotangent,
    w_query,
    key_weight,
    value_weight,
    w_out,
    w_gate,
    w_up,
    w_down,
    gain_attn,
    gain_ffn,
    block_order,
    sel_mid,
    live_mid,
    sel_last,
    live_last,
):
    (
        full_query,
        full_key,
        full_value,
        full_out,
        full_gate,
        full_up,
        full_down,
        full_gain_a,
        full_gain_f,
    ) = (
        lax.all_gather(w_query, "ws", axis=0, tiled=True),
        lax.all_gather(key_weight, "ws", axis=0, tiled=True),
        lax.all_gather(value_weight, "ws", axis=0, tiled=True),
        lax.all_gather(w_out, "ws", axis=0, tiled=True),
        lax.all_gather(w_gate, "ws", axis=0, tiled=True),
        lax.all_gather(w_up, "ws", axis=0, tiled=True),
        lax.all_gather(w_down, "ws", axis=0, tiled=True),
        lax.all_gather(gain_attn, "ws", axis=0, tiled=True),
        lax.all_gather(gain_ffn, "ws", axis=0, tiled=True),
    )
    w_qkv = jnp.concatenate([full_query, full_key, full_value], axis=1)
    w_pair = jnp.concatenate([full_gate, full_up], axis=1)
    gain_one = full_gain_a.astype(jnp.float32)
    gain_two = full_gain_f.astype(jnp.float32)
    hidden_width = full_gate.shape[1]
    query_row_width = QUERY_HEADS * HEAD_SIZE
    key_row_width = KEY_VALUE_HEADS * HEAD_SIZE
    ctx_count = lax.axis_size("ctx")
    ctx_here = lax.axis_index("ctx")
    tok_local = tokens.shape[1]
    token_positions = (
        block_order[:, None] * BLK + jnp.arange(BLK, dtype=jnp.int32)[None, :]
    ).reshape(-1)
    all_rows = token_positions.shape[0]
    prompt = all_rows // 2
    step_plans = [
        (
            jnp.arange(tok_local, dtype=jnp.int32),
            jnp.ones((tok_local,), jnp.int32),
            jnp.arange(all_rows, dtype=jnp.int32),
            jnp.ones((all_rows,), jnp.int32),
        )
    ]
    for selection, alive in ((sel_mid[0], live_mid[0]), (sel_last[0], live_last[0])):
        capacity = selection.shape[0] // ctx_count
        local_ids = lax.dynamic_slice_in_dim(selection, ctx_here * capacity, capacity)
        live_local = lax.dynamic_slice_in_dim(alive, ctx_here * capacity, capacity)
        key_rows = (
            jnp.arange(selection.shape[0], dtype=jnp.int32) // capacity * tok_local + selection
        )
        step_plans.append((local_ids, live_local, key_rows, alive))
    hidden_state = tokens[0].astype(jnp.float32)
    records = []
    for local_ids, live_local, key_rows, key_live in step_plans:
        current = jnp.take(hidden_state, local_ids, axis=0)
        query_places = jnp.take(token_positions, ctx_here * tok_local + local_ids)
        key_places = jnp.take(token_positions, key_rows)
        angle_tables = rotary_tables(query_places)
        normed_one, inv_one = normed_rows(current)
        first_in = (normed_one * gain_one).astype(jnp.bfloat16)
        projected_rows = jnp.dot(first_in, w_qkv, preferred_element_type=jnp.float32)
        query_matrix = turn_ahead(
            projected_rows[:, :query_row_width], angle_tables, QUERY_HEADS
        ).astype(jnp.bfloat16)
        key_local = turn_ahead(
            projected_rows[:, query_row_width : query_row_width + key_row_width],
            angle_tables,
            KEY_VALUE_HEADS,
        ).astype(jnp.bfloat16)
        value_local = projected_rows[:, query_row_width + key_row_width :].astype(jnp.bfloat16)
        every_key, every_value = (
            lax.all_gather(key_local, "ctx", axis=0, tiled=True),
            lax.all_gather(value_local, "ctx", axis=0, tiled=True),
        )
        mixed_low, exact_output, log_mass = attend(
            query_matrix, every_key, every_value, query_places, key_places, key_live, prompt
        )
        middle = current + jnp.dot(mixed_low, full_out, preferred_element_type=jnp.float32)
        normed_two, inv_two = normed_rows(middle)
        second_in = (normed_two * gain_two).astype(jnp.bfloat16)
        paired = jnp.dot(second_in, w_pair, preferred_element_type=jnp.float32)
        gate_lin = paired[:, :hidden_width]
        up_lin = paired[:, hidden_width:]
        hidden = (jax.nn.silu(gate_lin) * up_lin).astype(jnp.bfloat16)
        updated = middle + jnp.dot(hidden, full_down, preferred_element_type=jnp.float32)
        alive_rows = live_local[:, None] > 0
        hidden_state = hidden_state.at[local_ids].set(jnp.where(alive_rows, updated, current))
        records.append(
            (
                local_ids,
                live_local,
                alive_rows,
                key_places,
                key_live,
                query_places,
                angle_tables,
                normed_one,
                inv_one,
                first_in,
                query_matrix,
                key_local,
                value_local,
                every_key,
                every_value,
                mixed_low,
                exact_output,
                log_mass,
                normed_two,
                inv_two,
                second_in,
                gate_lin,
                up_lin,
                hidden,
            )
        )
    output = hidden_state.astype(jnp.bfloat16)[None]
    grad_state = cotangent[0].astype(jnp.float32)
    acc_qkv = jnp.zeros(w_qkv.shape, jnp.float32)
    acc_out = jnp.zeros(full_out.shape, jnp.float32)
    acc_pair = jnp.zeros(w_pair.shape, jnp.float32)
    acc_down = jnp.zeros(full_down.shape, jnp.float32)
    acc_gain_one = jnp.zeros(gain_one.shape, jnp.float32)
    acc_gain_two = jnp.zeros(gain_two.shape, jnp.float32)
    for record in records[::-1]:
        (
            local_ids,
            live_local,
            alive_rows,
            key_places,
            key_live,
            query_places,
            angle_tables,
            normed_one,
            inv_one,
            first_in,
            query_matrix,
            key_local,
            value_local,
            every_key,
            every_value,
            mixed_low,
            exact_output,
            log_mass,
            normed_two,
            inv_two,
            second_in,
            gate_lin,
            up_lin,
            hidden,
        ) = record
        grad_rows = jnp.take(grad_state, local_ids, axis=0)
        grad_update = jnp.where(alive_rows, grad_rows, 0.0)
        grad_low = grad_update.astype(jnp.bfloat16)
        acc_down = acc_down + jnp.einsum(
            "cf,cd->fd", hidden, grad_low, preferred_element_type=jnp.float32
        )
        grad_hidden = jnp.einsum(
            "cd,fd->cf", grad_low, full_down, preferred_element_type=jnp.float32
        )
        sigmoid_gate = jax.nn.sigmoid(gate_lin)
        grad_gate = grad_hidden * up_lin * sigmoid_gate * (1.0 + gate_lin * (1.0 - sigmoid_gate))
        grad_up = grad_hidden * gate_lin * sigmoid_gate
        grad_pair = jnp.concatenate([grad_gate, grad_up], axis=1).astype(jnp.bfloat16)
        acc_pair = acc_pair + jnp.einsum(
            "cd,ce->de", second_in, grad_pair, preferred_element_type=jnp.float32
        )
        grad_second = jnp.einsum("ce,de->cd", grad_pair, w_pair, preferred_element_type=jnp.float32)
        acc_gain_two = acc_gain_two + jnp.sum(grad_second * normed_two, axis=0)
        grad_middle = norm_back(grad_second, normed_two, inv_two, gain_two) + grad_update
        grad_mid_low = grad_middle.astype(jnp.bfloat16)
        acc_out = acc_out + jnp.einsum(
            "ce,cd->ed", mixed_low, grad_mid_low, preferred_element_type=jnp.float32
        )
        mixed_gradient = jnp.einsum(
            "cd,ed->ce", grad_mid_low, full_out, preferred_element_type=jnp.float32
        ).astype(jnp.bfloat16)
        query_weight_gradient, key_gradients, value_gradients, row_delta = attend_back(
            query_matrix,
            every_key,
            every_value,
            query_places,
            key_places,
            key_live,
            prompt,
            log_mass,
            mixed_gradient,
            exact_output,
        )
        key_gradient, value_gradient = (
            lax.psum_scatter(key_gradients, "ctx", scatter_dimension=0, tiled=True),
            lax.psum_scatter(value_gradients, "ctx", scatter_dimension=0, tiled=True),
        )
        grad_proj = jnp.concatenate(
            [
                rotate_backward(query_weight_gradient, angle_tables, QUERY_HEADS),
                rotate_backward(key_gradient, angle_tables, KEY_VALUE_HEADS),
                value_gradient,
            ],
            axis=1,
        ).astype(jnp.bfloat16)
        acc_qkv = acc_qkv + jnp.einsum(
            "cd,ce->de", first_in, grad_proj, preferred_element_type=jnp.float32
        )
        grad_first = jnp.einsum("ce,de->cd", grad_proj, w_qkv, preferred_element_type=jnp.float32)
        acc_gain_one = acc_gain_one + jnp.sum(grad_first * normed_one, axis=0)
        grad_current = norm_back(grad_first, normed_one, inv_one, gain_one) + grad_middle
        grad_state = grad_state.at[local_ids].set(jnp.where(alive_rows, grad_current, grad_rows))
    part_query = acc_qkv[:, :query_row_width]
    part_key = acc_qkv[:, query_row_width : query_row_width + key_row_width]
    part_value = acc_qkv[:, query_row_width + key_row_width :]
    part_gate = acc_pair[:, :hidden_width]
    part_up = acc_pair[:, hidden_width:]
    summed = lax.psum(
        (
            part_query,
            part_key,
            part_value,
            acc_out,
            part_gate,
            part_up,
            acc_down,
            acc_gain_one,
            acc_gain_two,
        ),
        ("ctx", "ws"),
    )
    ws_here = lax.axis_index("ws")
    ws_count = lax.axis_size("ws")
    shares = tuple(
        (
            lax.dynamic_slice_in_dim(
                summed_one,
                ws_here * (summed_one.shape[0] // ws_count),
                summed_one.shape[0] // ws_count,
                0,
            )
            for summed_one in summed
        )
    )
    return (
        output,
        grad_state[None],
        shares[0],
        shares[1],
        shares[2],
        shares[3],
        shares[4],
        shares[5],
        shares[6],
        shares[7],
        shares[8],
    )


def solution(mesh):
    in_specs = (
        P("ws", "ctx", None),
        P("ws", "ctx", None),
        P("ws", None),
        P("ws", None),
        P("ws", None),
        P("ws", None),
        P("ws", None),
        P("ws", None),
        P("ws", None),
        P("ws"),
        P("ws"),
        P(),
        P("ws", None),
        P("ws", None),
        P("ws", None),
        P("ws", None),
    )
    out_specs = (
        P("ws", "ctx", None),
        P("ws", "ctx", None),
        P("ws", None),
        P("ws", None),
        P("ws", None),
        P("ws", None),
        P("ws", None),
        P("ws", None),
        P("ws", None),
        P("ws"),
        P("ws"),
    )
    return jax.shard_map(
        on_device, mesh=mesh, in_specs=in_specs, out_specs=out_specs, check_vma=False
    )
```

profile of v0, /device:TPU:7, one launch (start us, length us, event | category | flops | bytes accessed | tf_op | source)
XLA Modules:
  0.0 1760.2 jit_solution(4233944160080275529)
XLA Ops:
  11.6 3.8 all-reduce.4
  17.6 16.4 all-gather
  34.3 16.6 all-gather.1
  51.5 4.1 all-gather.10.cloned.1.call-done
  55.5 5.7 concatenate.78
  75.7 6.2 gather_fusion.4
  81.9 8.4 gather_fusion.2
  90.3 11.8 gather_fusion
  107.2 4.4 reshape.1582
  114.4 30.0 %all-gather.12.cloned.1.call-done = bf16[2048,320]{0,1:T(8,128)(2,1)} async-done(((bf16[128,320]{0,1:T(8,128)(2,1)}), bf16[2048,320]{0,1:T(8,128)(2,1)}) %all-gather.12.cloned.1.call-update) | async-done | bytes 1310736 | tf_op jit(solution)/shard_map/all_gather | solution.py:315
  144.3 4.4 reshape.1580
  150.4 18.3 %while.89 = (s32[]{:T(128)}, f32[5,3,128]{2,1,0:T(4,128)S(1)}, f32[5,3,128]{2,1,0:T(4,128)S(1)}, f32[5,3,128,64]{2,3,1,0:T(8,128)S(1)}, f32[5,3,128,64]{2,3,1,0:...) while((s32[]{:T(128)}, f32[5,3,128]{2,1,0:T(4,128)S(1)}, ...), condition=%wide.region_4.6_spmd.clone, body=%wide.region_1.5_spmd.clone.sunk | while | flops 797556480 | bytes 45638892 | solution.py:140
  170.7 4.9 all-gather.16.cloned.1.call-done
  178.1 63.8 %all-gather.18.cloned.1.call-done = bf16[960,2560]{1,0:T(8,128)(2,1)} async-done(((bf16[480,2560]{1,0:T(8,128)(2,1)}), bf16[960,2560]{1,0:T(8,128)(2,1)}) %all-gather.18.cloned.1.call-update) | async-done | bytes 4915216 | tf_op jit(solution)/shard_map/all_gather | solution.py:258
  241.9 4.9 constant_dynamic-update-slice_fusion.1
  246.9 61.3 %all-gather.20.cloned.1.call-done = bf16[960,2560]{1,0:T(8,128)(2,1)} async-done(((bf16[480,2560]{1,0:T(8,128)(2,1)}), bf16[960,2560]{1,0:T(8,128)(2,1)}) %all-gather.20.cloned.1.call-update) | async-done | bytes 4915216 | tf_op jit(solution)/shard_map/all_gather | solution.py:259
  308.2 5.1 constant_dynamic-update-slice_fusion
  313.3 5.4 fusion.222
  320.6 54.0 %all-gather.22.cloned.1.call-done = bf16[2560,960]{0,1:T(8,128)(2,1)} async-done(((bf16[1280,960]{0,1:T(8,128)(2,1)}), bf16[2560,960]{0,1:T(8,128)(2,1)}) %all-gather.22.cloned.1.call-update) | async-done | bytes 4915216 | tf_op jit(solution)/shard_map/all_gather | solution.py:260
  374.7 3.8 convolution_add_fusion
  385.8 21.8 %all_gather.56 = bf16[1536,320]{1,0:T(8,128)(2,1)S(1)} all-gather(bf16[96,320]{1,0:T(8,128)(2,1)S(1)} %copy.123), channel_id=1, replica_groups=mesh['ctx'=16,'ws'=2] {'ctx'}, dimensions={0}, use_global_device_ids=true | all-gather | bytes 1044480 | tf_op jit(solution)/shard_map/all_gather | solution.py:315
  410.7 26.1 %all_gather.57 = bf16[1536,320]{1,0:T(8,128)(2,1)} all-gather(bf16[96,320]{1,0:T(8,128)(2,1)S(1)} %slice.310), channel_id=1, replica_groups=mesh['ctx'=16,'ws'=2] {'ctx'}, dimensions={0}, use_global_device_ids=true | all-gather | bytes 1044480 | tf_op jit(solution)/shard_map/all_gather | solution.py:316
  445.3 11.5 while.90
  460.1 5.7 fusion.221
  475.6 21.0 %all_gather.58 = bf16[1024,320]{1,0:T(8,128)(2,1)} all-gather(bf16[64,320]{1,0:T(8,128)(2,1)S(1)} %copy.130), channel_id=1, replica_groups=mesh['ctx'=16,'ws'=2] {'ctx'}, dimensions={0}, use_global_device_ids=true | all-gather | bytes 696320 | tf_op jit(solution)/shard_map/all_gather | solution.py:315
  501.9 23.3 %all_gather.59 = bf16[1024,320]{1,0:T(8,128)(2,1)} all-gather(bf16[64,320]{1,0:T(8,128)(2,1)S(1)} %slice.311), channel_id=1, replica_groups=mesh['ctx'=16,'ws'=2] {'ctx'}, dimensions={0}, use_global_device_ids=true | all-gather | bytes 696320 | tf_op jit(solution)/shard_map/all_gather | solution.py:316
  526.6 4.1 multiply_convert_fusion.9
  531.4 5.8 fusion.220
  537.3 4.3 multiply_convert_fusion.7
  546.4 3.8 fusion.141
  557.6 4.0 fusion.117
  573.1 39.6 %reduce-scatter.19.cloned.1.call-done = f32[64,320]{1,0:T(8,128)} async-done(((f32[1024,320]{1,0:T(8,128)}), f32[64,320]{1,0:T(8,128)}) %reduce-scatter.19.cloned.1.call-update) | async-done | bytes 81936
  613.9 61.6 %reduce-scatter.13.cloned.1.call-done = f32[64,320]{1,0:T(8,128)} async-done(((f32[1024,320]{1,0:T(8,128)}), f32[64,320]{1,0:T(8,128)}) %reduce-scatter.13.cloned.1.call-update) | async-done | bytes 81936 | tf_op jit(solution)/shard_map/reduce_scatter | solution.py:434
  677.2 4.3 multiply_reduce_fusion.13
  684.2 4.2 multiply_convert_fusion.4
  688.5 8.0 multiply_reduce_fusion.6
  699.7 56.9 %while.91 = (s32[]{:T(128)}, f32[96,5,3,64]{0,3,2,1:T(8,128)S(1)}, f32[2,768,5,64]{1,3,2,0:T(8,128)}, f32[2,768,5,64]{1,0,3,2:T(2,128)}, bf16[2,768,5,64]{1,3,2,...) while((s32[]{:T(128)}, f32[96,5,3,64]{0,3,2,1:T(8,128)S(1)}, ...), condition=%wide.region_28.32_spmd.clone, body=%wide.region_27.31_spmd.clone.sunk | while | flops 721778176 | bytes 33150300 | solution.py:211
  710.0 18.4 %dynamic_update_slice.46 = f32[2,768,5,64]{1,0,3,2:T(2,128)} dynamic-update-slice(f32[2,768,5,64]{1,0,3,2:T(2,128)} %get-tuple-element.1795, f32[1,768,5,64]{1,0,3,2:T(1,128)S(1)} %copy.228, s32[]{:T(128)S(6)} %copy.275, s32[]{:T(128)} %constant.680.clone.1..sunk.2, s32[]{:T(128)} %constant.680.clone.1..sunk.2, s32[]{:T(128)} %constant.680.clone.1..sunk.2) | dynamic-update-slice | bytes 1966084 | tf_op jit(solution)/shard_map/while/body/jit(dynamic_update_index_in_dim)/dynamic_update_slice | solution.py:211
  738.2 18.4 %dynamic_update_slice.46 = f32[2,768,5,64]{1,0,3,2:T(2,128)} dynamic-update-slice(f32[2,768,5,64]{1,0,3,2:T(2,128)} %get-tuple-element.1795, f32[1,768,5,64]{1,0,3,2:T(1,128)S(1)} %copy.228, s32[]{:T(128)S(6)} %copy.275, s32[]{:T(128)} %constant.680.clone.1..sunk.2, s32[]{:T(128)} %constant.680.clone.1..sunk.2, s32[]{:T(128)} %constant.680.clone.1..sunk.2) | dynamic-update-slice | bytes 1966084 | tf_op jit(solution)/shard_map/while/body/jit(dynamic_update_index_in_dim)/dynamic_update_slice | solution.py:211
  766.3 58.0 %reduce-scatter.21.cloned.1.call-done = f32[96,320]{1,0:T(8,128)} async-done(((f32[1536,320]{1,0:T(8,128)}), f32[96,320]{1,0:T(8,128)}) %reduce-scatter.21.cloned.1.call-update) | async-done | bytes 122896
  825.4 65.1 %reduce-scatter.23.cloned.1.call-done = f32[96,320]{1,0:T(8,128)} async-done(((f32[1536,320]{1,0:T(8,128)}), f32[96,320]{1,0:T(8,128)}) %reduce-scatter.23.cloned.1.call-update) | async-done | bytes 122896
  897.8 4.6 multiply_convert_fusion.1
  903.3 7.3 multiply_reduce_fusion
  913.5 74.7 %while.92 = (s32[]{:T(128)}, f32[128,5,3,64]{0,3,2,1:T(8,128)S(1)}, f32[2,1024,5,64]{1,3,2,0:T(8,128)}, f32[2,1024,5,64]{1,0,3,2:T(2,128)}, bf16[2,1024,5,64]{1,...) while((s32[]{:T(128)}, f32[128,5,3,64]{0,3,2,1:T(8,128)S(1)}, ...), condition=%wide.region_36.40_spmd.clone, body=%wide.region_35.39_spmd.clone.sunk | while | flops 1282677120 | bytes 52874952 | solution.py:211
  919.1 4.0 fusion.396
  927.8 23.1 %dynamic_update_slice.48 = f32[2,1024,5,64]{1,0,3,2:T(2,128)} dynamic-update-slice(f32[2,1024,5,64]{1,0,3,2:T(2,128)} %get-tuple-element.1839, f32[1,1024,5,64]{1,0,3,2:T(1,128)S(1)} %copy.229, s32[]{:T(128)S(6)} %copy.288, s32[]{:T(128)} %constant.680.clone.1..sunk.3, s32[]{:T(128)} %constant.680.clone.1..sunk.3, s32[]{:T(128)} %constant.680.clone.1..sunk.3) | dynamic-update-slice | bytes 2621444 | tf_op jit(solution)/shard_map/while/body/jit(dynamic_update_index_in_dim)/dynamic_update_slice | solution.py:211
  956.4 4.0 fusion.396
  965.0 23.1 %dynamic_update_slice.48 = f32[2,1024,5,64]{1,0,3,2:T(2,128)} dynamic-update-slice(f32[2,1024,5,64]{1,0,3,2:T(2,128)} %get-tuple-element.1839, f32[1,1024,5,64]{1,0,3,2:T(1,128)S(1)} %copy.229, s32[]{:T(128)S(6)} %copy.288, s32[]{:T(128)} %constant.680.clone.1..sunk.3, s32[]{:T(128)} %constant.680.clone.1..sunk.3, s32[]{:T(128)} %constant.680.clone.1..sunk.3) | dynamic-update-slice | bytes 2621444 | tf_op jit(solution)/shard_map/while/body/jit(dynamic_update_index_in_dim)/dynamic_update_slice | solution.py:211
  997.8 5.3 fusion.224
  1003.1 8.5 fusion.147
  1014.3 3.7 fusion.228
  1018.1 5.3 fusion.230
  1023.4 8.3 fusion.143
  1034.9 21.4 %add_add_fusion = f32[960,5120]{1,0:T(8,128)} fusion(f32[960,5120]{1,0:T(8,128)} %fusion.147, f32[960,5120]{1,0:T(8,128)} %fusion.143, bf16[128,2560]{1,0:T(8,128)(2,1)} %copy-done.90, bf16[128,2560]{1,0:T(8,128)(2,1)S(1)} %copy-done.89, f32[128,960]{0,1:T(8,128)S(1)} %copy-done.26, f32[960]{0:T(1024)S(1)} %convert_element_type.265, f32[128]{0:T(128)S(1)} %copy-done.153), kind=kOutput, calls=%fused_computation.192 | convolution fusion | flops 1271111680 | bytes 60788992 | tf_op jit(solution)/shard_map/cd,ce->de/dot_general | solution.py:407
  1056.4 4.4 fusion.174
  1064.9 14.2 add_add_fusion.1
  1080.7 7.2 fusion.237
  1088.9 35.8 %reduce-scatter.17.cloned.1.call-done = f32[128,320]{0,1:T(8,128)} async-done(((f32[2048,320]{0,1:T(8,128)}), f32[128,320]{0,1:T(8,128)}) %reduce-scatter.17.cloned.1.call-update) | async-done | bytes 163856 | tf_op jit(solution)/shard_map/reduce_scatter | solution.py:434
  1125.6 5.7 add_add_fusion.2
  1136.8 4.0 fusion.140
  1142.9 4.0 multiply_reduce_fusion.1
  1146.9 42.4 %all-reduce.2 = (f32[960]{0:T(1024)S(1)}, f32[960]{0:T(1024)S(1)}) all-reduce(f32[960]{0:T(1024)S(1)} %add_add_fusion.5, f32[960]{0:T(1024)S(1)} %add_add_fusion.4), channel_id=1, replica_groups=mesh['ctx'=16,'ws'=2] {'ctx','ws'}, use_global_device_ids=true, to_apply=%region_51.55 | all-reduce | flops 1920 | bytes 15360 | tf_op jit(solution)/shard_map/psum | solution.py:456
  1193.3 539.2 %all-reduce.7.cloned.1.call-done = (f32[960,960]{1,0:T(8,128)}, f32[960,320]{1,0:T(8,128)}, f32[960,320]{1,0:T(8,128)}, f32[960,960]{1,0:T(8,128)}, f32[960,2560...) async-done(((f32[960,960]{1,0:T(8,128)}, f32[960,320]{1,0:T(8,128)}, f32[960,320]{1,0:T(8,128)}, f32[960,960]{1,0:T(8,128)}, f32[960,2560]{1,0:T(8,128)}, ...) | async-done | bytes 39321616 | tf_op jit(solution)/shard_map/psum | solution.py:456
  1741.1 6.0 constant_dynamic-slice_fusion.4
  (741 shorter events, 246.1 us)
Async XLA Ops:
  7.2 48.4 %all-gather.10.cloned.1.call-start = ((), (), s32[]{:S(2)}) async-start(), calls=%async_computation.6 | async-start | bytes 2949120 | tf_op jit(solution)/shard_map/all_gather | solution.py:254
  7.9 99.3 %all-gather.14.cloned.1.call-start = ((), (), s32[]{:S(2)}) async-start(), calls=%async_computation.8 | async-start | bytes 1392640 | tf_op jit(solution)/shard_map/all_gather | solution.py:316
  16.5 17.8 %copy-start.161 = (s32[1024]{0:T(1024)}, s32[1024]{0:T(1024)S(1)}, u32[]{:S(2)}) copy-start(s32[1024]{0:T(1024)S(1)} %get-tuple-element.1381) | copy-start | bytes 12292
  17.6 158.0 %copy-start.20 = (f32[128,960]{0,1:T(8,128)}, f32[128,960]{0,1:T(8,128)S(1)}, u32[]{:S(2)}) copy-start(f32[128,960]{0,1:T(8,128)S(1)} %copy.114) | copy-start | bytes 1474564
  51.3 124.3 %copy-start.139 = (pred[128]{0:T(512)(128)(4,1)}, pred[128]{0:T(512)(128)(4,1)S(1)}, u32[]{:S(2)}) copy-start(pred[128]{0:T(512)(128)(4,1)S(1)} %broadcast_compare_fusion) | copy-start | bytes 388
  65.4 78.9 %all-gather.12.cloned.1.call-start = ((), (), s32[]{:S(2)}) async-start(), calls=%async_computation.7 | async-start | bytes 1392640 | tf_op jit(solution)/shard_map/all_gather | solution.py:315
  67.0 40.0 %copy-start.99 = (f32[128,32]{0,1:T(8,128)}, f32[128,32]{0,1:T(8,128)S(1)}, u32[]{:S(2)}) copy-start(f32[128,32]{0,1:T(8,128)S(1)} %get-tuple-element.1356) | copy-start | bytes 49156
  67.0 40.0 %copy-start.101 = (f32[128,32]{0,1:T(8,128)}, f32[128,32]{0,1:T(8,128)S(1)}, u32[]{:S(2)}) copy-start(f32[128,32]{0,1:T(8,128)S(1)} %get-tuple-element.1357) | copy-start | bytes 49156
  67.7 107.9 %all-gather.16.cloned.1.call-start = ((), (), s32[]{:S(2)}) async-start(), calls=%async_computation.9 | async-start | bytes 2949120 | tf_op jit(solution)/shard_map/all_gather | solution.py:257
  68.4 173.5 %all-gather.18.cloned.1.call-start = ((), (), s32[]{:S(2)}) async-start(), calls=%async_computation.10 | async-start | bytes 7372800 | tf_op jit(solution)/shard_map/all_gather | solution.py:258
  68.9 239.3 %all-gather.20.cloned.1.call-start = ((), (), s32[]{:S(2)}) async-start(), calls=%async_computation.11 | async-start | bytes 7372800 | tf_op jit(solution)/shard_map/all_gather | solution.py:259
  69.5 305.1 %all-gather.22.cloned.1.call-start = ((), (), s32[]{:S(2)}) async-start(), calls=%async_computation.12 | async-start | bytes 7372800 | tf_op jit(solution)/shard_map/all_gather | solution.py:260
  70.3 542.5 %reduce-scatter.19.cloned.1.call-start = ((), (), s32[]{:S(2)}) async-start(), calls=%async_computation.16 | async-start | bytes 1671168
  71.1 31.6 %copy-start.170 = (s32[1,64]{1,0:T(1,128)}, s32[1,64]{1,0:T(1,128)S(1)}, u32[]{:S(2)}) copy-start(s32[1,64]{1,0:T(1,128)S(1)} %get-tuple-element.1296) | copy-start | bytes 772
  71.9 309.1 %copy-start.136 = (pred[96]{0:T(512)(128)(4,1)}, pred[96]{0:T(512)(128)(4,1)S(1)}, u32[]{:S(2)}) copy-start(pred[96]{0:T(512)(128)(4,1)S(1)} %get-tuple-element.1299) | copy-start | bytes 292
  102.8 277.3 %copy-start.163 = (s32[1024]{0:T(1024)}, s32[1024]{0:T(1024)S(1)}, u32[]{:S(2)}) copy-start(s32[1024]{0:T(1024)S(1)} %pad_clamp_fusion.4) | copy-start | bytes 12292
  103.1 280.8 %copy-start.103 = (f32[96,32]{0,1:T(8,128)}, f32[96,32]{0,1:T(8,128)S(1)}, u32[]{:S(2)}) copy-start(f32[96,32]{0,1:T(8,128)S(1)} %get-tuple-element.1354) | copy-start | bytes 36868
  103.2 280.8 %copy-start.105 = (f32[96,32]{0,1:T(8,128)}, f32[96,32]{0,1:T(8,128)S(1)}, u32[]{:S(2)}) copy-start(f32[96,32]{0,1:T(8,128)S(1)} %get-tuple-element.1355) | copy-start | bytes 36868
  111.6 38.8 %copy-start.65 = (f32[5,3,128,64]{2,3,1,0:T(8,128)S(1)}, f32[5,3,128,64]{2,3,1,0:T(8,128)}, u32[]{:S(2)}) copy-start(f32[5,3,128,64]{2,3,1,0:T(8,128)} %custom-call.2) | copy-start | bytes 1474564
  168.8 78.1 %copy-start.6 = (bf16[2,1024,5,64]{1,3,2,0:T(8,128)(2,1)}, bf16[2,1024,5,64]{1,3,2,0:T(8,128)(2,1)S(1)}, u32[]{:S(2)}) copy-start(bf16[2,1024,5,64]{1,3,2,0:T(8,128)(2,1)S(1)} %get-tuple-element.1891) | copy-start | bytes 3932164
  168.8 78.1 %copy-start.8 = (bf16[128,5,3,64]{0,3,2,1:T(8,128)(2,1)}, bf16[128,5,3,64]{0,3,2,1:T(8,128)(2,1)S(1)}, u32[]{:S(2)}) copy-start(bf16[128,5,3,64]{0,3,2,1:T(8,128)(2,1)S(1)} %get-tuple-element.1892) | copy-start | bytes 737284
  168.8 78.1 %copy-start.117 = (s32[2,1024]{1,0:T(2,128)}, s32[2,1024]{1,0:T(2,128)S(1)}, u32[]{:S(2)}) copy-start(s32[2,1024]{1,0:T(2,128)S(1)} %get-tuple-element.1947) | copy-start | bytes 24580
  168.8 144.5 %copy-start.130 = (s32[128]{0:T(128)}, s32[128]{0:T(128)S(1)}, u32[]{:S(2)}) copy-start(s32[128]{0:T(128)S(1)} %get-tuple-element.1955) | copy-start | bytes 1540
  170.6 76.2 %copy-start.59 = (bf16[5,3,128,64]{2,3,1,0:T(8,128)(2,1)}, bf16[5,3,128,64]{2,3,1,0:T(8,128)(2,1)S(1)}, u32[]{:S(2)}) copy-start(bf16[5,3,128,64]{2,3,1,0:T(8,128)(2,1)S(1)} %multiply_convert_fusion.12) | copy-start | bytes 737284
  178.0 196.6 %copy-start.24 = (f32[128,960]{0,1:T(8,128)}, f32[128,960]{0,1:T(8,128)S(1)}, u32[]{:S(2)}) copy-start(f32[128,960]{0,1:T(8,128)S(1)} %get-tuple-element.1363) | copy-start | bytes 1474564
  178.1 135.2 %copy-start.152 = (f32[128]{0:T(128)}, f32[128]{0:T(128)S(1)}, u32[]{:S(2)}) copy-start(f32[128]{0:T(128)S(1)} %add_rsqrt_fusion.4) | copy-start | bytes 1540
  320.6 58.1 %copy-start.46 = (bf16[128,2560]{1,0:T(8,128)(2,1)}, bf16[128,2560]{1,0:T(8,128)(2,1)S(1)}, u32[]{:S(2)}) copy-start(bf16[128,2560]{1,0:T(8,128)(2,1)S(1)} %multiply_convert_fusion.2) | copy-start | bytes 1966084
  380.8 85.4 %copy-start.15 = (f32[96,960]{1,0:T(8,128)}, f32[96,960]{1,0:T(8,128)S(1)}, u32[]{:S(2)}) copy-start(f32[96,960]{1,0:T(8,128)S(1)} %gather_fusion.7) | copy-start | bytes 1105924
  410.7 34.5 %copy-start.98 = (bf16[96,15,32]{0,2,1:T(8,128)(2,1)S(1)}, bf16[96,15,32]{0,2,1:T(8,128)(2,1)}, u32[]{:S(2)}) copy-start(bf16[96,15,32]{0,2,1:T(8,128)(2,1)} %get-tuple-element.1329) | copy-start | bytes 276484
  410.7 34.6 %copy-start.63 = (f32[5,3,96,64]{2,3,1,0:T(8,128)S(1)}, f32[5,3,96,64]{2,3,1,0:T(8,128)}, u32[]{:S(2)}) copy-start(f32[5,3,96,64]{2,3,1,0:T(8,128)} %custom-call.6) | copy-start | bytes 1105924
  410.7 34.6 %copy-start.93 = (f32[5,3,96,64]{2,3,1,0:T(8,128)S(1)}, f32[5,3,96,64]{2,3,1,0:T(8,128)}, u32[]{:S(2)}) copy-start(f32[5,3,96,64]{2,3,1,0:T(8,128)} %custom-call.7) | copy-start | bytes 1105924
  410.7 34.6 %copy-start.109 = (f32[5,3,96]{2,1,0:T(4,128)S(1)}, f32[5,3,96]{2,1,0:T(4,128)}, u32[]{:S(2)}) copy-start(f32[5,3,96]{2,1,0:T(4,128)} %custom-call.5) | copy-start | bytes 17284
  410.7 34.6 %copy-start.126 = (s32[2,768]{1,0:T(2,128)S(1)}, s32[2,768]{1,0:T(2,128)}, u32[]{:S(2)}) copy-start(s32[2,768]{1,0:T(2,128)} %reshape_squeeze.4) | copy-start | bytes 18436
  410.7 34.6 %copy-start.132 = (s32[96]{0:T(128)S(1)}, s32[96]{0:T(128)}, u32[]{:S(2)}) copy-start(s32[96]{0:T(128)} %get-tuple-element.1783) | copy-start | bytes 1156
  460.0 236.4 %copy-start.27 = (f32[96,960]{1,0:T(8,128)}, f32[96,960]{1,0:T(8,128)S(1)}, u32[]{:S(2)}) copy-start(f32[96,960]{1,0:T(8,128)S(1)} %get-tuple-element.1365) | copy-start | bytes 1105924
  460.1 236.4 %copy-start.144 = (f32[96]{0:T(128)}, f32[96]{0:T(128)S(1)}, u32[]{:S(2)}) copy-start(f32[96]{0:T(128)S(1)} %add_rsqrt_fusion.2) | copy-start | bytes 1156
  470.0 211.5 %copy-start.18 = (f32[64,960]{1,0:T(8,128)}, f32[64,960]{1,0:T(8,128)S(1)}, u32[]{:S(2)}) copy-start(f32[64,960]{1,0:T(8,128)S(1)} %gather_fusion.8) | copy-start | bytes 737284
  470.2 211.3 %copy-start.150 = (f32[64]{0:T(128)}, f32[64]{0:T(128)S(1)}, u32[]{:S(2)}) copy-start(f32[64]{0:T(128)S(1)} %add_rsqrt_fusion.1) | copy-start | bytes 772
  472.8 25.2 %copy-start.81 = (pred[64,1024]{1,0:T(8,128)(4,1)S(1)}, pred[64,1024]{1,0:T(8,128)(4,1)}, u32[]{:S(2)}) copy-start(pred[64,1024]{1,0:T(8,128)(4,1)} %or_and_fusion.4) | copy-start | bytes 196612
  557.5 118.0 %reduce-scatter.13.cloned.1.call-start = ((), (), s32[]{:S(2)}) async-start(), calls=%async_computation.13 | async-start | bytes 1671168 | tf_op jit(solution)/shard_map/reduce_scatter | solution.py:434
  564.6 259.7 %reduce-scatter.21.cloned.1.call-start = ((), (), s32[]{:S(2)}) async-start(), calls=%async_computation.17 | async-start | bytes 2506752
  564.9 116.7 %copy-start.173 = (s32[64]{0:T(128)}, s32[64]{0:T(128)S(1)}, u32[]{:S(2)}) copy-start(s32[64]{0:T(128)S(1)} %fusion.203) | copy-start | bytes 772
  569.7 111.9 %copy-start.3 = (f32[128,960]{1,0:T(8,128)S(1)}, f32[128,960]{1,0:T(8,128)}, u32[]{:S(2)}) copy-start(f32[128,960]{1,0:T(8,128)} %copy-done.2) | copy-start | bytes 1474564
  762.2 128.3 %reduce-scatter.23.cloned.1.call-start = ((), (), s32[]{:S(2)}) async-start(), calls=%async_computation.18 | async-start | bytes 2506752
  764.0 127.6 %copy-start.16 = (f32[96,960]{1,0:T(8,128)S(1)}, f32[96,960]{1,0:T(8,128)}, u32[]{:S(2)}) copy-start(f32[96,960]{1,0:T(8,128)} %copy-done.15) | copy-start | bytes 1105924
  764.0 127.6 %copy-start.159 = (f32[96]{0:T(128)S(1)}, f32[96]{0:T(128)}, u32[]{:S(2)}) copy-start(f32[96]{0:T(128)} %copy-done.158) | copy-start | bytes 1156
  766.0 129.3 %copy-start.39 = (f32[96,960]{1,0:T(8,128)S(1)}, f32[96,960]{1,0:T(8,128)}, u32[]{:S(2)}) copy-start(f32[96,960]{1,0:T(8,128)} %copy-done.38) | copy-start | bytes 1105924
  766.0 129.3 %copy-start.43 = (f32[96,960]{1,0:T(8,128)S(1)}, f32[96,960]{1,0:T(8,128)}, u32[]{:S(2)}) copy-start(f32[96,960]{1,0:T(8,128)} %copy-done.41) | copy-start | bytes 1105924
  766.0 321.9 %reduce-scatter.15.cloned.1.call-start = ((), (), s32[]{:S(2)}) async-start(), calls=%async_computation.14 | async-start | bytes 2785280 | tf_op jit(solution)/shard_map/reduce_scatter | solution.py:433
  766.3 129.0 %copy-start.86 = (bf16[96,15,64]{0,2,1:T(8,128)(2,1)}, bf16[96,15,64]{0,2,1:T(8,128)(2,1)S(1)}, u32[]{:S(2)}) copy-start(bf16[96,15,64]{0,2,1:T(8,128)(2,1)S(1)} %pad_maximum_fusion.15) | copy-start | bytes 552964
  825.4 72.2 %copy-start.112 = (bf16[96,5,64]{0,2,1:T(8,128)(2,1)}, bf16[96,5,64]{0,2,1:T(8,128)(2,1)S(1)}, u32[]{:S(2)}) copy-start(bf16[96,5,64]{0,2,1:T(8,128)(2,1)S(1)} %pad_maximum_fusion.25) | copy-start | bytes 184324
  994.9 129.7 %reduce-scatter.17.cloned.1.call-start = ((), (), s32[]{:S(2)}) async-start(), calls=%async_computation.15 | async-start | bytes 2785280 | tf_op jit(solution)/shard_map/reduce_scatter | solution.py:434
  1034.6 21.8 %copy-start.17 = (f32[96,960]{1,0:T(8,128)S(1)}, f32[96,960]{1,0:T(8,128)}, u32[]{:S(2)}) copy-start(f32[96,960]{1,0:T(8,128)} %copy-done.15) | copy-start | bytes 1105924
  1034.6 21.8 %copy-start.87 = (bf16[96,15,64]{0,2,1:T(8,128)(2,1)S(1)}, bf16[96,15,64]{0,2,1:T(8,128)(2,1)}, u32[]{:S(2)}) copy-start(bf16[96,15,64]{0,2,1:T(8,128)(2,1)} %copy-done.86) | copy-start | bytes 552964
  1034.6 21.8 %copy-start.111 = (bf16[96,320]{0,1:T(8,128)(2,1)S(1)}, bf16[96,320]{0,1:T(8,128)(2,1)}, u32[]{:S(2)}) copy-start(bf16[96,320]{0,1:T(8,128)(2,1)} %copy-done.110) | copy-start | bytes 184324
  1034.6 21.8 %copy-start.113 = (bf16[96,5,64]{0,2,1:T(8,128)(2,1)S(1)}, bf16[96,5,64]{0,2,1:T(8,128)(2,1)}, u32[]{:S(2)}) copy-start(bf16[96,5,64]{0,2,1:T(8,128)(2,1)} %copy-done.112) | copy-start | bytes 184324
  1034.6 21.8 %copy-start.160 = (f32[96]{0:T(128)S(1)}, f32[96]{0:T(128)}, u32[]{:S(2)}) copy-start(f32[96]{0:T(128)} %copy-done.158) | copy-start | bytes 1156
  1034.6 697.8 %all-reduce.7.cloned.1.call-start = ((), (), s32[]{:S(2)}) async-start(), calls=%async_computation.19 | async-start | bytes 80609280 | tf_op jit(solution)/shard_map/psum | solution.py:456
  1062.1 17.0 slice-start.3
  1062.1 17.0 slice-start.4
  1064.8 15.9 slice-start.7
  1080.7 44.9 %copy-start.21 = (f32[128,960]{0,1:T(8,128)S(1)}, f32[128,960]{0,1:T(8,128)}, u32[]{:S(2)}) copy-start(f32[128,960]{0,1:T(8,128)} %copy-done.20) | copy-start | bytes 1474564
  1080.7 44.9 %copy-start.166 = (f32[128]{0:T(128)S(1)}, f32[128]{0:T(128)}, u32[]{:S(2)}) copy-start(f32[128]{0:T(128)} %copy-done.165) | copy-start | bytes 1540
  1142.9 48.1 %copy-start.5 = (f32[128,960]{1,0:T(8,128)S(1)}, f32[128,960]{1,0:T(8,128)}, u32[]{:S(2)}) copy-start(f32[128,960]{1,0:T(8,128)} %copy-done.4) | copy-start | bytes 1474564
  (145 other events, 686.6 us)
Sparse Core Ops, SparseCore 0:
  9.6 45.9 all-gather.9
  65.6 38.8 all-gather.13
  107.2 37.1 all-gather.11
  145.7 29.8 all-gather.15
  177.0 64.8 all-gather.17
  243.3 64.8 all-gather.19
  309.7 64.8 all-gather.21
  557.7 55.0 reduce-scatter.18
  616.9 58.5 reduce-scatter.12
  762.4 61.9 reduce-scatter.20
  828.6 61.9 reduce-scatter.22
  995.0 62.8 reduce-scatter.14
  1061.7 62.8 reduce-scatter.16
  1136.0 596.3 all-reduce.6
where the time goes:
time: 1780 us; the launch traced here: 1760 us
  waiting for transfers between devices  1020 us (57%)
  local copies, waits for them, and re-layouts  257 us (14%)
  matrix products  251 us (14%)
  blocking collectives  171 us (10%)
  other arithmetic  38.9 us (2%)
  between operations  18.2 us (1%)
    psum x1, waiting for transfers between devices, on_device(): lax.psum((part_query, part_key, part_value, acc_out, part_gate, part_up,...  539 us
    unnamed x17, waiting for transfers between devices  166 us
    reduce_scatter x2, waiting for transfers between devices, on_device(): lax.psum_scatter(value_gradients, 'ctx', scatter_dimension=0, tiled=True)  97.3 us
    dynamic_update_slice x8, local copies, waits for them, and re-layouts, attend_back(): lax.scan(sweep_back, initial_state, layout)  87.8 us
    all_gather x1, waiting for transfers between devices, on_device(): lax.all_gather(w_gate, 'ws', axis=0, tiled=True)  63.8 us
    all_gather x1, waiting for transfers between devices, on_device(): lax.all_gather(w_up, 'ws', axis=0, tiled=True)  61.3 us
    all_gather x1, waiting for transfers between devices, on_device(): lax.all_gather(w_down, 'ws', axis=0, tiled=True)  54 us
    unnamed x396, local copies, waits for them, and re-layouts  52.9 us
  transfers between devices with their start and end apart: 14, of which 12 were waited for; matrix products, arithmetic and copies ran while one was open for 13% of the time, Pallas kernels for 0%

commit v1 on v0

v1 whole, which is shorter than its diff:
```python
import functools

import jax
import jax.numpy as jnp
from jax import lax
from jax.experimental import pallas as pl
from jax.experimental.pallas import tpu as pltpu
from jax.sharding import PartitionSpec as P

QUERY_HEADS = 15
KEY_VALUE_HEADS = 5
HEAD_SIZE = 64
SHARE = QUERY_HEADS // KEY_VALUE_HEADS
BLK = 64
CONT_BITS = 10
EPSILON = 1e-05
ROPE_BASE = 10000.0
MASK_FLOOR = -1e30
SCALE = HEAD_SIZE ** (-0.5)

BF = jnp.bfloat16
F32 = jnp.float32
AXES = ("ctx", "ws")
FF_CHUNK = 512
VMEM_LIMIT = 60 * 1024 * 1024

Y_BIT, C_BIT, X_BIT, Z1_BIT, Z2_BIT = 1, 2, 4, 8, 16
NEAR = (0, X_BIT, Y_BIT, Z1_BIT, X_BIT | Y_BIT | Z1_BIT, X_BIT | Y_BIT, Y_BIT | Z1_BIT, Z1_BIT | X_BIT)


def hop(value, mask):
    return lax.ppermute(value, AXES, [(i, i ^ mask) for i in range(32)])


def swap_place(i):
    y, z2 = i & 1, (i >> 4) & 1
    return (i & ~(Y_BIT | Z2_BIT)) | (Z2_BIT if y else 0) | (Y_BIT if z2 else 0)


def move(value):
    return lax.ppermute(value, AXES, [(i, swap_place(i)) for i in range(32)])


def ctx_mask(mask):
    return (
        (1 if mask & C_BIT else 0)
        | (2 if mask & X_BIT else 0)
        | (4 if mask & Z1_BIT else 0)
        | (8 if mask & Y_BIT else 0)
    )


NT = (((1,), (1,)), ((), ()))
TN = (((0,), (0,)), ((), ()))
NN = (((1,), (0,)), ((), ()))


def mm(left, right, dims=NN, precision=None):
    return lax.dot_general(left, right, dims, precision=precision, preferred_element_type=F32)


def normed_rows(values):
    inverse = lax.rsqrt(jnp.mean(values * values, axis=-1, keepdims=True) + EPSILON)
    return values * inverse, inverse


def norm_back(grad_in, normed, inverse, gain):
    scaled = grad_in * gain
    return inverse * (scaled - normed * jnp.mean(scaled * normed, axis=-1, keepdims=True))


def turn(values, cosine, sine, back=False):
    rows, width = values.shape
    lane = lax.broadcasted_iota(jnp.int32, (rows, 128), 1)
    first = (lane & (HEAD_SIZE - 1)) < HEAD_SIZE // 2
    if back:
        sine = -sine
    pieces = []
    for start in range(0, width, 128):
        wide = min(128, width - start)
        part = values[:, start : start + wide]
        if wide < 128:
            part = jnp.concatenate([part, jnp.zeros((rows, 128 - wide), F32)], axis=1)
        other = jnp.where(first, pltpu.roll(part, 96, 1), pltpu.roll(part, 32, 1))
        pieces.append((part * cosine + other * sine)[:, :wide])
    return jnp.concatenate(pieces, axis=1)


def vm():
    return pl.BlockSpec(memory_space=pltpu.VMEM)


def sm():
    return pl.BlockSpec(memory_space=pltpu.SMEM)


def hbm():
    return pl.BlockSpec(memory_space=pl.ANY)


def shaped(shape, dtype):
    return jax.ShapeDtypeStruct(shape, dtype)


def params(**kw):
    return pltpu.CompilerParams(vmem_limit_bytes=VMEM_LIMIT, **kw)


def estimate(flops, nbytes):
    return pl.CostEstimate(flops=int(flops), bytes_accessed=int(nbytes), transcendentals=0)


class Weight:
    def __init__(self, shape, arrays, offsets):
        self.shape, self.arrays, self.offsets = shape, arrays, offsets


def start_weights(weights, refs, buffers, sems, coords):
    copies, at = [], 0
    for weight, buffer in zip(weights, buffers, strict=True):
        mine = []
        for offset in weight.offsets:
            ref = refs[at]
            row, col = offset(coords)
            rows, cols = ref.shape
            if not isinstance(row, int):
                row = pl.multiple_of(row, 16)
            if cols == buffer.shape[1]:
                target = buffer.at[pl.ds(row, rows), :]
            else:
                target = buffer.at[pl.ds(row, rows), pl.ds(pl.multiple_of(col, 128), cols)]
            copy = pltpu.make_async_copy(ref, target, sems.at[at])
            copy.start()
            mine.append(copy)
            at += 1
        copies.append(mine)
    return copies


def wait_all(copies):
    for copy in copies:
        copy.wait()


def read_coords(ref):
    return [ref[i] for i in range(4)]


def project(x, gain, wq, wk, wv, cosine, sine, first_ref, q_ref, kv_ref):
    normed, _ = normed_rows(x)
    first_in = (normed * gain).astype(BF)
    first_ref[...] = first_in
    key = turn(mm(first_in, wk[...]), cosine, sine)
    value = mm(first_in, wv[...])
    for h in range(KEY_VALUE_HEADS):
        at = slice(h * HEAD_SIZE, (h + 1) * HEAD_SIZE)
        kv_ref[:, h * 128 : (h + 1) * 128] = jnp.concatenate(
            [key[:, at], value[:, at]], axis=1
        ).astype(BF)
    query = (turn(mm(first_in, wq[...]), cosine, sine).astype(BF) * SCALE).astype(BF)
    wide = SHARE * HEAD_SIZE
    for h in range(KEY_VALUE_HEADS):
        q_ref[h] = query[:, h * wide : (h + 1) * wide]


def first_kernel(weights, n_pieces, coords_ref, x_ref, gain_ref, cos_ref, sin_ref, *rest):
    refs, rest = rest[:n_pieces], rest[n_pieces:]
    first_ref, q_ref, kv_ref, wq, wk, wv, sems = rest
    copies = start_weights(weights, refs, (wq, wk, wv), sems, read_coords(coords_ref))
    for mine in copies:
        wait_all(mine)
    project(
        x_ref[...].astype(F32), gain_ref[...], wq, wk, wv, cos_ref[...], sin_ref[...],
        first_ref, q_ref, kv_ref,
    )


def weight_scratch(weights):
    return [pltpu.VMEM(w.shape, BF) for w in weights]


def pieces_of(weights):
    return [a for w in weights for a in w.arrays]


def first_call(coords, tokens, gain, cosine, sine, weights):
    rows, width = tokens.shape
    kv_width = weights[1].shape[1]
    arrays = pieces_of(weights)
    return pl.pallas_call(
        functools.partial(first_kernel, weights, len(arrays)),
        name="first_projection",
        out_shape=(
            shaped((rows, width), BF),
            shaped((KEY_VALUE_HEADS, rows, SHARE * HEAD_SIZE), BF),
            shaped((rows, 2 * kv_width), BF),
        ),
        in_specs=[sm()] + [vm()] * 4 + [hbm()] * len(arrays),
        out_specs=(vm(), vm(), vm()),
        scratch_shapes=weight_scratch(weights) + [pltpu.SemaphoreType.DMA((len(arrays),))],
        compiler_params=params(),
        cost_estimate=estimate(2 * rows * width * 1600, 4e6),
    )(coords, tokens, gain, cosine, sine, *arrays)


def padded_heads(wide_rows, left):
    rows = wide_rows.shape[0]
    blank = jnp.zeros((rows, HEAD_SIZE), wide_rows.dtype)
    stacked = []
    for j in range(SHARE):
        part = wide_rows[:, j * HEAD_SIZE : (j + 1) * HEAD_SIZE]
        stacked.append(jnp.concatenate([part, blank] if left else [blank, part], axis=1))
    return jnp.concatenate(stacked, axis=0)


def attend_kernel(prompt, q_ref, a_ref, b_ref, kpos_ref, live_ref, qpos_ref, p_ref, o_ref, s_scr, bias_scr):
    rows = q_ref.shape[1]
    half = a_ref.shape[0]

    @pl.when(pl.program_id(0) == 0)
    def _():
        kpos = kpos_ref[...]
        klive = live_ref[...] > 0
        kseg = jnp.where(kpos < prompt, 0, 1 + ((kpos - prompt) >> CONT_BITS))

        def fill(i, carry):
            at = pl.ds(pl.multiple_of(i * 8, 8), 8)
            qpos = qpos_ref[at, :]
            qseg = jnp.where(qpos < prompt, 0, 1 + ((qpos - prompt) >> CONT_BITS))
            earlier = kpos <= qpos
            shared = (kseg == 0) | (kseg == qseg)
            seen = earlier & shared & (klive | (kpos == qpos))
            bias_scr[at, :] = jnp.where(seen, 0.0, MASK_FLOOR)
            return carry

        lax.fori_loop(0, rows // 8, fill, 0)

    stacked = padded_heads(q_ref[0], True)
    s_scr[:, :half] = mm(stacked, a_ref[...], NT)
    s_scr[:, half:] = mm(stacked, b_ref[...], NT)
    steps = rows // 16

    def soften(i, carry):
        at = pl.ds(pl.multiple_of(i * 16, 16), 16)
        bias_at = pl.ds(pl.multiple_of(lax.rem(i, steps) * 16, 16), 16)
        scores = s_scr[at, :] + bias_scr[bias_at, :]
        top = jnp.max(scores, axis=-1, keepdims=True)
        weights = jnp.exp(scores - top)
        mass = jnp.sum(weights, axis=-1, keepdims=True)
        p_ref[0, at, :] = (weights * (1.0 / mass)).astype(BF)
        return carry

    lax.fori_loop(0, SHARE * steps, soften, 0)
    mixed = mm(p_ref[0, :, :half], a_ref[...]) + mm(p_ref[0, :, half:], b_ref[...])
    o_ref[0] = jnp.concatenate(
        [mixed[j * rows : (j + 1) * rows, HEAD_SIZE:] for j in range(SHARE)], axis=1
    ).astype(BF)


def attend_call(query, part_a, part_b, kpos, klive, qpos, prompt):
    heads, rows, wide = query.shape
    half = part_a.shape[0]
    keys = 2 * half
    return pl.pallas_call(
        functools.partial(attend_kernel, prompt),
        name="attend",
        grid=(heads,),
        out_shape=(shaped((heads, SHARE * rows, keys), BF), shaped((heads, rows, wide), BF)),
        in_specs=[
            pl.BlockSpec((1, rows, wide), lambda h: (h, 0, 0)),
            pl.BlockSpec((half, 128), lambda h: (0, h)),
            pl.BlockSpec((half, 128), lambda h: (0, h)),
            pl.BlockSpec((1, keys), lambda h: (0, 0)),
            pl.BlockSpec((1, keys), lambda h: (0, 0)),
            pl.BlockSpec((rows, 1), lambda h: (0, 0)),
        ],
        out_specs=(
            pl.BlockSpec((1, SHARE * rows, keys), lambda h: (h, 0, 0)),
            pl.BlockSpec((1, rows, wide), lambda h: (h, 0, 0)),
        ),
        scratch_shapes=[pltpu.VMEM((SHARE * rows, keys), F32), pltpu.VMEM((rows, keys), F32)],
        compiler_params=params(dimension_semantics=("arbitrary",)),
        cost_estimate=estimate(8 * heads * SHARE * rows * keys * 128, heads * SHARE * rows * keys * 2),
    )(query, part_a, part_b, kpos, klive, qpos)


def attend_back_kernel(q_ref, do_ref, a_ref, b_ref, p_ref, dq_ref, da_ref, db_ref, dp_scr, ds_scr):
    rows = q_ref.shape[1]
    half = a_ref.shape[0]
    stacked = padded_heads(q_ref[0], True)
    grads = padded_heads(do_ref[0], False)
    dp_scr[:, :half] = mm(grads, a_ref[...], NT)
    dp_scr[:, half:] = mm(grads, b_ref[...], NT)

    def soften(i, carry):
        at = pl.ds(pl.multiple_of(i * 16, 16), 16)
        weights = p_ref[0, at, :].astype(F32)
        dp = dp_scr[at, :]
        delta = jnp.sum(weights * dp, axis=-1, keepdims=True)
        ds_scr[at, :] = (weights * (dp - delta)).astype(BF)
        return carry

    lax.fori_loop(0, SHARE * rows // 16, soften, 0)
    dq = (mm(ds_scr[:, :half], a_ref[...]) + mm(ds_scr[:, half:], b_ref[...])) * SCALE
    dq_ref[0] = jnp.concatenate(
        [dq[j * rows : (j + 1) * rows, :HEAD_SIZE] for j in range(SHARE)], axis=1
    )
    for at, out in ((slice(0, half), da_ref), (slice(half, 2 * half), db_ref)):
        turned = mm(stacked, ds_scr[:, at], TN) + mm(grads, p_ref[0, :, at], TN)
        out[...] = turned.T.astype(out.dtype)


def attend_back_call(query, d_out, part_a, part_b, weights):
    heads, rows, wide = query.shape
    half = part_a.shape[0]
    keys = 2 * half
    return pl.pallas_call(
        attend_back_kernel,
        name="attend_back",
        grid=(heads,),
        out_shape=(
            shaped((heads, rows, wide), F32),
            shaped((half, heads * 128), F32),
            shaped((half, heads * 128), BF),
        ),
        in_specs=[
            pl.BlockSpec((1, rows, wide), lambda h: (h, 0, 0)),
            pl.BlockSpec((1, rows, wide), lambda h: (h, 0, 0)),
            pl.BlockSpec((half, 128), lambda h: (0, h)),
            pl.BlockSpec((half, 128), lambda h: (0, h)),
            pl.BlockSpec((1, SHARE * rows, keys), lambda h: (h, 0, 0)),
        ],
        out_specs=(
            pl.BlockSpec((1, rows, wide), lambda h: (h, 0, 0)),
            pl.BlockSpec((half, 128), lambda h: (0, h)),
            pl.BlockSpec((half, 128), lambda h: (0, h)),
        ),
        scratch_shapes=[
            pltpu.VMEM((SHARE * rows, keys), F32),
            pltpu.VMEM((SHARE * rows, keys), BF),
        ],
        compiler_params=params(dimension_semantics=("arbitrary",)),
        cost_estimate=estimate(16 * heads * SHARE * rows * keys * 128, heads * SHARE * rows * keys * 2),
    )(query, d_out, part_a, part_b, weights)


def picks(sel_ref, total_rows):
    capacity = sel_ref.shape[1]
    row = lax.broadcasted_iota(jnp.int32, (total_rows, capacity), 0)
    return row == sel_ref[...]


def live_column(live_ref, rows):
    count = jnp.sum(live_ref[:, :].astype(F32), axis=1, keepdims=True)
    return lax.broadcasted_iota(jnp.int32, (rows, 1), 0).astype(F32) < count


def feed_forward(x, ao_ref, gain_two, wo, wg, wu, wd, waits, ao_out, mid_ref, second_ref, g_ref, u_ref, hid_ref, y_scr):
    rows = x.shape[0]
    mixed = jnp.concatenate([ao_ref[h] for h in range(KEY_VALUE_HEADS)], axis=1)
    ao_out[...] = mixed
    wait_all(waits[0])
    middle = x + mm(mixed, wo[...])
    mid_ref[...] = middle
    normed, _ = normed_rows(middle)
    second_ref[...] = (normed * gain_two).astype(BF)
    y_scr[...] = middle
    for mine in waits[1:]:
        wait_all(mine)

    def chunk(j, carry):
        at = pl.ds(pl.multiple_of(j * FF_CHUNK, FF_CHUNK), FF_CHUNK)
        second = second_ref[...]
        g = mm(second, wg[:, at])
        u = mm(second, wu[:, at])
        g_ref[:, at] = g
        u_ref[:, at] = u
        hidden = (g / (1.0 + jnp.exp(-g)) * u).astype(BF)
        hid_ref[:, at] = hidden
        y_scr[...] += mm(hidden, wd[at, :])
        return carry

    lax.fori_loop(0, wg.shape[1] // FF_CHUNK, chunk, 0)


def dense_kernel(step, weights, n_pieces, *args):
    args = list(args)
    take = lambda k: [args.pop(0) for _ in range(k)]
    coords_ref, x_ref, ao_ref, gain1_ref, gain2_ref = take(5)
    if step == 0:
        sel_ref, cos_ref, sin_ref = take(3)
    elif step == 1:
        live_ref, cos_ref, sin_ref = take(3)
    else:
        sel_ref, live2_ref, live_ref, h1_ref, h2_ref = take(5)
    refs = take(n_pieces)
    ao_out, mid_ref, second_ref, g_ref, u_ref, hid_ref = take(6)
    if step < 2:
        h_ref, next_ref, first_ref, q_ref, kv_ref = take(5)
    else:
        (out_ref,) = take(1)
    buffers = take(len(weights))
    y_scr, sems = take(2)
    waits = start_weights(weights, refs, buffers, sems, read_coords(coords_ref))
    rows = x_ref.shape[0]
    x = x_ref[...].astype(F32)
    wo, wg, wu, wd = buffers[:4]
    feed_forward(
        x, ao_ref, gain2_ref[...], wo, wg, wu, wd, waits[:4], ao_out, mid_ref, second_ref,
        g_ref, u_ref, hid_ref, y_scr,
    )
    for mine in waits[4:]:
        wait_all(mine)
    updated = y_scr[...]
    if step == 0:
        h_ref[...] = updated
        chosen = picks(sel_ref, rows).astype(F32)
        following = mm(chosen, updated, TN, lax.Precision.HIGHEST)
    else:
        updated = jnp.where(live_column(live_ref, rows), updated, x)
    if step == 1:
        h_ref[...] = updated
        following = updated[: next_ref.shape[0]]
    if step < 2:
        next_ref[...] = following
        project(
            following, gain1_ref[...], *buffers[4:], cos_ref[...], sin_ref[...],
            first_ref, q_ref, kv_ref,
        )
    else:
        slots = jnp.concatenate([updated, h2_ref[rows:, :]], axis=0).astype(BF)
        hit = picks(sel_ref, h1_ref.shape[0]) & (live2_ref[...] > 0)
        placed = mm(hit.astype(BF), slots)
        any_hit = jnp.sum(hit.astype(F32), axis=1, keepdims=True) > 0.5
        out_ref[...] = jnp.where(any_hit, placed, h1_ref[...]).astype(BF)


def dense_call(step, coords, x, mixed, gain1, gain2, extra, weights, next_rows):
    rows, width = x.shape
    hidden = weights[1].shape[1]
    arrays = pieces_of(weights)
    outs = [
        shaped((rows, width), BF),
        shaped((rows, width), F32),
        shaped((rows, width), BF),
        shaped((rows, hidden), F32),
        shaped((rows, hidden), F32),
        shaped((rows, hidden), BF),
    ]
    if step < 2:
        kv_width = weights[5].shape[1]
        outs += [
            shaped((rows, width), F32),
            shaped((next_rows, width), F32),
            shaped((next_rows, width), BF),
            shaped((KEY_VALUE_HEADS, next_rows, SHARE * HEAD_SIZE), BF),
            shaped((next_rows, 2 * kv_width), BF),
        ]
    else:
        outs += [shaped((next_rows, width), BF)]
    return pl.pallas_call(
        functools.partial(dense_kernel, step, weights, len(arrays)),
        name=f"dense_{step}",
        out_shape=tuple(outs),
        in_specs=[sm()] + [vm()] * (4 + len(extra)) + [hbm()] * len(arrays),
        out_specs=tuple(vm() for _ in outs),
        scratch_shapes=weight_scratch(weights)
        + [pltpu.VMEM((rows, width), F32), pltpu.SemaphoreType.DMA((len(arrays),))],
        compiler_params=params(),
        cost_estimate=estimate(2 * rows * 9.83e6, 2.4e7),
    )(coords, x, mixed, gain1, gain2, *extra, *arrays)


def feed_back(d_y, mid_ref, g_ref, u_ref, gain_two, wd, wg, wu, wo, waits, dyb_ref, dg_ref, du_ref, dmid_ref, dz_ref, dao_ref, sum_ref, acc_scr):
    dyb_ref[...] = d_y.astype(BF)
    acc_scr[...] = jnp.zeros_like(acc_scr)
    for mine in waits[:3]:
        wait_all(mine)

    def chunk(j, carry):
        at = pl.ds(pl.multiple_of(j * FF_CHUNK, FF_CHUNK), FF_CHUNK)
        d_hidden = mm(dyb_ref[...], wd[at, :], NT)
        g, u = g_ref[:, at], u_ref[:, at]
        sigma = 1.0 / (1.0 + jnp.exp(-g))
        d_gate = (d_hidden * u * sigma * (1.0 + g * (1.0 - sigma))).astype(BF)
        d_up = (d_hidden * (g * sigma)).astype(BF)
        dg_ref[:, at] = d_gate
        du_ref[:, at] = d_up
        acc_scr[...] += mm(d_gate, wg[:, at], NT) + mm(d_up, wu[:, at], NT)
        return carry

    lax.fori_loop(0, wg.shape[1] // FF_CHUNK, chunk, 0)
    d_second = acc_scr[...]
    normed, inverse = normed_rows(mid_ref[...])
    sum_ref[...] = jnp.sum(d_second * normed, axis=0, keepdims=True)
    d_mid = norm_back(d_second, normed, inverse, gain_two) + d_y
    dmid_ref[...] = d_mid
    d_low = d_mid.astype(BF)
    dz_ref[...] = d_low
    wait_all(waits[3])
    d_mixed = mm(d_low, wo[...], NT).astype(BF)
    wide = SHARE * HEAD_SIZE
    for h in range(KEY_VALUE_HEADS):
        dao_ref[h] = d_mixed[:, h * wide : (h + 1) * wide]


def project_back(own_ref, others, dq_ref, x, dmid_ref, gain_one, cosine, sine, wq, wk, wv, waits, dql_ref, dkl_ref, dvl_ref, sum_ref):
    total = own_ref[...].astype(F32)
    for other in others:
        total = total + other[...].astype(F32)
    d_key = jnp.concatenate(
        [total[:, h * 128 : h * 128 + HEAD_SIZE] for h in range(KEY_VALUE_HEADS)], axis=1
    )
    d_value = jnp.concatenate(
        [total[:, h * 128 + HEAD_SIZE : (h + 1) * 128] for h in range(KEY_VALUE_HEADS)], axis=1
    )
    d_query = jnp.concatenate([dq_ref[h] for h in range(KEY_VALUE_HEADS)], axis=1)
    dql_ref[...] = turn(d_query, cosine, sine, True).astype(BF)
    dkl_ref[...] = turn(d_key, cosine, sine, True).astype(BF)
    dvl_ref[...] = d_value.astype(BF)
    for mine in waits:
        wait_all(mine)
    d_first = (
        mm(dql_ref[...], wq[...], NT)
        + mm(dkl_ref[...], wk[...], NT)
        + mm(dvl_ref[...], wv[...], NT)
    )
    normed, inverse = normed_rows(x)
    sum_ref[...] = jnp.sum(d_first * normed, axis=0, keepdims=True)
    return norm_back(d_first, normed, inverse, gain_one) + dmid_ref[...]


def back_kernel(phase, weights, n_pieces, n_parts, *args):
    args = list(args)
    take = lambda k: [args.pop(0) for _ in range(k)]
    (coords_ref,) = take(1)
    if phase > 0:
        gain1_ref, cos_ref, sin_ref, x_ref, dmid_in, dq_ref = take(6)
        own_ref, *others = take(n_parts)
    if phase < 3:
        gain2_ref, mid_ref, g_ref, u_ref = take(4)
    if phase == 0:
        cot_ref, sel_ref, live3_ref = take(3)
    elif phase == 1:
        slots_ref, live3_ref, live2_ref = take(3)
    elif phase == 2:
        cot_ref, sel_ref, live2_ref = take(3)
    refs = take(n_pieces)
    if phase > 0:
        dql_ref, dkl_ref, dvl_ref, sum1_ref = take(4)
    if phase < 3:
        dyb_ref, dg_ref, du_ref, dmid_ref, dz_ref, dao_ref, sum2_ref = take(7)
    if phase == 0:
        (slots_out,) = take(1)
    elif phase == 3:
        (grad_ref,) = take(1)
    buffers = take(len(weights))
    if phase < 3:
        (acc_scr,) = take(1)
    (sems,) = take(1)
    waits = start_weights(weights, refs, buffers, sems, read_coords(coords_ref))
    at = 0
    if phase > 0:
        d_x = project_back(
            own_ref, others, dq_ref, x_ref[...].astype(F32), dmid_in, gain1_ref[...],
            cos_ref[...], sin_ref[...], *buffers[:3], waits[:3], dql_ref, dkl_ref, dvl_ref, sum1_ref,
        )
        at = 3
    if phase == 0:
        chosen = picks(sel_ref, cot_ref.shape[0]).astype(BF)
        slots = mm(chosen, cot_ref[...], TN)
        slots_out[...] = slots
        rows = mid_ref.shape[0]
        d_y = jnp.where(live_column(live3_ref, rows), slots[:rows], 0.0)
    elif phase == 1:
        rows = x_ref.shape[0]
        slots = slots_ref[...]
        head = jnp.where(live_column(live3_ref, rows), d_x, slots[:rows])
        slots = jnp.concatenate([head, slots[rows:]], axis=0)
        d_y = jnp.where(live_column(live2_ref, slots.shape[0]), slots, 0.0)
    elif phase == 2:
        hit = picks(sel_ref, cot_ref.shape[0]) & (live2_ref[...] > 0)
        placed = mm(hit.astype(F32), d_x, NN, lax.Precision.HIGHEST)
        any_hit = jnp.sum(hit.astype(F32), axis=1, keepdims=True) > 0.5
        d_y = jnp.where(any_hit, placed, cot_ref[...].astype(F32))
    else:
        grad_ref[...] = d_x
        return
    feed_back(
        d_y, mid_ref, g_ref, u_ref, gain2_ref[...], *buffers[at : at + 4], waits[at : at + 4],
        dyb_ref, dg_ref, du_ref, dmid_ref, dz_ref, dao_ref, sum2_ref, acc_scr,
    )


def back_call(phase, coords, before, parts, after, extra, weights, rows_next):
    arrays = pieces_of(weights)
    ins = list(before) + list(parts) + list(after) + list(extra)
    outs, scratch = [], weight_scratch(weights)
    if phase > 0:
        rows, width = before[3].shape
        kv_width = weights[1].shape[1]
        outs += [
            shaped((rows, width), BF),
            shaped((rows, kv_width), BF),
            shaped((rows, kv_width), BF),
            shaped((1, width), F32),
        ]
    if phase < 3:
        rows, hidden = after[2].shape
        width = after[1].shape[1]
        outs += [
            shaped((rows, width), BF),
            shaped((rows, hidden), BF),
            shaped((rows, hidden), BF),
            shaped((rows, width), F32),
            shaped((rows, width), BF),
            shaped((KEY_VALUE_HEADS, rows, SHARE * HEAD_SIZE), BF),
            shaped((1, width), F32),
        ]
        scratch += [pltpu.VMEM((rows, width), F32)]
    if phase == 0:
        outs += [shaped((rows_next, width), F32)]
    elif phase == 3:
        outs += [shaped((rows, width), F32)]
    return pl.pallas_call(
        functools.partial(back_kernel, phase, weights, len(arrays), len(parts)),
        name=f"back_{phase}",
        out_shape=tuple(outs),
        in_specs=[sm()] + [vm()] * len(ins) + [hbm()] * len(arrays),
        out_specs=tuple(vm() for _ in outs),
        scratch_shapes=scratch + [pltpu.SemaphoreType.DMA((len(arrays),))],
        compiler_params=params(),
        cost_estimate=estimate(2 * rows * 9.83e6, 2.4e7),
    )(coords, *ins, *arrays)


def stack_rows(refs, scratch):
    at = 0
    for ref in refs:
        scratch[at : at + ref.shape[0], :] = ref[...]
        at += ref.shape[0]


def put_blocks(value, x_of, coords, ref, per_row):
    y, _, x, z = coords
    depth = ref.shape[-2]
    for ya in range(2):
        for xa in range(2) if per_row else (None,):
            for za in range(4):
                row = (ya * (2 if per_row else 1) + (xa or 0)) * 4 + za
                ref[y ^ ya, (x ^ xa) if per_row else x_of, z ^ za] = value[
                    row * depth : (row + 1) * depth
                ].astype(BF)


def grad_cols_kernel(n_steps, coords_ref, *args):
    left, args = args[:n_steps], args[n_steps:]
    right, args = args[:n_steps], args[n_steps:]
    keep_ref, send_ref, l_scr, r_scr = args
    coords = read_coords(coords_ref)
    _, c, x, _ = coords
    stack_rows(left, l_scr)
    stack_rows(right, r_scr)
    block = keep_ref.shape[-1]
    for far, ref in ((1, send_ref), (0, keep_ref)):

        def body(rx, carry, far=far, ref=ref):
            start = pl.multiple_of(((c ^ far) * 2 + (x ^ rx)) * block, 128)
            value = mm(l_scr[...], r_scr[:, pl.ds(start, block)], TN)
            put_blocks(value, rx, coords, ref, False)
            return carry

        lax.fori_loop(0, 2, body, 0)


def grad_rows_kernel(n_steps, coords_ref, *args):
    left, args = args[:n_steps], args[n_steps:]
    right, args = args[:n_steps], args[n_steps:]
    keep_ref, send_ref, l_scr, r_scr = args
    coords = read_coords(coords_ref)
    y, c, x, z = coords
    stack_rows(left, l_scr)
    stack_rows(right, r_scr)
    depth = keep_ref.shape[-2]
    span = 8 * depth
    for far, ref in ((1, send_ref), (0, keep_ref)):

        def body(ry, carry, far=far, ref=ref):
            start = pl.multiple_of(((y ^ ry) * 2 + (c ^ far)) * span, 128)
            value = mm(l_scr[:, pl.ds(start, span)], r_scr[...], TN)
            for xa in range(2):
                for za in range(4):
                    row = (xa * 4 + za) * depth
                    ref[ry, x ^ xa, z ^ za] = value[row : row + depth].astype(BF)
            return carry

        lax.fori_loop(0, 2, body, 0)


def grad_mixed_kernel(n_steps, coords_ref, *args):
    groups = []
    for _ in range(6):
        groups.append(args[:n_steps])
        args = args[n_steps:]
    first, mixed, dq, dk, dv, dz = groups
    keep_ref, send_ref, first_scr, mixed_scr, q_scr, k_scr, v_scr, z_scr, val_scr = args
    coords = read_coords(coords_ref)
    _, c, x, _ = coords
    for refs, scr in zip(groups, (first_scr, mixed_scr, q_scr, k_scr, v_scr, z_scr), strict=True):
        stack_rows(refs, scr)
    block = keep_ref.shape[-1]
    edge = q_scr.shape[1] - block
    for ca in range(2):
        for xa in range(2):
            wide, left = (q_scr, first_scr) if ca == 0 else (z_scr, mixed_scr)
            thin = k_scr if ca == 0 else v_scr
            if xa == 0:
                val_scr[...] = mm(left[...], wide[:, :block], TN)
            else:
                val_scr[...] = jnp.concatenate(
                    [mm(left[...], wide[:, block:], TN), mm(first_scr[...], thin[...], TN)], axis=1
                )

            @pl.when(c == ca)
            def _(xa=xa):
                put_blocks(val_scr[...], x ^ xa, coords, keep_ref, False)

            @pl.when(c != ca)
            def _(xa=xa):
                put_blocks(val_scr[...], x ^ xa, coords, send_ref, False)


def grad_call(kind, coords, groups):
    n_steps = len(groups[0])
    rows = sum(a.shape[0] for a in groups[0])
    width, cols = groups[0][0].shape[1], groups[1][0].shape[1]
    scratch = [pltpu.VMEM((rows, g[0].shape[1]), BF) for g in groups]
    if kind == "rows":
        kernel, block = grad_rows_kernel, (width // 32, cols)
    elif kind == "cols":
        kernel, block = grad_cols_kernel, (width // 8, cols // 4)
    else:
        total = sum(g[0].shape[1] for g in groups[2:])
        kernel, block = grad_mixed_kernel, (width // 8, total // 4)
        scratch += [pltpu.VMEM((width, block[1]), F32)]
    out = shaped((2, 2, 4) + block, BF)
    ins = [a for g in groups for a in g]
    return pl.pallas_call(
        functools.partial(kernel, n_steps),
        name=f"grad_{kind}",
        out_shape=(out, out),
        in_specs=[sm()] + [vm()] * len(ins),
        out_specs=(vm(), vm()),
        scratch_shapes=scratch,
        compiler_params=params(),
        cost_estimate=estimate(2 * rows * 16 * 2 * block[0] * block[1], 1e7),
    )(coords, *ins)


def place_cols_kernel(coords_ref, near_ref, far_ref, *outs):
    _, c, x, z = read_coords(coords_ref)
    depth, block = near_ref.shape[-2:]
    target = outs[-1] if len(outs) > 1 else outs[0]
    for far, ref in ((0, near_ref), (1, far_ref)):
        for rx in range(2):
            cols = pl.ds(pl.multiple_of(((c ^ far) * 2 + (x ^ rx)) * block, 128), block)
            for rz in range(4):
                rows = pl.ds(pl.multiple_of((z ^ rz) * depth, 8), depth)
                target[rows, cols] = ref[rx, rz].astype(F32)
    if len(outs) > 1:
        at = 0
        for out in outs[:-1]:
            out[...] = target[:, at : at + out.shape[1]]
            at += out.shape[1]


def place_rows_kernel(coords_ref, near_ref, far_ref, out_ref):
    _, c, x, z = read_coords(coords_ref)
    depth = near_ref.shape[-2]
    for far, ref in ((0, near_ref), (1, far_ref)):
        for rx in range(2):
            for rz in range(4):
                row = (((c ^ far) * 2 + (x ^ rx)) * 4 + (z ^ rz)) * depth
                out_ref[pl.ds(pl.multiple_of(row, 8), depth), :] = ref[rx, rz].astype(F32)


def place_call(kind, coords, near, far, widths):
    depth, block = near.shape[-2:]
    scratch = []
    if kind == "rows":
        kernel, outs = place_rows_kernel, (shaped((16 * depth, block), F32),)
    else:
        kernel = place_cols_kernel
        outs = tuple(shaped((4 * depth, w), F32) for w in widths)
        if len(outs) > 1:
            scratch = [pltpu.VMEM((4 * depth, 4 * block), F32)]
    return pl.pallas_call(
        kernel,
        name=f"place_{kind}",
        out_shape=outs,
        in_specs=[sm(), vm(), vm()],
        out_specs=tuple(vm() for _ in outs),
        scratch_shapes=scratch,
        compiler_params=params(),
        cost_estimate=estimate(0, 1e7),
    )(coords, near, far)


def low_sum(left, right):
    return (left.astype(F32) + right.astype(F32)).astype(BF)


def gather_keys(kv, near):
    if not near:
        whole = lax.all_gather(kv, "ctx", axis=0, tiled=True)
        half = whole.shape[0] // 2
        return whole[:half], whole[half:]
    by_x, by_y, by_z = hop(kv, X_BIT), hop(kv, Y_BIT), hop(kv, Z1_BIT)
    across = hop(kv, X_BIT | Y_BIT | Z1_BIT)
    pieces = [kv, by_x, by_y, by_z, across, hop(by_x, Y_BIT), hop(by_y, Z1_BIT), hop(by_z, X_BIT)]
    part = jnp.concatenate(pieces, axis=0)
    return part, hop(part, C_BIT)


def scatter_keys(part_a, part_b, near):
    if not near:
        whole = jnp.concatenate([part_a, part_b.astype(F32)], axis=0)
        return [lax.psum_scatter(whole, "ctx", scatter_dimension=0, tiled=True)]
    total = part_a + hop(part_b, C_BIT).astype(F32)
    rows = total.shape[0] // len(NEAR)
    parts = [total[:rows]]
    low = total[rows:].astype(BF)
    for i, mask in enumerate(NEAR[1:]):
        parts.append(hop(low[i * rows : (i + 1) * rows], mask))
    return parts


def quarter(value, axis, index):
    size = value.shape[axis] // 4
    return lax.dynamic_slice_in_dim(value, index * size, size, axis)


def half_rows(value, index):
    size = value.shape[0] // 2
    return lax.dynamic_slice_in_dim(value, index * size, size, 0)


def whole_weight(own, near, coords, spread):
    rows, cols = own.shape
    shape = (2 * rows, cols)
    if not near:
        return Weight(shape, [lax.all_gather(own, "ws", axis=0, tiled=True)], [lambda k: (0, 0)])
    y, c, x, z = coords
    arrays, offsets = [own], [lambda k: (k[0] * rows, 0)]
    cut = own
    if spread is not None:
        cut = quarter(own, 1 if spread == "cols" else 0, x * 2 + (z & 1))
    mine = hop(half_rows(cut, c), Y_BIT)
    shared = [(mine, 0, 0)]
    if spread is not None:
        shared += [
            (hop(mine, X_BIT), 1, 0),
            (hop(mine, Z1_BIT), 0, 1),
            (hop(mine, X_BIT | Z1_BIT), 1, 1),
        ]
    depth, wide = mine.shape
    for far in (0, 1):
        for value, rx, rz in shared:
            arrays.append(hop(value, C_BIT) if far else value)

            def offset(k, far=far, rx=rx, rz=rz):
                ky, kc, kx, kz = k
                part = (kx ^ rx) * 2 + ((kz & 1) ^ rz)
                row = (1 - ky) * rows + (kc ^ far) * depth
                if spread == "cols":
                    return row, part * wide
                if spread == "rows":
                    return row + part * 2 * depth, 0
                return row, 0

            offsets.append(offset)
    return Weight(shape, arrays, offsets)


def reduce_blocks(keep, send, near, coords):
    if not near:
        both = lax.psum(jnp.stack([keep, send]).astype(F32), AXES)
        mine = lax.dynamic_index_in_dim(both, coords[0], 1, keepdims=False)
        return mine[0], mine[1]
    total = low_sum(keep, hop(send, C_BIT))
    total = low_sum(total[0], hop(total[1], Y_BIT))
    total = low_sum(total[0], hop(total[1], X_BIT))
    total = low_sum(total[:2], hop(total[2:], Z2_BIT))
    total = low_sum(total[0], hop(total[1], Z1_BIT))
    total = jnp.stack([total, hop(total, Z1_BIT)])
    total = jnp.concatenate([total, hop(total, Z2_BIT)])
    total = jnp.stack([total, hop(total, X_BIT)])
    return total, hop(total, C_BIT)


def sum_everywhere(value, near):
    if not near:
        return lax.psum(value, AXES)
    for mask in (C_BIT, X_BIT, Y_BIT, Z1_BIT, Z2_BIT):
        value = value + hop(value, mask)
    return value


def on_device(
    tokens, cotangent, w_query, key_weight, value_weight, w_out, w_gate, w_up, w_down,
    gain_attn, gain_ffn, block_order, sel_mid, live_mid, sel_last, live_last,
):
    ctx_count, ws_count = lax.axis_size("ctx"), lax.axis_size("ws")
    near = ctx_count == 16 and ws_count == 2
    ctx, y = lax.axis_index("ctx"), lax.axis_index("ws")
    tok_local = tokens.shape[1]
    cap_mid, cap_last = sel_mid.shape[1] // ctx_count, sel_last.shape[1] // ctx_count
    if near:
        c, x, z = ctx & 1, (ctx >> 1) & 1, ctx >> 2
        places = (y, c, x, z)
        here = (ctx & 7) | (y << 3)
        order = here ^ jnp.array([ctx_mask(m) for m in NEAR] + [ctx_mask(m) | 1 for m in NEAR], jnp.int32)
        relocate = move
    else:
        zero = jnp.int32(0)
        places = (y, zero, zero, zero)
        here = ctx
        order = jnp.arange(ctx_count, dtype=jnp.int32)
        relocate = lambda v: v
    own_first = near
    coords = jnp.stack([jnp.asarray(v, jnp.int32) for v in places])
    block_coords = coords if near else jnp.zeros((4,), jnp.int32)

    tok = relocate(tokens[0])
    plan = relocate(
        jnp.concatenate(
            [
                sel_mid.reshape(ctx_count, cap_mid),
                live_mid.reshape(ctx_count, cap_mid),
                live_last.reshape(ctx_count, cap_last),
            ],
            axis=1,
        )
    )
    weight_q = whole_weight(w_query, near, places, None)
    weight_k = whole_weight(key_weight, near, places, None)
    weight_v = whole_weight(value_weight, near, places, None)
    gains = jnp.concatenate([gain_attn.reshape(1, -1), gain_ffn.reshape(1, -1)], axis=0)
    if near:
        other = hop(gains, Y_BIT)
        gains = jnp.where(
            y == 0,
            jnp.concatenate([gains, other], axis=1),
            jnp.concatenate([other, gains], axis=1),
        )
    else:
        gains = lax.all_gather(gains, "ws", axis=1, tiled=True)
    gains = gains.astype(F32)
    gain1, gain2 = gains[0:1], gains[1:2]
    weight_g = whole_weight(w_gate, near, places, "cols")
    weight_u = whole_weight(w_up, near, places, "cols")
    weight_d = whole_weight(w_down, near, places, "rows")
    weight_o = whole_weight(w_out, near, places, None)
    cot = relocate(cotangent[0])

    per_device = tok_local // BLK
    blocks = jnp.take(block_order.reshape(ctx_count, per_device), order, axis=0)
    plan_order = jnp.take(plan, order, axis=0)
    sel_all = plan_order[:, :cap_mid]
    live_two = plan_order[:, cap_mid : 2 * cap_mid]
    live_three = plan_order[:, 2 * cap_mid :]
    place_one = (blocks[:, :, None] * BLK + jnp.arange(BLK, dtype=jnp.int32)).reshape(ctx_count, tok_local)
    place_two = sum(
        jnp.where(sel_all // BLK == k, blocks[:, k : k + 1], 0) for k in range(per_device)
    ) * BLK + sel_all % BLK
    place_three = place_two[:, :cap_last]
    if own_first:
        mine = lambda v: v[0:1]
    else:
        mine = lambda v: lax.dynamic_slice_in_dim(v, here, 1, 0)
    sel_own, live2_own, live3_own = mine(sel_all), mine(live_two), mine(live_three)
    own_places = jnp.concatenate([mine(place_one), mine(place_two)], axis=1).reshape(-1, 1)
    frequency = ROPE_BASE ** (-jnp.arange(HEAD_SIZE // 2, dtype=F32) / (HEAD_SIZE // 2))
    angles = own_places.astype(F32) * frequency[None, :]
    cosine, sine = jnp.cos(angles), jnp.sin(angles)
    cosine = jnp.concatenate([cosine] * 4, axis=1)
    sine = jnp.concatenate([-sine, sine, -sine, sine], axis=1)
    tables = [
        (cosine[:tok_local], sine[:tok_local]),
        (cosine[tok_local:], sine[tok_local:]),
        (cosine[tok_local : tok_local + cap_last], sine[tok_local : tok_local + cap_last]),
    ]
    query_places = [
        own_places[:tok_local],
        own_places[tok_local:],
        own_places[tok_local : tok_local + cap_last],
    ]
    key_places = [v.reshape(1, -1) for v in (place_one, place_two, place_three)]
    key_live = [
        jnp.ones((1, ctx_count * tok_local), jnp.int32),
        live_two.reshape(1, -1),
        live_three.reshape(1, -1),
    ]
    prompt = ctx_count * tok_local // 2

    dense_weights = (weight_o, weight_g, weight_u, weight_d)
    proj_weights = (weight_q, weight_k, weight_v)
    back_weights = (weight_d, weight_g, weight_u, weight_o)

    firsts, mixeds, seconds, hiddens = [], [], [], []
    records = []
    xs = [tok]
    first_in, query, kv = first_call(coords, tok, gain1, *tables[0], proj_weights)
    heights = []
    for step in range(3):
        part_a, part_b = gather_keys(kv, near)
        weights, mixed = attend_call(
            query, part_a, part_b, key_places[step], key_live[step], query_places[step], prompt
        )
        firsts.append(first_in)
        if step == 0:
            extra = (sel_own, *tables[1])
        elif step == 1:
            extra = (live2_own, *tables[2])
        else:
            extra = (sel_own, live2_own, live3_own, heights[0], heights[1])
        result = dense_call(
            step, coords, xs[step], mixed, gain1, gain2, extra,
            dense_weights + (proj_weights if step < 2 else ()),
            (cap_mid, cap_last, tok_local)[step],
        )
        mixed_rows, middle, second, gate, up, hidden = result[:6]
        mixeds.append(mixed_rows)
        seconds.append(second)
        hiddens.append(hidden)
        records.append((query, part_a, part_b, weights, middle, gate, up))
        if step < 2:
            height, following, first_in, query, kv = result[6:]
            heights.append(height)
            xs.append(following)
        else:
            output = relocate(result[6])

    d_firsts, d_seconds = [None] * 3, [None] * 3
    sums_one, sums_two = [], []
    slots = None
    parts, d_query, d_middle = (), None, None
    for phase in range(4):
        step = 2 - phase
        before, after = (), ()
        if phase > 0:
            before = (gain1, *tables[step + 1], xs[step + 1], d_middle, d_query)
        if phase < 3:
            after = (gain2, *records[step][4:7])
        if phase == 0:
            extra, weights = (cot, sel_own, live3_own), back_weights
        elif phase == 1:
            extra, weights = (slots, live3_own, live2_own), proj_weights + back_weights
        elif phase == 2:
            extra, weights = (cot, sel_own, live2_own), proj_weights + back_weights
        else:
            extra, weights = (), proj_weights
        result = list(back_call(phase, coords, before, parts, after, extra, weights, cap_mid))
        if phase > 0:
            *d_firsts[step + 1], total = result[:4]
            sums_one.append(total)
            result = result[4:]
        if phase < 3:
            d_low, d_gate, d_up, d_middle, d_mid_low, d_mixed, total = result[:7]
            d_seconds[step] = (d_low, d_gate, d_up, d_mid_low)
            sums_two.append(total)
            if phase == 0:
                slots = result[7]
            query, part_a, part_b, weights = records[step][:4]
            d_query, term_a, term_b = attend_back_call(query, d_mixed, part_a, part_b, weights)
            parts = scatter_keys(term_a, term_b, near)
        else:
            grad_tokens = relocate(result[0])

    column = lambda rows, i: [r[i] for r in rows]
    width = tok.shape[1]
    kv_width = key_weight.shape[1]
    hidden_width = w_gate.shape[1]
    half = width // 2
    down = grad_call("rows", block_coords, [hiddens, column(d_seconds, 0)])
    gate = grad_call("cols", block_coords, [seconds, column(d_seconds, 1)])
    up = grad_call("cols", block_coords, [seconds, column(d_seconds, 2)])
    rest = grad_call(
        "mixed", block_coords,
        [firsts, mixeds, column(d_firsts, 0), column(d_firsts, 1), column(d_firsts, 2), column(d_seconds, 3)],
    )
    grad_down = place_call("rows", block_coords, *reduce_blocks(*down, near, places), None)[0]
    grad_gate = place_call("cols", block_coords, *reduce_blocks(*gate, near, places), (hidden_width,))[0]
    grad_up = place_call("cols", block_coords, *reduce_blocks(*up, near, places), (hidden_width,))[0]
    grad_query, grad_key, grad_out, grad_value = place_call(
        "cols", block_coords, *reduce_blocks(*rest, near, places), (width, kv_width, width, kv_width)
    )
    gain_sums = sum_everywhere(jnp.concatenate([sum(sums_one), sum(sums_two)], axis=0), near)
    gain_sums = lax.dynamic_slice_in_dim(gain_sums, y * half, half, 1)
    return (
        output[None],
        grad_tokens[None],
        grad_query,
        grad_key,
        grad_value,
        grad_out,
        grad_gate,
        grad_up,
        grad_down,
        gain_sums[0],
        gain_sums[1],
    )


def solution(mesh):
    rows = P("ws", "ctx", None)
    flat = P("ws", None)
    in_specs = (rows, rows) + (flat,) * 7 + (P("ws"), P("ws"), P()) + (flat,) * 4
    out_specs = (rows, rows) + (flat,) * 7 + (P("ws"), P("ws"))
    return jax.shard_map(
        on_device, mesh=mesh, in_specs=in_specs, out_specs=out_specs, check_vma=False
    )
```

time: 1780 us -> 862 us (0.48)
  waiting for transfers between devices: 1020 us -> 300 us
  Pallas kernels: 0 us -> 285 us
  matrix products: 251 us -> 0 us
  local copies, waits for them, and re-layouts: 257 us -> 61.2 us
  starting transfers between devices: 1.24 us -> 178 us
  blocking collectives: 171 us -> 0 us
    psum x1 -> x0, waiting for transfers between devices: 539 us -> none  [on_device(): lax.psum((part_query, part_key, part_value, acc_out, part_gate, part_up,...]
    ppermute x0 -> x127, waiting for transfers between devices: none -> 300 us  [the longest x122 263 us: hop(): return lax.ppermute(value, AXES, [(i, i ^ mask) for i in range(32)])]
    pallas_call x0 -> x22, Pallas kernels: none -> 285 us  [the longest x3 82.2 us: attend_call(): pl.pallas_call(functools.partial(attend_kernel, prompt), name='attend', g...]
    dot_general x75 -> x0, matrix products: 251 us -> none  [the longest x3 38.2 us: on_device(): jnp.einsum('cd,ce->de', second_in, grad_pair, preferred_element_type=jnp....]
    all_gather x7 -> x0, waiting for transfers between devices: 218 us -> none  [the longest x1 63.8 us: on_device(): lax.all_gather(w_gate, 'ws', axis=0, tiled=True)]
    ppermute x0 -> x127, starting transfers between devices: none -> 178 us  [the longest x122 161 us: hop(): return lax.ppermute(value, AXES, [(i, i ^ mask) for i in range(32)])]
    unnamed x17 -> x0, waiting for transfers between devices: 166 us -> none
    all_gather x6 -> x0, blocking collectives: 125 us -> none  [the longest x2 49.4 us: on_device(): lax.all_gather(value_local, 'ctx', axis=0, tiled=True)]
  transfers between devices with their start and end apart: 14 -> 127, of which waited for: 12 -> 59; matrix products, arithmetic and copies ran while one was open for 13% -> 8% of each run, Pallas kernels for 0% -> 14%
where the time goes in v1:
time: 862 us; the launch traced here: 850 us
  waiting for transfers between devices  300 us (35%)
  Pallas kernels  285 us (33%)
  starting transfers between devices  178 us (21%)
  local copies, waits for them, and re-layouts  61.2 us (7%)
  other arithmetic  23.4 us (3%)
    ppermute x122, waiting for transfers between devices, hop(): return lax.ppermute(value, AXES, [(i, i ^ mask) for i in range(32)])  263 us
    ppermute x122, starting transfers between devices, hop(): return lax.ppermute(value, AXES, [(i, i ^ mask) for i in range(32)])  161 us
    pallas_call x3, Pallas kernels, attend_call(): pl.pallas_call(functools.partial(attend_kernel, prompt), name='attend', g...  82.2 us
    pallas_call x3, Pallas kernels, attend_back_call(): pl.pallas_call(attend_back_kernel, name='attend_back', grid=(heads,), out...  56 us
    pallas_call x4, Pallas kernels, back_call(): pl.pallas_call(functools.partial(back_kernel, phase, weights, len(arrays)...  53.8 us
    pallas_call x3, Pallas kernels, dense_call(): pl.pallas_call(functools.partial(dense_kernel, step, weights, len(arrays)...  38.5 us
    ppermute x5, waiting for transfers between devices, move(): return lax.ppermute(value, AXES, [(i, swap_place(i)) for i in range(32)])  37.4 us
    unnamed x200, local copies, waits for them, and re-layouts  34.8 us
  transfers between devices with their start and end apart: 127, of which 59 were waited for; matrix products, arithmetic and copies ran while one was open for 8% of the time, Pallas kernels for 14%

profile of v1, /device:TPU:7, one launch (start us, length us, event | category | flops | bytes accessed | tf_op | source)
XLA Modules:
  0.0 850.3 jit_solution(10262092349098840648)
XLA Ops:
  6.0 5.2 collective-permute-start.2
  23.8 3.0 copy.97.args_29_.args_31_.args_8_
  29.8 19.4 %collective-permute-done.3.rest_1_.args_39_.args_23_.args_16_ = bf16[240,960]{1,0:T(8,128)(2,1)} collective-permute-done((bf16[240,960]{1,0:T(8,128)(2,1)}, bf16[240,960]{1,0:T(8,128)(2,1)}, u32[]{:S(2)}, u32[]{:S(2)}) %collective-permute-start.3) | collective-permute-done | bytes 460832 | tf_op jit(solution)/shard_map/ppermute | solution.py:32
  55.1 4.8 first_projection.1
  74.7 2.8 collective-permute-done.13
  85.3 3.3 collective-permute-start.16
  88.6 3.8 collective-permute-done.35.args_30_.args_32_.args_9_
  102.2 9.6 %collective-permute-start.39 = (bf16[160,960]{1,0:T(8,128)(2,1)S(1)}, bf16[160,960]{1,0:T(8,128)(2,1)S(1)}, u32[]{:S(2)}, u32[]{:S(2)}) collective-permute-start(bf16[160,960]{1,0:T(8,128)(2,1)S(1)} %collective-permute-done.35.args_30_.args_32_.args_9_), channel_id=1, source_target_pairs={{0,2},{1,3},{2,0},{3,1},{4,6},{5,7},{6,4},{7,5},{8,10},{9,11},{10,... | collective-permute-start | bytes 921608 | tf_op jit(solution)/shard_map/ppermute | solution.py:32
  114.9 13.5 %collective-permute-start.34 = (bf16[240,640]{1,0:T(8,128)(2,1)S(1)}, bf16[240,640]{1,0:T(8,128)(2,1)S(1)}, u32[]{:S(2)}, u32[]{:S(2)}) collective-permute-start(bf16[240,640]{1,0:T(8,128)(2,1)S(1)} %collective-permute-done.30.args_24_.args_26_.args_30_.args_53_), channel_id=1, source_target_pairs={{0,2},{1,3},{2,0},{3,1},{4,6},{5,7},{6,4},{7,5},{8,10},{9,11},{10,... | collective-permute-start | bytes 921608 | tf_op jit(solution)/shard_map/ppermute | solution.py:32
  130.4 5.0 collective-permute-start.26
  143.4 38.2 %attend.3 = (bf16[5,384,2048]{2,1,0:T(8,128)(2,1)}, bf16[5,128,192]{2,1,0:T(8,128)(2,1)}) custom-call(bf16[5,128,192]{2,1,0:T(8,128)(2,1)} %get-tuple-element.105.q_ref, bf16[1024,640]{1,0:T(8,128)(2,1)} %constant_dynamic-update-slice_fusion.a_ref, bf16[1024,640]{1,0:T(8,128)(2,1)} %collective-permute-done.16.b_ref, s32[1,2048]{1,0:T(1,128)} %add.178.kpos_ref, ...), custom_call_target="tpu_custom_call" | custom-call | flops 4026531840 | bytes 7864320 | tf_op jit(solution)/shard_map/attend/pallas_call | solution.py:264
  182.9 13.3 %dense_0.1 = (bf16[128,960]{1,0:T(8,128)(2,1)}, f32[128,960]{1,0:T(8,128)}, bf16[128,960]{1,0:T(8,128)(2,1)}, f32[128,2560]{1,0:T(8,128)}, f32[128,2560]{1,0:T(8...) custom-call(s32[4]{0:T(128)} %pad_add_fusion.1.coords_ref.args_0_, ...), custom_call_target="tpu_custom_call" | custom-call | flops 2516480000 | bytes 24000000 | tf_op jit(solution)/shard_map/dense_0/pallas_call | solution.py:461
  196.4 3.7 collective-permute-start.46
  205.3 2.8 collective-permute-done.47
  208.3 3.4 collective-permute-start.50
  215.5 27.4 %attend.4 = (bf16[5,288,1536]{2,1,0:T(8,128)(2,1)}, bf16[5,96,192]{2,1,0:T(8,128)(2,1)}) custom-call(bf16[5,96,192]{2,1,0:T(8,128)(2,1)} %get-tuple-element.109.q_ref, bf16[768,640]{1,0:T(8,128)(2,1)} %copy-done.64, bf16[768,640]{1,0:T(8,128)(2,1)} %copy-done.74, s32[1,1536]{1,0:T(1,128)} %reshape.149.kpos_ref, s32[1,1536]{1,0:T(1,128)} %reshape.150.live_ref, ...), custom_call_target="tpu_custom_call" | custom-call | flops 2264924160 | bytes 4423680 | tf_op jit(solution)/shard_map/attend/pallas_call | solution.py:264
  242.9 13.1 %dense_1.1 = (bf16[96,960]{1,0:T(8,128)(2,1)}, f32[96,960]{1,0:T(8,128)}, bf16[96,960]{1,0:T(8,128)(2,1)}, f32[96,2560]{1,0:T(8,128)}, f32[96,2560]{1,0:T(8,128)...) custom-call(s32[4]{0:T(128)} %pad_add_fusion.1.coords_ref.args_0_, ...), custom_call_target="tpu_custom_call" | custom-call | flops 1887360000 | bytes 24000000 | tf_op jit(solution)/shard_map/dense_1/pallas_call | solution.py:461
  264.9 3.5 collective-permute-done.55
  271.1 3.5 collective-permute-start.60
  278.2 16.6 %attend.5 = (bf16[5,192,1024]{2,1,0:T(8,128)(2,1)}, bf16[5,64,192]{2,1,0:T(8,128)(2,1)}) custom-call(bf16[5,64,192]{2,1,0:T(8,128)(2,1)} %get-tuple-element.113.q_ref, bf16[512,640]{1,0:T(8,128)(2,1)} %copy-done.65, bf16[512,640]{1,0:T(8,128)(2,1)} %copy-done.75, s32[1,1024]{1,0:T(1,128)} %reshape.151.kpos_ref, s32[1,1024]{1,0:T(1,128)} %reshape.152.live_ref, ...), custom_call_target="tpu_custom_call" | custom-call | flops 1006632960 | bytes 1966080 | tf_op jit(solution)/shard_map/attend/pallas_call | solution.py:264
  294.7 12.1 %dense_2.1 = (bf16[64,960]{1,0:T(8,128)(2,1)}, f32[64,960]{1,0:T(8,128)}, bf16[64,960]{1,0:T(8,128)(2,1)}, f32[64,2560]{1,0:T(8,128)}, f32[64,2560]{1,0:T(8,128)...) custom-call(s32[4]{0:T(128)} %pad_add_fusion.1.coords_ref.args_0_, f32[64,960]{1,0:T(8,128)} %get-tuple-element.112.args_1_.args_4_, ...), custom_call_target="tpu_custom_call" | custom-call | flops 1258240000 | bytes 24000000 | tf_op jit(solution)/shard_map/dense_2/pallas_call | solution.py:461
  307.5 14.2 %back_0.1 = (bf16[64,960]{1,0:T(8,128)(2,1)}, bf16[64,2560]{1,0:T(8,128)(2,1)}, bf16[64,2560]{1,0:T(8,128)(2,1)}, f32[64,960]{1,0:T(8,128)}, bf16[64,960]{1,0:T(...) custom-call(s32[4]{0:T(128)} %pad_add_fusion.1.coords_ref.args_0_, ...), custom_call_target="tpu_custom_call" | custom-call | flops 1258240000 | bytes 24000000 | tf_op jit(solution)/shard_map/back_0/pallas_call | solution.py:625
  321.7 11.5 %attend_back.3 = (f32[5,64,192]{2,1,0:T(8,128)}, f32[512,640]{1,0:T(8,128)}, bf16[512,640]{1,0:T(8,128)(2,1)}) custom-call(bf16[5,64,192]{2,1,0:T(8,128)(2,1)} %get-tuple-element.113.q_ref, bf16[5,64,192]{2,1,0:T(8,128)(2,1)} %get-tuple-element.123.do_ref, bf16[512,640]{1,0:T(8,128)(2,1)} %copy-done.65, bf16[512,640]{1,0:T(8,128)(2,1)} %copy-done.75, ...), custom_call_target="tpu_custom_call" | custom-call | flops 2013265920 | bytes 1966080 | tf_op jit(solution)/shard_map/attend_back/pallas_call | solution.py:317
  349.2 16.2 %back_1.1 = (bf16[64,960]{1,0:T(8,128)(2,1)}, bf16[64,320]{1,0:T(8,128)(2,1)}, bf16[64,320]{1,0:T(8,128)(2,1)}, f32[1,960]{1,0:T(1,128)}, bf16[96,960]{1,0:T(8,1...) custom-call(s32[4]{0:T(128)} %pad_add_fusion.1.coords_ref.args_0_, ...), custom_call_target="tpu_custom_call" | custom-call | flops 1887360000 | bytes 24000000 | tf_op jit(solution)/shard_map/back_1/pallas_call | solution.py:625
  365.4 18.5 %attend_back.4 = (f32[5,96,192]{2,1,0:T(8,128)}, f32[768,640]{1,0:T(8,128)}, bf16[768,640]{1,0:T(8,128)(2,1)}) custom-call(bf16[5,96,192]{2,1,0:T(8,128)(2,1)} %get-tuple-element.109.q_ref, bf16[5,96,192]{2,1,0:T(8,128)(2,1)} %get-tuple-element.133.do_ref, bf16[768,640]{1,0:T(8,128)(2,1)} %copy-done.64, bf16[768,640]{1,0:T(8,128)(2,1)} %copy-done.74, ...), custom_call_target="tpu_custom_call" | custom-call | flops 4529848320 | bytes 4423680 | tf_op jit(solution)/shard_map/attend_back/pallas_call | solution.py:317
  403.4 2.9 collective-permute-done.71.args_9_
  407.0 17.2 %back_2.1 = (bf16[96,960]{1,0:T(8,128)(2,1)}, bf16[96,320]{1,0:T(8,128)(2,1)}, bf16[96,320]{1,0:T(8,128)(2,1)}, f32[1,960]{1,0:T(1,128)}, bf16[128,960]{1,0:T(8,...) custom-call(s32[4]{0:T(128)} %pad_add_fusion.1.coords_ref.args_0_, ...), custom_call_target="tpu_custom_call" | custom-call | flops 2516480000 | bytes 24000000 | tf_op jit(solution)/shard_map/back_2/pallas_call | solution.py:625
  424.2 26.0 %attend_back.5 = (f32[5,128,192]{2,1,0:T(8,128)}, f32[1024,640]{1,0:T(8,128)}, bf16[1024,640]{1,0:T(8,128)(2,1)}) custom-call(bf16[5,128,192]{2,1,0:T(8,128)(2,1)} %get-tuple-element.105.q_ref, bf16[5,128,192]{2,1,0:T(8,128)(2,1)} %get-tuple-element.142.do_ref, bf16[1024,640]{1,0:T(8,128)(2,1)} %constant_dynamic-update-slice_fusion.a_ref, ...), custom_call_target="tpu_custom_call" | custom-call | flops 8053063680 | bytes 7864320 | tf_op jit(solution)/shard_map/attend_back/pallas_call | solution.py:317
  450.7 7.5 grad_rows.1
  458.2 7.5 grad_cols.2
  466.2 7.6 grad_cols.3
  476.9 3.6 collective-permute-done.84.args_14_
  497.1 6.2 back_3.1
  503.3 9.6 %grad_mixed.1 = (bf16[2,2,4,120,640]{4,3,2,1,0:T(8,128)(2,1)}, bf16[2,2,4,120,640]{4,3,2,1,0:T(8,128)(2,1)}) custom-call(s32[4]{0:T(128)} %pad_add_fusion.1.coords_ref.args_0_, bf16[128,960]{1,0:T(8,128)(2,1)} %get-tuple-element.148.args_0_, bf16[96,960]{1,0:T(8,128)(2,1)} %get-tuple-element.149.args_1_, bf16[64,960]{1,0:T(8,128)(2,1)} %get-tuple-element.150.args_2_, ...), custom_call_target="tpu_custom_call" | custom-call | flops 1415577600 | bytes 10000000 | tf_op jit(solution)/shard_map/grad_mixed/pallas_call | solution.py:748
  513.0 5.2 collective-permute-start.86
  518.2 3.0 add_convert_fusion
  529.4 22.4 %collective-permute-done.114 = bf16[2,4,80,960]{3,2,1,0:T(8,128)(2,1)S(1)} collective-permute-done((bf16[2,4,80,960]{3,2,1,0:T(8,128)(2,1)S(1)}, bf16[2,4,80,960]{3,2,1,0:T(8,128)(2,1)S(1)}, u32[]{:S(2)}, u32[]{:S(2)}) %collective-permute-start.114) | collective-permute-done | bytes 1228832 | tf_op jit(solution)/shard_map/ppermute | solution.py:32
  554.2 23.9 %collective-permute-done.96 = bf16[2,4,120,640]{3,2,1,0:T(8,128)(2,1)S(1)} collective-permute-done((bf16[2,4,120,640]{3,2,1,0:T(8,128)(2,1)S(1)}, bf16[2,4,120,640]{3,2,1,0:T(8,128)(2,1)S(1)}, u32[]{:S(2)}, u32[]{:S(2)}) %collective-permute-start.96) | collective-permute-done | bytes 1228832 | tf_op jit(solution)/shard_map/ppermute | solution.py:32
  580.3 24.1 %collective-permute-done.105 = bf16[2,4,120,640]{3,2,1,0:T(8,128)(2,1)S(1)} collective-permute-done((bf16[2,4,120,640]{3,2,1,0:T(8,128)(2,1)S(1)}, bf16[2,4,120,640]{3,2,1,0:T(8,128)(2,1)S(1)}, u32[]{:S(2)}, u32[]{:S(2)}) %collective-permute-start.105) | collective-permute-done | bytes 1228832 | tf_op jit(solution)/shard_map/ppermute | solution.py:32
  610.8 9.3 %collective-permute-done.106 = bf16[4,120,640]{2,1,0:T(8,128)(2,1)S(1)} collective-permute-done((bf16[4,120,640]{2,1,0:T(8,128)(2,1)S(1)}, bf16[4,120,640]{2,1,0:T(8,128)(2,1)S(1)}, u32[]{:S(2)}, u32[]{:S(2)}) %collective-permute-start.106) | collective-permute-done | bytes 614432 | tf_op jit(solution)/shard_map/ppermute | solution.py:32
  621.8 16.0 %collective-permute-done.116 = bf16[2,80,960]{2,1,0:T(8,128)(2,1)S(1)} collective-permute-done((bf16[2,80,960]{2,1,0:T(8,128)(2,1)S(1)}, bf16[2,80,960]{2,1,0:T(8,128)(2,1)S(1)}, u32[]{:S(2)}, u32[]{:S(2)}) %collective-permute-start.116) | collective-permute-done | bytes 307232 | tf_op jit(solution)/shard_map/ppermute | solution.py:32
  638.0 6.4 collective-permute-done.98
  646.2 4.8 collective-permute-done.107
  651.2 4.3 collective-permute-done.117
  663.3 10.4 %collective-permute-done.89 = bf16[2,120,640]{2,1,0:T(8,128)(2,1)S(1)} collective-permute-done((bf16[2,120,640]{2,1,0:T(8,128)(2,1)S(1)}, bf16[2,120,640]{2,1,0:T(8,128)(2,1)S(1)}, u32[]{:S(2)}, u32[]{:S(2)}) %collective-permute-start.89) | collective-permute-done | bytes 307232 | tf_op jit(solution)/shard_map/ppermute | solution.py:32
  676.7 8.2 collective-permute-done.90
  686.7 11.3 %collective-permute-done.119 = bf16[2,80,960]{2,1,0:T(8,128)(2,1)S(1)} collective-permute-done((bf16[2,80,960]{2,1,0:T(8,128)(2,1)S(1)}, bf16[2,80,960]{2,1,0:T(8,128)(2,1)S(1)}, u32[]{:S(2)}, u32[]{:S(2)}) %collective-permute-start.119) | collective-permute-done | bytes 307232 | tf_op jit(solution)/shard_map/ppermute | solution.py:32
  699.4 10.7 %collective-permute-done.101 = bf16[2,120,640]{2,1,0:T(8,128)(2,1)S(1)} collective-permute-done((bf16[2,120,640]{2,1,0:T(8,128)(2,1)S(1)}, bf16[2,120,640]{2,1,0:T(8,128)(2,1)S(1)}, u32[]{:S(2)}, u32[]{:S(2)}) %collective-permute-start.101) | collective-permute-done | bytes 307232 | tf_op jit(solution)/shard_map/ppermute | solution.py:32
  711.2 12.1 %collective-permute-done.110 = bf16[2,120,640]{2,1,0:T(8,128)(2,1)S(1)} collective-permute-done((bf16[2,120,640]{2,1,0:T(8,128)(2,1)S(1)}, bf16[2,120,640]{2,1,0:T(8,128)(2,1)S(1)}, u32[]{:S(2)}, u32[]{:S(2)}) %collective-permute-start.110) | collective-permute-done | bytes 307232 | tf_op jit(solution)/shard_map/ppermute | solution.py:32
  724.4 5.5 collective-permute-done.92
  736.5 2.9 collective-permute-done.111
  740.6 9.1 %collective-permute-start.112 = (bf16[2,4,120,640]{3,2,1,0:T(8,128)(2,1)}, bf16[2,4,120,640]{3,2,1,0:T(8,128)(2,1)}, u32[]{:S(2)}, u32[]{:S(2)}) collective-permute-start(bf16[2,4,120,640]{3,2,1,0:T(8,128)(2,1)} %pad_maximum_fusion.3.near_ref), channel_id=1, source_target_pairs={{0,2},{1,3},{2,0},{3,1},{4,6},{5,7},{6,4},{7,5},{8,10},{9,11},{10,... | collective-permute-start | bytes 3686408 | tf_op jit(solution)/shard_map/ppermute | solution.py:32
  749.7 2.9 collective-permute-done.93
  752.7 4.8 collective-permute-start.94
  762.5 7.1 collective-permute-start.124
  773.2 4.4 collective-permute-start.59
  777.6 12.2 %collective-permute-done.59 = bf16[128,960]{1,0:T(8,128)(2,1)S(1)} collective-permute-done((bf16[128,960]{1,0:T(8,128)(2,1)S(1)}, bf16[128,960]{1,0:T(8,128)(2,1)S(1)}, u32[]{:S(2)}, u32[]{:S(2)}) %collective-permute-start.59) | collective-permute-done | bytes 245792 | tf_op jit(solution)/shard_map/ppermute | solution.py:41
  789.8 3.4 collective-permute-done.126
  796.9 25.2 %collective-permute-done.85 = f32[128,960]{1,0:T(8,128)S(1)} collective-permute-done((f32[128,960]{1,0:T(8,128)}, f32[128,960]{1,0:T(8,128)S(1)}, u32[]{:S(2)}, u32[]{:S(2)}) %collective-permute-start.85) | collective-permute-done | bytes 491552 | tf_op jit(solution)/shard_map/ppermute | solution.py:41
  823.1 4.4 place_rows.1
  827.5 5.8 copy.120
  833.3 4.2 place_cols.4
  837.6 4.2 place_cols.5
  841.8 4.7 place_cols.3
  (536 shorter events, 218.2 us)
Async XLA Ops:
  2.1 24.7 %collective-permute-start.1 = (bf16[2,480]{1,0:T(2,128)(2,1)S(1)}, bf16[2,480]{1,0:T(2,128)(2,1)S(1)}, u32[]{:S(2)}, u32[]{:S(2)}) collective-permute-start(bf16[2,480]{1,0:T(2,128)(2,1)S(1)} %pad_maximum_fusion.17), channel_id=1, source_target_pairs={{0,1},{1,0},{2,3},{3,2},{4,5},{5,4},{6,7},{7,6},{8,9},{9,8},{10,11... | collective-permute-start | bytes 5768 | tf_op jit(solution)/shard_map/ppermute | solution.py:32
  6.0 21.8 %collective-permute-start.2 = (s32[16,256]{1,0:T(8,128)S(1)}, s32[16,256]{1,0:T(8,128)S(1)}, u32[]{:S(2)}, u32[]{:S(2)}) collective-permute-start(s32[16,256]{1,0:T(8,128)S(1)} %pad_add_fusion), channel_id=1, source_target_pairs={{0,0},{1,16},{2,2},{3,18},{4,4},{5,20},{6,6},{7,22},{8,8},{9,24},{... | collective-permute-start | bytes 49160 | tf_op jit(solution)/shard_map/ppermute | solution.py:41
  13.0 40.5 %collective-permute-start = (bf16[128,960]{1,0:T(8,128)(2,1)}, bf16[128,960]{1,0:T(8,128)(2,1)}, u32[]{:S(2)}, u32[]{:S(2)}) collective-permute-start(bf16[128,960]{1,0:T(8,128)(2,1)} %bitcast.4), channel_id=1, source_target_pairs={{0,0},{1,16},{2,2},{3,18},{4,4},{5,20},{6,6},{7,22},{8,8},{9,24},{... | collective-permute-start | bytes 737288 | tf_op jit(solution)/shard_map/ppermute | solution.py:41
  16.9 62.3 %collective-permute-start.27 = (bf16[240,640]{1,0:T(8,128)(2,1)}, bf16[240,640]{1,0:T(8,128)(2,1)}, u32[]{:S(2)}, u32[]{:S(2)}) collective-permute-start(bf16[240,640]{1,0:T(8,128)(2,1)} %dynamic_slice.35), channel_id=1, source_target_pairs={{0,1},{1,0},{2,3},{3,2},{4,5},{5,4},{6,7},{7,6},{8,9},{9,8},{10,11... | collective-permute-start | bytes 921608 | tf_op jit(solution)/shard_map/ppermute | solution.py:32
  17.9 32.8 %collective-permute-start.5 = (bf16[240,320]{1,0:T(8,128)(2,1)}, bf16[240,320]{1,0:T(8,128)(2,1)S(1)}, u32[]{:S(2)}, u32[]{:S(2)}) collective-permute-start(bf16[240,320]{1,0:T(8,128)(2,1)} %constant_dynamic-slice_fusion.3), channel_id=1, source_target_pairs={{0,1},{1,0},{2,3},{3,2},{4,5},{5,4},{6,7},{7,6},{8,9},{9,8},{10,11... | collective-permute-start | bytes 460808 | tf_op jit(solution)/shard_map/ppermute | solution.py:32
  26.8 24.0 %collective-permute-start.7 = (bf16[240,320]{1,0:T(8,128)(2,1)S(1)}, bf16[240,320]{1,0:T(8,128)(2,1)S(1)}, u32[]{:S(2)}, u32[]{:S(2)}) collective-permute-start(bf16[240,320]{1,0:T(8,128)(2,1)S(1)} %copy-done.48), channel_id=1, source_target_pairs={{0,1},{1,0},{2,3},{3,2},{4,5},{5,4},{6,7},{7,6},{8,9},{9,8},{10,11... | collective-permute-start | bytes 460808 | tf_op jit(solution)/shard_map/ppermute | solution.py:32
  27.8 21.3 %collective-permute-start.3 = (bf16[240,960]{1,0:T(8,128)(2,1)}, bf16[240,960]{1,0:T(8,128)(2,1)}, u32[]{:S(2)}, u32[]{:S(2)}) collective-permute-start(bf16[240,960]{1,0:T(8,128)(2,1)} %constant_dynamic-slice_fusion.4), channel_id=1, source_target_pairs={{0,1},{1,0},{2,3},{3,2},{4,5},{5,4},{6,7},{7,6},{8,9},{9,8},{10,11... | collective-permute-start | bytes 1382408 | tf_op jit(solution)/shard_map/ppermute | solution.py:32
  53.5 40.4 %collective-permute-start.17 = (bf16[240,960]{1,0:T(8,128)(2,1)}, bf16[240,960]{1,0:T(8,128)(2,1)S(1)}, u32[]{:S(2)}, u32[]{:S(2)}) collective-permute-start(bf16[240,960]{1,0:T(8,128)(2,1)} %constant_dynamic-slice_fusion.1), channel_id=1, source_target_pairs={{0,1},{1,0},{2,3},{3,2},{4,5},{5,4},{6,7},{7,6},{8,9},{9,8},{10,11... | collective-permute-start | bytes 1382408 | tf_op jit(solution)/shard_map/ppermute | solution.py:32
  79.2 13.2 %collective-permute-start.35 = (bf16[160,960]{1,0:T(8,128)(2,1)S(1)}, bf16[160,960]{1,0:T(8,128)(2,1)S(1)}, u32[]{:S(2)}, u32[]{:S(2)}) collective-permute-start(bf16[160,960]{1,0:T(8,128)(2,1)S(1)} %constant_dynamic-slice_fusion), channel_id=1, source_target_pairs={{0,1},{1,0},{2,3},{3,2},{4,5},{5,4},{6,7},{7,6},{8,9},{9,8},{10,11... | collective-permute-start | bytes 921608 | tf_op jit(solution)/shard_map/ppermute | solution.py:32
  79.6 14.6 %collective-permute-start.31 = (bf16[240,640]{1,0:T(8,128)(2,1)}, bf16[240,640]{1,0:T(8,128)(2,1)S(1)}, u32[]{:S(2)}, u32[]{:S(2)}) collective-permute-start(bf16[240,640]{1,0:T(8,128)(2,1)} %collective-permute-done.27.args_21_.args_23_.args_27_.args_50_), channel_id=1, source_target_pairs={{0,2},{1,3},{2,0},{3,1},{4,6},{5,7},{6,4},{7,5},{8,10},{9,11},{10,... | collective-permute-start | bytes 921608 | tf_op jit(solution)/shard_map/ppermute | solution.py:32
  81.1 15.3 %collective-permute-start.30 = (bf16[240,640]{1,0:T(8,128)(2,1)}, bf16[240,640]{1,0:T(8,128)(2,1)S(1)}, u32[]{:S(2)}, u32[]{:S(2)}) collective-permute-start(bf16[240,640]{1,0:T(8,128)(2,1)} %collective-permute-done.27.args_21_.args_23_.args_27_.args_50_), channel_id=1, source_target_pairs={{0,12},{1,13},{2,14},{3,15},{4,8},{5,9},{6,10},{7,11},{8,4},{9,5},... | collective-permute-start | bytes 921608 | tf_op jit(solution)/shard_map/ppermute | solution.py:32
  85.3 57.1 %collective-permute-start.16 = (bf16[1024,640]{1,0:T(8,128)(2,1)}, bf16[1024,640]{1,0:T(8,128)(2,1)}, u32[]{:S(2)}, u32[]{:S(2)}) collective-permute-start(bf16[1024,640]{1,0:T(8,128)(2,1)} %constant_dynamic-update-slice_fusion.a_ref), channel_id=1, source_target_pairs={{0,2},{1,3},{2,0},{3,1},{4,6},{5,7},{6,4},{7,5},{8,10},{9,11},{10,... | collective-permute-start | bytes 3932168 | tf_op jit(solution)/shard_map/ppermute | solution.py:32
  96.4 15.4 %collective-permute-start.22 = (bf16[240,640]{1,0:T(8,128)(2,1)S(1)}, bf16[240,640]{1,0:T(8,128)(2,1)}, u32[]{:S(2)}, u32[]{:S(2)}) collective-permute-start(bf16[240,640]{1,0:T(8,128)(2,1)S(1)} %collective-permute-done.19.args_12_.args_14_.args_18_.args_41_), channel_id=1, source_target_pairs={{0,12},{1,13},{2,14},{3,15},{4,8},{5,9},{6,10},{7,11},{8,4},{9,5},... | collective-permute-start | bytes 921608 | tf_op jit(solution)/shard_map/ppermute | solution.py:32
  99.7 13.6 %collective-permute-start.21 = (bf16[240,640]{1,0:T(8,128)(2,1)S(1)}, bf16[240,640]{1,0:T(8,128)(2,1)}, u32[]{:S(2)}, u32[]{:S(2)}) collective-permute-start(bf16[240,640]{1,0:T(8,128)(2,1)S(1)} %collective-permute-done.19.args_12_.args_14_.args_18_.args_41_), channel_id=1, source_target_pairs={{0,8},{1,9},{2,10},{3,11},{4,12},{5,13},{6,14},{7,15},{8,0},{9,1},... | collective-permute-start | bytes 921608 | tf_op jit(solution)/shard_map/ppermute | solution.py:32
  102.2 12.6 %collective-permute-start.20 = (bf16[240,640]{1,0:T(8,128)(2,1)S(1)}, bf16[240,640]{1,0:T(8,128)(2,1)}, u32[]{:S(2)}, u32[]{:S(2)}) collective-permute-start(bf16[240,640]{1,0:T(8,128)(2,1)S(1)} %collective-permute-done.19.args_12_.args_14_.args_18_.args_41_), channel_id=1, source_target_pairs={{0,4},{1,5},{2,6},{3,7},{4,0},{5,1},{6,2},{7,3},{8,12},{9,13},{10,... | collective-permute-start | bytes 921608 | tf_op jit(solution)/shard_map/ppermute | solution.py:32
  102.2 12.7 %collective-permute-start.39 = (bf16[160,960]{1,0:T(8,128)(2,1)S(1)}, bf16[160,960]{1,0:T(8,128)(2,1)S(1)}, u32[]{:S(2)}, u32[]{:S(2)}) collective-permute-start(bf16[160,960]{1,0:T(8,128)(2,1)S(1)} %collective-permute-done.35.args_30_.args_32_.args_9_), channel_id=1, source_target_pairs={{0,2},{1,3},{2,0},{3,1},{4,6},{5,7},{6,4},{7,5},{8,10},{9,11},{10,... | collective-permute-start | bytes 921608 | tf_op jit(solution)/shard_map/ppermute | solution.py:32
  111.8 16.6 %collective-permute-start.38 = (bf16[160,960]{1,0:T(8,128)(2,1)S(1)}, bf16[160,960]{1,0:T(8,128)(2,1)S(1)}, u32[]{:S(2)}, u32[]{:S(2)}) collective-permute-start(bf16[160,960]{1,0:T(8,128)(2,1)S(1)} %collective-permute-done.35.args_30_.args_32_.args_9_), channel_id=1, source_target_pairs={{0,12},{1,13},{2,14},{3,15},{4,8},{5,9},{6,10},{7,11},{8,4},{9,5},... | collective-permute-start | bytes 921608 | tf_op jit(solution)/shard_map/ppermute | solution.py:32
  113.3 16.3 %collective-permute-start.37 = (bf16[160,960]{1,0:T(8,128)(2,1)S(1)}, bf16[160,960]{1,0:T(8,128)(2,1)S(1)}, u32[]{:S(2)}, u32[]{:S(2)}) collective-permute-start(bf16[160,960]{1,0:T(8,128)(2,1)S(1)} %collective-permute-done.35.args_30_.args_32_.args_9_), channel_id=1, source_target_pairs={{0,8},{1,9},{2,10},{3,11},{4,12},{5,13},{6,14},{7,15},{8,0},{9,1},... | collective-permute-start | bytes 921608 | tf_op jit(solution)/shard_map/ppermute | solution.py:32
  114.7 15.7 %collective-permute-start.36 = (bf16[160,960]{1,0:T(8,128)(2,1)S(1)}, bf16[160,960]{1,0:T(8,128)(2,1)S(1)}, u32[]{:S(2)}, u32[]{:S(2)}) collective-permute-start(bf16[160,960]{1,0:T(8,128)(2,1)S(1)} %collective-permute-done.35.args_30_.args_32_.args_9_), channel_id=1, source_target_pairs={{0,4},{1,5},{2,6},{3,7},{4,0},{5,1},{6,2},{7,3},{8,12},{9,13},{10,... | collective-permute-start | bytes 921608 | tf_op jit(solution)/shard_map/ppermute | solution.py:32
  114.9 20.5 %collective-permute-start.34 = (bf16[240,640]{1,0:T(8,128)(2,1)S(1)}, bf16[240,640]{1,0:T(8,128)(2,1)S(1)}, u32[]{:S(2)}, u32[]{:S(2)}) collective-permute-start(bf16[240,640]{1,0:T(8,128)(2,1)S(1)} %collective-permute-done.30.args_24_.args_26_.args_30_.args_53_), channel_id=1, source_target_pairs={{0,2},{1,3},{2,0},{3,1},{4,6},{5,7},{6,4},{7,5},{8,10},{9,11},{10,... | collective-permute-start | bytes 921608 | tf_op jit(solution)/shard_map/ppermute | solution.py:32
  137.6 44.0 %collective-permute-start.18 = (bf16[240,960]{1,0:T(8,128)(2,1)S(1)}, bf16[240,960]{1,0:T(8,128)(2,1)S(1)}, u32[]{:S(2)}, u32[]{:S(2)}) collective-permute-start(bf16[240,960]{1,0:T(8,128)(2,1)S(1)} %collective-permute-done.17.args_9_.args_11_.args_36_.args_59_), channel_id=1, source_target_pairs={{0,2},{1,3},{2,0},{3,1},{4,6},{5,7},{6,4},{7,5},{8,10},{9,11},{10,... | collective-permute-start | bytes 1382408 | tf_op jit(solution)/shard_map/ppermute | solution.py:32
  141.6 40.1 %collective-permute-start.24 = (bf16[240,640]{1,0:T(8,128)(2,1)}, bf16[240,640]{1,0:T(8,128)(2,1)}, u32[]{:S(2)}, u32[]{:S(2)}) collective-permute-start(bf16[240,640]{1,0:T(8,128)(2,1)} %collective-permute-done.20.args_13_.args_15_.args_19_.args_42_), channel_id=1, source_target_pairs={{0,2},{1,3},{2,0},{3,1},{4,6},{5,7},{6,4},{7,5},{8,10},{9,11},{10,... | collective-permute-start | bytes 921608 | tf_op jit(solution)/shard_map/ppermute | solution.py:32
  141.6 40.1 %collective-permute-start.42 = (bf16[160,960]{1,0:T(8,128)(2,1)S(1)}, bf16[160,960]{1,0:T(8,128)(2,1)S(1)}, u32[]{:S(2)}, u32[]{:S(2)}) collective-permute-start(bf16[160,960]{1,0:T(8,128)(2,1)S(1)} %collective-permute-done.38.args_33_.args_35_.args_12_), channel_id=1, source_target_pairs={{0,2},{1,3},{2,0},{3,1},{4,6},{5,7},{6,4},{7,5},{8,10},{9,11},{10,... | collective-permute-start | bytes 921608 | tf_op jit(solution)/shard_map/ppermute | solution.py:32
  142.3 39.4 %collective-permute-start.41 = (bf16[160,960]{1,0:T(8,128)(2,1)S(1)}, bf16[160,960]{1,0:T(8,128)(2,1)S(1)}, u32[]{:S(2)}, u32[]{:S(2)}) collective-permute-start(bf16[160,960]{1,0:T(8,128)(2,1)S(1)} %collective-permute-done.37.args_32_.args_34_.args_11_), channel_id=1, source_target_pairs={{0,2},{1,3},{2,0},{3,1},{4,6},{5,7},{6,4},{7,5},{8,10},{9,11},{10,... | collective-permute-start | bytes 921608 | tf_op jit(solution)/shard_map/ppermute | solution.py:32
  142.4 39.4 %collective-permute-start.40 = (bf16[160,960]{1,0:T(8,128)(2,1)S(1)}, bf16[160,960]{1,0:T(8,128)(2,1)S(1)}, u32[]{:S(2)}, u32[]{:S(2)}) collective-permute-start(bf16[160,960]{1,0:T(8,128)(2,1)S(1)} %collective-permute-done.36.args_31_.args_33_.args_10_), channel_id=1, source_target_pairs={{0,2},{1,3},{2,0},{3,1},{4,6},{5,7},{6,4},{7,5},{8,10},{9,11},{10,... | collective-permute-start | bytes 921608 | tf_op jit(solution)/shard_map/ppermute | solution.py:32
  271.1 35.7 %collective-permute-start.60 = (bf16[128,960]{1,0:T(8,128)(2,1)S(1)}, bf16[128,960]{1,0:T(8,128)(2,1)S(1)}, u32[]{:S(2)}, u32[]{:S(2)}) collective-permute-start(bf16[128,960]{1,0:T(8,128)(2,1)S(1)} %bitcast.141), channel_id=1, source_target_pairs={{0,0},{1,16},{2,2},{3,18},{4,4},{5,20},{6,6},{7,22},{8,8},{9,24},{... | collective-permute-start | bytes 737288 | tf_op jit(solution)/shard_map/ppermute | solution.py:41
  450.2 23.6 %collective-permute-start.77 = (bf16[1024,640]{1,0:T(8,128)(2,1)}, bf16[1024,640]{1,0:T(8,128)(2,1)S(1)}, u32[]{:S(2)}, u32[]{:S(2)}) collective-permute-start(bf16[1024,640]{1,0:T(8,128)(2,1)} %get-tuple-element.146), channel_id=1, source_target_pairs={{0,2},{1,3},{2,0},{3,1},{4,6},{5,7},{6,4},{7,5},{8,10},{9,11},{10,... | collective-permute-start | bytes 3932168 | tf_op jit(solution)/shard_map/ppermute | solution.py:32
  458.2 60.0 %collective-permute-start.113 = (bf16[2,2,4,80,960]{4,3,2,1,0:T(8,128)(2,1)}, bf16[2,2,4,80,960]{4,3,2,1,0:T(8,128)(2,1)}, u32[]{:S(2)}, u32[]{:S(2)}) collective-permute-start(bf16[2,2,4,80,960]{4,3,2,1,0:T(8,128)(2,1)} %get-tuple-element.192), channel_id=1, source_target_pairs={{0,2},{1,3},{2,0},{3,1},{4,6},{5,7},{6,4},{7,5},{8,10},{9,11},{10,... | collective-permute-start | bytes 7372808 | tf_op jit(solution)/shard_map/ppermute | solution.py:32
  465.7 55.7 %collective-permute-start.95 = (bf16[2,2,4,120,640]{4,3,2,1,0:T(8,128)(2,1)}, bf16[2,2,4,120,640]{4,3,2,1,0:T(8,128)(2,1)}, u32[]{:S(2)}, u32[]{:S(2)}) collective-permute-start(bf16[2,2,4,120,640]{4,3,2,1,0:T(8,128)(2,1)} %get-tuple-element.179), channel_id=1, source_target_pairs={{0,2},{1,3},{2,0},{3,1},{4,6},{5,7},{6,4},{7,5},{8,10},{9,11},{10,... | collective-permute-start | bytes 7372808 | tf_op jit(solution)/shard_map/ppermute | solution.py:32
  473.8 51.6 %collective-permute-start.104 = (bf16[2,2,4,120,640]{4,3,2,1,0:T(8,128)(2,1)}, bf16[2,2,4,120,640]{4,3,2,1,0:T(8,128)(2,1)}, u32[]{:S(2)}, u32[]{:S(2)}) collective-permute-start(bf16[2,2,4,120,640]{4,3,2,1,0:T(8,128)(2,1)} %get-tuple-element.184), channel_id=1, source_target_pairs={{0,2},{1,3},{2,0},{3,1},{4,6},{5,7},{6,4},{7,5},{8,10},{9,11},{10,... | collective-permute-start | bytes 7372808 | tf_op jit(solution)/shard_map/ppermute | solution.py:32
  513.0 93.7 %collective-permute-start.86 = (bf16[2,2,4,120,640]{4,3,2,1,0:T(8,128)(2,1)}, bf16[2,2,4,120,640]{4,3,2,1,0:T(8,128)(2,1)S(1)}, u32[]{:S(2)}, u32[]{:S(2)}) collective-permute-start(bf16[2,2,4,120,640]{4,3,2,1,0:T(8,128)(2,1)} %get-tuple-element.167), channel_id=1, source_target_pairs={{0,2},{1,3},{2,0},{3,1},{4,6},{5,7},{6,4},{7,5},{8,10},{9,11},{10,... | collective-permute-start | bytes 7372808 | tf_op jit(solution)/shard_map/ppermute | solution.py:32
  521.3 30.5 %collective-permute-start.114 = (bf16[2,4,80,960]{3,2,1,0:T(8,128)(2,1)S(1)}, bf16[2,4,80,960]{3,2,1,0:T(8,128)(2,1)S(1)}, u32[]{:S(2)}, u32[]{:S(2)}) collective-permute-start(bf16[2,4,80,960]{3,2,1,0:T(8,128)(2,1)S(1)} %slice_bitcast_fusion), channel_id=1, source_target_pairs={{0,1},{1,0},{2,3},{3,2},{4,5},{5,4},{6,7},{7,6},{8,9},{9,8},{10,11... | collective-permute-start | bytes 3686408 | tf_op jit(solution)/shard_map/ppermute | solution.py:32
  525.3 52.8 %collective-permute-start.96 = (bf16[2,4,120,640]{3,2,1,0:T(8,128)(2,1)S(1)}, bf16[2,4,120,640]{3,2,1,0:T(8,128)(2,1)S(1)}, u32[]{:S(2)}, u32[]{:S(2)}) collective-permute-start(bf16[2,4,120,640]{3,2,1,0:T(8,128)(2,1)S(1)} %slice_bitcast_fusion.4), channel_id=1, source_target_pairs={{0,1},{1,0},{2,3},{3,2},{4,5},{5,4},{6,7},{7,6},{8,9},{9,8},{10,11... | collective-permute-start | bytes 3686408 | tf_op jit(solution)/shard_map/ppermute | solution.py:32
  529.3 75.1 %collective-permute-start.105 = (bf16[2,4,120,640]{3,2,1,0:T(8,128)(2,1)S(1)}, bf16[2,4,120,640]{3,2,1,0:T(8,128)(2,1)S(1)}, u32[]{:S(2)}, u32[]{:S(2)}) collective-permute-start(bf16[2,4,120,640]{3,2,1,0:T(8,128)(2,1)S(1)} %slice_bitcast_fusion.2), channel_id=1, source_target_pairs={{0,1},{1,0},{2,3},{3,2},{4,5},{5,4},{6,7},{7,6},{8,9},{9,8},{10,11... | collective-permute-start | bytes 3686408 | tf_op jit(solution)/shard_map/ppermute | solution.py:32
  552.4 55.3 %collective-permute-start.115 = (bf16[4,80,960]{2,1,0:T(8,128)(2,1)S(1)}, bf16[4,80,960]{2,1,0:T(8,128)(2,1)S(1)}, u32[]{:S(2)}, u32[]{:S(2)}) collective-permute-start(bf16[4,80,960]{2,1,0:T(8,128)(2,1)S(1)} %slice_bitcast_fusion.8), channel_id=1, source_target_pairs={{0,4},{1,5},{2,6},{3,7},{4,0},{5,1},{6,2},{7,3},{8,12},{9,13},{10,... | collective-permute-start | bytes 1843208 | tf_op jit(solution)/shard_map/ppermute | solution.py:32
  578.5 32.0 %collective-permute-start.97 = (bf16[4,120,640]{2,1,0:T(8,128)(2,1)S(1)}, bf16[4,120,640]{2,1,0:T(8,128)(2,1)S(1)}, u32[]{:S(2)}, u32[]{:S(2)}) collective-permute-start(bf16[4,120,640]{2,1,0:T(8,128)(2,1)S(1)} %slice_bitcast_fusion.12), channel_id=1, source_target_pairs={{0,4},{1,5},{2,6},{3,7},{4,0},{5,1},{6,2},{7,3},{8,12},{9,13},{10,... | collective-permute-start | bytes 1843208 | tf_op jit(solution)/shard_map/ppermute | solution.py:32
  604.8 15.3 %collective-permute-start.106 = (bf16[4,120,640]{2,1,0:T(8,128)(2,1)S(1)}, bf16[4,120,640]{2,1,0:T(8,128)(2,1)S(1)}, u32[]{:S(2)}, u32[]{:S(2)}) collective-permute-start(bf16[4,120,640]{2,1,0:T(8,128)(2,1)S(1)} %slice_bitcast_fusion.10), channel_id=1, source_target_pairs={{0,4},{1,5},{2,6},{3,7},{4,0},{5,1},{6,2},{7,3},{8,12},{9,13},{10,... | collective-permute-start | bytes 1843208 | tf_op jit(solution)/shard_map/ppermute | solution.py:32
  607.5 37.2 %collective-permute-start.87 = (bf16[2,4,120,640]{3,2,1,0:T(8,128)(2,1)S(1)}, bf16[2,4,120,640]{3,2,1,0:T(8,128)(2,1)S(1)}, u32[]{:S(2)}, u32[]{:S(2)}) collective-permute-start(bf16[2,4,120,640]{3,2,1,0:T(8,128)(2,1)S(1)} %slice_bitcast_fusion.6), channel_id=1, source_target_pairs={{0,1},{1,0},{2,3},{3,2},{4,5},{5,4},{6,7},{7,6},{8,9},{9,8},{10,11... | collective-permute-start | bytes 3686408 | tf_op jit(solution)/shard_map/ppermute | solution.py:32
  608.0 29.8 %collective-permute-start.116 = (bf16[2,80,960]{2,1,0:T(8,128)(2,1)S(1)}, bf16[2,80,960]{2,1,0:T(8,128)(2,1)S(1)}, u32[]{:S(2)}, u32[]{:S(2)}) collective-permute-start(bf16[2,80,960]{2,1,0:T(8,128)(2,1)S(1)} %slice.438), channel_id=1, source_target_pairs={{0,16},{1,17},{2,18},{3,19},{4,20},{5,21},{6,22},{7,23},{8,24},{9,... | collective-permute-start | bytes 921608 | tf_op jit(solution)/shard_map/ppermute | solution.py:32
  610.7 33.7 %collective-permute-start.98 = (bf16[2,120,640]{2,1,0:T(8,128)(2,1)S(1)}, bf16[2,120,640]{2,1,0:T(8,128)(2,1)S(1)}, u32[]{:S(2)}, u32[]{:S(2)}) collective-permute-start(bf16[2,120,640]{2,1,0:T(8,128)(2,1)S(1)} %slice.422), channel_id=1, source_target_pairs={{0,16},{1,17},{2,18},{3,19},{4,20},{5,21},{6,22},{7,23},{8,24},{9,... | collective-permute-start | bytes 921608 | tf_op jit(solution)/shard_map/ppermute | solution.py:32
  620.3 30.7 %collective-permute-start.107 = (bf16[2,120,640]{2,1,0:T(8,128)(2,1)S(1)}, bf16[2,120,640]{2,1,0:T(8,128)(2,1)S(1)}, u32[]{:S(2)}, u32[]{:S(2)}) collective-permute-start(bf16[2,120,640]{2,1,0:T(8,128)(2,1)S(1)} %slice.430), channel_id=1, source_target_pairs={{0,16},{1,17},{2,18},{3,19},{4,20},{5,21},{6,22},{7,23},{8,24},{9,... | collective-permute-start | bytes 921608 | tf_op jit(solution)/shard_map/ppermute | solution.py:32
  637.9 17.6 %collective-permute-start.117 = (bf16[80,960]{1,0:T(8,128)(2,1)S(1)}, bf16[80,960]{1,0:T(8,128)(2,1)S(1)}, u32[]{:S(2)}, u32[]{:S(2)}) collective-permute-start(bf16[80,960]{1,0:T(8,128)(2,1)S(1)} %slice_bitcast_fusion.16), channel_id=1, source_target_pairs={{0,8},{1,9},{2,10},{3,11},{4,12},{5,13},{6,14},{7,15},{8,0},{9,1},... | collective-permute-start | bytes 460808 | tf_op jit(solution)/shard_map/ppermute | solution.py:32
  644.5 15.6 %collective-permute-start.99 = (bf16[120,640]{1,0:T(8,128)(2,1)S(1)}, bf16[120,640]{1,0:T(8,128)(2,1)S(1)}, u32[]{:S(2)}, u32[]{:S(2)}) collective-permute-start(bf16[120,640]{1,0:T(8,128)(2,1)S(1)} %slice_bitcast_fusion.20), channel_id=1, source_target_pairs={{0,8},{1,9},{2,10},{3,11},{4,12},{5,13},{6,14},{7,15},{8,0},{9,1},... | collective-permute-start | bytes 460808 | tf_op jit(solution)/shard_map/ppermute | solution.py:32
  645.0 12.7 %collective-permute-start.88 = (bf16[4,120,640]{2,1,0:T(8,128)(2,1)S(1)}, bf16[4,120,640]{2,1,0:T(8,128)(2,1)S(1)}, u32[]{:S(2)}, u32[]{:S(2)}) collective-permute-start(bf16[4,120,640]{2,1,0:T(8,128)(2,1)S(1)} %slice_bitcast_fusion.14), channel_id=1, source_target_pairs={{0,4},{1,5},{2,6},{3,7},{4,0},{5,1},{6,2},{7,3},{8,12},{9,13},{10,... | collective-permute-start | bytes 1843208 | tf_op jit(solution)/shard_map/ppermute | solution.py:32
  651.1 12.1 %collective-permute-start.108 = (bf16[120,640]{1,0:T(8,128)(2,1)S(1)}, bf16[120,640]{1,0:T(8,128)(2,1)S(1)}, u32[]{:S(2)}, u32[]{:S(2)}) collective-permute-start(bf16[120,640]{1,0:T(8,128)(2,1)S(1)} %slice_bitcast_fusion.18), channel_id=1, source_target_pairs={{0,8},{1,9},{2,10},{3,11},{4,12},{5,13},{6,14},{7,15},{8,0},{9,1},... | collective-permute-start | bytes 460808 | tf_op jit(solution)/shard_map/ppermute | solution.py:32
  655.6 18.3 %collective-permute-start.118 = (bf16[80,960]{1,0:T(8,128)(2,1)S(1)}, bf16[80,960]{1,0:T(8,128)(2,1)S(1)}, u32[]{:S(2)}, u32[]{:S(2)}) collective-permute-start(bf16[80,960]{1,0:T(8,128)(2,1)S(1)} %fusion.8), channel_id=1, source_target_pairs={{0,8},{1,9},{2,10},{3,11},{4,12},{5,13},{6,14},{7,15},{8,0},{9,1},... | collective-permute-start | bytes 460808 | tf_op jit(solution)/shard_map/ppermute | solution.py:32
  657.9 15.8 %collective-permute-start.89 = (bf16[2,120,640]{2,1,0:T(8,128)(2,1)S(1)}, bf16[2,120,640]{2,1,0:T(8,128)(2,1)S(1)}, u32[]{:S(2)}, u32[]{:S(2)}) collective-permute-start(bf16[2,120,640]{2,1,0:T(8,128)(2,1)S(1)} %slice.414), channel_id=1, source_target_pairs={{0,16},{1,17},{2,18},{3,19},{4,20},{5,21},{6,22},{7,23},{8,24},{9,... | collective-permute-start | bytes 921608 | tf_op jit(solution)/shard_map/ppermute | solution.py:32
  660.2 16.4 %collective-permute-start.100 = (bf16[120,640]{1,0:T(8,128)(2,1)S(1)}, bf16[120,640]{1,0:T(8,128)(2,1)S(1)}, u32[]{:S(2)}, u32[]{:S(2)}) collective-permute-start(bf16[120,640]{1,0:T(8,128)(2,1)S(1)} %fusion.10), channel_id=1, source_target_pairs={{0,8},{1,9},{2,10},{3,11},{4,12},{5,13},{6,14},{7,15},{8,0},{9,1},... | collective-permute-start | bytes 460808 | tf_op jit(solution)/shard_map/ppermute | solution.py:32
  663.2 21.8 %collective-permute-start.109 = (bf16[120,640]{1,0:T(8,128)(2,1)S(1)}, bf16[120,640]{1,0:T(8,128)(2,1)S(1)}, u32[]{:S(2)}, u32[]{:S(2)}) collective-permute-start(bf16[120,640]{1,0:T(8,128)(2,1)S(1)} %fusion.9), channel_id=1, source_target_pairs={{0,8},{1,9},{2,10},{3,11},{4,12},{5,13},{6,14},{7,15},{8,0},{9,1},... | collective-permute-start | bytes 460808 | tf_op jit(solution)/shard_map/ppermute | solution.py:32
  673.9 24.0 %collective-permute-start.119 = (bf16[2,80,960]{2,1,0:T(8,128)(2,1)S(1)}, bf16[2,80,960]{2,1,0:T(8,128)(2,1)S(1)}, u32[]{:S(2)}, u32[]{:S(2)}) collective-permute-start(bf16[2,80,960]{2,1,0:T(8,128)(2,1)S(1)} %pad_maximum_fusion.8), channel_id=1, source_target_pairs={{0,16},{1,17},{2,18},{3,19},{4,20},{5,21},{6,22},{7,23},{8,24},{9,... | collective-permute-start | bytes 921608 | tf_op jit(solution)/shard_map/ppermute | solution.py:32
  676.6 33.5 %collective-permute-start.101 = (bf16[2,120,640]{2,1,0:T(8,128)(2,1)S(1)}, bf16[2,120,640]{2,1,0:T(8,128)(2,1)S(1)}, u32[]{:S(2)}, u32[]{:S(2)}) collective-permute-start(bf16[2,120,640]{2,1,0:T(8,128)(2,1)S(1)} %pad_maximum_fusion.10), channel_id=1, source_target_pairs={{0,16},{1,17},{2,18},{3,19},{4,20},{5,21},{6,22},{7,23},{8,24},{9,... | collective-permute-start | bytes 921608 | tf_op jit(solution)/shard_map/ppermute | solution.py:32
  685.0 14.2 %collective-permute-start.91 = (bf16[120,640]{1,0:T(8,128)(2,1)S(1)}, bf16[120,640]{1,0:T(8,128)(2,1)S(1)}, u32[]{:S(2)}, u32[]{:S(2)}) collective-permute-start(bf16[120,640]{1,0:T(8,128)(2,1)S(1)} %fusion.11), channel_id=1, source_target_pairs={{0,8},{1,9},{2,10},{3,11},{4,12},{5,13},{6,14},{7,15},{8,0},{9,1},... | collective-permute-start | bytes 460808 | tf_op jit(solution)/shard_map/ppermute | solution.py:32
  685.1 38.1 %collective-permute-start.110 = (bf16[2,120,640]{2,1,0:T(8,128)(2,1)S(1)}, bf16[2,120,640]{2,1,0:T(8,128)(2,1)S(1)}, u32[]{:S(2)}, u32[]{:S(2)}) collective-permute-start(bf16[2,120,640]{2,1,0:T(8,128)(2,1)S(1)} %pad_maximum_fusion.11), channel_id=1, source_target_pairs={{0,16},{1,17},{2,18},{3,19},{4,20},{5,21},{6,22},{7,23},{8,24},{9,... | collective-permute-start | bytes 921608 | tf_op jit(solution)/shard_map/ppermute | solution.py:32
  698.1 32.9 %collective-permute-start.120 = (bf16[4,80,960]{2,1,0:T(8,128)(2,1)S(1)}, bf16[4,80,960]{2,1,0:T(8,128)(2,1)S(1)}, u32[]{:S(2)}, u32[]{:S(2)}) collective-permute-start(bf16[4,80,960]{2,1,0:T(8,128)(2,1)S(1)} %get-tuple-element.259), channel_id=1, source_target_pairs={{0,4},{1,5},{2,6},{3,7},{4,0},{5,1},{6,2},{7,3},{8,12},{9,13},{10,... | collective-permute-start | bytes 1843208 | tf_op jit(solution)/shard_map/ppermute | solution.py:32
  699.3 30.6 %collective-permute-start.92 = (bf16[2,120,640]{2,1,0:T(8,128)(2,1)S(1)}, bf16[2,120,640]{2,1,0:T(8,128)(2,1)S(1)}, u32[]{:S(2)}, u32[]{:S(2)}) collective-permute-start(bf16[2,120,640]{2,1,0:T(8,128)(2,1)S(1)} %pad_maximum_fusion.9), channel_id=1, source_target_pairs={{0,16},{1,17},{2,18},{3,19},{4,20},{5,21},{6,22},{7,23},{8,24},{9,... | collective-permute-start | bytes 921608 | tf_op jit(solution)/shard_map/ppermute | solution.py:32
  710.2 23.2 %collective-permute-start.102 = (bf16[4,120,640]{2,1,0:T(8,128)(2,1)S(1)}, bf16[4,120,640]{2,1,0:T(8,128)(2,1)S(1)}, u32[]{:S(2)}, u32[]{:S(2)}) collective-permute-start(bf16[4,120,640]{2,1,0:T(8,128)(2,1)S(1)} %get-tuple-element.270), channel_id=1, source_target_pairs={{0,4},{1,5},{2,6},{3,7},{4,0},{5,1},{6,2},{7,3},{8,12},{9,13},{10,... | collective-permute-start | bytes 1843208 | tf_op jit(solution)/shard_map/ppermute | solution.py:32
  723.4 16.0 %collective-permute-start.111 = (bf16[4,120,640]{2,1,0:T(8,128)(2,1)S(1)}, bf16[4,120,640]{2,1,0:T(8,128)(2,1)S(1)}, u32[]{:S(2)}, u32[]{:S(2)}) collective-permute-start(bf16[4,120,640]{2,1,0:T(8,128)(2,1)S(1)} %get-tuple-element.268), channel_id=1, source_target_pairs={{0,4},{1,5},{2,6},{3,7},{4,0},{5,1},{6,2},{7,3},{8,12},{9,13},{10,... | collective-permute-start | bytes 1843208 | tf_op jit(solution)/shard_map/ppermute | solution.py:32
  729.9 22.6 %collective-permute-start.93 = (bf16[4,120,640]{2,1,0:T(8,128)(2,1)S(1)}, bf16[4,120,640]{2,1,0:T(8,128)(2,1)S(1)}, u32[]{:S(2)}, u32[]{:S(2)}) collective-permute-start(bf16[4,120,640]{2,1,0:T(8,128)(2,1)S(1)} %get-tuple-element.272), channel_id=1, source_target_pairs={{0,4},{1,5},{2,6},{3,7},{4,0},{5,1},{6,2},{7,3},{8,12},{9,13},{10,... | collective-permute-start | bytes 1843208 | tf_op jit(solution)/shard_map/ppermute | solution.py:32
  731.1 92.0 %collective-permute-start.121 = (bf16[2,4,80,960]{3,2,1,0:T(8,128)(2,1)S(1)}, bf16[2,4,80,960]{3,2,1,0:T(8,128)(2,1)}, u32[]{:S(2)}, u32[]{:S(2)}) collective-permute-start(bf16[2,4,80,960]{3,2,1,0:T(8,128)(2,1)S(1)} %pad_maximum_fusion.near_ref), channel_id=1, source_target_pairs={{0,2},{1,3},{2,0},{3,1},{4,6},{5,7},{6,4},{7,5},{8,10},{9,11},{10,... | collective-permute-start | bytes 3686408 | tf_op jit(solution)/shard_map/ppermute | solution.py:32
  734.6 98.8 %collective-permute-start.103 = (bf16[2,4,120,640]{3,2,1,0:T(8,128)(2,1)}, bf16[2,4,120,640]{3,2,1,0:T(8,128)(2,1)}, u32[]{:S(2)}, u32[]{:S(2)}) collective-permute-start(bf16[2,4,120,640]{3,2,1,0:T(8,128)(2,1)} %pad_maximum_fusion.2.near_ref), channel_id=1, source_target_pairs={{0,2},{1,3},{2,0},{3,1},{4,6},{5,7},{6,4},{7,5},{8,10},{9,11},{10,... | collective-permute-start | bytes 3686408 | tf_op jit(solution)/shard_map/ppermute | solution.py:32
  740.6 97.0 %collective-permute-start.112 = (bf16[2,4,120,640]{3,2,1,0:T(8,128)(2,1)}, bf16[2,4,120,640]{3,2,1,0:T(8,128)(2,1)}, u32[]{:S(2)}, u32[]{:S(2)}) collective-permute-start(bf16[2,4,120,640]{3,2,1,0:T(8,128)(2,1)} %pad_maximum_fusion.3.near_ref), channel_id=1, source_target_pairs={{0,2},{1,3},{2,0},{3,1},{4,6},{5,7},{6,4},{7,5},{8,10},{9,11},{10,... | collective-permute-start | bytes 3686408 | tf_op jit(solution)/shard_map/ppermute | solution.py:32
  752.7 89.1 %collective-permute-start.94 = (bf16[2,4,120,640]{3,2,1,0:T(8,128)(2,1)S(1)}, bf16[2,4,120,640]{3,2,1,0:T(8,128)(2,1)}, u32[]{:S(2)}, u32[]{:S(2)}) collective-permute-start(bf16[2,4,120,640]{3,2,1,0:T(8,128)(2,1)S(1)} %pad_maximum_fusion.1.near_ref), channel_id=1, source_target_pairs={{0,2},{1,3},{2,0},{3,1},{4,6},{5,7},{6,4},{7,5},{8,10},{9,11},{10,... | collective-permute-start | bytes 3686408 | tf_op jit(solution)/shard_map/ppermute | solution.py:32
  773.2 16.6 %collective-permute-start.59 = (bf16[128,960]{1,0:T(8,128)(2,1)S(1)}, bf16[128,960]{1,0:T(8,128)(2,1)S(1)}, u32[]{:S(2)}, u32[]{:S(2)}) collective-permute-start(bf16[128,960]{1,0:T(8,128)(2,1)S(1)} %copy-done.76), channel_id=1, source_target_pairs={{0,0},{1,16},{2,2},{3,18},{4,4},{5,20},{6,6},{7,22},{8,8},{9,24},{... | collective-permute-start | bytes 737288 | tf_op jit(solution)/shard_map/ppermute | solution.py:41
  793.2 28.9 %collective-permute-start.85 = (f32[128,960]{1,0:T(8,128)}, f32[128,960]{1,0:T(8,128)S(1)}, u32[]{:S(2)}, u32[]{:S(2)}) collective-permute-start(f32[128,960]{1,0:T(8,128)} %get-tuple-element.147), channel_id=1, source_target_pairs={{0,0},{1,16},{2,2},{3,18},{4,4},{5,20},{6,6},{7,22},{8,8},{9,24},{... | collective-permute-start | bytes 1474568 | tf_op jit(solution)/shard_map/ppermute | solution.py:41
  (147 other events, 1533.6 us)

commit v2 on v1

v2 whole, which is shorter than its diff:
```python
import functools

import jax
import jax.numpy as jnp
from jax import lax
from jax.experimental import pallas as pl
from jax.experimental.pallas import tpu as pltpu
from jax.sharding import PartitionSpec as P

QUERY_HEADS = 15
KEY_VALUE_HEADS = 5
HEAD_SIZE = 64
SHARE = QUERY_HEADS // KEY_VALUE_HEADS
BLK = 64
CONT_BITS = 10
EPSILON = 1e-05
ROPE_BASE = 10000.0
MASK_FLOOR = -1e30
SCALE = HEAD_SIZE ** (-0.5)

BF = jnp.bfloat16
F32 = jnp.float32
AXES = ("ctx", "ws")
FF_CHUNK = 512
MIB = 1024 * 1024
VMEM_JOIN = 24 * MIB

Y_BIT, C_BIT, X_BIT, Z1_BIT, Z2_BIT = 1, 2, 4, 8, 16
NEAR = (0, X_BIT, Y_BIT, Z1_BIT, X_BIT | Y_BIT | Z1_BIT, X_BIT | Y_BIT, Y_BIT | Z1_BIT, Z1_BIT | X_BIT)


def hop(value, mask):
    return lax.ppermute(value, AXES, [(i, i ^ mask) for i in range(32)])


def swap_place(i):
    y, z2 = i & 1, (i >> 4) & 1
    return (i & ~(Y_BIT | Z2_BIT)) | (Z2_BIT if y else 0) | (Y_BIT if z2 else 0)


def move(value):
    return lax.ppermute(value, AXES, [(i, swap_place(i)) for i in range(32)])


def ctx_mask(mask):
    return (
        (1 if mask & C_BIT else 0)
        | (2 if mask & X_BIT else 0)
        | (4 if mask & Z1_BIT else 0)
        | (8 if mask & Y_BIT else 0)
    )


NT = (((1,), (1,)), ((), ()))
TN = (((0,), (0,)), ((), ()))
NN = (((1,), (0,)), ((), ()))


def mm(left, right, dims=NN, precision=None):
    return lax.dot_general(left, right, dims, precision=precision, preferred_element_type=F32)


def normed_rows(values):
    inverse = lax.rsqrt(jnp.mean(values * values, axis=-1, keepdims=True) + EPSILON)
    return values * inverse, inverse


def norm_back(grad_in, normed, inverse, gain):
    scaled = grad_in * gain
    return inverse * (scaled - normed * jnp.mean(scaled * normed, axis=-1, keepdims=True))


def turn(values, cosine, sine, back=False):
    rows, width = values.shape
    lane = lax.broadcasted_iota(jnp.int32, (rows, 128), 1)
    first = (lane & (HEAD_SIZE - 1)) < HEAD_SIZE // 2
    if back:
        sine = -sine
    pieces = []
    for start in range(0, width, 128):
        wide = min(128, width - start)
        part = values[:, start : start + wide]
        if wide < 128:
            part = jnp.concatenate([part, jnp.zeros((rows, 128 - wide), F32)], axis=1)
        other = jnp.where(first, pltpu.roll(part, 96, 1), pltpu.roll(part, 32, 1))
        pieces.append((part * cosine + other * sine)[:, :wide])
    return jnp.concatenate(pieces, axis=1)


def vm():
    return pl.BlockSpec(memory_space=pltpu.VMEM)


def sm():
    return pl.BlockSpec(memory_space=pltpu.SMEM)


def hbm():
    return pl.BlockSpec(memory_space=pl.ANY)


def shaped(shape, dtype):
    return jax.ShapeDtypeStruct(shape, dtype)


def params(mib, **kw):
    return pltpu.CompilerParams(vmem_limit_bytes=mib * MIB, **kw)


def estimate(flops, nbytes):
    return pl.CostEstimate(flops=int(flops), bytes_accessed=int(nbytes), transcendentals=0)


class Order:
    def __init__(self, token):
        self.token = token

    def take(self, *values):
        *values, self.token = lax.optimization_barrier(values + (self.token,))
        return values[0] if len(values) == 1 else values


def read_coords(ref):
    return [ref[i] for i in range(4)]


def aligned(row):
    return row if isinstance(row, int) else pl.multiple_of(row, 8)


def join_kernel(plans, n_arrays, coords_ref, *args):
    refs, outs, sems = args[:n_arrays], args[n_arrays:-1], args[-1]
    coords = read_coords(coords_ref)
    copies = []
    for out, plan in zip(outs, plans, strict=True):
        for array, index, first, rows, place in plan:
            source = refs[array] if index is None else refs[array].at[index]
            source = source.at[pl.ds(first, rows), :]
            cols = source.shape[1]
            row, col = place(*coords)
            target = out.at[pl.ds(aligned(row), rows), :]
            if cols != out.shape[1]:
                target = out.at[pl.ds(aligned(row), rows), pl.ds(pl.multiple_of(col, 128), cols)]
            copy = pltpu.make_async_copy(source, target, sems.at[len(copies)])
            copy.start()
            copies.append(copy)
    for copy in copies:
        copy.wait()


def join_call(coords, arrays, shapes, plans):
    count = sum(len(plan) for plan in plans)
    return pl.pallas_call(
        functools.partial(join_kernel, plans, len(arrays)),
        name="join_weights",
        out_shape=tuple(pltpu.VMEM(shape, BF) for shape in shapes),
        in_specs=[sm()] + [hbm()] * len(arrays),
        out_specs=tuple(vm() for _ in shapes),
        scratch_shapes=[pltpu.SemaphoreType.DMA((count,))],
        compiler_params=pltpu.CompilerParams(vmem_limit_bytes=VMEM_JOIN),
        cost_estimate=estimate(0, sum(2 * a * b for a, b in shapes)),
    )(coords, *arrays)


def pack_kernel(coords_ref, q_ref, k_ref, v_ref, gain1_ref, gain2_ref, own_ref, piece_ref):
    half, width = q_ref.shape
    kv_width = k_ref.shape[0]
    own_ref[:, :width] = q_ref[...]
    own_ref[:, width : width + kv_width] = k_ref[...].T
    own_ref[:, width + kv_width :] = v_ref[...].T
    depth = half // 2
    start = pl.multiple_of(coords_ref[1] * depth, 8)
    piece_ref[:depth, :] = own_ref[pl.ds(start, depth), :]
    blank = jnp.zeros((1, own_ref.shape[1] - 2 * half), BF)
    row = jnp.concatenate([gain1_ref[...], gain2_ref[...], blank], axis=1)
    piece_ref[depth:, :] = jnp.broadcast_to(row, (8, row.shape[1]))


def pack_call(coords, w_query, key_t, value_t, gain_attn, gain_ffn):
    half, width = w_query.shape
    total = width + 2 * key_t.shape[0]
    return pl.pallas_call(
        pack_kernel,
        name="pack",
        out_shape=(shaped((half, total), BF), shaped((half // 2 + 8, total), BF)),
        in_specs=[sm()] + [vm()] * 5,
        out_specs=(vm(), vm()),
        compiler_params=params(12),
        cost_estimate=estimate(0, 4e6),
    )(coords, w_query, key_t, value_t, gain_attn, gain_ffn)


def stack_kernel(*refs):
    out_ref = refs[-1]
    at = 0
    for ref in refs[:-1]:
        out_ref[at : at + ref.shape[0], :] = ref[...]
        at += ref.shape[0]


def stack_call(pieces):
    rows = sum(p.shape[0] for p in pieces)
    return pl.pallas_call(
        stack_kernel,
        name="stack",
        out_shape=shaped((rows, pieces[0].shape[1]), pieces[0].dtype),
        in_specs=[vm()] * len(pieces),
        out_specs=vm(),
        compiler_params=params(8),
        cost_estimate=estimate(0, 2e6),
    )(*pieces)


def split_kernel(total_ref, other_ref, *outs):
    rows = outs[0].shape[0]
    for i, out in enumerate(outs):
        at = slice(i * rows, (i + 1) * rows)
        out[...] = (total_ref[at, :] + other_ref[at, :].astype(F32)).astype(out.dtype)


def split_call(total, other):
    rows, width = total.shape[0] // len(NEAR), total.shape[1]
    outs = [shaped((rows, width), F32)] + [shaped((rows, width), BF)] * (len(NEAR) - 1)
    return pl.pallas_call(
        split_kernel,
        name="split",
        out_shape=tuple(outs),
        in_specs=[vm(), vm()],
        out_specs=tuple(vm() for _ in outs),
        compiler_params=params(10),
        cost_estimate=estimate(0, 4e6),
    )(total, other)


def project(x, gain, wqkv_ref, cosine, sine, first_ref, q_ref, kv_ref):
    normed, _ = normed_rows(x)
    first_in = (normed * gain).astype(BF)
    first_ref[...] = first_in
    rows = mm(first_in, wqkv_ref[...])
    wide = SHARE * HEAD_SIZE
    q_width = KEY_VALUE_HEADS * wide
    kv_width = KEY_VALUE_HEADS * HEAD_SIZE
    key = turn(rows[:, q_width : q_width + kv_width], cosine, sine)
    value = rows[:, q_width + kv_width :]
    for h in range(KEY_VALUE_HEADS):
        at = slice(h * HEAD_SIZE, (h + 1) * HEAD_SIZE)
        kv_ref[:, h * 128 : (h + 1) * 128] = jnp.concatenate(
            [key[:, at], value[:, at]], axis=1
        ).astype(BF)
    query = (turn(rows[:, :q_width], cosine, sine).astype(BF) * SCALE).astype(BF)
    for h in range(KEY_VALUE_HEADS):
        q_ref[h] = query[:, h * wide : (h + 1) * wide]


def first_kernel(x_ref, gain_ref, cos_ref, sin_ref, wqkv_ref, first_ref, q_ref, kv_ref):
    project(
        x_ref[...].astype(F32), gain_ref[...], wqkv_ref, cos_ref[...], sin_ref[...],
        first_ref, q_ref, kv_ref,
    )


def first_call(tokens, gain, cosine, sine, wqkv):
    rows, width = tokens.shape
    return pl.pallas_call(
        first_kernel,
        name="first_projection",
        out_shape=(
            shaped((rows, width), BF),
            shaped((KEY_VALUE_HEADS, rows, SHARE * HEAD_SIZE), BF),
            shaped((rows, KEY_VALUE_HEADS * 128), BF),
        ),
        in_specs=[vm()] * 5,
        out_specs=(vm(), vm(), vm()),
        compiler_params=params(10),
        cost_estimate=estimate(2 * rows * width * 1600, 4e6),
    )(tokens, gain, cosine, sine, wqkv)


def padded_heads(wide_rows, left):
    rows = wide_rows.shape[0]
    blank = jnp.zeros((rows, HEAD_SIZE), wide_rows.dtype)
    stacked = []
    for j in range(SHARE):
        part = wide_rows[:, j * HEAD_SIZE : (j + 1) * HEAD_SIZE]
        stacked.append(jnp.concatenate([part, blank] if left else [blank, part], axis=1))
    return jnp.concatenate(stacked, axis=0)


def attend_kernel(prompt, q_ref, a_ref, b_ref, kpos_ref, live_ref, qpos_ref, p_ref, o_ref, bias_scr):
    rows = q_ref.shape[1]
    half = a_ref.shape[0]

    @pl.when(pl.program_id(0) == 0)
    def _():
        kpos = kpos_ref[...]
        klive = live_ref[...] > 0
        kseg = jnp.where(kpos < prompt, 0, 1 + ((kpos - prompt) >> CONT_BITS))

        def fill(i, carry):
            at = pl.ds(pl.multiple_of(i * 8, 8), 8)
            qpos = qpos_ref[at, :]
            qseg = jnp.where(qpos < prompt, 0, 1 + ((qpos - prompt) >> CONT_BITS))
            earlier = kpos <= qpos
            shared = (kseg == 0) | (kseg == qseg)
            seen = earlier & shared & (klive | (kpos == qpos))
            bias_scr[at, :] = jnp.where(seen, 0.0, MASK_FLOOR)
            return carry

        lax.fori_loop(0, rows // 8, fill, 0)

    together = rows < 128
    if together:
        stacked = padded_heads(q_ref[0], True)
        all_a, all_b = mm(stacked, a_ref[...], NT), mm(stacked, b_ref[...], NT)
    blank = jnp.zeros((rows, HEAD_SIZE), BF)
    outs = []
    for j in range(SHARE):
        at = slice(j * rows, (j + 1) * rows)
        if together:
            s_a, s_b = all_a[at], all_b[at]
        else:
            part = jnp.concatenate([q_ref[0, :, j * HEAD_SIZE : (j + 1) * HEAD_SIZE], blank], axis=1)
            s_a, s_b = mm(part, a_ref[...], NT), mm(part, b_ref[...], NT)
        s_a = s_a + bias_scr[:, :half]
        s_b = s_b + bias_scr[:, half:]
        top = jnp.maximum(
            jnp.max(s_a, axis=-1, keepdims=True), jnp.max(s_b, axis=-1, keepdims=True)
        )
        w_a, w_b = jnp.exp(s_a - top), jnp.exp(s_b - top)
        mass = jnp.sum(w_a, axis=-1, keepdims=True) + jnp.sum(w_b, axis=-1, keepdims=True)
        inverse = 1.0 / mass
        p_a, p_b = (w_a * inverse).astype(BF), (w_b * inverse).astype(BF)
        p_ref[0, at, :half] = p_a
        p_ref[0, at, half:] = p_b
        if not together:
            outs.append((mm(p_a, a_ref[...]) + mm(p_b, b_ref[...]))[:, HEAD_SIZE:])
    if together:
        mixed = mm(p_ref[0, :, :half], a_ref[...]) + mm(p_ref[0, :, half:], b_ref[...])
        outs = [mixed[j * rows : (j + 1) * rows, HEAD_SIZE:] for j in range(SHARE)]
    o_ref[0] = jnp.concatenate(outs, axis=1).astype(BF)


def attend_call(query, part_a, part_b, kpos, klive, qpos, prompt):
    heads, rows, wide = query.shape
    half = part_a.shape[0]
    keys = 2 * half
    return pl.pallas_call(
        functools.partial(attend_kernel, prompt),
        name="attend",
        grid=(heads,),
        out_shape=(pltpu.HBM((heads, SHARE * rows, keys), BF), shaped((heads, rows, wide), BF)),
        in_specs=[
            pl.BlockSpec((1, rows, wide), lambda h: (h, 0, 0)),
            pl.BlockSpec((half, 128), lambda h: (0, h)),
            pl.BlockSpec((half, 128), lambda h: (0, h)),
            pl.BlockSpec((1, keys), lambda h: (0, 0)),
            pl.BlockSpec((1, keys), lambda h: (0, 0)),
            pl.BlockSpec((rows, 1), lambda h: (0, 0)),
        ],
        out_specs=(
            pl.BlockSpec((1, SHARE * rows, keys), lambda h: (h, 0, 0)),
            pl.BlockSpec((1, rows, wide), lambda h: (h, 0, 0)),
        ),
        scratch_shapes=[pltpu.VMEM((rows, keys), F32)],
        compiler_params=params(12 if keys <= 2048 else 56, dimension_semantics=("arbitrary",)),
        cost_estimate=estimate(8 * heads * SHARE * rows * keys * 128, heads * SHARE * rows * keys * 2),
    )(query, part_a, part_b, kpos, klive, qpos)


def attend_back_kernel(q_ref, do_ref, a_ref, b_ref, p_ref, dq_ref, da_ref, db_ref, dp_scr, ds_scr):
    rows = q_ref.shape[1]
    half = a_ref.shape[0]
    stacked = padded_heads(q_ref[0], True)
    grads = padded_heads(do_ref[0], False)
    dp_scr[:, :half] = mm(grads, a_ref[...], NT)
    dp_scr[:, half:] = mm(grads, b_ref[...], NT)

    for j in range(SHARE):
        at = slice(j * rows, (j + 1) * rows)
        weights = p_ref[0, at, :].astype(F32)
        dp = dp_scr[at, :]
        delta = jnp.sum(weights * dp, axis=-1, keepdims=True)
        ds_scr[at, :] = (weights * (dp - delta)).astype(BF)
    dq = (mm(ds_scr[:, :half], a_ref[...]) + mm(ds_scr[:, half:], b_ref[...])) * SCALE
    dq_ref[0] = jnp.concatenate(
        [dq[j * rows : (j + 1) * rows, :HEAD_SIZE] for j in range(SHARE)], axis=1
    )
    for at, out in ((slice(0, half), da_ref), (slice(half, 2 * half), db_ref)):
        turned = mm(stacked, ds_scr[:, at], TN) + mm(grads, p_ref[0, :, at], TN)
        out[...] = turned.T.astype(out.dtype)


def attend_back_call(query, d_out, part_a, part_b, weights):
    heads, rows, wide = query.shape
    half = part_a.shape[0]
    keys = 2 * half
    return pl.pallas_call(
        attend_back_kernel,
        name="attend_back",
        grid=(heads,),
        out_shape=(
            shaped((heads, rows, wide), F32),
            shaped((half, heads * 128), F32),
            shaped((half, heads * 128), BF),
        ),
        in_specs=[
            pl.BlockSpec((1, rows, wide), lambda h: (h, 0, 0)),
            pl.BlockSpec((1, rows, wide), lambda h: (h, 0, 0)),
            pl.BlockSpec((half, 128), lambda h: (0, h)),
            pl.BlockSpec((half, 128), lambda h: (0, h)),
            pl.BlockSpec((1, SHARE * rows, keys), lambda h: (h, 0, 0)),
        ],
        out_specs=(
            pl.BlockSpec((1, rows, wide), lambda h: (h, 0, 0)),
            pl.BlockSpec((half, 128), lambda h: (0, h)),
            pl.BlockSpec((half, 128), lambda h: (0, h)),
        ),
        scratch_shapes=[
            pltpu.VMEM((SHARE * rows, keys), F32),
            pltpu.VMEM((SHARE * rows, keys), BF),
        ],
        compiler_params=params(14 if keys <= 2048 else 60, dimension_semantics=("arbitrary",)),
        cost_estimate=estimate(16 * heads * SHARE * rows * keys * 128, heads * SHARE * rows * keys * 2),
    )(query, d_out, part_a, part_b, weights)


def picks(sel_ref, total_rows):
    capacity = sel_ref.shape[1]
    row = lax.broadcasted_iota(jnp.int32, (total_rows, capacity), 0)
    return row == sel_ref[...]


def live_column(live_ref, rows):
    count = jnp.sum(live_ref[:, :].astype(F32), axis=1, keepdims=True)
    return lax.broadcasted_iota(jnp.int32, (rows, 1), 0).astype(F32) < count


def feed_forward(x, ao_ref, gain_two, wo, wg, wu, wd, ao_out, mid_ref, second_ref, g_ref, u_ref, hid_ref, y_scr):
    rows = x.shape[0]
    mixed = jnp.concatenate([ao_ref[h] for h in range(KEY_VALUE_HEADS)], axis=1)
    ao_out[...] = mixed
    middle = x + mm(mixed, wo[...])
    mid_ref[...] = middle
    normed, _ = normed_rows(middle)
    second_ref[...] = (normed * gain_two).astype(BF)
    y_scr[...] = middle

    def chunk(j, carry):
        at = pl.ds(pl.multiple_of(j * FF_CHUNK, FF_CHUNK), FF_CHUNK)
        second = second_ref[...]
        g = mm(second, wg[:, at])
        u = mm(second, wu[:, at])
        g_ref[:, at] = g
        u_ref[:, at] = u
        hidden = (g / (1.0 + jnp.exp(-g)) * u).astype(BF)
        hid_ref[:, at] = hidden
        y_scr[...] += mm(hidden, wd[:, at], NT)
        return carry

    lax.fori_loop(0, wg.shape[1] // FF_CHUNK, chunk, 0)


def dense_kernel(step, *args):
    args = list(args)
    take = lambda k: [args.pop(0) for _ in range(k)]
    x_ref, ao_ref, gain1_ref, gain2_ref = take(4)
    if step == 0:
        sel_ref, cos_ref, sin_ref = take(3)
    elif step == 1:
        live_ref, cos_ref, sin_ref = take(3)
    else:
        sel_ref, live2_ref, live_ref, h1_ref, h2_ref = take(5)
    wo, wg, wu, wd = take(4)
    if step < 2:
        (wqkv,) = take(1)
    ao_out, mid_ref, second_ref, g_ref, u_ref, hid_ref = take(6)
    if step < 2:
        h_ref, next_ref, first_ref, q_ref, kv_ref = take(5)
    else:
        (out_ref,) = take(1)
    (y_scr,) = take(1)
    rows = x_ref.shape[0]
    x = x_ref[...].astype(F32)
    feed_forward(
        x, ao_ref, gain2_ref[...], wo, wg, wu, wd, ao_out, mid_ref, second_ref,
        g_ref, u_ref, hid_ref, y_scr,
    )
    updated = y_scr[...]
    if step == 0:
        h_ref[...] = updated
        chosen = picks(sel_ref, rows).astype(F32)
        following = mm(chosen, updated, TN, lax.Precision.HIGHEST)
    else:
        updated = jnp.where(live_column(live_ref, rows), updated, x)
    if step == 1:
        h_ref[...] = updated
        following = updated[: next_ref.shape[0]]
    if step < 2:
        next_ref[...] = following
        project(
            following, gain1_ref[...], wqkv, cos_ref[...], sin_ref[...],
            first_ref, q_ref, kv_ref,
        )
    else:
        slots = jnp.concatenate([updated, h2_ref[rows:, :]], axis=0).astype(BF)
        hit = picks(sel_ref, h1_ref.shape[0]) & (live2_ref[...] > 0)
        placed = mm(hit.astype(BF), slots)
        any_hit = jnp.sum(hit.astype(F32), axis=1, keepdims=True) > 0.5
        out_ref[...] = jnp.where(any_hit, placed, h1_ref[...]).astype(BF)


def dense_call(near, step, x, mixed, gain1, gain2, extra, weights, next_rows):
    rows, width = x.shape
    hidden = weights[1].shape[1]
    outs = [
        shaped((rows, width), BF),
        shaped((rows, width), F32),
        shaped((rows, width), BF),
        shaped((rows, hidden), F32),
        shaped((rows, hidden), F32),
        shaped((rows, hidden), BF),
    ]
    if step < 2:
        outs += [
            shaped((rows, width), F32),
            shaped((next_rows, width), F32),
            shaped((next_rows, width), BF),
            shaped((KEY_VALUE_HEADS, next_rows, SHARE * HEAD_SIZE), BF),
            shaped((next_rows, KEY_VALUE_HEADS * 128), BF),
        ]
    else:
        outs += [shaped((next_rows, width), BF)]
    return pl.pallas_call(
        functools.partial(dense_kernel, step),
        name=f"dense_{step}",
        out_shape=tuple(outs),
        in_specs=[vm()] * (4 + len(extra) + len(weights)),
        out_specs=tuple(vm() for _ in outs),
        scratch_shapes=[pltpu.VMEM((rows, width), F32)],
        compiler_params=params(10 if near else 56),
        cost_estimate=estimate(2 * rows * 9.83e6, 2.4e7),
    )(x, mixed, gain1, gain2, *extra, *weights)


def feed_back(d_y, mid_ref, g_ref, u_ref, gain_two, wd, wg, wu, wo, dyb_ref, dg_ref, du_ref, dmid_ref, dz_ref, dao_ref, sum_ref, acc_scr):
    dyb_ref[...] = d_y.astype(BF)
    acc_scr[...] = jnp.zeros_like(acc_scr)

    def chunk(j, carry):
        at = pl.ds(pl.multiple_of(j * FF_CHUNK, FF_CHUNK), FF_CHUNK)
        d_hidden = mm(dyb_ref[...], wd[:, at])
        g, u = g_ref[:, at], u_ref[:, at]
        sigma = 1.0 / (1.0 + jnp.exp(-g))
        d_gate = (d_hidden * u * sigma * (1.0 + g * (1.0 - sigma))).astype(BF)
        d_up = (d_hidden * (g * sigma)).astype(BF)
        dg_ref[:, at] = d_gate
        du_ref[:, at] = d_up
        acc_scr[...] += mm(d_gate, wg[:, at], NT) + mm(d_up, wu[:, at], NT)
        return carry

    lax.fori_loop(0, wg.shape[1] // FF_CHUNK, chunk, 0)
    d_second = acc_scr[...]
    normed, inverse = normed_rows(mid_ref[...])
    sum_ref[...] = jnp.sum(d_second * normed, axis=0, keepdims=True)
    d_mid = norm_back(d_second, normed, inverse, gain_two) + d_y
    dmid_ref[...] = d_mid
    d_low = d_mid.astype(BF)
    dz_ref[...] = d_low
    d_mixed = mm(d_low, wo[...], NT).astype(BF)
    wide = SHARE * HEAD_SIZE
    for h in range(KEY_VALUE_HEADS):
        dao_ref[h] = d_mixed[:, h * wide : (h + 1) * wide]


def project_back(own_ref, others, dq_ref, x, dmid_ref, gain_one, cosine, sine, wqkv, dqkv_ref, sum_ref):
    total = own_ref[...].astype(F32)
    for other in others:
        total = total + other[...].astype(F32)
    d_key = jnp.concatenate(
        [total[:, h * 128 : h * 128 + HEAD_SIZE] for h in range(KEY_VALUE_HEADS)], axis=1
    )
    d_value = jnp.concatenate(
        [total[:, h * 128 + HEAD_SIZE : (h + 1) * 128] for h in range(KEY_VALUE_HEADS)], axis=1
    )
    d_query = jnp.concatenate([dq_ref[h] for h in range(KEY_VALUE_HEADS)], axis=1)
    d_rows = jnp.concatenate(
        [turn(d_query, cosine, sine, True), turn(d_key, cosine, sine, True), d_value], axis=1
    ).astype(BF)
    dqkv_ref[...] = d_rows
    d_first = mm(d_rows, wqkv[...], NT)
    normed, inverse = normed_rows(x)
    sum_ref[...] = jnp.sum(d_first * normed, axis=0, keepdims=True)
    return norm_back(d_first, normed, inverse, gain_one) + dmid_ref[...]


def back_kernel(phase, n_parts, *args):
    args = list(args)
    take = lambda k: [args.pop(0) for _ in range(k)]
    if phase > 0:
        gain1_ref, cos_ref, sin_ref, x_ref, dmid_in, dq_ref = take(6)
        own_ref, *others = take(n_parts)
    if phase < 3:
        gain2_ref, mid_ref, g_ref, u_ref = take(4)
    if phase == 0:
        cot_ref, sel_ref, live3_ref = take(3)
    elif phase == 1:
        slots_ref, live3_ref, live2_ref = take(3)
    elif phase == 2:
        cot_ref, sel_ref, live2_ref = take(3)
    if phase > 0:
        (wqkv,) = take(1)
    if phase < 3:
        mats = take(4)
    if phase > 0:
        dqkv_ref, sum1_ref = take(2)
    if phase < 3:
        dyb_ref, dg_ref, du_ref, dmid_ref, dz_ref, dao_ref, sum2_ref = take(7)
    if phase == 0:
        (slots_out,) = take(1)
    elif phase == 3:
        (grad_ref,) = take(1)
    if phase < 3:
        (acc_scr,) = take(1)
    if phase > 0:
        d_x = project_back(
            own_ref, others, dq_ref, x_ref[...].astype(F32), dmid_in, gain1_ref[...],
            cos_ref[...], sin_ref[...], wqkv, dqkv_ref, sum1_ref,
        )
    if phase == 0:
        chosen = picks(sel_ref, cot_ref.shape[0]).astype(BF)
        slots = mm(chosen, cot_ref[...], TN)
        slots_out[...] = slots
        rows = mid_ref.shape[0]
        d_y = jnp.where(live_column(live3_ref, rows), slots[:rows], 0.0)
    elif phase == 1:
        rows = x_ref.shape[0]
        slots = slots_ref[...]
        head = jnp.where(live_column(live3_ref, rows), d_x, slots[:rows])
        slots = jnp.concatenate([head, slots[rows:]], axis=0)
        d_y = jnp.where(live_column(live2_ref, slots.shape[0]), slots, 0.0)
    elif phase == 2:
        hit = picks(sel_ref, cot_ref.shape[0]) & (live2_ref[...] > 0)
        placed = mm(hit.astype(F32), d_x, NN, lax.Precision.HIGHEST)
        any_hit = jnp.sum(hit.astype(F32), axis=1, keepdims=True) > 0.5
        d_y = jnp.where(any_hit, placed, cot_ref[...].astype(F32))
    else:
        grad_ref[...] = d_x
        return
    feed_back(
        d_y, mid_ref, g_ref, u_ref, gain2_ref[...], *mats,
        dyb_ref, dg_ref, du_ref, dmid_ref, dz_ref, dao_ref, sum2_ref, acc_scr,
    )


def back_call(near, phase, before, parts, into, extra, weights, rows_next):
    ins = list(before) + list(parts) + list(into) + list(extra) + list(weights)
    outs, scratch = [], []
    if phase > 0:
        rows, width = before[3].shape
        outs += [
            shaped((rows, weights[0].shape[1]), BF),
            shaped((1, width), F32),
        ]
    if phase < 3:
        rows, hidden = into[2].shape
        width = into[1].shape[1]
        outs += [
            shaped((rows, width), BF),
            shaped((rows, hidden), BF),
            shaped((rows, hidden), BF),
            shaped((rows, width), F32),
            shaped((rows, width), BF),
            shaped((KEY_VALUE_HEADS, rows, SHARE * HEAD_SIZE), BF),
            shaped((1, width), F32),
        ]
        scratch += [pltpu.VMEM((rows, width), F32)]
    if phase == 0:
        outs += [shaped((rows_next, width), F32)]
    elif phase == 3:
        outs += [shaped((rows, width), F32)]
    return pl.pallas_call(
        functools.partial(back_kernel, phase, len(parts)),
        name=f"back_{phase}",
        out_shape=tuple(outs),
        in_specs=[vm()] * len(ins),
        out_specs=tuple(vm() for _ in outs),
        scratch_shapes=scratch,
        compiler_params=params(10 if near else 56),
        cost_estimate=estimate(2 * rows * 9.83e6, 2.4e7),
    )(*ins)


def stack_rows(refs, scratch):
    at = 0
    for ref in refs:
        scratch[at : at + ref.shape[0], :] = ref[...]
        at += ref.shape[0]


def put_blocks(value, x_of, coords, ref, per_row):
    y, _, x, z = coords
    depth = ref.shape[-2]
    for ya in range(2):
        for xa in range(2) if per_row else (None,):
            for za in range(4):
                row = (ya * (2 if per_row else 1) + (xa or 0)) * 4 + za
                ref[y ^ ya, (x ^ xa) if per_row else x_of, z ^ za] = value[
                    row * depth : (row + 1) * depth
                ].astype(BF)


def grad_cols_kernel(n_steps, coords_ref, *args):
    left, args = args[:n_steps], args[n_steps:]
    right, args = args[:n_steps], args[n_steps:]
    keep_ref, send_ref, l_scr, r_scr = args
    coords = read_coords(coords_ref)
    _, c, x, _ = coords
    stack_rows(left, l_scr)
    stack_rows(right, r_scr)
    block = keep_ref.shape[-1]
    for far, ref in ((1, send_ref), (0, keep_ref)):

        def body(rx, carry, far=far, ref=ref):
            start = pl.multiple_of(((c ^ far) * 2 + (x ^ rx)) * block, 128)
            value = mm(l_scr[...], r_scr[:, pl.ds(start, block)], TN)
            put_blocks(value, rx, coords, ref, False)
            return carry

        lax.fori_loop(0, 2, body, 0)


def grad_rows_kernel(n_steps, coords_ref, *args):
    left, args = args[:n_steps], args[n_steps:]
    right, args = args[:n_steps], args[n_steps:]
    keep_ref, send_ref, l_scr, r_scr = args
    coords = read_coords(coords_ref)
    y, c, x, z = coords
    stack_rows(left, l_scr)
    stack_rows(right, r_scr)
    depth = keep_ref.shape[-2]
    span = 8 * depth
    for far, ref in ((1, send_ref), (0, keep_ref)):

        def body(ry, carry, far=far, ref=ref):
            start = pl.multiple_of(((y ^ ry) * 2 + (c ^ far)) * span, 128)
            value = mm(l_scr[:, pl.ds(start, span)], r_scr[...], TN)
            for xa in range(2):
                for za in range(4):
                    row = (xa * 4 + za) * depth
                    ref[ry, x ^ xa, z ^ za] = value[row : row + depth].astype(BF)
            return carry

        lax.fori_loop(0, 2, body, 0)


def grad_mixed_kernel(n_steps, coords_ref, *args):
    groups = []
    for _ in range(4):
        groups.append(args[:n_steps])
        args = args[n_steps:]
    keep_ref, send_ref, first_scr, mixed_scr, qkv_scr, z_scr, val_scr = args
    coords = read_coords(coords_ref)
    _, c, x, _ = coords
    for refs, scr in zip(groups, (first_scr, mixed_scr, qkv_scr, z_scr), strict=True):
        stack_rows(refs, scr)
    block = keep_ref.shape[-1]
    width = z_scr.shape[1]
    kv_width = (qkv_scr.shape[1] - width) // 2
    for ca in range(2):
        for xa in range(2):
            if ca == 0:
                val_scr[...] = mm(first_scr[...], qkv_scr[:, xa * block : (xa + 1) * block], TN)
            elif xa == 0:
                val_scr[...] = mm(mixed_scr[...], z_scr[:, :block], TN)
            else:
                val_scr[...] = jnp.concatenate(
                    [
                        mm(mixed_scr[...], z_scr[:, block:], TN),
                        mm(first_scr[...], qkv_scr[:, width + kv_width :], TN),
                    ],
                    axis=1,
                )

            @pl.when(c == ca)
            def _(xa=xa):
                put_blocks(val_scr[...], x ^ xa, coords, keep_ref, False)

            @pl.when(c != ca)
            def _(xa=xa):
                put_blocks(val_scr[...], x ^ xa, coords, send_ref, False)


def grad_call(kind, coords, groups):
    n_steps = len(groups[0])
    rows = sum(a.shape[0] for a in groups[0])
    width, cols = groups[0][0].shape[1], groups[1][0].shape[1]
    scratch = [pltpu.VMEM((rows, g[0].shape[1]), BF) for g in groups]
    if kind == "rows":
        kernel, block = grad_rows_kernel, (width // 32, cols)
    elif kind == "cols":
        kernel, block = grad_cols_kernel, (width // 8, cols // 4)
    else:
        total = sum(g[0].shape[1] for g in groups[2:])
        kernel, block = grad_mixed_kernel, (width // 8, total // 4)
        scratch += [pltpu.VMEM((width, block[1]), F32)]
    out = shaped((2, 2, 4) + block, BF)
    ins = [a for g in groups for a in g]
    return pl.pallas_call(
        functools.partial(kernel, n_steps),
        name=f"grad_{kind}",
        out_shape=(out, out),
        in_specs=[sm()] + [vm()] * len(ins),
        out_specs=(vm(), vm()),
        scratch_shapes=scratch,
        compiler_params=params(16),
        cost_estimate=estimate(2 * rows * 16 * 2 * block[0] * block[1], 1e7),
    )(coords, *ins)


def place_cols_kernel(coords_ref, near_ref, far_ref, *outs):
    _, c, x, _ = read_coords(coords_ref)
    block = near_ref.shape[-1]
    target = outs[-1]
    for far, ref in ((0, near_ref), (1, far_ref)):
        for rx in range(2):
            cols = pl.ds(pl.multiple_of(((c ^ far) * 2 + (x ^ rx)) * block, 128), block)
            target[:, cols] = ref[rx, 0].astype(F32)
    if len(outs) > 1:
        at = 0
        for out in outs[:-1]:
            out[...] = target[:, at : at + out.shape[1]]
            at += out.shape[1]


def place_rows_kernel(coords_ref, near_ref, far_ref, out_ref, scr):
    _, _, x, z = read_coords(coords_ref)
    depth = near_ref.shape[-2]

    def put(ref):
        for rx in range(2):
            for rz in range(4):
                row = pl.multiple_of(((x ^ rx) * 4 + (z ^ rz)) * depth, 8)
                scr[pl.ds(row, depth), :] = ref[rx, rz].astype(F32)

    @pl.when(pl.program_id(0) == 0)
    def _():
        put(near_ref)

    @pl.when(pl.program_id(0) == 1)
    def _():
        put(far_ref)

    out_ref[...] = scr[...].T


def place_call(kind, coords, near, far, widths):
    depth, block = near.shape[-2:]
    scratch = []
    if kind == "rows":
        kernel, grid = place_rows_kernel, (2,)
        outs = (shaped((block, 16 * depth), F32),)
        source = pl.BlockSpec((2, 4, depth, block), lambda f, k: (0, 0, 0, 0))
        targets = (pl.BlockSpec((block, 8 * depth), lambda f, k: (0, k[1] ^ f)),)
        scratch = [pltpu.VMEM((8 * depth, block), F32)]
    else:
        kernel, grid = place_cols_kernel, (4,)
        outs = tuple(shaped((4 * depth, w), F32) for w in widths)
        source = pl.BlockSpec((2, 1, depth, block), lambda i, k: (0, i, 0, 0))
        targets = tuple(pl.BlockSpec((depth, w), lambda i, k: (k[3] ^ i, 0)) for w in widths)
        if len(outs) > 1:
            scratch = [pltpu.VMEM((depth, 4 * block), F32)]
    return pl.pallas_call(
        kernel,
        name=f"place_{kind}",
        grid_spec=pltpu.PrefetchScalarGridSpec(
            num_scalar_prefetch=1,
            grid=grid,
            in_specs=[source, source],
            out_specs=targets,
            scratch_shapes=scratch,
        ),
        out_shape=outs,
        compiler_params=params(12),
        cost_estimate=estimate(0, 1e7),
    )(coords, near, far)


def low_sum(left, right):
    return (left.astype(F32) + right.astype(F32)).astype(BF)


def gather_keys(kv, order, near, beside=((), (), ())):
    if not near:
        whole = lax.all_gather(kv, "ctx", axis=0, tiled=True)
        half = whole.shape[0] // 2
        return whole[:half], whole[half:]
    kv = order.take(kv)
    hops = [hop(kv, m) for m in (X_BIT, Y_BIT, Z1_BIT, X_BIT | Y_BIT | Z1_BIT)]
    for start in beside[0]:
        start()
    by_x, by_y, by_z, across = order.take(*hops)
    hops = [hop(by_x, Y_BIT), hop(by_y, Z1_BIT), hop(by_z, X_BIT)]
    for start in beside[1]:
        start()
    hops = order.take(*hops)
    part = stack_call([kv, by_x, by_y, by_z, across, *hops])
    far = hop(part, C_BIT)
    for start in beside[2]:
        start()
    return part, order.take(far)


def scatter_keys(part_a, part_b, order, near, while_one=lambda: None, while_two=lambda: None):
    if not near:
        while_one()
        while_two()
        whole = jnp.concatenate([part_a, part_b.astype(F32)], axis=0)
        return [lax.psum_scatter(whole, "ctx", scatter_dimension=0, tiled=True)]
    part_a, part_b = order.take(part_a, part_b)
    far = hop(part_b, C_BIT)
    while_one()
    own, *others = split_call(part_a, order.take(far))
    others = order.take(*others)
    others = [hop(value, mask) for value, mask in zip(others, NEAR[1:], strict=True)]
    while_two()
    return [own, *order.take(*others)]


def cut_rows(value, index, count):
    size = value.shape[0] // count
    return lax.dynamic_slice_in_dim(value, index * size, size, 0)


def cut_cols(value, index, count):
    size = value.shape[1] // count
    return lax.dynamic_slice_in_dim(value, index * size, size, 1)


def spread(mine):
    return mine, hop(mine, X_BIT), hop(mine, Z1_BIT), hop(mine, X_BIT | Z1_BIT)


BESIDE = ((0, 0), (1, 0), (0, 1), (1, 1))


def pair_sum(keep, send, near):
    if near:
        return low_sum(keep, hop(send, C_BIT))
    return lax.psum(jnp.stack([keep, send]).astype(F32), AXES)


def block_sums(total):
    (got,) = yield [hop(total[1], Y_BIT)]
    total = low_sum(total[0], got)
    (got,) = yield [hop(total[1], X_BIT)]
    total = low_sum(total[0], got)
    along_z = (Z1_BIT, Z2_BIT, Z1_BIT | Z2_BIT)
    got = yield [hop(total[i + 1], mask) for i, mask in enumerate(along_z)]
    mine = total[0].astype(F32)
    for value in got:
        mine = mine + value.astype(F32)
    mine = mine.astype(BF)
    got = yield [hop(mine, mask) for mask in along_z]
    total = jnp.stack([mine, *got])
    (got,) = yield [hop(total, X_BIT)]
    total = jnp.stack([total, got])
    (got,) = yield [hop(total, C_BIT)]
    return total, got


def sums_by_hops(value):
    for mask in (C_BIT, X_BIT, Y_BIT, Z1_BIT, Z2_BIT):
        (got,) = yield [hop(value, mask)]
        value = value + got
    return value


class Course:
    def __init__(self, order, chain, value):
        self.order, self.chain = order, chain(order.take(value))
        self.waiting, self.result = next(self.chain), None

    def step(self):
        got = self.order.take(*self.waiting)
        got = got if isinstance(got, (list, tuple)) else [got]
        try:
            self.waiting = self.chain.send(got)
        except StopIteration as end:
            self.waiting, self.result = None, end.value


def on_device(
    tokens, cotangent, w_query, key_weight, value_weight, w_out, w_gate, w_up, w_down,
    gain_attn, gain_ffn, block_order, sel_mid, live_mid, sel_last, live_last,
):
    ctx_count, ws_count = lax.axis_size("ctx"), lax.axis_size("ws")
    near = ctx_count == 16 and ws_count == 2
    ctx, y = lax.axis_index("ctx"), lax.axis_index("ws")
    tok_local = tokens.shape[1]
    cap_mid, cap_last = sel_mid.shape[1] // ctx_count, sel_last.shape[1] // ctx_count
    if near:
        c, x, z = ctx & 1, (ctx >> 1) & 1, ctx >> 2
        places = (y, c, x, z)
        here = (ctx & 7) | (y << 3)
        turn_order = here ^ jnp.array([ctx_mask(m) for m in NEAR] + [ctx_mask(m) | 1 for m in NEAR], jnp.int32)
        relocate = move
    else:
        zero = jnp.int32(0)
        places = (y, zero, zero, zero)
        here = ctx
        turn_order = jnp.arange(ctx_count, dtype=jnp.int32)
        relocate = lambda v: v
    coords = jnp.stack([jnp.asarray(v, jnp.int32) for v in places])
    block_coords = coords if near else jnp.zeros((4,), jnp.int32)
    width = tokens.shape[2]
    half = w_query.shape[0]
    plan = jnp.concatenate(
        [
            sel_mid.reshape(ctx_count, cap_mid),
            live_mid.reshape(ctx_count, cap_mid),
            live_last.reshape(ctx_count, cap_last),
        ],
        axis=1,
    )
    qkv_width = w_query.shape[1] + 2 * key_weight.shape[1]
    order = Order(coords)
    if near:
        assert tok_local <= 256
        own_qkv, piece = pack_call(
            coords, w_query, key_weight.T, value_weight.T, gain_attn.reshape(1, -1), gain_ffn.reshape(1, -1)
        )
        fetched = hop(piece, Y_BIT)
        marks = jnp.pad(plan.astype(BF), ((0, 0), (0, width - plan.shape[1])))
        tok = move(jnp.concatenate([tokens[0], marks], axis=0))
        quad = x * 2 + (z & 1)
        own_down = w_down.T
        fetched, cut_gate, cut_up, cut_out, cut_down = order.take(
            fetched,
            *(cut_cols(cut_rows(w, c, 2), quad, 4) for w in (w_gate, w_up)),
            cut_rows(w_out, c, 2),
            cut_rows(own_down, c, 2),
        )
        far = hop(fetched, C_BIT)
        gate_mine, up_mine = hop(cut_gate, Y_BIT), hop(cut_up, Y_BIT)
        out_mine, down_mine = hop(cut_out, Y_BIT), hop(cut_down, Y_BIT)
        far, tok = order.take(far, tok)
        plan = tok[tok_local:, : plan.shape[1]].astype(jnp.int32)
        tok = tok[:tok_local]
        depth = half // 2
        beyond = [fetched[depth : depth + 1, i * half : (i + 1) * half] for i in range(2)]
        gains = [
            jnp.where(y == 0, jnp.concatenate([own, other], axis=1), jnp.concatenate([other, own], axis=1))
            for own, other in zip((gain_attn.reshape(1, -1), gain_ffn.reshape(1, -1)), beyond, strict=True)
        ]
        (wqkv,) = join_call(
            coords,
            [own_qkv, fetched, far],
            [(2 * half, qkv_width)],
            [
                [
                    (0, None, 0, half, lambda ky, kc, kx, kz: (ky * half, 0)),
                    (1, None, 0, depth, lambda ky, kc, kx, kz: ((1 - ky) * half + kc * depth, 0)),
                    (2, None, 0, depth, lambda ky, kc, kx, kz: ((1 - ky) * half + (kc ^ 1) * depth, 0)),
                ]
            ],
        )
        state = {}

        def start_gate():
            state["gate"] = spread(order.take(gate_mine))

        def start_up():
            state["up"] = spread(order.take(up_mine))

        def share_gate():
            state["gate"] = stack_call(order.take(*state["gate"]))
            state["gate_far"] = hop(state["gate"], C_BIT)

        beside = ((start_gate,), (start_up,), (share_gate,))

        def fetch_rest():
            up = order.take(*state["up"])
            out, down = order.take(out_mine, down_mine)
            up = stack_call(up)
            fars = [hop(v, C_BIT) for v in (out, up, down)]
            out_far, up_far, down_far, gate_far = order.take(*fars, state["gate_far"])
            hidden_half = own_down.shape[1]
            block = cut_gate.shape[1]
            plans = [[(0, None, 0, half, lambda ky, kc, kx, kz: (ky * half, 0))]]
            for array, far in ((1, 0), (2, 1)):
                plans[0].append(
                    (array, None, 0, depth,
                     lambda ky, kc, kx, kz, far=far: ((1 - ky) * half + (kc ^ far) * depth, 0))
                )
            for first in (3, 6):
                steps = [(first, None, 0, half, lambda ky, kc, kx, kz: (ky * half, 0))]
                for array, far in ((first + 1, 0), (first + 2, 1)):
                    for k, (rx, rz) in enumerate(BESIDE):
                        steps.append(
                            (array, None, k * depth, depth,
                             lambda ky, kc, kx, kz, far=far, rx=rx, rz=rz: (
                                 (1 - ky) * half + (kc ^ far) * depth,
                                 ((kx ^ rx) * 2 + ((kz & 1) ^ rz)) * block,
                             ))
                        )
                plans.append(steps)
            steps = [(9, None, 0, width, lambda ky, kc, kx, kz: (0, ky * hidden_half))]
            for array, far in ((10, 0), (11, 1)):
                steps.append(
                    (array, None, 0, width // 2,
                     lambda ky, kc, kx, kz, far=far: (
                         (kc ^ far) * (width // 2), (1 - ky) * hidden_half
                     ))
                )
            plans.append(steps)
            return join_call(
                coords,
                [w_out, out, out_far, w_gate, state["gate"], gate_far, w_up, up, up_far,
                 own_down, down, down_far],
                [(2 * half, w_out.shape[1]), (2 * half, w_gate.shape[1]), (2 * half, w_up.shape[1]),
                 (width, 2 * hidden_half)],
                plans,
            )
    else:
        tok = tokens[0]
        whole = lambda w: lax.all_gather(w, "ws", axis=0, tiled=True)
        wqkv = whole(jnp.concatenate([w_query, key_weight, value_weight], axis=1))
        gains = [whole(g).reshape(1, -1) for g in (gain_attn, gain_ffn)]
        rest = [whole(w) for w in (w_out, w_gate, w_up)] + [whole(w_down).T]
        beside, fetch_rest = ((), (), ()), lambda: rest
    gain1, gain2 = (g.astype(F32) for g in gains)

    per_device = tok_local // BLK
    blocks = jnp.take(block_order.reshape(ctx_count, per_device), turn_order, axis=0)
    plan_order = jnp.take(plan, turn_order, axis=0)
    sel_all = plan_order[:, :cap_mid]
    live_two = plan_order[:, cap_mid : 2 * cap_mid]
    live_three = plan_order[:, 2 * cap_mid :]
    place_one = (blocks[:, :, None] * BLK + jnp.arange(BLK, dtype=jnp.int32)).reshape(ctx_count, tok_local)
    place_two = sum(
        jnp.where(sel_all // BLK == k, blocks[:, k : k + 1], 0) for k in range(per_device)
    ) * BLK + sel_all % BLK
    place_three = place_two[:, :cap_last]
    if near:
        mine = lambda v: v[0:1]
    else:
        mine = lambda v: lax.dynamic_slice_in_dim(v, here, 1, 0)
    sel_own, live2_own, live3_own = mine(sel_all), mine(live_two), mine(live_three)
    own_places = jnp.concatenate([mine(place_one), mine(place_two)], axis=1).reshape(-1, 1)
    frequency = ROPE_BASE ** (-jnp.arange(HEAD_SIZE // 2, dtype=F32) / (HEAD_SIZE // 2))
    angles = own_places.astype(F32) * frequency[None, :]
    cosine, sine = jnp.cos(angles), jnp.sin(angles)
    cosine = jnp.concatenate([cosine] * 4, axis=1)
    sine = jnp.concatenate([-sine, sine, -sine, sine], axis=1)
    tables = [
        (cosine[:tok_local], sine[:tok_local]),
        (cosine[tok_local:], sine[tok_local:]),
        (cosine[tok_local : tok_local + cap_last], sine[tok_local : tok_local + cap_last]),
    ]
    query_places = [
        own_places[:tok_local],
        own_places[tok_local:],
        own_places[tok_local : tok_local + cap_last],
    ]
    key_places = [v.reshape(1, -1) for v in (place_one, place_two, place_three)]
    key_live = [
        jnp.ones((1, ctx_count * tok_local), jnp.int32),
        live_two.reshape(1, -1),
        live_three.reshape(1, -1),
    ]
    prompt = ctx_count * tok_local // 2

    firsts, mixeds, seconds, hiddens = [], [], [], []
    records = []
    xs = [tok]
    first_in, query, kv = first_call(tok, gain1, *tables[0], wqkv)
    heights = []
    for step in range(3):
        part_a, part_b = gather_keys(kv, order, near, beside if step == 0 else ((), (), ()))
        weights, mixed = attend_call(
            query, part_a, part_b, key_places[step], key_live[step], query_places[step], prompt
        )
        firsts.append(first_in)
        if step == 0:
            extra = (sel_own, *tables[1])
            mixed, cot = order.take(mixed, cotangent[0])
            cot = relocate(cot)
            wo, wg, wu, wd = fetch_rest()
        elif step == 1:
            extra = (live2_own, *tables[2])
        else:
            extra = (sel_own, live2_own, live3_own, heights[0], heights[1])
        result = dense_call(
            near, step, xs[step], mixed, gain1, gain2, extra,
            (wo, wg, wu, wd) + ((wqkv,) if step < 2 else ()),
            (cap_mid, cap_last, tok_local)[step],
        )
        mixed_rows, middle, second, gate, up, hidden = result[:6]
        mixeds.append(mixed_rows)
        seconds.append(second)
        hiddens.append(hidden)
        records.append((query, part_a, part_b, weights, middle, gate, up))
        if step < 2:
            height, following, first_in, query, kv = result[6:]
            heights.append(height)
            xs.append(following)
        else:
            output = relocate(order.take(result[6]))

    d_firsts, d_seconds = [None] * 3, [None] * 3
    sums_one, sums_two = [], []
    slots = None
    parts, d_query, d_middle = (), None, None
    column = lambda rows, i: [r[i] for r in rows]
    courses = {}

    def begin(name, value, chain=block_sums):
        if near:
            courses[name] = Course(order, chain, value)
        else:
            courses[name] = value

    def step_of(*names):
        if near:
            for name in names:
                courses[name].step()

    def grads(kind, groups):
        return pair_sum(*grad_call(kind, block_coords, groups), near)

    for phase in range(4):
        step = 2 - phase
        before, into = (), ()
        if phase > 0:
            before = (gain1, *tables[step + 1], xs[step + 1], d_middle, d_query)
        if phase < 3:
            into = (gain2, *records[step][4:7])
        mats = (wd, wg, wu, wo)
        if phase == 0:
            extra, mats = (cot, sel_own, live3_own), mats
        elif phase == 1:
            extra, mats = (slots, live3_own, live2_own), (wqkv,) + mats
        elif phase == 2:
            extra, mats = (cot, sel_own, live2_own), (wqkv,) + mats
        else:
            extra, mats = (), (wqkv,)
        result = list(back_call(near, phase, before, parts, into, extra, mats, cap_mid))
        if phase > 0:
            d_firsts[step + 1], total = result[:2]
            sums_one.append(total)
            result = result[2:]
        if phase == 3:
            grad_tokens = result[0]
            break
        d_low, d_gate, d_up, d_middle, d_mid_low, d_mixed, total = result[:7]
        d_seconds[step] = (d_low, d_gate, d_up, d_mid_low)
        sums_two.append(total)
        if phase == 0:
            slots = result[7]
        elif phase == 1:
            output = order.take(output)
        else:
            begin("down", grads("rows", [hiddens, column(d_seconds, 0)]))
        d_mixed = order.take(d_mixed)
        query, part_a, part_b, weights = records[step][:4]
        d_query, term_a, term_b = attend_back_call(query, d_mixed, part_a, part_b, weights)
        if phase < 2:
            parts = scatter_keys(term_a, term_b, order, near)
        else:
            ready = {}

            def while_one():
                ready["gate"] = grads("cols", [seconds, order.take(*column(d_seconds, 1))])

            def while_two():
                ready["up"] = grads("cols", [seconds, order.take(*column(d_seconds, 2))])
                step_of("down")
                begin("gate", ready["gate"])

            parts = scatter_keys(term_a, term_b, order, near, while_one, while_two)

    rest = grads("mixed", [firsts, mixeds, d_firsts, column(d_seconds, 3)])
    sums = jnp.concatenate([sum(sums_one), sum(sums_two)], axis=0)
    begin("gains", sums, sums_by_hops)
    grad_tokens = relocate(grad_tokens)
    kv_width = key_weight.shape[1]
    hidden_width = w_gate.shape[1]
    placed = {}

    def place(name, kind, widths):
        got = courses[name]
        if near:
            got = got.result
        else:
            mine = lax.dynamic_index_in_dim(got, y, 1, keepdims=False)
            got = (mine[0], mine[1])
        where = order.token if near else block_coords
        placed[name] = order.take(*place_call(kind, where, *got, widths))

    step_of("down", "gains", "gate")
    begin("up", ready["up"])
    step_of("down", "gains", "gate", "down", "gains", "up")
    begin("rest", rest)
    step_of("gate", "gains", "down")
    grad_tokens = order.take(grad_tokens)
    step_of("up", "gate", "gains", "down")
    place("down", "rows", None)
    step_of("rest", "up", "gate", "rest", "up", "gate")
    place("gate", "cols", (hidden_width,))
    step_of("rest", "up", "rest", "up")
    place("up", "cols", (hidden_width,))
    step_of("rest", "rest")
    place("rest", "cols", (width, kv_width, width, kv_width))
    grad_down, grad_gate, grad_up = placed["down"].T, placed["gate"], placed["up"]
    grad_query, grad_key, grad_out, grad_value = placed["rest"]
    gain_sums = courses["gains"].result if near else lax.psum(sums, AXES)
    gain_sums = lax.dynamic_slice_in_dim(gain_sums, y * half, half, 1)
    return (
        output[None],
        grad_tokens[None],
        grad_query,
        grad_key,
        grad_value,
        grad_out,
        grad_gate,
        grad_up,
        grad_down,
        gain_sums[0],
        gain_sums[1],
    )


def solution(mesh):
    rows = P("ws", "ctx", None)
    flat = P("ws", None)
    in_specs = (rows, rows) + (flat,) * 7 + (P("ws"), P("ws"), P()) + (flat,) * 4
    out_specs = (rows, rows) + (flat,) * 7 + (P("ws"), P("ws"))
    return jax.shard_map(
        on_device, mesh=mesh, in_specs=in_specs, out_specs=out_specs, check_vma=False
    )
```

time: 862 us -> 624 us (0.72)
  Pallas kernels: 285 us -> 146 us
  waiting for transfers between devices: 300 us -> 226 us
  starting transfers between devices: 178 us -> 147 us
  local copies, waits for them, and re-layouts: 61.2 us -> 78.2 us
  other arithmetic: 23.4 us -> 12.6 us
    ppermute x122 -> x113, waiting for transfers between devices: 263 us -> 207 us  [hop(): return lax.ppermute(value, AXES, [(i, i ^ mask) for i in range(32)])]
    pallas_call x3, Pallas kernels: 82.2 us -> 33.3 us  [attend_call(): pl.pallas_call(functools.partial(attend_kernel, prompt), name='attend', g...]
    pallas_call x12 -> x23, Pallas kernels: 115 us -> 68.6 us  [the longest x4 24.7 us: back_call(): pl.pallas_call(functools.partial(back_kernel, phase, len(parts)), name=f'...]
    ppermute x122 -> x113, starting transfers between devices: 161 us -> 125 us  [hop(): return lax.ppermute(value, AXES, [(i, i ^ mask) for i in range(32)])]
    pallas_call x3, Pallas kernels: 56 us -> 25.5 us  [attend_back_call(): pl.pallas_call(attend_back_kernel, name='attend_back', grid=(heads,), out...]
    unnamed x200 -> x264, local copies, waits for them, and re-layouts: 34.8 us -> 55.2 us
    ppermute x5 -> x4, waiting for transfers between devices: 37.4 us -> 18.9 us  [move(): return lax.ppermute(value, AXES, [(i, swap_place(i)) for i in range(32)])]
    pallas_call x4, Pallas kernels: 32.3 us -> 18.6 us  [grad_call(): pl.pallas_call(functools.partial(kernel, n_steps), name=f'grad_{kind}', o...]
  transfers between devices with their start and end apart: 127 -> 117, of which waited for: 59 -> 58; matrix products, arithmetic and copies ran while one was open for 8% -> 6% of each run, Pallas kernels for 14% -> 9%
where the time goes in v2:
time: 624 us; the launch traced here: 612 us
  waiting for transfers between devices  226 us (36%)
  starting transfers between devices  147 us (24%)
  Pallas kernels  146 us (23%)
  local copies, waits for them, and re-layouts  78.2 us (13%)
  other arithmetic  12.6 us (2%)
    ppermute x113, waiting for transfers between devices, hop(): return lax.ppermute(value, AXES, [(i, i ^ mask) for i in range(32)])  207 us
    ppermute x113, starting transfers between devices, hop(): return lax.ppermute(value, AXES, [(i, i ^ mask) for i in range(32)])  125 us
    unnamed x264, local copies, waits for them, and re-layouts  55.2 us
    pallas_call x3, Pallas kernels, attend_call(): pl.pallas_call(functools.partial(attend_kernel, prompt), name='attend', g...  33.3 us
    pallas_call x3, Pallas kernels, attend_back_call(): pl.pallas_call(attend_back_kernel, name='attend_back', grid=(heads,), out...  25.5 us
    pallas_call x4, Pallas kernels, back_call(): pl.pallas_call(functools.partial(back_kernel, phase, len(parts)), name=f'...  24.7 us
    ppermute x4, starting transfers between devices, move(): return lax.ppermute(value, AXES, [(i, swap_place(i)) for i in range(32)])  21.9 us
    ppermute x4, waiting for transfers between devices, move(): return lax.ppermute(value, AXES, [(i, swap_place(i)) for i in range(32)])  18.9 us
  transfers between devices with their start and end apart: 117, of which 58 were waited for; matrix products, arithmetic and copies ran while one was open for 6% of the time, Pallas kernels for 9%

profile of v2, /device:TPU:7, one launch (start us, length us, event | category | flops | bytes accessed | tf_op | source)
XLA Modules:
  0.0 612.2 jit_solution(3376796282705269626)
XLA Ops:
  12.2 5.2 collective-permute-start.2
  23.7 10.8 %collective-permute-done = bf16[248,1600]{0,1:T(8,128)(2,1)} collective-permute-done((bf16[248,1600]{0,1:T(8,128)(2,1)}, bf16[248,1600]{0,1:T(8,128)(2,1)}, u32[]{:S(2)}, u32[]{:S(2)}) %collective-permute-start) | collective-permute-done | bytes 793632 | tf_op jit(solution)/shard_map/ppermute | solution.py:33
  50.6 2.4 collective-permute-start.6
  58.1 2.7 collective-permute-done.5.refs_3_
  65.1 3.7 collective-permute-done.11.refs_0_
  68.8 3.4 collective-permute-done.8.refs_5_
  77.4 7.1 %collective-permute-done.15.refs_3_ = bf16[240,640]{1,0:T(8,128)(2,1)S(1)} collective-permute-done((bf16[240,640]{1,0:T(8,128)(2,1)}, bf16[240,640]{1,0:T(8,128)(2,1)S(1)}, u32[]{:S(2)}, u32[]{:S(2)}) %collective-permute-start.15) | collective-permute-done | bytes 307232 | tf_op jit(solution)/shard_map/ppermute | solution.py:33
  87.8 3.0 collective-permute-done.14.refs_2_
  96.2 15.4 %attend.3 = (bf16[5,384,2048]{2,1,0:T(8,128)(2,1)}, bf16[5,128,192]{2,1,0:T(8,128)(2,1)S(1)}) custom-call(bf16[5,128,192]{2,1,0:T(8,128)(2,1)S(1)} %copy-done.74, bf16[1024,640]{1,0:T(8,128)(2,1)} %stack.153.a_ref, bf16[1024,640]{1,0:T(8,128)(2,1)} %collective-permute-done.12.b_ref, s32[1,2048]{1,0:T(1,128)S(1)} %add.176.kpos_ref, ...), custom_call_target="tpu_custom_call" | custom-call | flops 4026531840 | bytes 7864320 | tf_op jit(solution)/shard_map/attend/pallas_call | solution.py:347
  120.5 4.5 join_weights.3
  125.1 6.2 %dense_0.1 = (bf16[128,960]{1,0:T(8,128)(2,1)S(1)}, f32[128,960]{1,0:T(8,128)S(1)}, bf16[128,960]{1,0:T(8,128)(2,1)S(1)}, f32[128,2560]{1,0:T(8,128)S(1)}, f32[1...) custom-call(bf16[128,960]{1,0:T(8,128)(2,1)S(1)} %slice.187.x_ref.ar, ...), custom_call_target="tpu_custom_call" | custom-call | flops 2516480000 | bytes 24000000 | tf_op jit(solution)/shard_map/dense_0/pallas_call | solution.py:533
  136.0 2.5 collective-permute-start.28
  139.9 2.5 collective-permute-done.28.refs_4_
  159.2 11.4 %attend.4 = (bf16[5,288,1536]{2,1,0:T(8,128)(2,1)}, bf16[5,96,192]{2,1,0:T(8,128)(2,1)S(1)}) custom-call(bf16[5,96,192]{2,1,0:T(8,128)(2,1)S(1)} %copy-done.83, bf16[768,640]{1,0:T(8,128)(2,1)} %stack.156.a_ref, bf16[768,640]{1,0:T(8,128)(2,1)} %collective-permute-done.32.b_ref, s32[1,1536]{1,0:T(1,128)S(1)} %reshape.282.kpos_ref, ...), custom_call_target="tpu_custom_call" | custom-call | flops 2264924160 | bytes 4423680 | tf_op jit(solution)/shard_map/attend/pallas_call | solution.py:347
  173.0 2.4 copy-done.7
  175.4 5.6 dense_1.1
  197.8 2.8 collective-permute-start.40
  200.5 4.1 collective-permute-start.42
  209.7 6.5 %attend.5 = (bf16[5,192,1024]{2,1,0:T(8,128)(2,1)}, bf16[5,64,192]{2,1,0:T(8,128)(2,1)S(1)}) custom-call(bf16[5,64,192]{2,1,0:T(8,128)(2,1)S(1)} %copy-done.92, bf16[512,640]{1,0:T(8,128)(2,1)} %stack.157.a_ref, bf16[512,640]{1,0:T(8,128)(2,1)} %collective-permute-done.40.b_ref, s32[1,1024]{1,0:T(1,128)S(1)} %copy-done.68, s32[1,1024]{1,0:T(1,128)S(1)} %copy-done.67, ...), custom_call_target="tpu_custom_call" | custom-call | flops 1006632960 | bytes 1966080 | tf_op jit(solution)/shard_map/attend/pallas_call | solution.py:347
  223.5 4.6 dense_2.1
  233.0 6.8 %back_0.1 = (bf16[64,960]{1,0:T(8,128)(2,1)S(1)}, bf16[64,2560]{1,0:T(8,128)(2,1)S(1)}, bf16[64,2560]{1,0:T(8,128)(2,1)S(1)}, f32[64,960]{1,0:T(8,128)S(1)}, bf1...) custom-call(f32[1,960]{1,0:T(1,128)S(1)} %copy-done.58, ...), custom_call_target="tpu_custom_call" | custom-call | flops 1258240000 | bytes 24000000 | tf_op jit(solution)/shard_map/back_0/pallas_call | solution.py:681
  239.8 6.3 %attend_back.3 = (f32[5,64,192]{2,1,0:T(8,128)S(1)}, f32[512,640]{1,0:T(8,128)S(1)}, bf16[512,640]{1,0:T(8,128)(2,1)S(1)}) custom-call(bf16[5,64,192]{2,1,0:T(8,128)(2,1)S(1)} %copy-done.93, bf16[5,64,192]{2,1,0:T(8,128)(2,1)S(1)} %get-tuple-element.478.do_ref, bf16[512,640]{1,0:T(8,128)(2,1)} %stack.157.a_ref, ...), custom_call_target="tpu_custom_call" | custom-call | flops 2013265920 | bytes 1966080 | tf_op jit(solution)/shard_map/attend_back/pallas_call | solution.py:397
  246.4 2.9 collective-permute-start.41
  255.1 8.9 %collective-permute-start.49 = (bf16[64,640]{1,0:T(8,128)(2,1)S(1)}, bf16[64,640]{1,0:T(8,128)(2,1)S(1)}, u32[]{:S(2)}, u32[]{:S(2)}) collective-permute-start(bf16[64,640]{1,0:T(8,128)(2,1)S(1)} %get-tuple-element.500), channel_id=1, source_target_pairs={{0,9},{1,8},{2,11},{3,10},{4,13},{5,12},{6,15},{7,14},{8,1},{9,0},... | collective-permute-start | bytes 245768 | tf_op jit(solution)/shard_map/ppermute | solution.py:33
  266.4 3.0 collective-permute-done.50.args_13_
  269.5 7.3 %back_1.1 = (bf16[64,1600]{1,0:T(8,128)(2,1)S(1)}, f32[1,960]{1,0:T(1,128)S(1)}, bf16[96,960]{1,0:T(8,128)(2,1)S(1)}, bf16[96,2560]{1,0:T(8,128)(2,1)S(1)}, bf16...) custom-call(f32[1,960]{1,0:T(1,128)S(1)} %copy-done.56, ...), custom_call_target="tpu_custom_call" | custom-call | flops 1887360000 | bytes 24000000 | tf_op jit(solution)/shard_map/back_1/pallas_call | solution.py:681
  279.1 8.1 %attend_back.4 = (f32[5,96,192]{2,1,0:T(8,128)S(1)}, f32[768,640]{1,0:T(8,128)S(1)}, bf16[768,640]{1,0:T(8,128)(2,1)S(1)}) custom-call(bf16[5,96,192]{2,1,0:T(8,128)(2,1)S(1)} %copy-done.84, bf16[5,96,192]{2,1,0:T(8,128)(2,1)S(1)} %get-tuple-element.522.do_ref, bf16[768,640]{1,0:T(8,128)(2,1)} %stack.156.a_ref, ...), custom_call_target="tpu_custom_call" | custom-call | flops 4529848320 | bytes 4423680 | tf_op jit(solution)/shard_map/attend_back/pallas_call | solution.py:397
  300.0 5.5 collective-permute-done.56.args_11_
  305.6 9.0 %back_2.1 = (bf16[96,1600]{1,0:T(8,128)(2,1)S(1)}, f32[1,960]{1,0:T(1,128)S(1)}, bf16[128,960]{1,0:T(8,128)(2,1)S(1)}, bf16[128,2560]{1,0:T(8,128)(2,1)S(1)}, bf...) custom-call(f32[1,960]{1,0:T(1,128)S(1)} %copy-done.56, ...), custom_call_target="tpu_custom_call" | custom-call | flops 2516480000 | bytes 24000000 | tf_op jit(solution)/shard_map/back_2/pallas_call | solution.py:681
  314.6 4.2 grad_rows.1
  320.8 4.5 collective-permute-done.59
  326.6 3.2 copy-done.98
  329.8 11.2 %attend_back.5 = (f32[5,128,192]{2,1,0:T(8,128)S(1)}, f32[1024,640]{1,0:T(8,128)S(1)}, bf16[1024,640]{1,0:T(8,128)(2,1)S(1)}) custom-call(bf16[5,128,192]{2,1,0:T(8,128)(2,1)S(1)} %copy-done.75, bf16[5,128,192]{2,1,0:T(8,128)(2,1)S(1)} %get-tuple-element.571.do_ref, bf16[1024,640]{1,0:T(8,128)(2,1)} %stack.153.a_ref, ...), custom_call_target="tpu_custom_call" | custom-call | flops 8053063680 | bytes 7864320 | tf_op jit(solution)/shard_map/attend_back/pallas_call | solution.py:397
  341.0 4.5 grad_cols.2
  346.7 5.5 collective-permute-done.60.other_ref
  352.4 24.0 %collective-permute-done.69 = bf16[2,4,80,960]{3,2,1,0:T(8,128)(2,1)S(1)} collective-permute-done((bf16[2,4,80,960]{3,2,1,0:T(8,128)(2,1)S(1)}, bf16[2,4,80,960]{3,2,1,0:T(8,128)(2,1)S(1)}, u32[]{:S(2)}, u32[]{:S(2)}) %collective-permute-start.69) | collective-permute-done | bytes 1228832 | tf_op jit(solution)/shard_map/ppermute | solution.py:33
  380.1 4.3 grad_cols.3
  392.8 3.9 collective-permute-done.65.args_11_
  397.8 3.5 collective-permute-done.67.args_13_
  403.1 8.4 %collective-permute-done.71 = bf16[4,80,960]{2,1,0:T(8,128)(2,1)S(1)} collective-permute-done((bf16[4,80,960]{2,1,0:T(8,128)(2,1)S(1)}, bf16[4,80,960]{2,1,0:T(8,128)(2,1)S(1)}, u32[]{:S(2)}, u32[]{:S(2)}) %collective-permute-start.71) | collective-permute-done | bytes 614432 | tf_op jit(solution)/shard_map/ppermute | solution.py:33
  412.9 5.5 grad_mixed.1
  421.0 2.7 collective-permute-done.76
  426.6 8.7 %collective-permute-done.73 = bf16[80,960]{1,0:T(8,128)(2,1)S(1)} collective-permute-done((bf16[80,960]{1,0:T(8,128)(2,1)S(1)}, bf16[80,960]{1,0:T(8,128)(2,1)S(1)}, u32[]{:S(2)}, u32[]{:S(2)}) %collective-permute-start.73) | collective-permute-done | bytes 153632 | tf_op jit(solution)/shard_map/ppermute | solution.py:33
  435.4 2.5 collective-permute-start.80
  443.6 6.5 %collective-permute-done.79 = bf16[80,960]{1,0:T(8,128)(2,1)S(1)} collective-permute-done((bf16[80,960]{1,0:T(8,128)(2,1)S(1)}, bf16[80,960]{1,0:T(8,128)(2,1)S(1)}, u32[]{:S(2)}, u32[]{:S(2)}) %collective-permute-start.79) | collective-permute-done | bytes 153632 | tf_op jit(solution)/shard_map/ppermute | solution.py:33
  450.1 15.5 %collective-permute-done.84 = f32[2,960]{1,0:T(2,128)S(1)} collective-permute-done((f32[2,960]{1,0:T(2,128)S(1)}, f32[2,960]{1,0:T(2,128)S(1)}, u32[]{:S(2)}, u32[]{:S(2)}) %collective-permute-start.84) | collective-permute-done | bytes 7712 | tf_op jit(solution)/shard_map/ppermute | solution.py:33
  471.9 9.7 %collective-permute-start.70 = (f32[128,960]{1,0:T(8,128)S(1)}, f32[128,960]{1,0:T(8,128)S(1)}, u32[]{:S(2)}, u32[]{:S(2)}) collective-permute-start(f32[128,960]{1,0:T(8,128)S(1)} %get-tuple-element.624), channel_id=1, source_target_pairs={{0,0},{1,16},{2,2},{3,18},{4,4},{5,20},{6,6},{7,22},{8,8},{9,24},{... | collective-permute-start | bytes 1474568 | tf_op jit(solution)/shard_map/ppermute | solution.py:42
  482.7 3.8 collective-permute-start.92
  488.9 18.9 %collective-permute-done.70 = f32[128,960]{1,0:T(8,128)S(1)} collective-permute-done((f32[128,960]{1,0:T(8,128)S(1)}, f32[128,960]{1,0:T(8,128)S(1)}, u32[]{:S(2)}, u32[]{:S(2)}) %collective-permute-start.70) | collective-permute-done | bytes 491552 | tf_op jit(solution)/shard_map/ppermute | solution.py:42
  508.0 2.6 collective-permute-start.93
  518.9 3.8 place_rows.1
  526.2 3.4 collective-permute-done.101
  529.8 2.9 collective-permute-start.106
  532.8 4.6 collective-permute-start.109
  537.8 2.6 collective-permute-done.98
  541.8 9.3 %collective-permute-done.108 = bf16[120,640]{1,0:T(8,128)(2,1)S(1)} collective-permute-done((bf16[120,640]{1,0:T(8,128)(2,1)S(1)}, bf16[120,640]{1,0:T(8,128)(2,1)S(1)}, u32[]{:S(2)}, u32[]{:S(2)}) %collective-permute-start.108) | collective-permute-done | bytes 153632 | tf_op jit(solution)/shard_map/ppermute | solution.py:33
  552.1 3.3 collective-permute-start.105
  555.8 3.4 place_cols.3
  559.2 7.8 %collective-permute-done.104 = bf16[120,640]{1,0:T(8,128)(2,1)S(1)} collective-permute-done((bf16[120,640]{1,0:T(8,128)(2,1)S(1)}, bf16[120,640]{1,0:T(8,128)(2,1)S(1)}, u32[]{:S(2)}, u32[]{:S(2)}) %collective-permute-start.104) | collective-permute-done | bytes 153632 | tf_op jit(solution)/shard_map/ppermute | solution.py:33
  572.5 3.9 collective-permute-done.112
  576.4 7.6 %collective-permute-done.111 = bf16[120,640]{1,0:T(8,128)(2,1)S(1)} collective-permute-done((bf16[120,640]{1,0:T(8,128)(2,1)S(1)}, bf16[120,640]{1,0:T(8,128)(2,1)S(1)}, u32[]{:S(2)}, u32[]{:S(2)}) %collective-permute-start.111) | collective-permute-done | bytes 153632 | tf_op jit(solution)/shard_map/ppermute | solution.py:33
  584.4 3.4 place_cols.4
  587.7 11.1 %collective-permute-done.114 = bf16[4,120,640]{2,1,0:T(8,128)(2,1)S(1)} collective-permute-done((bf16[4,120,640]{2,1,0:T(8,128)(2,1)S(1)}, bf16[4,120,640]{2,1,0:T(8,128)(2,1)S(1)}, u32[]{:S(2)}, u32[]{:S(2)}) %collective-permute-start.114) | collective-permute-done | bytes 614432 | tf_op jit(solution)/shard_map/ppermute | solution.py:33
  604.3 3.4 place_cols.5
  (574 shorter events, 221.0 us)
Async XLA Ops:
  8.8 25.7 %collective-permute-start = (bf16[248,1600]{0,1:T(8,128)(2,1)}, bf16[248,1600]{0,1:T(8,128)(2,1)}, u32[]{:S(2)}, u32[]{:S(2)}) collective-permute-start(bf16[248,1600]{0,1:T(8,128)(2,1)} %copy.59), channel_id=1, source_target_pairs={{0,1},{1,0},{2,3},{3,2},{4,5},{5,4},{6,7},{7,6},{8,9},{9,8},{10,11... | collective-permute-start | bytes 2380808 | tf_op jit(solution)/shard_map/ppermute | solution.py:33
  12.2 26.3 %collective-permute-start.2 = (bf16[144,960]{1,0:T(8,128)(2,1)}, bf16[144,960]{1,0:T(8,128)(2,1)}, u32[]{:S(2)}, u32[]{:S(2)}) collective-permute-start(bf16[144,960]{1,0:T(8,128)(2,1)} %pad_maximum_fusion.8), channel_id=1, source_target_pairs={{0,0},{1,16},{2,2},{3,18},{4,4},{5,20},{6,6},{7,22},{8,8},{9,24},{... | collective-permute-start | bytes 829448 | tf_op jit(solution)/shard_map/ppermute | solution.py:42
  38.2 16.3 %collective-permute-start.7 = (bf16[240,640]{1,0:T(8,128)(2,1)}, bf16[240,640]{1,0:T(8,128)(2,1)}, u32[]{:S(2)}, u32[]{:S(2)}) collective-permute-start(bf16[240,640]{1,0:T(8,128)(2,1)} %dynamic_slice.17), channel_id=1, source_target_pairs={{0,1},{1,0},{2,3},{3,2},{4,5},{5,4},{6,7},{7,6},{8,9},{9,8},{10,11... | collective-permute-start | bytes 921608 | tf_op jit(solution)/shard_map/ppermute | solution.py:33
  53.4 9.1 %collective-permute-start.3 = (bf16[128,640]{1,0:T(8,128)(2,1)S(1)}, bf16[128,640]{1,0:T(8,128)(2,1)S(1)}, u32[]{:S(2)}, u32[]{:S(2)}) collective-permute-start(bf16[128,640]{1,0:T(8,128)(2,1)S(1)} %get-tuple-element.388.refs_0_), channel_id=1, source_target_pairs={{0,4},{1,5},{2,6},{3,7},{4,0},{5,1},{6,2},{7,3},{8,12},{9,13},{10,... | collective-permute-start | bytes 491528 | tf_op jit(solution)/shard_map/ppermute | solution.py:33
  54.5 14.3 %collective-permute-start.11 = (bf16[240,640]{1,0:T(8,128)(2,1)S(1)}, bf16[240,640]{1,0:T(8,128)(2,1)}, u32[]{:S(2)}, u32[]{:S(2)}) collective-permute-start(bf16[240,640]{1,0:T(8,128)(2,1)S(1)} %copy-done.106), channel_id=1, source_target_pairs={{0,1},{1,0},{2,3},{3,2},{4,5},{5,4},{6,7},{7,6},{8,9},{9,8},{10,11... | collective-permute-start | bytes 921608 | tf_op jit(solution)/shard_map/ppermute | solution.py:33
  62.4 9.7 %collective-permute-start.8 = (bf16[128,640]{1,0:T(8,128)(2,1)S(1)}, bf16[128,640]{1,0:T(8,128)(2,1)S(1)}, u32[]{:S(2)}, u32[]{:S(2)}) collective-permute-start(bf16[128,640]{1,0:T(8,128)(2,1)S(1)} %collective-permute-done.3.refs_1_), channel_id=1, source_target_pairs={{0,1},{1,0},{2,3},{3,2},{4,5},{5,4},{6,7},{7,6},{8,9},{9,8},{10,11... | collective-permute-start | bytes 491528 | tf_op jit(solution)/shard_map/ppermute | solution.py:33
  62.5 9.7 %collective-permute-start.9 = (bf16[128,640]{1,0:T(8,128)(2,1)S(1)}, bf16[128,640]{1,0:T(8,128)(2,1)S(1)}, u32[]{:S(2)}, u32[]{:S(2)}) collective-permute-start(bf16[128,640]{1,0:T(8,128)(2,1)S(1)} %collective-permute-done.4.refs_2_), channel_id=1, source_target_pairs={{0,8},{1,9},{2,10},{3,11},{4,12},{5,13},{6,14},{7,15},{8,0},{9,1},... | collective-permute-start | bytes 491528 | tf_op jit(solution)/shard_map/ppermute | solution.py:33
  73.3 21.9 %collective-permute-start.12 = (bf16[1024,640]{1,0:T(8,128)(2,1)}, bf16[1024,640]{1,0:T(8,128)(2,1)}, u32[]{:S(2)}, u32[]{:S(2)}) collective-permute-start(bf16[1024,640]{1,0:T(8,128)(2,1)} %stack.153.a_ref), channel_id=1, source_target_pairs={{0,2},{1,3},{2,0},{3,1},{4,6},{5,7},{6,4},{7,5},{8,10},{9,11},{10,... | collective-permute-start | bytes 3932168 | tf_op jit(solution)/shard_map/ppermute | solution.py:33
  73.8 39.5 %collective-permute-start.17 = (bf16[480,1280]{1,0:T(8,128)(2,1)}, bf16[480,1280]{1,0:T(8,128)(2,1)}, u32[]{:S(2)}, u32[]{:S(2)}) collective-permute-start(bf16[480,1280]{1,0:T(8,128)(2,1)} %dynamic-slice_bitcast_fusion), channel_id=1, source_target_pairs={{0,1},{1,0},{2,3},{3,2},{4,5},{5,4},{6,7},{7,6},{8,9},{9,8},{10,11... | collective-permute-start | bytes 3686408 | tf_op jit(solution)/shard_map/ppermute | solution.py:33
  74.8 9.7 %collective-permute-start.15 = (bf16[240,640]{1,0:T(8,128)(2,1)}, bf16[240,640]{1,0:T(8,128)(2,1)S(1)}, u32[]{:S(2)}, u32[]{:S(2)}) collective-permute-start(bf16[240,640]{1,0:T(8,128)(2,1)} %collective-permute-done.7.refs_0_), channel_id=1, source_target_pairs={{0,12},{1,13},{2,14},{3,15},{4,8},{5,9},{6,10},{7,11},{8,4},{9,5},... | collective-permute-start | bytes 921608 | tf_op jit(solution)/shard_map/ppermute | solution.py:33
  76.5 14.2 %collective-permute-start.14 = (bf16[240,640]{1,0:T(8,128)(2,1)}, bf16[240,640]{1,0:T(8,128)(2,1)}, u32[]{:S(2)}, u32[]{:S(2)}) collective-permute-start(bf16[240,640]{1,0:T(8,128)(2,1)} %collective-permute-done.7.refs_0_), channel_id=1, source_target_pairs={{0,8},{1,9},{2,10},{3,11},{4,12},{5,13},{6,14},{7,15},{8,0},{9,1},... | collective-permute-start | bytes 921608 | tf_op jit(solution)/shard_map/ppermute | solution.py:33
  76.7 15.7 %collective-permute-start.13 = (bf16[240,640]{1,0:T(8,128)(2,1)}, bf16[240,640]{1,0:T(8,128)(2,1)}, u32[]{:S(2)}, u32[]{:S(2)}) collective-permute-start(bf16[240,640]{1,0:T(8,128)(2,1)} %collective-permute-done.7.refs_0_), channel_id=1, source_target_pairs={{0,4},{1,5},{2,6},{3,7},{4,0},{5,1},{6,2},{7,3},{8,12},{9,13},{10,... | collective-permute-start | bytes 921608 | tf_op jit(solution)/shard_map/ppermute | solution.py:33
  85.2 28.1 %collective-permute-start.16 = (bf16[240,960]{1,0:T(8,128)(2,1)}, bf16[240,960]{1,0:T(8,128)(2,1)}, u32[]{:S(2)}, u32[]{:S(2)}) collective-permute-start(bf16[240,960]{1,0:T(8,128)(2,1)} %constant_dynamic-slice_fusion), channel_id=1, source_target_pairs={{0,1},{1,0},{2,3},{3,2},{4,5},{5,4},{6,7},{7,6},{8,9},{9,8},{10,11... | collective-permute-start | bytes 1382408 | tf_op jit(solution)/shard_map/ppermute | solution.py:33
  90.8 20.9 %collective-permute-start.20 = (bf16[240,640]{1,0:T(8,128)(2,1)}, bf16[240,640]{1,0:T(8,128)(2,1)S(1)}, u32[]{:S(2)}, u32[]{:S(2)}) collective-permute-start(bf16[240,640]{1,0:T(8,128)(2,1)} %collective-permute-done.11.refs_0_), channel_id=1, source_target_pairs={{0,12},{1,13},{2,14},{3,15},{4,8},{5,9},{6,10},{7,11},{8,4},{9,5},... | collective-permute-start | bytes 921608 | tf_op jit(solution)/shard_map/ppermute | solution.py:33
  92.4 20.8 %collective-permute-start.19 = (bf16[240,640]{1,0:T(8,128)(2,1)}, bf16[240,640]{1,0:T(8,128)(2,1)S(1)}, u32[]{:S(2)}, u32[]{:S(2)}) collective-permute-start(bf16[240,640]{1,0:T(8,128)(2,1)} %collective-permute-done.11.refs_0_), channel_id=1, source_target_pairs={{0,8},{1,9},{2,10},{3,11},{4,12},{5,13},{6,14},{7,15},{8,0},{9,1},... | collective-permute-start | bytes 921608 | tf_op jit(solution)/shard_map/ppermute | solution.py:33
  95.2 18.0 %collective-permute-start.18 = (bf16[240,640]{1,0:T(8,128)(2,1)}, bf16[240,640]{1,0:T(8,128)(2,1)S(1)}, u32[]{:S(2)}, u32[]{:S(2)}) collective-permute-start(bf16[240,640]{1,0:T(8,128)(2,1)} %collective-permute-done.11.refs_0_), channel_id=1, source_target_pairs={{0,4},{1,5},{2,6},{3,7},{4,0},{5,1},{6,2},{7,3},{8,12},{9,13},{10,... | collective-permute-start | bytes 921608 | tf_op jit(solution)/shard_map/ppermute | solution.py:33
  197.8 9.7 %collective-permute-start.40 = (bf16[512,640]{1,0:T(8,128)(2,1)}, bf16[512,640]{1,0:T(8,128)(2,1)}, u32[]{:S(2)}, u32[]{:S(2)}) collective-permute-start(bf16[512,640]{1,0:T(8,128)(2,1)} %stack.157.a_ref), channel_id=1, source_target_pairs={{0,2},{1,3},{2,0},{3,1},{4,6},{5,7},{6,4},{7,5},{8,10},{9,11},{10,... | collective-permute-start | bytes 1966088 | tf_op jit(solution)/shard_map/ppermute | solution.py:33
  200.5 27.6 %collective-permute-start.42 = (bf16[128,960]{1,0:T(8,128)(2,1)}, bf16[128,960]{1,0:T(8,128)(2,1)}, u32[]{:S(2)}, u32[]{:S(2)}) collective-permute-start(bf16[128,960]{1,0:T(8,128)(2,1)} %bitcast.9), channel_id=1, source_target_pairs={{0,0},{1,16},{2,2},{3,18},{4,4},{5,20},{6,6},{7,22},{8,8},{9,24},{... | collective-permute-start | bytes 737288 | tf_op jit(solution)/shard_map/ppermute | solution.py:42
  246.4 23.0 %collective-permute-start.41 = (bf16[128,960]{1,0:T(8,128)(2,1)S(1)}, bf16[128,960]{1,0:T(8,128)(2,1)S(1)}, u32[]{:S(2)}, u32[]{:S(2)}) collective-permute-start(bf16[128,960]{1,0:T(8,128)(2,1)S(1)} %get-tuple-element.471), channel_id=1, source_target_pairs={{0,0},{1,16},{2,2},{3,18},{4,4},{5,20},{6,6},{7,22},{8,8},{9,24},{... | collective-permute-start | bytes 737288 | tf_op jit(solution)/shard_map/ppermute | solution.py:42
  250.5 13.5 %collective-permute-start.46 = (bf16[64,640]{1,0:T(8,128)(2,1)S(1)}, bf16[64,640]{1,0:T(8,128)(2,1)S(1)}, u32[]{:S(2)}, u32[]{:S(2)}) collective-permute-start(bf16[64,640]{1,0:T(8,128)(2,1)S(1)} %get-tuple-element.497), channel_id=1, source_target_pairs={{0,8},{1,9},{2,10},{3,11},{4,12},{5,13},{6,14},{7,15},{8,0},{9,1},... | collective-permute-start | bytes 245768 | tf_op jit(solution)/shard_map/ppermute | solution.py:33
  251.8 13.6 %collective-permute-start.47 = (bf16[64,640]{1,0:T(8,128)(2,1)S(1)}, bf16[64,640]{1,0:T(8,128)(2,1)S(1)}, u32[]{:S(2)}, u32[]{:S(2)}) collective-permute-start(bf16[64,640]{1,0:T(8,128)(2,1)S(1)} %get-tuple-element.498), channel_id=1, source_target_pairs={{0,13},{1,12},{2,15},{3,14},{4,9},{5,8},{6,11},{7,10},{8,5},{9,4},... | collective-permute-start | bytes 245768 | tf_op jit(solution)/shard_map/ppermute | solution.py:33
  253.4 12.0 %collective-permute-start.48 = (bf16[64,640]{1,0:T(8,128)(2,1)S(1)}, bf16[64,640]{1,0:T(8,128)(2,1)S(1)}, u32[]{:S(2)}, u32[]{:S(2)}) collective-permute-start(bf16[64,640]{1,0:T(8,128)(2,1)S(1)} %get-tuple-element.499), channel_id=1, source_target_pairs={{0,5},{1,4},{2,7},{3,6},{4,1},{5,0},{6,3},{7,2},{8,13},{9,12},{10,... | collective-permute-start | bytes 245768 | tf_op jit(solution)/shard_map/ppermute | solution.py:33
  255.1 11.2 %collective-permute-start.49 = (bf16[64,640]{1,0:T(8,128)(2,1)S(1)}, bf16[64,640]{1,0:T(8,128)(2,1)S(1)}, u32[]{:S(2)}, u32[]{:S(2)}) collective-permute-start(bf16[64,640]{1,0:T(8,128)(2,1)S(1)} %get-tuple-element.500), channel_id=1, source_target_pairs={{0,9},{1,8},{2,11},{3,10},{4,13},{5,12},{6,15},{7,14},{8,1},{9,0},... | collective-permute-start | bytes 245768 | tf_op jit(solution)/shard_map/ppermute | solution.py:33
  295.0 10.5 %collective-permute-start.56 = (bf16[96,640]{1,0:T(8,128)(2,1)S(1)}, bf16[96,640]{1,0:T(8,128)(2,1)S(1)}, u32[]{:S(2)}, u32[]{:S(2)}) collective-permute-start(bf16[96,640]{1,0:T(8,128)(2,1)S(1)} %get-tuple-element.545), channel_id=1, source_target_pairs={{0,5},{1,4},{2,7},{3,6},{4,1},{5,0},{6,3},{7,2},{8,13},{9,12},{10,... | collective-permute-start | bytes 368648 | tf_op jit(solution)/shard_map/ppermute | solution.py:33
  345.5 39.6 %collective-permute-start.68 = (bf16[2,2,4,120,640]{4,3,2,1,0:T(8,128)(2,1)S(1)}, bf16[2,2,4,120,640]{4,3,2,1,0:T(8,128)(2,1)S(1)}, u32[]{:S(2)}, u32[]{:S(2)}) collective-permute-start(bf16[2,2,4,120,640]{4,3,2,1,0:T(8,128)(2,1)S(1)} %get-tuple-element.608), channel_id=1, source_target_pairs={{0,2},{1,3},{2,0},{3,1},{4,6},{5,7},{6,4},{7,5},{8,10},{9,11},{10,... | collective-permute-start | bytes 7372808 | tf_op jit(solution)/shard_map/ppermute | solution.py:33
  346.3 30.1 %collective-permute-start.69 = (bf16[2,4,80,960]{3,2,1,0:T(8,128)(2,1)S(1)}, bf16[2,4,80,960]{3,2,1,0:T(8,128)(2,1)S(1)}, u32[]{:S(2)}, u32[]{:S(2)}) collective-permute-start(bf16[2,4,80,960]{3,2,1,0:T(8,128)(2,1)S(1)} %slice_bitcast_fusion), channel_id=1, source_target_pairs={{0,1},{1,0},{2,3},{3,2},{4,5},{5,4},{6,7},{7,6},{8,9},{9,8},{10,11... | collective-permute-start | bytes 3686408 | tf_op jit(solution)/shard_map/ppermute | solution.py:33
  376.3 11.8 %collective-permute-start.61 = (bf16[128,640]{1,0:T(8,128)(2,1)S(1)}, bf16[128,640]{1,0:T(8,128)(2,1)S(1)}, u32[]{:S(2)}, u32[]{:S(2)}) collective-permute-start(bf16[128,640]{1,0:T(8,128)(2,1)S(1)} %get-tuple-element.594), channel_id=1, source_target_pairs={{0,4},{1,5},{2,6},{3,7},{4,0},{5,1},{6,2},{7,3},{8,12},{9,13},{10,... | collective-permute-start | bytes 491528 | tf_op jit(solution)/shard_map/ppermute | solution.py:33
  377.2 12.0 %collective-permute-start.62 = (bf16[128,640]{1,0:T(8,128)(2,1)S(1)}, bf16[128,640]{1,0:T(8,128)(2,1)S(1)}, u32[]{:S(2)}, u32[]{:S(2)}) collective-permute-start(bf16[128,640]{1,0:T(8,128)(2,1)S(1)} %get-tuple-element.595), channel_id=1, source_target_pairs={{0,1},{1,0},{2,3},{3,2},{4,5},{5,4},{6,7},{7,6},{8,9},{9,8},{10,11... | collective-permute-start | bytes 491528 | tf_op jit(solution)/shard_map/ppermute | solution.py:33
  377.5 13.5 %collective-permute-start.63 = (bf16[128,640]{1,0:T(8,128)(2,1)S(1)}, bf16[128,640]{1,0:T(8,128)(2,1)S(1)}, u32[]{:S(2)}, u32[]{:S(2)}) collective-permute-start(bf16[128,640]{1,0:T(8,128)(2,1)S(1)} %get-tuple-element.596), channel_id=1, source_target_pairs={{0,8},{1,9},{2,10},{3,11},{4,12},{5,13},{6,14},{7,15},{8,0},{9,1},... | collective-permute-start | bytes 491528 | tf_op jit(solution)/shard_map/ppermute | solution.py:33
  378.3 13.6 %collective-permute-start.64 = (bf16[128,640]{1,0:T(8,128)(2,1)S(1)}, bf16[128,640]{1,0:T(8,128)(2,1)S(1)}, u32[]{:S(2)}, u32[]{:S(2)}) collective-permute-start(bf16[128,640]{1,0:T(8,128)(2,1)S(1)} %get-tuple-element.597), channel_id=1, source_target_pairs={{0,13},{1,12},{2,15},{3,14},{4,9},{5,8},{6,11},{7,10},{8,5},{9,4},... | collective-permute-start | bytes 491528 | tf_op jit(solution)/shard_map/ppermute | solution.py:33
  385.1 39.9 %collective-permute-start.75 = (bf16[2,2,4,120,640]{4,3,2,1,0:T(8,128)(2,1)S(1)}, bf16[2,2,4,120,640]{4,3,2,1,0:T(8,128)(2,1)S(1)}, u32[]{:S(2)}, u32[]{:S(2)}) collective-permute-start(bf16[2,2,4,120,640]{4,3,2,1,0:T(8,128)(2,1)S(1)} %get-tuple-element.639), channel_id=1, source_target_pairs={{0,2},{1,3},{2,0},{3,1},{4,6},{5,7},{6,4},{7,5},{8,10},{9,11},{10,... | collective-permute-start | bytes 7372808 | tf_op jit(solution)/shard_map/ppermute | solution.py:33
  391.0 10.3 %collective-permute-start.67 = (bf16[128,640]{1,0:T(8,128)(2,1)S(1)}, bf16[128,640]{1,0:T(8,128)(2,1)S(1)}, u32[]{:S(2)}, u32[]{:S(2)}) collective-permute-start(bf16[128,640]{1,0:T(8,128)(2,1)S(1)} %get-tuple-element.600), channel_id=1, source_target_pairs={{0,12},{1,13},{2,14},{3,15},{4,8},{5,9},{6,10},{7,11},{8,4},{9,5},... | collective-permute-start | bytes 491528 | tf_op jit(solution)/shard_map/ppermute | solution.py:33
  391.9 19.5 %collective-permute-start.71 = (bf16[4,80,960]{2,1,0:T(8,128)(2,1)S(1)}, bf16[4,80,960]{2,1,0:T(8,128)(2,1)S(1)}, u32[]{:S(2)}, u32[]{:S(2)}) collective-permute-start(bf16[4,80,960]{2,1,0:T(8,128)(2,1)S(1)} %slice_bitcast_fusion.4), channel_id=1, source_target_pairs={{0,4},{1,5},{2,6},{3,7},{4,0},{5,1},{6,2},{7,3},{8,12},{9,13},{10,... | collective-permute-start | bytes 1843208 | tf_op jit(solution)/shard_map/ppermute | solution.py:33
  396.7 27.0 %collective-permute-start.76 = (bf16[2,4,120,640]{3,2,1,0:T(8,128)(2,1)S(1)}, bf16[2,4,120,640]{3,2,1,0:T(8,128)(2,1)S(1)}, u32[]{:S(2)}, u32[]{:S(2)}) collective-permute-start(bf16[2,4,120,640]{3,2,1,0:T(8,128)(2,1)S(1)} %slice_bitcast_fusion.3), channel_id=1, source_target_pairs={{0,1},{1,0},{2,3},{3,2},{4,5},{5,4},{6,7},{7,6},{8,9},{9,8},{10,11... | collective-permute-start | bytes 3686408 | tf_op jit(solution)/shard_map/ppermute | solution.py:33
  418.4 50.2 %collective-permute-start.89 = (bf16[2,2,4,120,640]{4,3,2,1,0:T(8,128)(2,1)S(1)}, bf16[2,2,4,120,640]{4,3,2,1,0:T(8,128)(2,1)S(1)}, u32[]{:S(2)}, u32[]{:S(2)}) collective-permute-start(bf16[2,2,4,120,640]{4,3,2,1,0:T(8,128)(2,1)S(1)} %get-tuple-element.674), channel_id=1, source_target_pairs={{0,2},{1,3},{2,0},{3,1},{4,6},{5,7},{6,4},{7,5},{8,10},{9,11},{10,... | collective-permute-start | bytes 7372808 | tf_op jit(solution)/shard_map/ppermute | solution.py:33
  420.1 15.2 %collective-permute-start.73 = (bf16[80,960]{1,0:T(8,128)(2,1)S(1)}, bf16[80,960]{1,0:T(8,128)(2,1)S(1)}, u32[]{:S(2)}, u32[]{:S(2)}) collective-permute-start(bf16[80,960]{1,0:T(8,128)(2,1)S(1)} %get-tuple-element.802), channel_id=1, source_target_pairs={{0,16},{1,17},{2,18},{3,19},{4,20},{5,21},{6,22},{7,23},{8,24},{9,... | collective-permute-start | bytes 460808 | tf_op jit(solution)/shard_map/ppermute | solution.py:33
  423.7 11.6 %collective-permute-start.72 = (bf16[80,960]{1,0:T(8,128)(2,1)S(1)}, bf16[80,960]{1,0:T(8,128)(2,1)S(1)}, u32[]{:S(2)}, u32[]{:S(2)}) collective-permute-start(bf16[80,960]{1,0:T(8,128)(2,1)S(1)} %get-tuple-element.803), channel_id=1, source_target_pairs={{0,8},{1,9},{2,10},{3,11},{4,12},{5,13},{6,14},{7,15},{8,0},{9,1},... | collective-permute-start | bytes 460808 | tf_op jit(solution)/shard_map/ppermute | solution.py:33
  425.0 18.4 %collective-permute-start.81 = (bf16[4,120,640]{2,1,0:T(8,128)(2,1)S(1)}, bf16[4,120,640]{2,1,0:T(8,128)(2,1)S(1)}, u32[]{:S(2)}, u32[]{:S(2)}) collective-permute-start(bf16[4,120,640]{2,1,0:T(8,128)(2,1)S(1)} %slice_bitcast_fusion.11), channel_id=1, source_target_pairs={{0,4},{1,5},{2,6},{3,7},{4,0},{5,1},{6,2},{7,3},{8,12},{9,13},{10,... | collective-permute-start | bytes 1843208 | tf_op jit(solution)/shard_map/ppermute | solution.py:33
  438.0 31.4 %collective-permute-start.90 = (bf16[2,4,120,640]{3,2,1,0:T(8,128)(2,1)S(1)}, bf16[2,4,120,640]{3,2,1,0:T(8,128)(2,1)S(1)}, u32[]{:S(2)}, u32[]{:S(2)}) collective-permute-start(bf16[2,4,120,640]{3,2,1,0:T(8,128)(2,1)S(1)} %slice_bitcast_fusion.2), channel_id=1, source_target_pairs={{0,1},{1,0},{2,3},{3,2},{4,5},{5,4},{6,7},{7,6},{8,9},{9,8},{10,11... | collective-permute-start | bytes 3686408 | tf_op jit(solution)/shard_map/ppermute | solution.py:33
  443.4 22.1 %collective-permute-start.84 = (f32[2,960]{1,0:T(2,128)S(1)}, f32[2,960]{1,0:T(2,128)S(1)}, u32[]{:S(2)}, u32[]{:S(2)}) collective-permute-start(f32[2,960]{1,0:T(2,128)S(1)} %add.191), channel_id=1, source_target_pairs={{0,1},{1,0},{2,3},{3,2},{4,5},{5,4},{6,7},{7,6},{8,9},{9,8},{10,11... | collective-permute-start | bytes 23048 | tf_op jit(solution)/shard_map/ppermute | solution.py:33
  465.6 17.0 %collective-permute-start.85 = (f32[2,960]{1,0:T(2,128)S(1)}, f32[2,960]{1,0:T(2,128)S(1)}, u32[]{:S(2)}, u32[]{:S(2)}) collective-permute-start(f32[2,960]{1,0:T(2,128)S(1)} %add.192), channel_id=1, source_target_pairs={{0,8},{1,9},{2,10},{3,11},{4,12},{5,13},{6,14},{7,15},{8,0},{9,1},... | collective-permute-start | bytes 23048 | tf_op jit(solution)/shard_map/ppermute | solution.py:33
  466.7 15.4 %collective-permute-start.87 = (bf16[120,640]{1,0:T(8,128)(2,1)S(1)}, bf16[120,640]{1,0:T(8,128)(2,1)S(1)}, u32[]{:S(2)}, u32[]{:S(2)}) collective-permute-start(bf16[120,640]{1,0:T(8,128)(2,1)S(1)} %get-tuple-element.817), channel_id=1, source_target_pairs={{0,16},{1,17},{2,18},{3,19},{4,20},{5,21},{6,22},{7,23},{8,24},{9,... | collective-permute-start | bytes 460808 | tf_op jit(solution)/shard_map/ppermute | solution.py:33
  468.6 14.0 %collective-permute-start.83 = (bf16[4,80,960]{2,1,0:T(8,128)(2,1)S(1)}, bf16[4,80,960]{2,1,0:T(8,128)(2,1)S(1)}, u32[]{:S(2)}, u32[]{:S(2)}) collective-permute-start(bf16[4,80,960]{2,1,0:T(8,128)(2,1)S(1)} %get-tuple-element.800), channel_id=1, source_target_pairs={{0,4},{1,5},{2,6},{3,7},{4,0},{5,1},{6,2},{7,3},{8,12},{9,13},{10,... | collective-permute-start | bytes 1843208 | tf_op jit(solution)/shard_map/ppermute | solution.py:33
  469.4 13.1 %collective-permute-start.86 = (bf16[120,640]{1,0:T(8,128)(2,1)S(1)}, bf16[120,640]{1,0:T(8,128)(2,1)S(1)}, u32[]{:S(2)}, u32[]{:S(2)}) collective-permute-start(bf16[120,640]{1,0:T(8,128)(2,1)S(1)} %get-tuple-element.818), channel_id=1, source_target_pairs={{0,8},{1,9},{2,10},{3,11},{4,12},{5,13},{6,14},{7,15},{8,0},{9,1},... | collective-permute-start | bytes 460808 | tf_op jit(solution)/shard_map/ppermute | solution.py:33
  471.9 35.9 %collective-permute-start.70 = (f32[128,960]{1,0:T(8,128)S(1)}, f32[128,960]{1,0:T(8,128)S(1)}, u32[]{:S(2)}, u32[]{:S(2)}) collective-permute-start(f32[128,960]{1,0:T(8,128)S(1)} %get-tuple-element.624), channel_id=1, source_target_pairs={{0,0},{1,16},{2,2},{3,18},{4,4},{5,20},{6,6},{7,22},{8,8},{9,24},{... | collective-permute-start | bytes 1474568 | tf_op jit(solution)/shard_map/ppermute | solution.py:42
  482.1 25.7 %collective-permute-start.97 = (bf16[4,120,640]{2,1,0:T(8,128)(2,1)S(1)}, bf16[4,120,640]{2,1,0:T(8,128)(2,1)S(1)}, u32[]{:S(2)}, u32[]{:S(2)}) collective-permute-start(bf16[4,120,640]{2,1,0:T(8,128)(2,1)S(1)} %slice_bitcast_fusion.9), channel_id=1, source_target_pairs={{0,4},{1,5},{2,6},{3,7},{4,0},{5,1},{6,2},{7,3},{8,12},{9,13},{10,... | collective-permute-start | bytes 1843208 | tf_op jit(solution)/shard_map/ppermute | solution.py:33
  482.7 34.6 %collective-permute-start.92 = (bf16[2,4,80,960]{3,2,1,0:T(8,128)(2,1)S(1)}, bf16[2,4,80,960]{3,2,1,0:T(8,128)(2,1)S(1)}, u32[]{:S(2)}, u32[]{:S(2)}) collective-permute-start(bf16[2,4,80,960]{3,2,1,0:T(8,128)(2,1)S(1)} %pad_maximum_fusion.near_ref), channel_id=1, source_target_pairs={{0,2},{1,3},{2,0},{3,1},{4,6},{5,7},{6,4},{7,5},{8,10},{9,11},{10,... | collective-permute-start | bytes 3686408 | tf_op jit(solution)/shard_map/ppermute | solution.py:33
  486.7 38.3 %collective-permute-start.91 = (bf16[2,4,120,640]{3,2,1,0:T(8,128)(2,1)S(1)}, bf16[2,4,120,640]{3,2,1,0:T(8,128)(2,1)S(1)}, u32[]{:S(2)}, u32[]{:S(2)}) collective-permute-start(bf16[2,4,120,640]{3,2,1,0:T(8,128)(2,1)S(1)} %slice_bitcast_fusion.1), channel_id=1, source_target_pairs={{0,1},{1,0},{2,3},{3,2},{4,5},{5,4},{6,7},{7,6},{8,9},{9,8},{10,11... | collective-permute-start | bytes 3686408 | tf_op jit(solution)/shard_map/ppermute | solution.py:33
  487.9 20.1 %collective-permute-start.96 = (bf16[120,640]{1,0:T(8,128)(2,1)S(1)}, bf16[120,640]{1,0:T(8,128)(2,1)S(1)}, u32[]{:S(2)}, u32[]{:S(2)}) collective-permute-start(bf16[120,640]{1,0:T(8,128)(2,1)S(1)} %fusion.19), channel_id=1, source_target_pairs={{0,24},{1,25},{2,26},{3,27},{4,28},{5,29},{6,30},{7,31},{8,16},{9,... | collective-permute-start | bytes 460808 | tf_op jit(solution)/shard_map/ppermute | solution.py:33
  514.1 15.5 %collective-permute-start.99 = (bf16[4,120,640]{2,1,0:T(8,128)(2,1)S(1)}, bf16[4,120,640]{2,1,0:T(8,128)(2,1)S(1)}, u32[]{:S(2)}, u32[]{:S(2)}) collective-permute-start(bf16[4,120,640]{2,1,0:T(8,128)(2,1)S(1)} %get-tuple-element.809), channel_id=1, source_target_pairs={{0,4},{1,5},{2,6},{3,7},{4,0},{5,1},{6,2},{7,3},{8,12},{9,13},{10,... | collective-permute-start | bytes 1843208 | tf_op jit(solution)/shard_map/ppermute | solution.py:33
  515.3 11.0 %collective-permute-start.102 = (bf16[120,640]{1,0:T(8,128)(2,1)S(1)}, bf16[120,640]{1,0:T(8,128)(2,1)S(1)}, u32[]{:S(2)}, u32[]{:S(2)}) collective-permute-start(bf16[120,640]{1,0:T(8,128)(2,1)S(1)} %get-tuple-element.813), channel_id=1, source_target_pairs={{0,24},{1,25},{2,26},{3,27},{4,28},{5,29},{6,30},{7,31},{8,16},{9,... | collective-permute-start | bytes 460808 | tf_op jit(solution)/shard_map/ppermute | solution.py:33
  517.1 12.6 %collective-permute-start.101 = (bf16[120,640]{1,0:T(8,128)(2,1)S(1)}, bf16[120,640]{1,0:T(8,128)(2,1)S(1)}, u32[]{:S(2)}, u32[]{:S(2)}) collective-permute-start(bf16[120,640]{1,0:T(8,128)(2,1)S(1)} %get-tuple-element.814), channel_id=1, source_target_pairs={{0,16},{1,17},{2,18},{3,19},{4,20},{5,21},{6,22},{7,23},{8,24},{9,... | collective-permute-start | bytes 460808 | tf_op jit(solution)/shard_map/ppermute | solution.py:33
  517.3 12.3 %collective-permute-start.100 = (bf16[120,640]{1,0:T(8,128)(2,1)S(1)}, bf16[120,640]{1,0:T(8,128)(2,1)S(1)}, u32[]{:S(2)}, u32[]{:S(2)}) collective-permute-start(bf16[120,640]{1,0:T(8,128)(2,1)S(1)} %get-tuple-element.815), channel_id=1, source_target_pairs={{0,8},{1,9},{2,10},{3,11},{4,12},{5,13},{6,14},{7,15},{8,0},{9,1},... | collective-permute-start | bytes 460808 | tf_op jit(solution)/shard_map/ppermute | solution.py:33
  525.3 15.0 %collective-permute-start.98 = (bf16[4,120,640]{2,1,0:T(8,128)(2,1)S(1)}, bf16[4,120,640]{2,1,0:T(8,128)(2,1)S(1)}, u32[]{:S(2)}, u32[]{:S(2)}) collective-permute-start(bf16[4,120,640]{2,1,0:T(8,128)(2,1)S(1)} %slice_bitcast_fusion.7), channel_id=1, source_target_pairs={{0,4},{1,5},{2,6},{3,7},{4,0},{5,1},{6,2},{7,3},{8,12},{9,13},{10,... | collective-permute-start | bytes 1843208 | tf_op jit(solution)/shard_map/ppermute | solution.py:33
  529.8 26.0 %collective-permute-start.106 = (bf16[2,4,120,640]{3,2,1,0:T(8,128)(2,1)S(1)}, bf16[2,4,120,640]{3,2,1,0:T(8,128)(2,1)S(1)}, u32[]{:S(2)}, u32[]{:S(2)}) collective-permute-start(bf16[2,4,120,640]{3,2,1,0:T(8,128)(2,1)S(1)} %pad_maximum_fusion.1.near_ref), channel_id=1, source_target_pairs={{0,2},{1,3},{2,0},{3,1},{4,6},{5,7},{6,4},{7,5},{8,10},{9,11},{10,... | collective-permute-start | bytes 3686408 | tf_op jit(solution)/shard_map/ppermute | solution.py:33
  537.4 13.6 %collective-permute-start.108 = (bf16[120,640]{1,0:T(8,128)(2,1)S(1)}, bf16[120,640]{1,0:T(8,128)(2,1)S(1)}, u32[]{:S(2)}, u32[]{:S(2)}) collective-permute-start(bf16[120,640]{1,0:T(8,128)(2,1)S(1)} %fusion.13), channel_id=1, source_target_pairs={{0,16},{1,17},{2,18},{3,19},{4,20},{5,21},{6,22},{7,23},{8,24},{9,... | collective-permute-start | bytes 460808 | tf_op jit(solution)/shard_map/ppermute | solution.py:33
  537.4 13.6 %collective-permute-start.107 = (bf16[120,640]{1,0:T(8,128)(2,1)S(1)}, bf16[120,640]{1,0:T(8,128)(2,1)S(1)}, u32[]{:S(2)}, u32[]{:S(2)}) collective-permute-start(bf16[120,640]{1,0:T(8,128)(2,1)S(1)} %fusion.13), channel_id=1, source_target_pairs={{0,8},{1,9},{2,10},{3,11},{4,12},{5,13},{6,14},{7,15},{8,0},{9,1},... | collective-permute-start | bytes 460808 | tf_op jit(solution)/shard_map/ppermute | solution.py:33
  551.2 15.8 %collective-permute-start.113 = (bf16[4,120,640]{2,1,0:T(8,128)(2,1)S(1)}, bf16[4,120,640]{2,1,0:T(8,128)(2,1)S(1)}, u32[]{:S(2)}, u32[]{:S(2)}) collective-permute-start(bf16[4,120,640]{2,1,0:T(8,128)(2,1)S(1)} %get-tuple-element.807), channel_id=1, source_target_pairs={{0,4},{1,5},{2,6},{3,7},{4,0},{5,1},{6,2},{7,3},{8,12},{9,13},{10,... | collective-permute-start | bytes 1843208 | tf_op jit(solution)/shard_map/ppermute | solution.py:33
  555.4 11.5 %collective-permute-start.104 = (bf16[120,640]{1,0:T(8,128)(2,1)S(1)}, bf16[120,640]{1,0:T(8,128)(2,1)S(1)}, u32[]{:S(2)}, u32[]{:S(2)}) collective-permute-start(bf16[120,640]{1,0:T(8,128)(2,1)S(1)} %get-tuple-element.811), channel_id=1, source_target_pairs={{0,16},{1,17},{2,18},{3,19},{4,20},{5,21},{6,22},{7,23},{8,24},{9,... | collective-permute-start | bytes 460808 | tf_op jit(solution)/shard_map/ppermute | solution.py:33
  555.4 11.5 %collective-permute-start.103 = (bf16[120,640]{1,0:T(8,128)(2,1)S(1)}, bf16[120,640]{1,0:T(8,128)(2,1)S(1)}, u32[]{:S(2)}, u32[]{:S(2)}) collective-permute-start(bf16[120,640]{1,0:T(8,128)(2,1)S(1)} %get-tuple-element.812), channel_id=1, source_target_pairs={{0,8},{1,9},{2,10},{3,11},{4,12},{5,13},{6,14},{7,15},{8,0},{9,1},... | collective-permute-start | bytes 460808 | tf_op jit(solution)/shard_map/ppermute | solution.py:33
  567.1 17.2 %collective-permute-start.115 = (bf16[2,4,120,640]{3,2,1,0:T(8,128)(2,1)S(1)}, bf16[2,4,120,640]{3,2,1,0:T(8,128)(2,1)S(1)}, u32[]{:S(2)}, u32[]{:S(2)}) collective-permute-start(bf16[2,4,120,640]{3,2,1,0:T(8,128)(2,1)S(1)} %pad_maximum_fusion.2.near_ref), channel_id=1, source_target_pairs={{0,2},{1,3},{2,0},{3,1},{4,6},{5,7},{6,4},{7,5},{8,10},{9,11},{10,... | collective-permute-start | bytes 3686408 | tf_op jit(solution)/shard_map/ppermute | solution.py:33
  570.3 13.7 %collective-permute-start.111 = (bf16[120,640]{1,0:T(8,128)(2,1)S(1)}, bf16[120,640]{1,0:T(8,128)(2,1)S(1)}, u32[]{:S(2)}, u32[]{:S(2)}) collective-permute-start(bf16[120,640]{1,0:T(8,128)(2,1)S(1)} %fusion.16), channel_id=1, source_target_pairs={{0,16},{1,17},{2,18},{3,19},{4,20},{5,21},{6,22},{7,23},{8,24},{9,... | collective-permute-start | bytes 460808 | tf_op jit(solution)/shard_map/ppermute | solution.py:33
  570.3 13.7 %collective-permute-start.110 = (bf16[120,640]{1,0:T(8,128)(2,1)S(1)}, bf16[120,640]{1,0:T(8,128)(2,1)S(1)}, u32[]{:S(2)}, u32[]{:S(2)}) collective-permute-start(bf16[120,640]{1,0:T(8,128)(2,1)S(1)} %fusion.16), channel_id=1, source_target_pairs={{0,8},{1,9},{2,10},{3,11},{4,12},{5,13},{6,14},{7,15},{8,0},{9,1},... | collective-permute-start | bytes 460808 | tf_op jit(solution)/shard_map/ppermute | solution.py:33
  584.2 14.7 %collective-permute-start.114 = (bf16[4,120,640]{2,1,0:T(8,128)(2,1)S(1)}, bf16[4,120,640]{2,1,0:T(8,128)(2,1)S(1)}, u32[]{:S(2)}, u32[]{:S(2)}) collective-permute-start(bf16[4,120,640]{2,1,0:T(8,128)(2,1)S(1)} %get-tuple-element.805), channel_id=1, source_target_pairs={{0,4},{1,5},{2,6},{3,7},{4,0},{5,1},{6,2},{7,3},{8,12},{9,13},{10,... | collective-permute-start | bytes 1843208 | tf_op jit(solution)/shard_map/ppermute | solution.py:33
  (182 other events, 1677.9 us)

commit v3 on v2

v3 whole, which is shorter than its diff:
```python
import functools

import jax
import jax.numpy as jnp
from jax import lax
from jax.experimental import pallas as pl
from jax.experimental.pallas import tpu as pltpu
from jax.sharding import PartitionSpec as P

QUERY_HEADS = 15
KEY_VALUE_HEADS = 5
HEAD_SIZE = 64
SHARE = QUERY_HEADS // KEY_VALUE_HEADS
BLK = 64
CONT_BITS = 10
EPSILON = 1e-05
ROPE_BASE = 10000.0
MASK_FLOOR = -1e30
SCALE = HEAD_SIZE ** (-0.5)

BF = jnp.bfloat16
F32 = jnp.float32
AXES = ("ctx", "ws")
FF_CHUNKS = 4
MIB = 1024 * 1024

Y_BIT, C_BIT, X_BIT, Z1_BIT, Z2_BIT = 1, 2, 4, 8, 16
NEAR = (0, X_BIT, Y_BIT, Z1_BIT, X_BIT | Y_BIT | Z1_BIT, X_BIT | Y_BIT, Y_BIT | Z1_BIT, Z1_BIT | X_BIT)


def hop(value, mask):
    return lax.ppermute(value, AXES, [(i, i ^ mask) for i in range(32)])


def swap_place(i):
    y, z2 = i & 1, (i >> 4) & 1
    return (i & ~(Y_BIT | Z2_BIT)) | (Z2_BIT if y else 0) | (Y_BIT if z2 else 0)


def move(value):
    return lax.ppermute(value, AXES, [(i, swap_place(i)) for i in range(32)])


def ctx_mask(mask):
    return (
        (1 if mask & C_BIT else 0)
        | (2 if mask & X_BIT else 0)
        | (4 if mask & Z1_BIT else 0)
        | (8 if mask & Y_BIT else 0)
    )


NT = (((1,), (1,)), ((), ()))
TN = (((0,), (0,)), ((), ()))
NN = (((1,), (0,)), ((), ()))


def mm(left, right, dims=NN, precision=None):
    return lax.dot_general(left, right, dims, precision=precision, preferred_element_type=F32)


def normed_rows(values):
    inverse = lax.rsqrt(jnp.mean(values * values, axis=-1, keepdims=True) + EPSILON)
    return values * inverse, inverse


def norm_back(grad_in, normed, inverse, gain):
    scaled = grad_in * gain
    return inverse * (scaled - normed * jnp.mean(scaled * normed, axis=-1, keepdims=True))


def turn(values, cosine, sine, back=False):
    rows, width = values.shape
    lane = lax.broadcasted_iota(jnp.int32, (rows, 128), 1)
    first = (lane & (HEAD_SIZE - 1)) < HEAD_SIZE // 2
    if back:
        sine = -sine
    pieces = []
    for start in range(0, width, 128):
        wide = min(128, width - start)
        part = values[:, start : start + wide]
        if wide < 128:
            part = jnp.concatenate([part, jnp.zeros((rows, 128 - wide), F32)], axis=1)
        other = jnp.where(first, pltpu.roll(part, 96, 1), pltpu.roll(part, 32, 1))
        pieces.append((part * cosine + other * sine)[:, :wide])
    return jnp.concatenate(pieces, axis=1)


def vm():
    return pl.BlockSpec(memory_space=pltpu.VMEM)


def sm():
    return pl.BlockSpec(memory_space=pltpu.SMEM)


def hbm():
    return pl.BlockSpec(memory_space=pltpu.HBM)


def shaped(shape, dtype):
    return jax.ShapeDtypeStruct(shape, dtype)


def stored(shape, dtype):
    return pltpu.HBM(shape, dtype)


def apart(arrays):
    return [pltpu.with_memory_space_constraint(a, pltpu.HBM) for a in arrays]


def params(mib, **kw):
    return pltpu.CompilerParams(vmem_limit_bytes=mib * MIB, **kw)


def estimate(micros=1.0):
    return pl.CostEstimate(flops=0, bytes_accessed=int(micros * 3.7e6 / 4), transcendentals=0)


class Order:
    def __init__(self, token):
        self.token = token

    def all(self, *values):
        *values, self.token = lax.optimization_barrier(values + (self.token,))
        return values

    def take(self, *values):
        *values, self.token = lax.optimization_barrier(tuple(values) + (self.token,))
        return values[0] if len(values) == 1 else values


def read_coords(ref):
    return [ref[i] for i in range(4)]


class Weight:
    def __init__(self, shape, arrays, groups):
        self.shape, self.arrays, self.groups = shape, arrays, groups


def at_place(ref, place, rows, cols, coords):
    row, col = place(*coords)
    if rows != ref.shape[0] and not isinstance(row, int):
        row = pl.multiple_of(row, 16)
    if cols != ref.shape[1] and not isinstance(col, int):
        col = pl.multiple_of(col, 128)
    if cols == ref.shape[1]:
        return ref if rows == ref.shape[0] else ref.at[pl.ds(row, rows), :]
    return ref.at[pl.ds(row, rows), pl.ds(col, cols)]


def bring(weights, refs, buffers, sems, coords, turns, ahead=3):
    firsts, at = [], 0
    for weight in weights:
        firsts.append(at)
        at += len(weight.arrays)
    copies, count = {}, 0
    for which, group in turns:
        copies[which, group] = []
        for array, rows, cols, source, target in weights[which].groups[group]:
            copies[which, group].append(
                pltpu.make_async_copy(
                    at_place(refs[firsts[which] + array], source, rows, cols, coords),
                    at_place(buffers[which], target, rows, cols, coords),
                    sems.at[count],
                )
            )
            count += 1
    queue = list(turns)

    def start():
        if queue:
            for copy in copies[queue.pop(0)]:
                copy.start()

    for _ in range(ahead):
        start()

    def wait(which, group=0):
        for copy in copies[which, group]:
            copy.wait()
        start()

    return wait


def arrays_of(weights):
    return [a for w in weights for a in w.arrays]


def weights_in(near, weights):
    arrays = arrays_of(weights)
    if near:
        return [vm()] * len(arrays), arrays, []
    return [hbm()] * len(arrays), apart(arrays), scratch_of(weights)


def weights_here(near, weights, refs, scratch, coords_ref, turns):
    if near:
        return refs, lambda *which: None
    buffers, sems = scratch[: len(weights)], scratch[len(weights)]
    return buffers, bring(weights, refs, buffers, sems, read_coords(coords_ref), turns)


def join_kernel(weights, coords_ref, *args):
    count = len(arrays_of(weights))
    refs, outs, sems = args[:count], args[count:-1], args[-1]
    turns = [(i, g) for i, w in enumerate(weights) for g in range(len(w.groups))]
    wait = bring(weights, refs, outs, sems, read_coords(coords_ref), turns, len(turns))
    for turn in turns:
        wait(*turn)


def join_call(coords, weights):
    arrays = arrays_of(weights)
    joined = pl.pallas_call(
        functools.partial(join_kernel, weights),
        name="join_weights",
        out_shape=tuple(pltpu.VMEM(w.shape, BF) for w in weights),
        in_specs=[sm()] + [hbm()] * len(arrays),
        out_specs=tuple(vm() for _ in weights),
        scratch_shapes=scratch_of(weights)[-1:],
        compiler_params=params(24),
        cost_estimate=estimate(),
    )(coords, *apart(arrays))
    return tuple(one_piece(w) for w in joined)


def scratch_of(weights):
    copies = sum(len(g) for w in weights for g in w.groups)
    return [pltpu.VMEM(w.shape, BF) for w in weights] + [pltpu.SemaphoreType.DMA((copies,))]


def one_piece(array):
    rows, cols = array.shape
    origin = lambda *k: (0, 0)
    return Weight(array.shape, [array], [[(0, rows, cols, origin, origin)]])


def in_columns(array):
    rows, cols = array.shape
    wide = cols // FF_CHUNKS
    place = lambda j: (lambda *k: (0, j * wide))
    return Weight(
        array.shape, [array], [[(0, rows, wide, place(j), place(j))] for j in range(FF_CHUNKS)]
    )


def part_of(j, coords):
    rx, rz = BESIDE[j]
    return (coords[2] ^ rx) * 2 + ((coords[3] & 1) ^ rz)


BESIDE = ((0, 0), (1, 0), (0, 1), (1, 1))


def pack_kernel(coords_ref, q_hbm, k_hbm, v_hbm, own_ref, piece_ref, q_ref, k_ref, v_ref, sems):
    copies = [
        pltpu.make_async_copy(a, b, sems.at[i])
        for i, (a, b) in enumerate(((q_hbm, q_ref), (k_hbm, k_ref), (v_hbm, v_ref)))
    ]
    for copy in copies:
        copy.start()
    half, width = q_ref.shape
    kv_width = k_ref.shape[0]
    end = width + 2 * kv_width
    own_ref[:, end:] = jnp.zeros((half, own_ref.shape[1] - end), BF)
    for copy in copies:
        copy.wait()
    own_ref[:, :width] = q_ref[...]
    own_ref[:, width : width + kv_width] = k_ref[...].T
    own_ref[:, width + kv_width : end] = v_ref[...].T
    depth = half // 2
    start = pl.multiple_of(coords_ref[1] * depth, 16)
    piece_ref[...] = own_ref[pl.ds(start, depth), :]


def pack_call(coords, w_query, key_t, value_t):
    half, width = w_query.shape
    total = -(-(width + 2 * key_t.shape[0]) // 128) * 128
    return pl.pallas_call(
        pack_kernel,
        name="pack",
        out_shape=(stored((half, total), BF), shaped((half // 2, total), BF)),
        in_specs=[sm()] + [hbm()] * 3,
        out_specs=(vm(), vm()),
        scratch_shapes=[pltpu.VMEM(a.shape, BF) for a in (w_query, key_t, value_t)]
        + [pltpu.SemaphoreType.DMA((3,))],
        compiler_params=params(12),
        cost_estimate=estimate(),
    )(coords, *apart([w_query, key_t, value_t]))


def pack_rows_kernel(tokens_ref, plan_ref, out_ref):
    width, rows = tokens_ref.shape
    out_ref[:rows, :] = tokens_ref[...].T
    marks = plan_ref[...].astype(F32).astype(BF)
    out_ref[rows:, : marks.shape[1]] = marks
    out_ref[rows:, marks.shape[1] :] = jnp.zeros((marks.shape[0], width - marks.shape[1]), BF)


def pack_rows_call(tokens_t, plan):
    width, rows = tokens_t.shape
    return pl.pallas_call(
        pack_rows_kernel,
        name="pack_rows",
        out_shape=shaped((rows + plan.shape[0], width), BF),
        in_specs=[vm()] * 2,
        out_specs=vm(),
        compiler_params=params(8),
        cost_estimate=estimate(),
    )(*apart([tokens_t, plan]))


def stack_kernel(*refs):
    out_ref = refs[-1]
    at = 0
    for ref in refs[:-1]:
        out_ref[at : at + ref.shape[0], :] = ref[...]
        at += ref.shape[0]


def stack_call(pieces):
    rows = sum(p.shape[0] for p in pieces)
    return pl.pallas_call(
        stack_kernel,
        name="stack",
        out_shape=shaped((rows, pieces[0].shape[1]), pieces[0].dtype),
        in_specs=[vm()] * len(pieces),
        out_specs=vm(),
        compiler_params=params(8),
        cost_estimate=estimate(),
    )(*pieces)


def split_kernel(total_ref, other_ref, *outs):
    rows = outs[0].shape[0]
    for i, out in enumerate(outs):
        at = slice(i * rows, (i + 1) * rows)
        out[...] = (total_ref[at, :] + other_ref[at, :].astype(F32)).astype(out.dtype)


def split_call(total, other):
    rows, width = total.shape[0] // len(NEAR), total.shape[1]
    outs = [shaped((rows, width), F32)] + [shaped((rows, width), BF)] * (len(NEAR) - 1)
    return pl.pallas_call(
        split_kernel,
        name="split",
        out_shape=tuple(outs),
        in_specs=[vm(), vm()],
        out_specs=tuple(vm() for _ in outs),
        compiler_params=params(10),
        cost_estimate=estimate(),
    )(total, other)


def project(x, gain, wqkv_ref, cosine, sine, first_ref, q_ref, kv_ref):
    normed, _ = normed_rows(x)
    first_in = (normed * gain).astype(BF)
    first_ref[...] = first_in
    rows = mm(first_in, wqkv_ref[...])
    wide = SHARE * HEAD_SIZE
    q_width = KEY_VALUE_HEADS * wide
    kv_width = KEY_VALUE_HEADS * HEAD_SIZE
    key = turn(rows[:, q_width : q_width + kv_width], cosine, sine)
    value = rows[:, q_width + kv_width : q_width + 2 * kv_width]
    for h in range(KEY_VALUE_HEADS):
        at = slice(h * HEAD_SIZE, (h + 1) * HEAD_SIZE)
        kv_ref[:, h * 128 : (h + 1) * 128] = jnp.concatenate(
            [key[:, at], value[:, at]], axis=1
        ).astype(BF)
    query = (turn(rows[:, :q_width], cosine, sine).astype(BF) * SCALE).astype(BF)
    for h in range(KEY_VALUE_HEADS):
        q_ref[h] = query[:, h * wide : (h + 1) * wide]


def first_kernel(near, weights, coords_ref, x_ref, gain_ref, cos_ref, sin_ref, *rest):
    count = len(arrays_of(weights))
    refs, (first_ref, q_ref, kv_ref, *scratch) = rest[:count], rest[count:]
    (wqkv,), wait = weights_here(near, weights, refs, scratch, coords_ref, ((0, 0),))
    wait(0)
    project(
        x_ref[...].astype(F32), gain_ref[...], wqkv, cos_ref[...], sin_ref[...],
        first_ref, q_ref, kv_ref,
    )


def first_call(near, coords, tokens, gain, cosine, sine, weights):
    rows, width = tokens.shape
    specs, arrays, scratch = weights_in(near, weights)
    return pl.pallas_call(
        functools.partial(first_kernel, near, weights),
        name="first_projection",
        out_shape=(
            stored((rows, width), BF),
            shaped((KEY_VALUE_HEADS, rows, SHARE * HEAD_SIZE), BF),
            shaped((rows, KEY_VALUE_HEADS * 128), BF),
        ),
        in_specs=[sm()] + [vm()] * 4 + specs,
        out_specs=(vm(), vm(), vm()),
        scratch_shapes=scratch,
        compiler_params=params(10),
        cost_estimate=estimate(),
    )(coords, tokens, gain, cosine, sine, *arrays)


def padded_heads(wide_rows, left):
    rows = wide_rows.shape[0]
    blank = jnp.zeros((rows, HEAD_SIZE), wide_rows.dtype)
    stacked = []
    for j in range(SHARE):
        part = wide_rows[:, j * HEAD_SIZE : (j + 1) * HEAD_SIZE]
        stacked.append(jnp.concatenate([part, blank] if left else [blank, part], axis=1))
    return jnp.concatenate(stacked, axis=0)


def fill_bias(prompt, kpos_ref, live_ref, qpos_ref, bias_scr, col_scr):
    kpos = kpos_ref[...]
    klive = live_ref[...] > 0
    rows = bias_scr.shape[0]
    square = lambda axis: lax.broadcasted_iota(jnp.int32, (rows, rows), axis)
    own = jnp.where(square(0) == square(1), qpos_ref[...].astype(F32), 0.0)
    col_scr[...] = jnp.sum(own, axis=1, keepdims=True).astype(jnp.int32)
    kseg = jnp.where(kpos < prompt, 0, 1 + ((kpos - prompt) >> CONT_BITS))

    def fill(i, carry):
        at = pl.ds(pl.multiple_of(i * 8, 8), 8)
        qpos = col_scr[at, :]
        qseg = jnp.where(qpos < prompt, 0, 1 + ((qpos - prompt) >> CONT_BITS))
        earlier = kpos <= qpos
        shared = (kseg == 0) | (kseg == qseg)
        seen = earlier & shared & (klive | (kpos == qpos))
        bias_scr[at, :] = jnp.where(seen, 0.0, MASK_FLOOR)
        return carry

    lax.fori_loop(0, bias_scr.shape[0] // 8, fill, 0)


def attend_kernel(prompt, q_ref, a_ref, b_ref, kpos_ref, live_ref, qpos_ref, p_ref, o_ref, bias_scr, col_scr):
    @pl.when(pl.program_id(0) == 0)
    def _():
        fill_bias(prompt, kpos_ref, live_ref, qpos_ref, bias_scr, col_scr)

    o_ref[0] = attend_heads(q_ref, a_ref, b_ref, p_ref, bias_scr)


def attend_heads(q_ref, a_ref, b_ref, p_ref, bias_scr):
    rows = q_ref.shape[1]
    half = a_ref.shape[0]
    together = rows < 128
    if together:
        stacked = padded_heads(q_ref[0], True)
        all_a, all_b = mm(stacked, a_ref[...], NT), mm(stacked, b_ref[...], NT)
    blank = jnp.zeros((rows, HEAD_SIZE), BF)
    outs = []
    for j in range(SHARE):
        at = slice(j * rows, (j + 1) * rows)
        if together:
            s_a, s_b = all_a[at], all_b[at]
        else:
            part = jnp.concatenate([q_ref[0, :, j * HEAD_SIZE : (j + 1) * HEAD_SIZE], blank], axis=1)
            s_a, s_b = mm(part, a_ref[...], NT), mm(part, b_ref[...], NT)
        s_a = s_a + bias_scr[:, :half]
        s_b = s_b + bias_scr[:, half:]
        top = jnp.maximum(
            jnp.max(s_a, axis=-1, keepdims=True), jnp.max(s_b, axis=-1, keepdims=True)
        )
        w_a, w_b = jnp.exp(s_a - top), jnp.exp(s_b - top)
        mass = jnp.sum(w_a, axis=-1, keepdims=True) + jnp.sum(w_b, axis=-1, keepdims=True)
        inverse = 1.0 / mass
        p_a, p_b = (w_a * inverse).astype(BF), (w_b * inverse).astype(BF)
        p_ref[0, at, :half] = p_a
        p_ref[0, at, half:] = p_b
        if not together:
            outs.append((mm(p_a, a_ref[...]) + mm(p_b, b_ref[...]))[:, HEAD_SIZE:])
    if together:
        mixed = mm(p_ref[0, :, :half], a_ref[...]) + mm(p_ref[0, :, half:], b_ref[...])
        outs = [mixed[j * rows : (j + 1) * rows, HEAD_SIZE:] for j in range(SHARE)]
    return jnp.concatenate(outs, axis=1).astype(BF)


def attend_call(query, part_a, part_b, kpos, klive, qpos, prompt):
    heads, rows, wide = query.shape
    half = part_a.shape[0]
    keys = 2 * half
    return pl.pallas_call(
        functools.partial(attend_kernel, prompt),
        name="attend",
        grid=(heads,),
        out_shape=(stored((heads, SHARE * rows, keys), BF), shaped((heads, rows, wide), BF)),
        in_specs=[
            pl.BlockSpec((1, rows, wide), lambda h: (h, 0, 0)),
            pl.BlockSpec((half, 128), lambda h: (0, h)),
            pl.BlockSpec((half, 128), lambda h: (0, h)),
            pl.BlockSpec((1, keys), lambda h: (0, 0)),
            pl.BlockSpec((1, keys), lambda h: (0, 0)),
            pl.BlockSpec((1, rows), lambda h: (0, 0)),
        ],
        out_specs=(
            pl.BlockSpec((1, SHARE * rows, keys), lambda h: (h, 0, 0)),
            pl.BlockSpec((1, rows, wide), lambda h: (h, 0, 0)),
        ),
        scratch_shapes=[pltpu.VMEM((rows, keys), F32), pltpu.VMEM((rows, 1), jnp.int32)],
        compiler_params=params(12 if keys <= 2048 else 56, dimension_semantics=("arbitrary",)),
        cost_estimate=estimate(rows * keys / 17000),
    )(query, part_a, part_b, kpos, klive, qpos)


def attend_back_kernel(q_ref, do_ref, a_ref, b_ref, p_ref, dq_ref, da_ref, db_ref, dp_scr, ds_scr):
    rows = q_ref.shape[1]
    half = a_ref.shape[0]
    stacked = padded_heads(q_ref[0], True)
    grads = padded_heads(do_ref[0], False)
    dp_scr[:, :half] = mm(grads, a_ref[...], NT)
    dp_scr[:, half:] = mm(grads, b_ref[...], NT)

    for j in range(SHARE):
        at = slice(j * rows, (j + 1) * rows)
        weights = p_ref[0, at, :].astype(F32)
        dp = dp_scr[at, :]
        delta = jnp.sum(weights * dp, axis=-1, keepdims=True)
        ds_scr[at, :] = (weights * (dp - delta)).astype(BF)
    dq = (mm(ds_scr[:, :half], a_ref[...]) + mm(ds_scr[:, half:], b_ref[...])) * SCALE
    dq_ref[0] = jnp.concatenate(
        [dq[j * rows : (j + 1) * rows, :HEAD_SIZE] for j in range(SHARE)], axis=1
    )
    for at, out in ((slice(0, half), da_ref), (slice(half, 2 * half), db_ref)):
        turned = mm(stacked, ds_scr[:, at], TN) + mm(grads, p_ref[0, :, at], TN)
        out[...] = turned.T.astype(out.dtype)


def attend_back_call(query, d_out, part_a, part_b, weights):
    heads, rows, wide = query.shape
    half = part_a.shape[0]
    keys = 2 * half
    return pl.pallas_call(
        attend_back_kernel,
        name="attend_back",
        grid=(heads,),
        out_shape=(
            shaped((heads, rows, wide), F32),
            shaped((half, heads * 128), F32),
            shaped((half, heads * 128), BF),
        ),
        in_specs=[
            pl.BlockSpec((1, rows, wide), lambda h: (h, 0, 0)),
            pl.BlockSpec((1, rows, wide), lambda h: (h, 0, 0)),
            pl.BlockSpec((half, 128), lambda h: (0, h)),
            pl.BlockSpec((half, 128), lambda h: (0, h)),
            pl.BlockSpec((1, SHARE * rows, keys), lambda h: (h, 0, 0)),
        ],
        out_specs=(
            pl.BlockSpec((1, rows, wide), lambda h: (h, 0, 0)),
            pl.BlockSpec((half, 128), lambda h: (0, h)),
            pl.BlockSpec((half, 128), lambda h: (0, h)),
        ),
        scratch_shapes=[
            pltpu.VMEM((SHARE * rows, keys), F32),
            pltpu.VMEM((SHARE * rows, keys), BF),
        ],
        compiler_params=params(14 if keys <= 2048 else 60, dimension_semantics=("arbitrary",)),
        cost_estimate=estimate(rows * keys / 22000),
    )(query, d_out, part_a, part_b, *apart([weights]))


def picks(sel_ref, total_rows):
    capacity = sel_ref.shape[1]
    row = lax.broadcasted_iota(jnp.int32, (total_rows, capacity), 0)
    return row == sel_ref[...]


def live_column(live_ref, rows):
    count = jnp.sum(live_ref[:, :].astype(F32), axis=1, keepdims=True)
    return lax.broadcasted_iota(jnp.int32, (rows, 1), 0).astype(F32) < count


def feed_forward(wait, x, mixed, gain_two, wo, wg, wu, wd, ao_out, mid_ref, second_ref, g_ref, u_ref, hid_ref):
    ao_out[...] = mixed
    wait(0)
    middle = x + mm(mixed, wo[...])
    mid_ref[...] = middle
    normed, _ = normed_rows(middle)
    second = (normed * gain_two).astype(BF)
    second_ref[...] = second
    wide = wg.shape[1] // FF_CHUNKS
    for j in range(FF_CHUNKS):
        at = slice(j * wide, (j + 1) * wide)
        wait(1, j)
        g = mm(second, wg[:, at])
        wait(2, j)
        u = mm(second, wu[:, at])
        g_ref[:, at] = g.astype(BF)
        u_ref[:, at] = u.astype(BF)
        hid_ref[:, at] = (g / (1.0 + jnp.exp(-g)) * u).astype(BF)
    wait(3)
    return middle + mm(hid_ref[...], wd[...], NT)


DENSE_TURNS = ((0, 0),) + tuple((w, j) for j in range(FF_CHUNKS) for w in (1, 2)) + ((3, 0),)


def dense_body(near, step, weights, mixed, args):
    args = list(args)
    take = lambda k: [args.pop(0) for _ in range(k)]
    coords_ref, x_ref, gain1_ref, gain2_ref = take(4)
    if step == 0:
        sel_ref, cos_ref, sin_ref = take(3)
    elif step == 1:
        live_ref, cos_ref, sin_ref = take(3)
    else:
        sel_ref, live2_ref, live_ref, h1_ref, h2_ref = take(5)
    refs = take(len(arrays_of(weights)))
    ao_out, mid_ref, second_ref, g_ref, u_ref, hid_ref = take(6)
    if step < 2:
        h_ref, next_ref, first_ref, q_ref, kv_ref = take(5)
    else:
        (out_ref,) = take(1)
    turns = DENSE_TURNS + (((4, 0),) if step < 2 else ())

    def work():
        buffers, wait = weights_here(near, weights, refs, args, coords_ref, turns)
        rows = x_ref.shape[0]
        x = x_ref[...].astype(F32)
        updated = feed_forward(
            wait, x, mixed(), gain2_ref[...], *buffers[:4], ao_out, mid_ref,
            second_ref, g_ref, u_ref, hid_ref,
        )
        if step == 0:
            h_ref[...] = updated
            chosen = picks(sel_ref, rows).astype(F32)
            following = mm(chosen, updated, TN, lax.Precision.HIGHEST)
        else:
            updated = jnp.where(live_column(live_ref, rows), updated, x)
        if step == 1:
            h_ref[...] = updated
            following = updated[: next_ref.shape[0]]
        if step < 2:
            next_ref[...] = following
            wait(4)
            project(
                following, gain1_ref[...], buffers[4], cos_ref[...], sin_ref[...],
                first_ref, q_ref, kv_ref,
            )
        else:
            slots = jnp.concatenate([updated, h2_ref[rows:, :]], axis=0).astype(BF)
            hit = picks(sel_ref, h1_ref.shape[0]) & (live2_ref[...] > 0)
            placed = mm(hit.astype(BF), slots)
            any_hit = jnp.sum(hit.astype(F32), axis=1, keepdims=True) > 0.5
            out_ref[...] = jnp.where(any_hit, placed, h1_ref[...]).T.astype(BF)

    return work


def joined_heads(ao_ref):
    return jnp.concatenate([ao_ref[h] for h in range(KEY_VALUE_HEADS)], axis=1)


def dense_kernel(near, step, weights, ao_ref, *args):
    dense_body(near, step, weights, lambda: joined_heads(ao_ref), args)()


def dense_outs(step, x, weights, next_rows):
    rows, width = x.shape
    hidden = weights[1].shape[1]
    outs = [
        stored((rows, width), BF),
        stored((rows, width), F32),
        stored((rows, width), BF),
        stored((rows, hidden), BF),
        stored((rows, hidden), BF),
        stored((rows, hidden), BF),
    ]
    if step < 2:
        outs += [
            stored((rows, width), F32),
            shaped((next_rows, width), F32),
            stored((next_rows, width), BF),
            shaped((KEY_VALUE_HEADS, next_rows, SHARE * HEAD_SIZE), BF),
            shaped((next_rows, KEY_VALUE_HEADS * 128), BF),
        ]
    else:
        outs += [stored((width, next_rows), BF)]
    return outs


def dense_call(near, step, coords, x, mixed, gain1, gain2, extra, weights, next_rows):
    specs, arrays, scratch = weights_in(near, weights)
    outs = dense_outs(step, x, weights, next_rows)
    return pl.pallas_call(
        functools.partial(dense_kernel, near, step, weights),
        name=f"dense_{step}",
        out_shape=tuple(outs),
        in_specs=[vm(), sm()] + [vm()] * (3 + len(extra)) + specs,
        out_specs=tuple(vm() for _ in outs),
        scratch_shapes=scratch,
        compiler_params=params(12 if near else 50),
        cost_estimate=estimate(6),
    )(mixed, coords, x, gain1, gain2, *extra, *arrays)


def feed_back(wait, first, d_y, mid_ref, g_ref, u_ref, gain_two, wd, wg, wu, wo, dyb_ref, dg_ref, du_ref, dmid_ref, dz_ref, dao_ref, sum_ref):
    d_low = d_y.astype(BF)
    dyb_ref[...] = d_low
    wide = wg.shape[1] // FF_CHUNKS
    d_second = jnp.zeros(d_y.shape, F32)
    wait(first)
    for j in range(FF_CHUNKS):
        at = slice(j * wide, (j + 1) * wide)
        d_hidden = mm(d_low, wd[:, at])
        g, u = g_ref[:, at].astype(F32), u_ref[:, at].astype(F32)
        sigma = 1.0 / (1.0 + jnp.exp(-g))
        d_gate = (d_hidden * u * sigma * (1.0 + g * (1.0 - sigma))).astype(BF)
        d_up = (d_hidden * (g * sigma)).astype(BF)
        dg_ref[:, at] = d_gate
        du_ref[:, at] = d_up
        wait(first + 1, j)
        wait(first + 2, j)
        d_second += mm(d_gate, wg[:, at], NT) + mm(d_up, wu[:, at], NT)
    normed, inverse = normed_rows(mid_ref[...])
    sum_ref[...] = jnp.sum(d_second * normed, axis=0, keepdims=True)
    d_mid = norm_back(d_second, normed, inverse, gain_two) + d_y
    dmid_ref[...] = d_mid
    d_low = d_mid.astype(BF)
    dz_ref[...] = d_low
    wait(first + 3)
    d_mixed = mm(d_low, wo[...], NT).astype(BF)
    wide = SHARE * HEAD_SIZE
    for h in range(KEY_VALUE_HEADS):
        dao_ref[h] = d_mixed[:, h * wide : (h + 1) * wide]


def project_back(own_ref, others, dq_ref, x, dmid_ref, gain_one, cosine, sine, wait, wqkv, dqkv_ref, sum_ref):
    total = own_ref[...].astype(F32)
    for other in others:
        total = total + other[...].astype(F32)
    d_key = jnp.concatenate(
        [total[:, h * 128 : h * 128 + HEAD_SIZE] for h in range(KEY_VALUE_HEADS)], axis=1
    )
    d_value = jnp.concatenate(
        [total[:, h * 128 + HEAD_SIZE : (h + 1) * 128] for h in range(KEY_VALUE_HEADS)], axis=1
    )
    d_query = jnp.concatenate([dq_ref[h] for h in range(KEY_VALUE_HEADS)], axis=1)
    d_rows = jnp.concatenate(
        [turn(d_query, cosine, sine, True), turn(d_key, cosine, sine, True), d_value], axis=1
    ).astype(BF)
    dqkv_ref[...] = d_rows
    wait(0)
    d_first = mm(d_rows, wqkv[:, : d_rows.shape[1]], NT)
    normed, inverse = normed_rows(x)
    sum_ref[...] = jnp.sum(d_first * normed, axis=0, keepdims=True)
    return norm_back(d_first, normed, inverse, gain_one) + dmid_ref[...]


def back_kernel(near, phase, weights, n_parts, *args):
    args = list(args)
    take = lambda k: [args.pop(0) for _ in range(k)]
    (coords_ref,) = take(1)
    if phase > 0:
        gain1_ref, cos_ref, sin_ref, x_ref, dmid_in, dq_ref = take(6)
        own_ref, *others = take(n_parts)
    if phase < 3:
        gain2_ref, mid_ref, g_ref, u_ref = take(4)
    if phase == 0:
        cot_ref, sel_ref, live3_ref = take(3)
    elif phase == 1:
        slots_ref, live3_ref, live2_ref = take(3)
    elif phase == 2:
        cot_ref, sel_ref, live2_ref = take(3)
    refs = take(len(arrays_of(weights)))
    if phase > 0:
        dqkv_ref, sum1_ref = take(2)
    if phase < 3:
        outs = take(7)
    if phase == 0:
        (slots_out,) = take(1)
    elif phase == 3:
        (grad_ref,) = take(1)
    turns = ((0, 0),) if phase > 0 else ()
    first = len(turns)
    if phase < 3:
        turns += ((first, 0),)
        turns += tuple((first + w, j) for j in range(FF_CHUNKS) for w in (1, 2))
        turns += ((first + 3, 0),)
    buffers, wait = weights_here(near, weights, refs, args, coords_ref, turns)
    if phase > 0:
        d_x = project_back(
            own_ref, others, dq_ref, x_ref[...].astype(F32), dmid_in, gain1_ref[...],
            cos_ref[...], sin_ref[...], wait, buffers[0], dqkv_ref, sum1_ref,
        )
    if phase == 0:
        chosen = picks(sel_ref, cot_ref.shape[1]).astype(BF)
        slots = mm(chosen, cot_ref[...].T, TN)
        slots_out[...] = slots
        rows = mid_ref.shape[0]
        d_y = jnp.where(live_column(live3_ref, rows), slots[:rows], 0.0)
    elif phase == 1:
        rows = x_ref.shape[0]
        slots = slots_ref[...]
        head = jnp.where(live_column(live3_ref, rows), d_x, slots[:rows])
        slots = jnp.concatenate([head, slots[rows:]], axis=0)
        d_y = jnp.where(live_column(live2_ref, slots.shape[0]), slots, 0.0)
    elif phase == 2:
        hit = picks(sel_ref, cot_ref.shape[1]) & (live2_ref[...] > 0)
        placed = mm(hit.astype(F32), d_x, NN, lax.Precision.HIGHEST)
        any_hit = jnp.sum(hit.astype(F32), axis=1, keepdims=True) > 0.5
        d_y = jnp.where(any_hit, placed, cot_ref[...].astype(F32).T)
    else:
        grad_ref[...] = d_x.T.astype(BF)
        return
    feed_back(
        wait, first, d_y, mid_ref, g_ref, u_ref, gain2_ref[...],
        *buffers[first : first + 4], *outs,
    )


def back_call(near, phase, coords, before, parts, into, extra, weights, rows_next):
    specs, arrays, scratch = weights_in(near, weights)
    ins = list(before) + list(parts) + list(into) + list(extra)
    outs = []
    if phase > 0:
        rows, width = before[3].shape
        qkv_width = width + 2 * KEY_VALUE_HEADS * HEAD_SIZE
        outs += [stored((rows, qkv_width), BF), stored((1, width), F32)]
    if phase < 3:
        rows, hidden = into[2].shape
        width = into[1].shape[1]
        outs += [
            stored((rows, width), BF),
            stored((rows, hidden), BF),
            stored((rows, hidden), BF),
            stored((rows, width), F32),
            stored((rows, width), BF),
            shaped((KEY_VALUE_HEADS, rows, SHARE * HEAD_SIZE), BF),
            stored((1, width), F32),
        ]
    if phase == 0:
        outs += [stored((rows_next, width), F32)]
    elif phase == 3:
        outs += [stored((width, rows), BF)]
    return pl.pallas_call(
        functools.partial(back_kernel, near, phase, weights, len(parts)),
        name=f"back_{phase}",
        out_shape=tuple(outs),
        in_specs=[sm()] + [vm()] * len(ins) + specs,
        out_specs=tuple(vm() for _ in outs),
        scratch_shapes=scratch,
        compiler_params=params(12 if near else 50),
        cost_estimate=estimate(6),
    )(coords, *before, *parts, *into[:1], *apart(into[1:]), *extra, *arrays)


def stack_rows(refs, scratch):
    at = 0
    for ref in refs:
        scratch[at : at + ref.shape[0], :] = ref[...]
        at += ref.shape[0]


def put_blocks(value, x_of, coords, ref, per_row):
    y, _, x, z = coords
    depth = ref.shape[-2]
    for ya in range(2):
        for xa in range(2) if per_row else (None,):
            for za in range(4):
                row = (ya * (2 if per_row else 1) + (xa or 0)) * 4 + za
                ref[y ^ ya, (x ^ xa) if per_row else x_of, z ^ za] = value[
                    row * depth : (row + 1) * depth
                ].astype(BF)


def grad_cols_kernel(n_steps, coords_ref, *args):
    left, args = args[:n_steps], args[n_steps:]
    right, args = args[:n_steps], args[n_steps:]
    keep_ref, send_ref, l_scr, r_scr = args
    coords = read_coords(coords_ref)
    _, c, x, _ = coords
    stack_rows(left, l_scr)
    stack_rows(right, r_scr)
    block = keep_ref.shape[-1]
    for far, ref in ((1, send_ref), (0, keep_ref)):

        def body(rx, carry, far=far, ref=ref):
            start = pl.multiple_of(((c ^ far) * 2 + (x ^ rx)) * block, 128)
            value = mm(l_scr[...], r_scr[:, pl.ds(start, block)], TN)
            put_blocks(value, rx, coords, ref, False)
            return carry

        lax.fori_loop(0, 2, body, 0)


def grad_rows_kernel(n_steps, coords_ref, *args):
    left, args = args[:n_steps], args[n_steps:]
    right, args = args[:n_steps], args[n_steps:]
    keep_ref, send_ref, l_scr, r_scr = args
    coords = read_coords(coords_ref)
    y, c, x, z = coords
    stack_rows(left, l_scr)
    stack_rows(right, r_scr)
    depth = keep_ref.shape[-2]
    span = 8 * depth
    for far, ref in ((1, send_ref), (0, keep_ref)):

        def body(ry, carry, far=far, ref=ref):
            start = pl.multiple_of(((y ^ ry) * 2 + (c ^ far)) * span, 128)
            value = mm(l_scr[:, pl.ds(start, span)], r_scr[...], TN)
            for xa in range(2):
                for za in range(4):
                    row = (xa * 4 + za) * depth
                    ref[ry, x ^ xa, z ^ za] = value[row : row + depth].astype(BF)
            return carry

        lax.fori_loop(0, 2, body, 0)


def grad_mixed_kernel(n_steps, coords_ref, *args):
    groups = []
    for _ in range(4):
        groups.append(args[:n_steps])
        args = args[n_steps:]
    keep_ref, send_ref, first_scr, mixed_scr, qkv_scr, z_scr, val_scr = args
    coords = read_coords(coords_ref)
    _, c, x, _ = coords
    for refs, scr in zip(groups, (first_scr, mixed_scr, qkv_scr, z_scr), strict=True):
        stack_rows(refs, scr)
    block = keep_ref.shape[-1]
    width = z_scr.shape[1]
    kv_width = (qkv_scr.shape[1] - width) // 2
    for ca in range(2):
        for xa in range(2):
            if ca == 0:
                val_scr[...] = mm(first_scr[...], qkv_scr[:, xa * block : (xa + 1) * block], TN)
            elif xa == 0:
                val_scr[...] = mm(mixed_scr[...], z_scr[:, :block], TN)
            else:
                val_scr[...] = jnp.concatenate(
                    [
                        mm(mixed_scr[...], z_scr[:, block:], TN),
                        mm(first_scr[...], qkv_scr[:, width + kv_width :], TN),
                    ],
                    axis=1,
                )

            @pl.when(c == ca)
            def _(xa=xa):
                put_blocks(val_scr[...], x ^ xa, coords, keep_ref, False)

            @pl.when(c != ca)
            def _(xa=xa):
                put_blocks(val_scr[...], x ^ xa, coords, send_ref, False)


def grad_call(kind, coords, groups):
    n_steps = len(groups[0])
    rows = sum(a.shape[0] for a in groups[0])
    width, cols = groups[0][0].shape[1], groups[1][0].shape[1]
    scratch = [pltpu.VMEM((rows, g[0].shape[1]), BF) for g in groups]
    if kind == "rows":
        kernel, block = grad_rows_kernel, (width // 32, cols)
    elif kind == "cols":
        kernel, block = grad_cols_kernel, (width // 8, cols // 4)
    else:
        total = sum(g[0].shape[1] for g in groups[2:])
        kernel, block = grad_mixed_kernel, (width // 8, total // 4)
        scratch += [pltpu.VMEM((width, block[1]), F32)]
    out = shaped((2, 2, 4) + block, BF)
    ins = [a for g in groups for a in g]
    return pl.pallas_call(
        functools.partial(kernel, n_steps),
        name=f"grad_{kind}",
        out_shape=(out, out),
        in_specs=[sm()] + [vm()] * len(ins),
        out_specs=(vm(), vm()),
        scratch_shapes=scratch,
        compiler_params=params(16),
        cost_estimate=estimate(6),
    )(coords, *apart(ins))


def place_cols_kernel(coords_ref, near_ref, far_ref, *outs):
    _, c, x, _ = read_coords(coords_ref)
    block = near_ref.shape[-1]
    mixed = len(outs) > 1
    target = outs[4] if mixed else outs[0]
    for far, ref in ((0, near_ref), (1, far_ref)):
        for rx in range(2):
            cols = pl.ds(pl.multiple_of(((c ^ far) * 2 + (x ^ rx)) * block, 128), block)
            target[:, cols] = ref[rx, 0].astype(F32)
    if mixed:
        q_ref, k_ref, o_ref, v_ref, _, k_scr, v_scr = outs
        width, kv_width = q_ref.shape[1], k_ref.shape[0]
        depth = q_ref.shape[0]
        rows = pl.ds(pl.multiple_of((coords_ref[3] ^ pl.program_id(0)) * depth, 8), depth)
        q_ref[...] = target[:, :width]
        k_scr[rows, :] = target[:, width : width + kv_width]
        o_ref[...] = target[:, width + kv_width : 2 * width + kv_width]
        v_scr[rows, :] = target[:, 2 * width + kv_width :]

        @pl.when(pl.program_id(0) == 3)
        def _():
            k_ref[...] = k_scr[...].T
            v_ref[...] = v_scr[...].T


def place_rows_kernel(coords_ref, near_ref, far_ref, out_ref, scr):
    _, _, x, z = read_coords(coords_ref)
    depth = near_ref.shape[-2]

    def put(ref):
        for rx in range(2):
            for rz in range(4):
                row = pl.multiple_of(((x ^ rx) * 4 + (z ^ rz)) * depth, 8)
                scr[pl.ds(row, depth), :] = ref[rx, rz].astype(F32)

    @pl.when(pl.program_id(0) == 0)
    def _():
        put(near_ref)

    @pl.when(pl.program_id(0) == 1)
    def _():
        put(far_ref)

    out_ref[...] = scr[...].T


def place_call(kind, coords, near, far, widths):
    depth, block = near.shape[-2:]
    scratch = []
    if kind == "rows":
        kernel, grid = place_rows_kernel, (2,)
        outs = (stored((block, 16 * depth), F32),)
        source = pl.BlockSpec((2, 4, depth, block), lambda f, k: (0, 0, 0, 0))
        targets = (pl.BlockSpec((block, 8 * depth), lambda f, k: (0, k[1] ^ f)),)
        scratch = [pltpu.VMEM((8 * depth, block), F32)]
    else:
        kernel, grid = place_cols_kernel, (4,)
        source = pl.BlockSpec((2, 1, depth, block), lambda i, k: (0, i, 0, 0))
        straight = lambda w: (
            stored((4 * depth, w), F32), pl.BlockSpec((depth, w), lambda i, k: (k[3] ^ i, 0))
        )
        turned = lambda w: (
            stored((w, 4 * depth), F32), pl.BlockSpec((w, 4 * depth), lambda i, k: (0, 0))
        )
        outs, targets = zip(
            *((turned if i % 2 else straight)(w) for i, w in enumerate(widths)), strict=True
        )
        if len(outs) > 1:
            scratch = [pltpu.VMEM((depth, 4 * block), F32)]
            scratch += [pltpu.VMEM((4 * depth, w), F32) for w in widths[1::2]]
    return pl.pallas_call(
        kernel,
        name=f"place_{kind}",
        grid_spec=pltpu.PrefetchScalarGridSpec(
            num_scalar_prefetch=1,
            grid=grid,
            in_specs=[source, source],
            out_specs=targets,
            scratch_shapes=scratch,
        ),
        out_shape=outs,
        compiler_params=params(12),
        cost_estimate=estimate(),
    )(coords, near, far)


def low_sum(left, right):
    return (left.astype(F32) + right.astype(F32)).astype(BF)


def split_list(values, count):
    return values[:count], values[count:]


def gather_keys(kv, order, near, beside=((), ()), meanwhile=([], [])):
    if not near:
        whole = lax.all_gather(kv, "ctx", axis=0, tiled=True)
        half = whole.shape[0] // 2
        return whole[:half], whole[half:]
    kv = order.take(kv)
    hops = [hop(kv, m) for m in (X_BIT, Y_BIT, Z1_BIT, X_BIT | Y_BIT | Z1_BIT)]
    for start in beside[0]:
        start()
    (by_x, by_y, by_z, across), meanwhile[0][:] = split_list(order.all(*hops, *meanwhile[0]), 4)
    hops = [hop(by_x, Y_BIT), hop(by_y, Z1_BIT), hop(by_z, X_BIT)]
    for start in beside[1]:
        start()
    hops, meanwhile[1][:] = split_list(order.all(*hops, *meanwhile[1]), 3)
    part = stack_call([kv, by_x, by_y, by_z, across, *hops])
    return part, order.take(hop(part, C_BIT))


class KeySums:
    def __init__(self, own, others):
        self.own, self.others = own, others

    def sends(self, turn):
        return list(zip(self.others, NEAR[1:], strict=True))

    def got(self, turn, values):
        self.result = [self.own, *values]


class Hop:
    def __init__(self, value, mask):
        self.value, self.mask = value, mask

    def sends(self, turn):
        return [(self.value, self.mask)]

    def got(self, turn, values):
        (self.result,) = values


def scatter_keys(part_a, part_b, order, near):
    if not near:
        whole = jnp.concatenate([part_a, part_b.astype(F32)], axis=0)
        return [lax.psum_scatter(whole, "ctx", scatter_dimension=0, tiled=True)]
    far = Hop(part_b, C_BIT)
    (part_a,) = wave(order, [(far, 0)], lambda a: (a,), (part_a,))
    own, *others = split_call(part_a, far.result)
    sums = KeySums(own, others)
    wave(order, [(sums, 0)])
    return sums.result


def cut_rows(value, index, count):
    size = value.shape[0] // count
    return lax.dynamic_slice_in_dim(value, index * size, size, 0)


def cut_cols(value, index, count):
    size = value.shape[1] // count
    return lax.dynamic_slice_in_dim(value, index * size, size, 1)


def spread(mine):
    return mine, hop(mine, X_BIT), hop(mine, Z1_BIT), hop(mine, X_BIT | Z1_BIT)


def pair_sum(keep, send, near):
    if near:
        return low_sum(keep, hop(send, C_BIT))
    return lax.psum(jnp.stack([keep, send]).astype(F32), AXES)


ALONG_Z = (Z1_BIT, Z2_BIT, Z1_BIT | Z2_BIT)
FAR_FIRST = (2, 1, 0)


class BlockSums:
    rounds = 6

    def __init__(self, total):
        self.total = total

    def sends(self, turn):
        if turn == 0:
            return [(self.total[1, 1], Y_BIT)]
        if turn == 1:
            return [(self.total[1, 0], Y_BIT), (low_sum(self.total[0, 1], self.came), X_BIT)]
        if turn == 2:
            return [(self.total[i + 1], ALONG_Z[i]) for i in FAR_FIRST]
        if turn == 3:
            return [(self.mine, ALONG_Z[i]) for i in FAR_FIRST]
        if turn == 4:
            return [(self.total, X_BIT)]
        return [(self.total, C_BIT)]

    def got(self, turn, values):
        if turn == 0:
            (self.came,) = values
        elif turn == 1:
            total = self.total[0, 0].astype(F32)
            for value in values:
                total = total + value.astype(F32)
            self.total = total.astype(BF)
        elif turn == 2:
            mine = self.total[0].astype(F32)
            for value in values:
                mine = mine + value.astype(F32)
            self.mine = mine.astype(BF)
        elif turn == 3:
            self.total = jnp.stack([self.mine, *values[::-1]])
        elif turn == 4:
            self.total = jnp.stack([self.total, *values])
        else:
            self.result = (self.total, *values)


class RunningSum:
    rounds = 5

    def __init__(self, value):
        self.result = value

    def sends(self, turn):
        return [(self.result, (X_BIT, C_BIT, Y_BIT, Z1_BIT, Z2_BIT)[turn])]

    def got(self, turn, values):
        self.result = self.result + values[0]


class Move:
    rounds = 1

    def __init__(self, value):
        self.value = value

    def sends(self, turn):
        return [(self.value, None)]

    def got(self, turn, values):
        (self.result,) = values


def wave(order, steps, work=None, uses=()):
    plans = [chain.sends(turn) for chain, turn in steps]
    flat = [value for plan in plans for value, _ in plan]
    taken = order.all(*flat, *uses)
    sent, uses = taken[: len(flat)], taken[len(flat) :]
    masks = [mask for plan in plans for _, mask in plan]
    came = [move(v) if mask is None else hop(v, mask) for v, mask in zip(sent, masks, strict=True)]
    made = list(work(*uses)) if work else []
    came = order.all(*came, *made)
    came, made = came[: len(flat)], came[len(flat) :]
    for (chain, turn), plan in zip(steps, plans, strict=True):
        chain.got(turn, came[: len(plan)])
        came = came[len(plan) :]
    return made


def on_device(
    tokens, cotangent, w_query, key_weight, value_weight, w_out, w_gate, w_up, w_down,
    gain_attn, gain_ffn, block_order, sel_mid, live_mid, sel_last, live_last,
):
    ctx_count, ws_count = lax.axis_size("ctx"), lax.axis_size("ws")
    near = ctx_count == 16 and ws_count == 2
    ctx, y = lax.axis_index("ctx"), lax.axis_index("ws")
    tok_local = tokens.shape[1]
    cap_mid, cap_last = sel_mid.shape[1] // ctx_count, sel_last.shape[1] // ctx_count
    if near:
        c, x, z = ctx & 1, (ctx >> 1) & 1, ctx >> 2
        places = (y, c, x, z)
        here = (ctx & 7) | (y << 3)
        turn_order = here ^ jnp.array([ctx_mask(m) for m in NEAR] + [ctx_mask(m) | 1 for m in NEAR], jnp.int32)
        relocate = move
    else:
        zero = jnp.int32(0)
        places = (y, zero, zero, zero)
        here = ctx
        turn_order = jnp.arange(ctx_count, dtype=jnp.int32)
        relocate = lambda v: v
    coords = jnp.stack([jnp.asarray(v, jnp.int32) for v in places])
    block_coords = coords if near else jnp.zeros((4,), jnp.int32)
    width = tokens.shape[2]
    half = w_query.shape[0]
    plan = jnp.concatenate(
        [
            sel_mid.reshape(ctx_count, cap_mid),
            live_mid.reshape(ctx_count, cap_mid),
            live_last.reshape(ctx_count, cap_last),
        ],
        axis=1,
    )
    order = Order(coords)
    if near:
        assert tok_local <= 256
        own_qkv, piece = pack_call(coords, w_query, key_weight.T, value_weight.T)
        fetched = hop(piece, Y_BIT)
        tok = move(pack_rows_call(tokens[0].T, plan))
        gains = jnp.concatenate([gain_attn.reshape(1, -1), gain_ffn.reshape(1, -1)], axis=0)
        beyond = hop(gains, Y_BIT)
        quad = x * 2 + (z & 1)
        own_down = w_down.T
        fetched, cut_gate, cut_up, cut_out, cut_down = order.take(
            fetched,
            *(cut_cols(cut_rows(w, c, 2), quad, 4) for w in (w_gate, w_up)),
            cut_rows(w_out, c, 2),
            cut_rows(own_down, c, 2),
        )
        far = hop(fetched, C_BIT)
        gate_mine, up_mine = hop(cut_gate, Y_BIT), hop(cut_up, Y_BIT)
        out_mine, down_mine = hop(cut_out, Y_BIT), hop(cut_down, Y_BIT)
        far, tok, beyond = order.take(far, tok, beyond)
        plan = tok[tok_local:, : plan.shape[1]].astype(jnp.int32)
        tok = tok[:tok_local]
        depth = half // 2
        gains = jnp.where(
            y == 0,
            jnp.concatenate([gains, beyond], axis=1),
            jnp.concatenate([beyond, gains], axis=1),
        )
        gains = [gains[0:1], gains[1:2]]
        origin = lambda *k: (0, 0)

        def in_rows(own, mine, other):
            wide = own.shape[1]
            return Weight(
                (2 * half, wide),
                [own, mine, other],
                [
                    [
                        (0, half, wide, origin, lambda ky, kc, kx, kz: (ky * half, 0)),
                        (1, depth, wide, origin, lambda ky, kc, kx, kz: ((1 - ky) * half + kc * depth, 0)),
                        (2, depth, wide, origin, lambda ky, kc, kx, kz: ((1 - ky) * half + (1 - kc) * depth, 0)),
                    ]
                ],
            )

        def in_parts(own, mine, other):
            wide = mine.shape[1]
            groups = []
            for j in range(FF_CHUNKS):
                column = lambda *k, j=j: part_of(j, k) * wide
                block = lambda *k, j=j: (j * depth, 0)
                groups.append(
                    [
                        (0, half, wide,
                         lambda *k, column=column: (0, column(*k)),
                         lambda *k, column=column: (k[0] * half, column(*k))),
                        (1, depth, wide, block,
                         lambda *k, column=column: ((1 - k[0]) * half + k[1] * depth, column(*k))),
                        (2, depth, wide, block,
                         lambda *k, column=column: ((1 - k[0]) * half + (1 - k[1]) * depth, column(*k))),
                    ]
                )
            return Weight((2 * half, own.shape[1]), [own, mine, other], groups)

        (weight_qkv,) = join_call(coords, (in_rows(own_qkv, fetched, far),))
        state, marks = {}, {}

        def start_gate():
            state["gate"] = spread(order.take(gate_mine))

        def start_up():
            state["up"] = spread(order.take(up_mine))

        beside = ((start_gate,), (start_up,))

        def fetch_rest():
            gate = stack_call(order.take(*state["gate"]))
            out, down = order.take(out_mine, down_mine)
            fars = [hop(v, C_BIT) for v in (gate, out, down)]
            up = stack_call(order.take(*state["up"]))
            gate_far, out_far, down_far, up_far = order.take(*fars, hop(up, C_BIT))
            wide = own_down.shape[1]
            weight_d = Weight(
                (width, 2 * wide),
                [own_down, down, down_far],
                [
                    [
                        (0, width, wide, origin, lambda ky, kc, kx, kz: (0, ky * wide)),
                        (1, width // 2, wide, origin, lambda ky, kc, kx, kz: (kc * (width // 2), (1 - ky) * wide)),
                        (2, width // 2, wide, origin, lambda ky, kc, kx, kz: ((1 - kc) * (width // 2), (1 - ky) * wide)),
                    ]
                ],
            )
            return join_call(
                coords,
                (
                    in_rows(w_out, out, out_far),
                    in_parts(w_gate, gate, gate_far),
                    in_parts(w_up, up, up_far),
                    weight_d,
                ),
            )
    else:
        tok = tokens[0]
        whole = lambda w: lax.all_gather(w, "ws", axis=0, tiled=True)
        weight_qkv = one_piece(whole(jnp.concatenate([w_query, key_weight, value_weight], axis=1)))
        gains = [whole(g).reshape(1, -1) for g in (gain_attn, gain_ffn)]
        far_weights = (
            one_piece(whole(w_out)), in_columns(whole(w_gate)), in_columns(whole(w_up)),
            one_piece(whole(w_down).T),
        )
        beside, fetch_rest = ((), ()), lambda: far_weights
    gain1, gain2 = (g.astype(F32) for g in gains)

    per_device = tok_local // BLK
    blocks = jnp.take(block_order.reshape(ctx_count, per_device), turn_order, axis=0)
    plan_order = jnp.take(plan, turn_order, axis=0)
    sel_all = plan_order[:, :cap_mid]
    live_two = plan_order[:, cap_mid : 2 * cap_mid]
    live_three = plan_order[:, 2 * cap_mid :]
    place_one = (blocks[:, :, None] * BLK + jnp.arange(BLK, dtype=jnp.int32)).reshape(ctx_count, tok_local)
    place_two = sum(
        jnp.where(sel_all // BLK == k, blocks[:, k : k + 1], 0) for k in range(per_device)
    ) * BLK + sel_all % BLK
    place_three = place_two[:, :cap_last]
    if near:
        mine = lambda v: v[0:1]
    else:
        mine = lambda v: lax.dynamic_slice_in_dim(v, here, 1, 0)
    sel_own, live2_own, live3_own = mine(sel_all), mine(live_two), mine(live_three)
    own_places = jnp.concatenate([mine(place_one), mine(place_two)], axis=1).reshape(-1, 1)
    frequency = ROPE_BASE ** (-jnp.arange(HEAD_SIZE // 2, dtype=F32) / (HEAD_SIZE // 2))
    angles = own_places.astype(F32) * frequency[None, :]
    cosine, sine = jnp.cos(angles), jnp.sin(angles)
    cosine = jnp.concatenate([cosine] * 4, axis=1)
    sine = jnp.concatenate([-sine, sine, -sine, sine], axis=1)
    tables = [
        (cosine[:tok_local], sine[:tok_local]),
        (cosine[tok_local:], sine[tok_local:]),
        (cosine[tok_local : tok_local + cap_last], sine[tok_local : tok_local + cap_last]),
    ]
    query_places = [mine(v) for v in (place_one, place_two, place_three)]
    key_places = [v.reshape(1, -1) for v in (place_one, place_two, place_three)]
    key_live = [
        jnp.ones((1, ctx_count * tok_local), jnp.int32),
        live_two.reshape(1, -1),
        live_three.reshape(1, -1),
    ]
    prompt = ctx_count * tok_local // 2
    if near:
        key_places[0], query_places[0] = order.take(key_places[0], query_places[0])
        marks["places"] = [*query_places[1:], *key_places[1:], *key_live[1:], sel_own, live2_own, live3_own]
        marks["tables"] = [*tables[1], *tables[2]]

    firsts, mixeds, seconds, hiddens = [], [], [], []
    records = []
    xs = [tok]
    first_in, query, kv = first_call(near, coords, tok, gain1, *tables[0], (weight_qkv,))
    heights = []
    for step in range(3):
        if near and step == 0:
            waits = (marks["places"], marks["tables"])
            part_a, part_b = gather_keys(kv, order, near, beside, waits)
        else:
            part_a, part_b = gather_keys(kv, order, near)
        if near and step == 1:
            query_places[1:], key_places[1:], key_live[1:] = (marks["places"][i : i + 2] for i in (0, 2, 4))
        firsts.append(first_in)
        next_rows = (cap_mid, cap_last, tok_local)[step]
        attention = (query, part_a, part_b, key_places[step], key_live[step], query_places[step], prompt)
        weights, mixed = attend_call(*attention)
        if step == 0:
            mixed = order.take(mixed)
            dense_weights = fetch_rest()
            if near:
                sel_own, live2_own, live3_own = marks["places"][6:]
                tables[1:] = [marks["tables"][:2], marks["tables"][2:]]
        if step == 1:
            mixed, cot = order.take(mixed, cotangent[0].T)
            cot = relocate(cot)
        if step == 0:
            extra = (sel_own, *tables[1])
        elif step == 1:
            extra = (live2_own, *tables[2])
        else:
            extra = (sel_own, live2_own, live3_own, heights[0], heights[1])
        mats = dense_weights + ((weight_qkv,) if step < 2 else ())
        result = dense_call(
            near, step, coords, xs[step], mixed, gain1, gain2, extra, mats, next_rows
        )
        mixed_rows, middle, second, gate, up, hidden = result[:6]
        mixeds.append(mixed_rows)
        seconds.append(second)
        hiddens.append(hidden)
        records.append((query, part_a, part_b, weights, middle, gate, up))
        if step < 2:
            height, following, first_in, query, kv = result[6:]
            if step == 1:
                following, cot = order.take(following, cot)
            heights.append(height)
            xs.append(following)
        else:
            output = relocate(order.take(result[6]))

    d_firsts, d_seconds = [None] * 3, [None] * 3
    sums_one, sums_two = [], []
    slots = None
    parts, d_query, d_middle = (), None, None
    column = lambda rows, i: [r[i] for r in rows]

    def grads(kind, groups):
        return grad_call(kind, block_coords, groups)

    for phase in range(4):
        step = 2 - phase
        before, into = (), ()
        if phase > 0:
            before = (gain1, *tables[step + 1], xs[step + 1], d_middle, d_query)
        if phase < 3:
            into = (gain2, *records[step][4:7])
        mats = (dense_weights[3], dense_weights[1], dense_weights[2], dense_weights[0])
        if phase == 0:
            extra, mats = (cot, sel_own, live3_own), mats
        elif phase == 1:
            extra, mats = (slots, live3_own, live2_own), (weight_qkv,) + mats
        elif phase == 2:
            extra, mats = (cot, sel_own, live2_own), (weight_qkv,) + mats
        else:
            extra, mats = (), (weight_qkv,)
        result = list(back_call(near, phase, coords, before, parts, into, extra, mats, cap_mid))
        if phase > 0:
            d_firsts[step + 1], total = result[:2]
            sums_one.append(total)
            result = result[2:]
        if phase == 3:
            grad_tokens = result[0]
            break
        d_low, d_gate, d_up, d_middle, d_mid_low, d_mixed, total = result[:7]
        d_seconds[step] = (d_low, d_gate, d_up, d_mid_low)
        sums_two.append(total)
        if phase == 0:
            slots = result[7]
        query, part_a, part_b, weights = records[step][:4]
        if phase < 2:
            d_mixed = order.take(d_mixed)
            d_query, term_a, term_b = attend_back_call(query, d_mixed, part_a, part_b, weights)
            if phase == 0:
                output, term_b = order.take(output, term_b)
            parts = scatter_keys(term_a, term_b, order, near)

        else:
            attend_last = lambda d: attend_back_call(query, d, part_a, part_b, weights)
            gate_grads = lambda *d: grads("cols", [seconds, list(d)])
            down_grads = grads("rows", [hiddens, column(d_seconds, 0)])
            if not near:
                d_query, term_a, term_b = attend_last(d_mixed)
                parts = scatter_keys(term_a, term_b, order, near)
                sums_of = [
                    pair_sum(*g, near)
                    for g in (down_grads, gate_grads(*column(d_seconds, 1)), gate_grads(*column(d_seconds, 2)))
                ]
                continue
            down = Hop(down_grads[1], C_BIT)
            gate_grads_made = wave(
                order, [(down, 0)], gate_grads, column(d_seconds, 1)
            )
            down = BlockSums(low_sum(down_grads[0], down.result))
            gate = Hop(gate_grads_made[1], C_BIT)
            d_query, term_a, term_b = wave(order, [(down, 0), (gate, 0)], attend_last, (d_mixed,))
            gate = BlockSums(low_sum(gate_grads_made[0], gate.result))
            far = Hop(term_b, C_BIT)
            up_made = wave(order, [(down, 1), (far, 0)], gate_grads, column(d_seconds, 2))
            own, *others = split_call(term_a, far.result)
            keys, up = KeySums(own, others), Hop(up_made[1], C_BIT)
            wave(order, [(keys, 0), (up, 0)])
            up = BlockSums(low_sum(up_made[0], up.result))
            parts = keys.result

    kv_width = key_weight.shape[1]
    hidden_width = w_gate.shape[1]
    mixed_grads = lambda *d: grads("mixed", [firsts, mixeds, list(d), column(d_seconds, 3)])
    sums = jnp.concatenate([sum(sums_one), sum(sums_two)], axis=0)
    placed = {}

    if near:
        def place(kind, widths):
            return lambda near_blocks, far_blocks, at: place_call(kind, at, near_blocks, far_blocks, widths)

        placing = lambda chain: (*chain.result, coords)
        rest_made = wave(order, [(gate, 0), (down, 2)], mixed_grads, d_firsts)
        rest, gains_sum = Hop(rest_made[1], C_BIT), RunningSum(sums)
        wave(order, [(gate, 1), (down, 3), (rest, 0)])
        rest = BlockSums(low_sum(rest_made[0], rest.result))
        wave(order, [(up, 0), (gate, 2), (down, 4)])
        wave(order, [(up, 1), (gate, 3), (down, 5)])
        placed["down"] = wave(
            order, [(rest, 0), (up, 2), (gate, 4)], place("rows", None), placing(down)
        )
        wave(order, [(rest, 1), (up, 3), (gate, 5), (gains_sum, 1)])
        placed["gate"] = wave(
            order, [(rest, 2), (up, 4)], place("cols", (hidden_width,)), placing(gate)
        )
        tokens_back = Move(grad_tokens)
        wave(order, [(rest, 3), (up, 5), (gains_sum, 0)])
        placed["up"] = wave(
            order, [(rest, 4), (gains_sum, 2), (tokens_back, 0)], place("cols", (hidden_width,)), placing(up)
        )
        grad_tokens = tokens_back.result.astype(F32)
        wave(order, [(rest, 5), (gains_sum, 3)])
        wave(order, [(gains_sum, 4)])
        placed["rest"] = order.all(
            *place("cols", (width, kv_width, width, kv_width))(*rest.result, order.token)
        )
        for name in ("down", "gate", "up"):
            (placed[name],) = placed[name]
        gain_sums = gains_sum.result
    else:
        sums_of.append(pair_sum(*mixed_grads(*d_firsts), near))
        for name, kind, widths, total in zip(
            ("down", "gate", "up", "rest"),
            ("rows", "cols", "cols", "cols"),
            (None, (hidden_width,), (hidden_width,), (width, kv_width, width, kv_width)),
            sums_of,
            strict=True,
        ):
            mine = lax.dynamic_index_in_dim(total, y, 1, keepdims=False)
            placed[name] = place_call(kind, block_coords, mine[0], mine[1], widths)
        for name in ("down", "gate", "up"):
            (placed[name],) = placed[name]
        gain_sums = lax.psum(sums, AXES)
        grad_tokens = grad_tokens.astype(F32)
    grad_down, grad_gate, grad_up = placed["down"].T, placed["gate"], placed["up"]
    grad_query, grad_key, grad_out, grad_value = placed["rest"]
    grad_key, grad_value = grad_key.T, grad_value.T
    gain_sums = lax.dynamic_slice_in_dim(gain_sums, y * half, half, 1)
    return (
        output.T[None],
        grad_tokens.T[None],
        grad_query,
        grad_key,
        grad_value,
        grad_out,
        grad_gate,
        grad_up,
        grad_down,
        gain_sums[0],
        gain_sums[1],
    )


def solution(mesh):
    rows = P("ws", "ctx", None)
    flat = P("ws", None)
    in_specs = (rows, rows) + (flat,) * 7 + (P("ws"), P("ws"), P()) + (flat,) * 4
    out_specs = (rows, rows) + (flat,) * 7 + (P("ws"), P("ws"))
    return jax.shard_map(
        on_device, mesh=mesh, in_specs=in_specs, out_specs=out_specs, check_vma=False
    )
```

time: 624 us -> 535 us (0.86)
  local copies, waits for them, and re-layouts: 78.2 us -> 26.3 us
  waiting for transfers between devices: 226 us -> 182 us
  Pallas kernels: 146 us -> 161 us
  starting transfers between devices: 147 us -> 138 us
    unnamed x264 -> x104, local copies, waits for them, and re-layouts: 55.2 us -> 5.72 us
    ppermute x113 -> x118, waiting for transfers between devices: 207 us -> 166 us  [hop(): return lax.ppermute(value, AXES, [(i, i ^ mask) for i in range(32)])]
    pallas_call x11 -> x12, Pallas kernels: 48.7 us -> 62 us  [the longest x4 26.4 us: back_call(): pl.pallas_call(functools.partial(back_kernel, near, phase, weights, len(p...]
    ppermute x113 -> x118, starting transfers between devices: 125 us -> 122 us  [hop(): return lax.ppermute(value, AXES, [(i, i ^ mask) for i in range(32)])]
  transfers between devices with their start and end apart: 117 -> 122, of which waited for: 58 -> 58; matrix products, arithmetic and copies ran while one was open for 6% -> 6% of each run, Pallas kernels for 9% -> 15%
where the time goes in v3:
time: 535 us; the launch traced here: 526 us
  waiting for transfers between devices  182 us (34%)
  Pallas kernels  161 us (30%)
  starting transfers between devices  138 us (26%)
  local copies, waits for them, and re-layouts  26.3 us (5%)
  other arithmetic  16.1 us (3%)
    ppermute x118, waiting for transfers between devices, hop(): return lax.ppermute(value, AXES, [(i, i ^ mask) for i in range(32)])  166 us
    ppermute x118, starting transfers between devices, hop(): return lax.ppermute(value, AXES, [(i, i ^ mask) for i in range(32)])  122 us
    pallas_call x3, Pallas kernels, attend_call(): pl.pallas_call(functools.partial(attend_kernel, prompt), name='attend', g...  30.5 us
    pallas_call x4, Pallas kernels, back_call(): pl.pallas_call(functools.partial(back_kernel, near, phase, weights, len(p...  26.4 us
    pallas_call x3, Pallas kernels, attend_back_call(): pl.pallas_call(attend_back_kernel, name='attend_back', grid=(heads,), out...  26.4 us
    pallas_call x4, Pallas kernels, grad_call(): pl.pallas_call(functools.partial(kernel, n_steps), name=f'grad_{kind}', o...  22.6 us
    pallas_call x3, Pallas kernels, dense_call(): pl.pallas_call(functools.partial(dense_kernel, near, step, weights), name...  19.3 us
    ppermute x4, starting transfers between devices, move(): return lax.ppermute(value, AXES, [(i, swap_place(i)) for i in range(32)])  16.2 us
  transfers between devices with their start and end apart: 122, of which 58 were waited for; matrix products, arithmetic and copies ran while one was open for 6% of the time, Pallas kernels for 15%

profile of v3, /device:TPU:7, one launch (start us, length us, event | category | flops | bytes accessed | tf_op | source)
XLA Modules:
  0.0 525.8 jit_solution(12107094374742932102)
XLA Ops:
  0.7 3.7 pack.1
  13.2 4.2 collective-permute-start.2
  44.4 5.1 collective-permute-start.7
  67.5 2.9 collective-permute-start.13
  74.4 7.0 %collective-permute-done.18.refs_3_ = bf16[240,640]{1,0:T(8,128)(2,1)S(1)} collective-permute-done((bf16[240,640]{1,0:T(8,128)(2,1)}, bf16[240,640]{1,0:T(8,128)(2,1)S(1)}, u32[]{:S(2)}, u32[]{:S(2)}) %collective-permute-start.18) | collective-permute-done | bytes 307232 | tf_op jit(solution)/shard_map/ppermute | solution.py:32
  81.6 6.5 %collective-permute-done.17.refs_2_ = bf16[240,640]{1,0:T(8,128)(2,1)S(1)} collective-permute-done((bf16[240,640]{1,0:T(8,128)(2,1)}, bf16[240,640]{1,0:T(8,128)(2,1)S(1)}, u32[]{:S(2)}, u32[]{:S(2)}) %collective-permute-start.17) | collective-permute-done | bytes 307232 | tf_op jit(solution)/shard_map/ppermute | solution.py:32
  91.4 15.0 %attend.3 = (bf16[5,384,2048]{2,1,0:T(8,128)(2,1)}, bf16[5,128,192]{2,1,0:T(8,128)(2,1)S(1)}) custom-call(bf16[5,128,192]{2,1,0:T(8,128)(2,1)S(1)} %copy-done.3, bf16[1024,640]{1,0:T(8,128)(2,1)S(1)} %stack.153.a_ref, bf16[1024,640]{1,0:T(8,128)(2,1)S(1)} %collective-permute-done.13.b_ref, s32[1,2048]{1,0:T(1,128)S(1)} %add.186.kpos_ref, ...), custom_call_target="tpu_custom_call" | custom-call | bytes 14263717 | tf_op jit(solution)/shard_map/attend/pallas_call | solution.py:488
  106.4 3.1 collective-permute-done.14.args_1_
  113.7 4.9 collective-permute-done.20.args_2_
  120.6 6.7 %join_weights.3 = (bf16[960,960]{1,0:T(8,128)(2,1)S(1)}, bf16[960,2560]{1,0:T(8,128)(2,1)S(1)}, bf16[960,2560]{1,0:T(8,128)(2,1)S(1)}, bf16[960,2560]{1,0:T(8,128)(2,1)S(1)}) custom-call(s32[4]{0:T(128)S(1)} %pad_add_fusion.1.coords_ref.args_0_, bf16[480,960]{1,0:T(8,128)(2,1)} %args_0_.4, bf16[240,960]{1,0:T(8,128)(2,1)} %copy-done.31, ...), custom_call_target="tpu_custom_call" | custom-call | bytes 925000 | tf_op jit(solution)/shard_map/join_weights/pallas_call | solution.py:218
  127.2 6.9 %dense_0.1 = (bf16[128,960]{1,0:T(8,128)(2,1)}, f32[128,960]{1,0:T(8,128)}, bf16[128,960]{1,0:T(8,128)(2,1)}, bf16[128,2560]{1,0:T(8,128)(2,1)}, bf16[128,2560]{...) custom-call(bf16[5,128,192]{2,1,0:T(8,128)(2,1)S(1)} %get-tuple-elem, ...), custom_call_target="tpu_custom_call" | custom-call | bytes 5550000 | tf_op jit(solution)/shard_map/dense_0/pallas_call | solution.py:691
  138.0 2.5 collective-permute-done.29.refs_4_
  140.5 2.8 collective-permute-done.28.refs_3_
  153.4 10.1 %attend.4 = (bf16[5,288,1536]{2,1,0:T(8,128)(2,1)}, bf16[5,96,192]{2,1,0:T(8,128)(2,1)S(1)}) custom-call(bf16[5,96,192]{2,1,0:T(8,128)(2,1)S(1)} %get-tuple-element.527.q_ref, bf16[768,640]{1,0:T(8,128)(2,1)S(1)} %stack.156.a_ref, bf16[768,640]{1,0:T(8,128)(2,1)S(1)} %collective-permute-done.33.b_ref, s32[1,1536]{1,0:T(1,128)S(1)} %reshape.145.kpos_ref, ...), custom_call_target="tpu_custom_call" | custom-call | bytes 8023341 | tf_op jit(solution)/shard_map/attend/pallas_call | solution.py:488
  163.5 4.7 collective-permute-start.34
  168.2 6.9 %dense_1.1 = (bf16[96,960]{1,0:T(8,128)(2,1)}, f32[96,960]{1,0:T(8,128)}, bf16[96,960]{1,0:T(8,128)(2,1)}, bf16[96,2560]{1,0:T(8,128)(2,1)}, bf16[96,2560]{1,0:T...) custom-call(bf16[5,96,192]{2,1,0:T(8,128)(2,1)S(1)} %get-tuple-eleme, ...), custom_call_target="tpu_custom_call" | custom-call | bytes 5550000 | tf_op jit(solution)/shard_map/dense_1/pallas_call | solution.py:691
  175.1 4.5 collective-permute-done.34.args_5_.args_19_
  179.6 3.4 collective-permute-start.36
  190.9 3.2 collective-permute-start.42
  195.8 5.4 %attend.5 = (bf16[5,192,1024]{2,1,0:T(8,128)(2,1)}, bf16[5,64,192]{2,1,0:T(8,128)(2,1)S(1)}) custom-call(bf16[5,64,192]{2,1,0:T(8,128)(2,1)S(1)} %get-tuple-element.552.q_ref, bf16[512,640]{1,0:T(8,128)(2,1)S(1)} %stack.157.a_ref, bf16[512,640]{1,0:T(8,128)(2,1)S(1)} %collective-permute-done.42.b_ref, s32[1,1024]{1,0:T(1,128)S(1)} %copy-done.13, ...), custom_call_target="tpu_custom_call" | custom-call | bytes 3565929 | tf_op jit(solution)/shard_map/attend/pallas_call | solution.py:488
  201.3 5.5 %dense_2.1 = (bf16[64,960]{1,0:T(8,128)(2,1)}, f32[64,960]{1,0:T(8,128)}, bf16[64,960]{1,0:T(8,128)(2,1)}, bf16[64,2560]{1,0:T(8,128)(2,1)}, bf16[64,2560]{1,0:T...) custom-call(bf16[5,64,192]{2,1,0:T(8,128)(2,1)S(1)} %get-tuple-element.573.ao_ref, ...), custom_call_target="tpu_custom_call" | custom-call | bytes 5550000 | tf_op jit(solution)/shard_map/dense_2/pallas_call | solution.py:691
  206.7 5.1 collective-permute-start.43
  211.8 6.5 %back_0.1 = (bf16[64,960]{1,0:T(8,128)(2,1)}, bf16[64,2560]{1,0:T(8,128)(2,1)}, bf16[64,2560]{1,0:T(8,128)(2,1)}, f32[64,960]{1,0:T(8,128)}, bf16[64,960]{1,0:T(...) custom-call(s32[4]{0:T(128)S(1)} %pad_add_fusion.1.coords_ref.args_0_, ...), custom_call_target="tpu_custom_call" | custom-call | bytes 5550000 | tf_op jit(solution)/shard_map/back_0/pallas_call | solution.py:842
  218.3 5.8 %attend_back.3 = (f32[5,64,192]{2,1,0:T(8,128)S(1)}, f32[512,640]{1,0:T(8,128)S(1)}, bf16[512,640]{1,0:T(8,128)(2,1)S(1)}) custom-call(bf16[5,64,192]{2,1,0:T(8,128)(2,1)S(1)} %get-tuple-element.552.q_ref, bf16[5,64,192]{2,1,0:T(8,128)(2,1)S(1)} %get-tuple-element.587.do_ref, bf16[512,640]{1,0:T(8,128)(2,1)S(1)} %stack.157.a_ref, ...), custom_call_target="tpu_custom_call" | custom-call | bytes 2755490 | tf_op jit(solution)/shard_map/attend_back/pallas_call | solution.py:538
  227.4 3.2 collective-permute-start.48
  237.2 8.1 %back_1.1 = (bf16[64,1600]{1,0:T(8,128)(2,1)}, f32[1,960]{1,0:T(1,128)}, bf16[96,960]{1,0:T(8,128)(2,1)}, bf16[96,2560]{1,0:T(8,128)(2,1)}, bf16[96,2560]{1,0:T(...) custom-call(s32[4]{0:T(128)S(1)} %pad_add_fusion.1.coords_ref.args_0, ...), custom_call_target="tpu_custom_call" | custom-call | bytes 5550000 | tf_op jit(solution)/shard_map/back_1/pallas_call | solution.py:842
  245.3 8.6 %attend_back.4 = (f32[5,96,192]{2,1,0:T(8,128)S(1)}, f32[768,640]{1,0:T(8,128)S(1)}, bf16[768,640]{1,0:T(8,128)(2,1)S(1)}) custom-call(bf16[5,96,192]{2,1,0:T(8,128)(2,1)S(1)} %get-tuple-element.527.q_ref, bf16[5,96,192]{2,1,0:T(8,128)(2,1)S(1)} %get-tuple-element.636.do_ref, bf16[768,640]{1,0:T(8,128)(2,1)S(1)} %stack.156.a_ref, ...), custom_call_target="tpu_custom_call" | custom-call | bytes 6199854 | tf_op jit(solution)/shard_map/attend_back/pallas_call | solution.py:538
  253.9 2.7 collective-permute-start.52
  268.5 3.7 collective-permute-done.57.args_12_
  273.0 8.8 %back_2.1 = (bf16[96,1600]{1,0:T(8,128)(2,1)}, f32[1,960]{1,0:T(1,128)}, bf16[128,960]{1,0:T(8,128)(2,1)}, bf16[128,2560]{1,0:T(8,128)(2,1)}, bf16[128,2560]{1,0...) custom-call(s32[4]{0:T(128)S(1)} %pad_add_fusion.1.coords_ref.args_0, ...), custom_call_target="tpu_custom_call" | custom-call | bytes 5550000 | tf_op jit(solution)/shard_map/back_2/pallas_call | solution.py:842
  281.8 5.2 grad_rows.1
  289.4 5.4 %grad_cols.2 = (bf16[2,2,4,120,640]{4,3,2,1,0:T(8,128)(2,1)S(1)}, bf16[2,2,4,120,640]{4,3,2,1,0:T(8,128)(2,1)S(1)}) custom-call(s32[4]{0:T(128)S(1)} %pad_add_fusion.1.coords_ref.args_0_, bf16[128,960]{1,0:T(8,128)(2,1)} %get-tuple-element.683.args_0_, bf16[96,960]{1,0:T(8,128)(2,1)} %get-tuple-element.684.args_1_, ...), custom_call_target="tpu_custom_call" | custom-call | bytes 5550000 | tf_op jit(solution)/shard_map/grad_cols/pallas_call | solution.py:969
  296.5 12.0 %attend_back.5 = (f32[5,128,192]{2,1,0:T(8,128)S(1)}, f32[1024,640]{1,0:T(8,128)S(1)}, bf16[1024,640]{1,0:T(8,128)(2,1)S(1)}) custom-call(bf16[5,128,192]{2,1,0:T(8,128)(2,1)S(1)} %copy-done.3, bf16[5,128,192]{2,1,0:T(8,128)(2,1)S(1)} %get-tuple-element.700.do_ref, bf16[1024,640]{1,0:T(8,128)(2,1)S(1)} %stack.153.a_ref, ...), custom_call_target="tpu_custom_call" | custom-call | bytes 11021963 | tf_op jit(solution)/shard_map/attend_back/pallas_call | solution.py:538
  308.5 3.7 collective-permute-done.61
  314.5 5.4 %grad_cols.3 = (bf16[2,2,4,120,640]{4,3,2,1,0:T(8,128)(2,1)S(1)}, bf16[2,2,4,120,640]{4,3,2,1,0:T(8,128)(2,1)S(1)}) custom-call(s32[4]{0:T(128)S(1)} %pad_add_fusion.1.coords_ref.args_0_, bf16[128,960]{1,0:T(8,128)(2,1)} %get-tuple-element.683.args_0_, bf16[96,960]{1,0:T(8,128)(2,1)} %get-tuple-element.684.args_1_, ...), custom_call_target="tpu_custom_call" | custom-call | bytes 5550000 | tf_op jit(solution)/shard_map/grad_cols/pallas_call | solution.py:969
  319.8 10.2 %collective-permute-done.63 = bf16[4,80,960]{2,1,0:T(8,128)(2,1)S(1)} collective-permute-done((bf16[4,80,960]{2,1,0:T(8,128)(2,1)S(1)}, bf16[4,80,960]{2,1,0:T(8,128)(2,1)S(1)}, u32[]{:S(2)}, u32[]{:S(2)}) %collective-permute-start.63) | collective-permute-done | bytes 614432 | tf_op jit(solution)/shard_map/ppermute | solution.py:32
  343.3 9.6 %collective-permute-done.70.args_12_ = bf16[128,640]{1,0:T(8,128)(2,1)S(1)} collective-permute-done((bf16[128,640]{1,0:T(8,128)(2,1)S(1)}, bf16[128,640]{1,0:T(8,128)(2,1)S(1)}, u32[]{:S(2)}, u32[]{:S(2)}) %collective-permute-start.70) | collective-permute-done | bytes 163872 | tf_op jit(solution)/shard_map/ppermute | solution.py:32
  353.0 3.0 back_3.1
  358.1 2.8 collective-permute-start.77
  360.9 6.7 %grad_mixed.1 = (bf16[2,2,4,120,640]{4,3,2,1,0:T(8,128)(2,1)S(1)}, bf16[2,2,4,120,640]{4,3,2,1,0:T(8,128)(2,1)S(1)}) custom-call(s32[4]{0:T(128)S(1)} %pad_add_fusion.1.coords_ref.args_0_, bf16[128,960]{1,0:T(8,128)(2,1)} %get-tuple-element.762.args_0_, bf16[96,960]{1,0:T(8,128)(2,1)} %get-tuple-element.763.args_1_, ...), custom_call_target="tpu_custom_call" | custom-call | bytes 5550000 | tf_op jit(solution)/shard_map/grad_mixed/pallas_call | solution.py:969
  367.6 4.6 collective-permute-done.76
  378.7 2.9 collective-permute-done.80
  381.6 4.2 collective-permute-start.82
  385.9 3.4 collective-permute-done.81
  389.3 3.8 collective-permute-done.82
  396.1 2.5 collective-permute-start.87
  398.6 2.7 collective-permute-done.85
  401.3 8.3 %collective-permute-done.86 = bf16[120,640]{1,0:T(8,128)(2,1)S(1)} collective-permute-done((bf16[120,640]{1,0:T(8,128)(2,1)S(1)}, bf16[120,640]{1,0:T(8,128)(2,1)S(1)}, u32[]{:S(2)}, u32[]{:S(2)}) %collective-permute-start.86) | collective-permute-done | bytes 153632 | tf_op jit(solution)/shard_map/ppermute | solution.py:32
  415.3 3.4 collective-permute-done.91
  418.8 7.1 %collective-permute-done.92 = bf16[120,640]{1,0:T(8,128)(2,1)S(1)} collective-permute-done((bf16[120,640]{1,0:T(8,128)(2,1)S(1)}, bf16[120,640]{1,0:T(8,128)(2,1)S(1)}, u32[]{:S(2)}, u32[]{:S(2)}) %collective-permute-start.92) | collective-permute-done | bytes 153632 | tf_op jit(solution)/shard_map/ppermute | solution.py:32
  430.5 3.1 collective-permute-start.96
  434.2 3.9 place_rows.1
  438.0 7.0 %collective-permute-done.97 = bf16[120,640]{1,0:T(8,128)(2,1)S(1)} collective-permute-done((bf16[120,640]{1,0:T(8,128)(2,1)S(1)}, bf16[120,640]{1,0:T(8,128)(2,1)S(1)}, u32[]{:S(2)}, u32[]{:S(2)}) %collective-permute-start.97) | collective-permute-done | bytes 153632 | tf_op jit(solution)/shard_map/ppermute | solution.py:32
  452.6 2.7 collective-permute-done.102
  455.3 7.7 %collective-permute-done.103 = bf16[120,640]{1,0:T(8,128)(2,1)S(1)} collective-permute-done((bf16[120,640]{1,0:T(8,128)(2,1)S(1)}, bf16[120,640]{1,0:T(8,128)(2,1)S(1)}, u32[]{:S(2)}, u32[]{:S(2)}) %collective-permute-start.103) | collective-permute-done | bytes 153632 | tf_op jit(solution)/shard_map/ppermute | solution.py:32
  468.5 3.4 place_cols.3
  471.9 7.0 %collective-permute-done.108 = bf16[120,640]{1,0:T(8,128)(2,1)S(1)} collective-permute-done((bf16[120,640]{1,0:T(8,128)(2,1)S(1)}, bf16[120,640]{1,0:T(8,128)(2,1)S(1)}, u32[]{:S(2)}, u32[]{:S(2)}) %collective-permute-start.108) | collective-permute-done | bytes 153632 | tf_op jit(solution)/shard_map/ppermute | solution.py:32
  479.1 2.5 collective-permute-start.114
  489.1 6.9 %collective-permute-done.112 = bf16[120,640]{1,0:T(8,128)(2,1)S(1)} collective-permute-done((bf16[120,640]{1,0:T(8,128)(2,1)S(1)}, bf16[120,640]{1,0:T(8,128)(2,1)S(1)}, u32[]{:S(2)}, u32[]{:S(2)}) %collective-permute-start.112) | collective-permute-done | bytes 153632 | tf_op jit(solution)/shard_map/ppermute | solution.py:32
  499.4 3.4 place_cols.4
  502.7 10.2 %collective-permute-done.118 = bf16[960,128]{1,0:T(8,128)(2,1)S(1)} collective-permute-done((bf16[960,128]{1,0:T(8,128)(2,1)S(1)}, bf16[960,128]{1,0:T(8,128)(2,1)S(1)}, u32[]{:S(2)}, u32[]{:S(2)}) %collective-permute-start.118) | collective-permute-done | bytes 245792 | tf_op jit(solution)/shard_map/ppermute | solution.py:41
  513.6 2.5 collective-permute-done.120
  517.0 2.6 collective-permute-done.121
  520.3 4.3 place_cols.5
  (411 shorter events, 181.8 us)
Async XLA Ops:
  4.4 20.0 %collective-permute-start = (bf16[240,1664]{1,0:T(8,128)(2,1)S(1)}, bf16[240,1664]{1,0:T(8,128)(2,1)}, u32[]{:S(2)}, u32[]{:S(2)}) collective-permute-start(bf16[240,1664]{1,0:T(8,128)(2,1)S(1)} %get-tuple-element.466), channel_id=1, source_target_pairs={{0,1},{1,0},{2,3},{3,2},{4,5},{5,4},{6,7},{7,6},{8,9},{9,8},{10,11... | collective-permute-start | bytes 2396168 | tf_op jit(solution)/shard_map/ppermute | solution.py:32
  6.7 23.3 %collective-permute-start.3 = (bf16[2,480]{1,0:T(2,128)(2,1)}, bf16[2,480]{1,0:T(2,128)(2,1)}, u32[]{:S(2)}, u32[]{:S(2)}) collective-permute-start(bf16[2,480]{1,0:T(2,128)(2,1)} %pad_maximum_fusion.13), channel_id=1, source_target_pairs={{0,1},{1,0},{2,3},{3,2},{4,5},{5,4},{6,7},{7,6},{8,9},{9,8},{10,11... | collective-permute-start | bytes 5768 | tf_op jit(solution)/shard_map/ppermute | solution.py:32
  13.2 18.0 %collective-permute-start.2 = (bf16[144,960]{1,0:T(8,128)(2,1)S(1)}, bf16[144,960]{1,0:T(8,128)(2,1)}, u32[]{:S(2)}, u32[]{:S(2)}) collective-permute-start(bf16[144,960]{1,0:T(8,128)(2,1)S(1)} %pack_rows.1), channel_id=1, source_target_pairs={{0,0},{1,16},{2,2},{3,18},{4,4},{5,20},{6,6},{7,22},{8,8},{9,24},{... | collective-permute-start | bytes 829448 | tf_op jit(solution)/shard_map/ppermute | solution.py:41
  28.5 25.9 %collective-permute-start.8 = (bf16[240,640]{1,0:T(8,128)(2,1)}, bf16[240,640]{1,0:T(8,128)(2,1)}, u32[]{:S(2)}, u32[]{:S(2)}) collective-permute-start(bf16[240,640]{1,0:T(8,128)(2,1)} %dynamic_slice.17), channel_id=1, source_target_pairs={{0,1},{1,0},{2,3},{3,2},{4,5},{5,4},{6,7},{7,6},{8,9},{9,8},{10,11... | collective-permute-start | bytes 921608 | tf_op jit(solution)/shard_map/ppermute | solution.py:32
  28.5 36.3 %collective-permute-start.12 = (bf16[240,640]{1,0:T(8,128)(2,1)}, bf16[240,640]{1,0:T(8,128)(2,1)}, u32[]{:S(2)}, u32[]{:S(2)}) collective-permute-start(bf16[240,640]{1,0:T(8,128)(2,1)} %dynamic_slice.18), channel_id=1, source_target_pairs={{0,1},{1,0},{2,3},{3,2},{4,5},{5,4},{6,7},{7,6},{8,9},{9,8},{10,11... | collective-permute-start | bytes 921608 | tf_op jit(solution)/shard_map/ppermute | solution.py:32
  44.4 12.1 %collective-permute-start.7 = (bf16[128,640]{1,0:T(8,128)(2,1)}, bf16[128,640]{1,0:T(8,128)(2,1)}, u32[]{:S(2)}, u32[]{:S(2)}) collective-permute-start(bf16[128,640]{1,0:T(8,128)(2,1)} %get-tuple-element.477.refs_0_), channel_id=1, source_target_pairs={{0,13},{1,12},{2,15},{3,14},{4,9},{5,8},{6,11},{7,10},{8,5},{9,4},... | collective-permute-start | bytes 491528 | tf_op jit(solution)/shard_map/ppermute | solution.py:32
  49.5 8.1 %collective-permute-start.6 = (bf16[128,640]{1,0:T(8,128)(2,1)}, bf16[128,640]{1,0:T(8,128)(2,1)}, u32[]{:S(2)}, u32[]{:S(2)}) collective-permute-start(bf16[128,640]{1,0:T(8,128)(2,1)} %get-tuple-element.477.refs_0_), channel_id=1, source_target_pairs={{0,8},{1,9},{2,10},{3,11},{4,12},{5,13},{6,14},{7,15},{8,0},{9,1},... | collective-permute-start | bytes 491528 | tf_op jit(solution)/shard_map/ppermute | solution.py:32
  49.7 8.2 %collective-permute-start.5 = (bf16[128,640]{1,0:T(8,128)(2,1)}, bf16[128,640]{1,0:T(8,128)(2,1)}, u32[]{:S(2)}, u32[]{:S(2)}) collective-permute-start(bf16[128,640]{1,0:T(8,128)(2,1)} %get-tuple-element.477.refs_0_), channel_id=1, source_target_pairs={{0,1},{1,0},{2,3},{3,2},{4,5},{5,4},{6,7},{7,6},{8,9},{9,8},{10,11... | collective-permute-start | bytes 491528 | tf_op jit(solution)/shard_map/ppermute | solution.py:32
  67.5 22.0 %collective-permute-start.13 = (bf16[1024,640]{1,0:T(8,128)(2,1)S(1)}, bf16[1024,640]{1,0:T(8,128)(2,1)S(1)}, u32[]{:S(2)}, u32[]{:S(2)}) collective-permute-start(bf16[1024,640]{1,0:T(8,128)(2,1)S(1)} %stack.153.a_ref), channel_id=1, source_target_pairs={{0,2},{1,3},{2,0},{3,1},{4,6},{5,7},{6,4},{7,5},{8,10},{9,11},{10,... | collective-permute-start | bytes 3932168 | tf_op jit(solution)/shard_map/ppermute | solution.py:32
  70.4 39.1 %collective-permute-start.15 = (bf16[480,1280]{1,0:T(8,128)(2,1)S(1)}, bf16[480,1280]{1,0:T(8,128)(2,1)S(1)}, u32[]{:S(2)}, u32[]{:S(2)}) collective-permute-start(bf16[480,1280]{1,0:T(8,128)(2,1)S(1)} %copy-done.25), channel_id=1, source_target_pairs={{0,1},{1,0},{2,3},{3,2},{4,5},{5,4},{6,7},{7,6},{8,9},{9,8},{10,11... | collective-permute-start | bytes 3686408 | tf_op jit(solution)/shard_map/ppermute | solution.py:32
  71.8 9.7 %collective-permute-start.18 = (bf16[240,640]{1,0:T(8,128)(2,1)}, bf16[240,640]{1,0:T(8,128)(2,1)S(1)}, u32[]{:S(2)}, u32[]{:S(2)}) collective-permute-start(bf16[240,640]{1,0:T(8,128)(2,1)} %collective-permute-done.8.refs_0_), channel_id=1, source_target_pairs={{0,12},{1,13},{2,14},{3,15},{4,8},{5,9},{6,10},{7,11},{8,4},{9,5},... | collective-permute-start | bytes 921608 | tf_op jit(solution)/shard_map/ppermute | solution.py:32
  72.6 15.4 %collective-permute-start.17 = (bf16[240,640]{1,0:T(8,128)(2,1)}, bf16[240,640]{1,0:T(8,128)(2,1)S(1)}, u32[]{:S(2)}, u32[]{:S(2)}) collective-permute-start(bf16[240,640]{1,0:T(8,128)(2,1)} %collective-permute-done.8.refs_0_), channel_id=1, source_target_pairs={{0,8},{1,9},{2,10},{3,11},{4,12},{5,13},{6,14},{7,15},{8,0},{9,1},... | collective-permute-start | bytes 921608 | tf_op jit(solution)/shard_map/ppermute | solution.py:32
  74.2 14.5 %collective-permute-start.16 = (bf16[240,640]{1,0:T(8,128)(2,1)}, bf16[240,640]{1,0:T(8,128)(2,1)S(1)}, u32[]{:S(2)}, u32[]{:S(2)}) collective-permute-start(bf16[240,640]{1,0:T(8,128)(2,1)} %collective-permute-done.8.refs_0_), channel_id=1, source_target_pairs={{0,4},{1,5},{2,6},{3,7},{4,0},{5,1},{6,2},{7,3},{8,12},{9,13},{10,... | collective-permute-start | bytes 921608 | tf_op jit(solution)/shard_map/ppermute | solution.py:32
  81.4 28.1 %collective-permute-start.14 = (bf16[240,960]{1,0:T(8,128)(2,1)S(1)}, bf16[240,960]{1,0:T(8,128)(2,1)S(1)}, u32[]{:S(2)}, u32[]{:S(2)}) collective-permute-start(bf16[240,960]{1,0:T(8,128)(2,1)S(1)} %copy-done.30), channel_id=1, source_target_pairs={{0,1},{1,0},{2,3},{3,2},{4,5},{5,4},{6,7},{7,6},{8,9},{9,8},{10,11... | collective-permute-start | bytes 1382408 | tf_op jit(solution)/shard_map/ppermute | solution.py:32
  88.0 21.5 %collective-permute-start.24 = (bf16[240,640]{1,0:T(8,128)(2,1)}, bf16[240,640]{1,0:T(8,128)(2,1)S(1)}, u32[]{:S(2)}, u32[]{:S(2)}) collective-permute-start(bf16[240,640]{1,0:T(8,128)(2,1)} %collective-permute-done.12.refs_0_), channel_id=1, source_target_pairs={{0,12},{1,13},{2,14},{3,15},{4,8},{5,9},{6,10},{7,11},{8,4},{9,5},... | collective-permute-start | bytes 921608 | tf_op jit(solution)/shard_map/ppermute | solution.py:32
  88.6 20.9 %collective-permute-start.23 = (bf16[240,640]{1,0:T(8,128)(2,1)}, bf16[240,640]{1,0:T(8,128)(2,1)S(1)}, u32[]{:S(2)}, u32[]{:S(2)}) collective-permute-start(bf16[240,640]{1,0:T(8,128)(2,1)} %collective-permute-done.12.refs_0_), channel_id=1, source_target_pairs={{0,8},{1,9},{2,10},{3,11},{4,12},{5,13},{6,14},{7,15},{8,0},{9,1},... | collective-permute-start | bytes 921608 | tf_op jit(solution)/shard_map/ppermute | solution.py:32
  89.5 20.1 %collective-permute-start.22 = (bf16[240,640]{1,0:T(8,128)(2,1)}, bf16[240,640]{1,0:T(8,128)(2,1)S(1)}, u32[]{:S(2)}, u32[]{:S(2)}) collective-permute-start(bf16[240,640]{1,0:T(8,128)(2,1)} %collective-permute-done.12.refs_0_), channel_id=1, source_target_pairs={{0,4},{1,5},{2,6},{3,7},{4,0},{5,1},{6,2},{7,3},{8,12},{9,13},{10,... | collective-permute-start | bytes 921608 | tf_op jit(solution)/shard_map/ppermute | solution.py:32
  163.5 16.1 %collective-permute-start.34 = (bf16[960,128]{1,0:T(8,128)(2,1)S(1)}, bf16[960,128]{1,0:T(8,128)(2,1)S(1)}, u32[]{:S(2)}, u32[]{:S(2)}) collective-permute-start(bf16[960,128]{1,0:T(8,128)(2,1)S(1)} %bitcast.189), channel_id=1, source_target_pairs={{0,0},{1,16},{2,2},{3,18},{4,4},{5,20},{6,6},{7,22},{8,8},{9,24},{... | collective-permute-start | bytes 737288 | tf_op jit(solution)/shard_map/ppermute | solution.py:41
  206.7 17.4 %collective-permute-start.43 = (bf16[960,128]{1,0:T(8,128)(2,1)}, bf16[960,128]{1,0:T(8,128)(2,1)S(1)}, u32[]{:S(2)}, u32[]{:S(2)}) collective-permute-start(bf16[960,128]{1,0:T(8,128)(2,1)} %get-tuple-element.580), channel_id=1, source_target_pairs={{0,0},{1,16},{2,2},{3,18},{4,4},{5,20},{6,6},{7,22},{8,8},{9,24},{... | collective-permute-start | bytes 737288 | tf_op jit(solution)/shard_map/ppermute | solution.py:41
  262.9 9.3 %collective-permute-start.57 = (bf16[96,640]{1,0:T(8,128)(2,1)S(1)}, bf16[96,640]{1,0:T(8,128)(2,1)S(1)}, u32[]{:S(2)}, u32[]{:S(2)}) collective-permute-start(bf16[96,640]{1,0:T(8,128)(2,1)S(1)} %get-tuple-element.660), channel_id=1, source_target_pairs={{0,5},{1,4},{2,7},{3,6},{4,1},{5,0},{6,3},{7,2},{8,13},{9,12},{10,... | collective-permute-start | bytes 368648 | tf_op jit(solution)/shard_map/ppermute | solution.py:32
  263.6 8.6 %collective-permute-start.58 = (bf16[96,640]{1,0:T(8,128)(2,1)S(1)}, bf16[96,640]{1,0:T(8,128)(2,1)S(1)}, u32[]{:S(2)}, u32[]{:S(2)}) collective-permute-start(bf16[96,640]{1,0:T(8,128)(2,1)S(1)} %get-tuple-element.661), channel_id=1, source_target_pairs={{0,9},{1,8},{2,11},{3,10},{4,13},{5,12},{6,15},{7,14},{8,1},{9,0},... | collective-permute-start | bytes 368648 | tf_op jit(solution)/shard_map/ppermute | solution.py:32
  296.1 16.0 %collective-permute-start.62 = (bf16[2,2,4,120,640]{4,3,2,1,0:T(8,128)(2,1)S(1)}, bf16[2,2,4,120,640]{4,3,2,1,0:T(8,128)(2,1)S(1)}, u32[]{:S(2)}, u32[]{:S(2)}) collective-permute-start(bf16[2,2,4,120,640]{4,3,2,1,0:T(8,128)(2,1)S(1)} %get-tuple-element.699), channel_id=1, source_target_pairs={{0,2},{1,3},{2,0},{3,1},{4,6},{5,7},{6,4},{7,5},{8,10},{9,11},{10,... | collective-permute-start | bytes 7372808 | tf_op jit(solution)/shard_map/ppermute | solution.py:32
  296.2 15.9 %collective-permute-start.61 = (bf16[4,80,960]{2,1,0:T(8,128)(2,1)S(1)}, bf16[4,80,960]{2,1,0:T(8,128)(2,1)S(1)}, u32[]{:S(2)}, u32[]{:S(2)}) collective-permute-start(bf16[4,80,960]{2,1,0:T(8,128)(2,1)S(1)} %get-tuple-element.698), channel_id=1, source_target_pairs={{0,1},{1,0},{2,3},{3,2},{4,5},{5,4},{6,7},{7,6},{8,9},{9,8},{10,11... | collective-permute-start | bytes 1843208 | tf_op jit(solution)/shard_map/ppermute | solution.py:32
  312.4 17.7 %collective-permute-start.65 = (bf16[1024,640]{1,0:T(8,128)(2,1)S(1)}, bf16[1024,640]{1,0:T(8,128)(2,1)S(1)}, u32[]{:S(2)}, u32[]{:S(2)}) collective-permute-start(bf16[1024,640]{1,0:T(8,128)(2,1)S(1)} %get-tuple-element.715), channel_id=1, source_target_pairs={{0,2},{1,3},{2,0},{3,1},{4,6},{5,7},{6,4},{7,5},{8,10},{9,11},{10,... | collective-permute-start | bytes 3932168 | tf_op jit(solution)/shard_map/ppermute | solution.py:32
  313.8 16.3 %collective-permute-start.63 = (bf16[4,80,960]{2,1,0:T(8,128)(2,1)S(1)}, bf16[4,80,960]{2,1,0:T(8,128)(2,1)S(1)}, u32[]{:S(2)}, u32[]{:S(2)}) collective-permute-start(bf16[4,80,960]{2,1,0:T(8,128)(2,1)S(1)} %get-tuple-element.713), channel_id=1, source_target_pairs={{0,1},{1,0},{2,3},{3,2},{4,5},{5,4},{6,7},{7,6},{8,9},{9,8},{10,11... | collective-permute-start | bytes 1843208 | tf_op jit(solution)/shard_map/ppermute | solution.py:32
  313.9 16.1 %collective-permute-start.64 = (bf16[4,80,960]{2,1,0:T(8,128)(2,1)S(1)}, bf16[4,80,960]{2,1,0:T(8,128)(2,1)S(1)}, u32[]{:S(2)}, u32[]{:S(2)}) collective-permute-start(bf16[4,80,960]{2,1,0:T(8,128)(2,1)S(1)} %fusion), channel_id=1, source_target_pairs={{0,4},{1,5},{2,6},{3,7},{4,0},{5,1},{6,2},{7,3},{8,12},{9,13},{10,... | collective-permute-start | bytes 1843208 | tf_op jit(solution)/shard_map/ppermute | solution.py:32
  330.3 22.7 %collective-permute-start.73 = (bf16[2,2,4,120,640]{4,3,2,1,0:T(8,128)(2,1)S(1)}, bf16[2,2,4,120,640]{4,3,2,1,0:T(8,128)(2,1)S(1)}, u32[]{:S(2)}, u32[]{:S(2)}) collective-permute-start(bf16[2,2,4,120,640]{4,3,2,1,0:T(8,128)(2,1)S(1)} %get-tuple-element.745), channel_id=1, source_target_pairs={{0,2},{1,3},{2,0},{3,1},{4,6},{5,7},{6,4},{7,5},{8,10},{9,11},{10,... | collective-permute-start | bytes 7372808 | tf_op jit(solution)/shard_map/ppermute | solution.py:32
  334.5 8.8 %collective-permute-start.69 = (bf16[128,640]{1,0:T(8,128)(2,1)S(1)}, bf16[128,640]{1,0:T(8,128)(2,1)S(1)}, u32[]{:S(2)}, u32[]{:S(2)}) collective-permute-start(bf16[128,640]{1,0:T(8,128)(2,1)S(1)} %get-tuple-element.741), channel_id=1, source_target_pairs={{0,13},{1,12},{2,15},{3,14},{4,9},{5,8},{6,11},{7,10},{8,5},{9,4},... | collective-permute-start | bytes 491528 | tf_op jit(solution)/shard_map/ppermute | solution.py:32
  338.0 15.0 %collective-permute-start.70 = (bf16[128,640]{1,0:T(8,128)(2,1)S(1)}, bf16[128,640]{1,0:T(8,128)(2,1)S(1)}, u32[]{:S(2)}, u32[]{:S(2)}) collective-permute-start(bf16[128,640]{1,0:T(8,128)(2,1)S(1)} %get-tuple-element.742), channel_id=1, source_target_pairs={{0,5},{1,4},{2,7},{3,6},{4,1},{5,0},{6,3},{7,2},{8,13},{9,12},{10,... | collective-permute-start | bytes 491528 | tf_op jit(solution)/shard_map/ppermute | solution.py:32
  339.0 14.0 %collective-permute-start.71 = (bf16[128,640]{1,0:T(8,128)(2,1)S(1)}, bf16[128,640]{1,0:T(8,128)(2,1)S(1)}, u32[]{:S(2)}, u32[]{:S(2)}) collective-permute-start(bf16[128,640]{1,0:T(8,128)(2,1)S(1)} %get-tuple-element.743), channel_id=1, source_target_pairs={{0,9},{1,8},{2,11},{3,10},{4,13},{5,12},{6,15},{7,14},{8,1},{9,0},... | collective-permute-start | bytes 491528 | tf_op jit(solution)/shard_map/ppermute | solution.py:32
  340.9 12.1 %collective-permute-start.72 = (bf16[128,640]{1,0:T(8,128)(2,1)S(1)}, bf16[128,640]{1,0:T(8,128)(2,1)S(1)}, u32[]{:S(2)}, u32[]{:S(2)}) collective-permute-start(bf16[128,640]{1,0:T(8,128)(2,1)S(1)} %get-tuple-element.744), channel_id=1, source_target_pairs={{0,12},{1,13},{2,14},{3,15},{4,8},{5,9},{6,10},{7,11},{8,4},{9,5},... | collective-permute-start | bytes 491528 | tf_op jit(solution)/shard_map/ppermute | solution.py:32
  356.0 16.2 %collective-permute-start.74 = (bf16[4,120,640]{2,1,0:T(8,128)(2,1)S(1)}, bf16[4,120,640]{2,1,0:T(8,128)(2,1)S(1)}, u32[]{:S(2)}, u32[]{:S(2)}) collective-permute-start(bf16[4,120,640]{2,1,0:T(8,128)(2,1)S(1)} %get-tuple-element.758), channel_id=1, source_target_pairs={{0,1},{1,0},{2,3},{3,2},{4,5},{5,4},{6,7},{7,6},{8,9},{9,8},{10,11... | collective-permute-start | bytes 1843208 | tf_op jit(solution)/shard_map/ppermute | solution.py:32
  357.3 10.3 %collective-permute-start.75 = (bf16[80,960]{1,0:T(8,128)(2,1)S(1)}, bf16[80,960]{1,0:T(8,128)(2,1)S(1)}, u32[]{:S(2)}, u32[]{:S(2)}) collective-permute-start(bf16[80,960]{1,0:T(8,128)(2,1)S(1)} %get-tuple-element.759), channel_id=1, source_target_pairs={{0,24},{1,25},{2,26},{3,27},{4,28},{5,29},{6,30},{7,31},{8,16},{9,... | collective-permute-start | bytes 460808 | tf_op jit(solution)/shard_map/ppermute | solution.py:32
  358.1 14.2 %collective-permute-start.76 = (bf16[80,960]{1,0:T(8,128)(2,1)S(1)}, bf16[80,960]{1,0:T(8,128)(2,1)S(1)}, u32[]{:S(2)}, u32[]{:S(2)}) collective-permute-start(bf16[80,960]{1,0:T(8,128)(2,1)S(1)} %get-tuple-element.760), channel_id=1, source_target_pairs={{0,16},{1,17},{2,18},{3,19},{4,20},{5,21},{6,22},{7,23},{8,24},{9,... | collective-permute-start | bytes 460808 | tf_op jit(solution)/shard_map/ppermute | solution.py:32
  358.1 14.2 %collective-permute-start.77 = (bf16[80,960]{1,0:T(8,128)(2,1)S(1)}, bf16[80,960]{1,0:T(8,128)(2,1)S(1)}, u32[]{:S(2)}, u32[]{:S(2)}) collective-permute-start(bf16[80,960]{1,0:T(8,128)(2,1)S(1)} %get-tuple-element.761), channel_id=1, source_target_pairs={{0,8},{1,9},{2,10},{3,11},{4,12},{5,13},{6,14},{7,15},{8,0},{9,1},... | collective-permute-start | bytes 460808 | tf_op jit(solution)/shard_map/ppermute | solution.py:32
  372.5 20.6 %collective-permute-start.83 = (bf16[2,2,4,120,640]{4,3,2,1,0:T(8,128)(2,1)S(1)}, bf16[2,2,4,120,640]{4,3,2,1,0:T(8,128)(2,1)S(1)}, u32[]{:S(2)}, u32[]{:S(2)}) collective-permute-start(bf16[2,2,4,120,640]{4,3,2,1,0:T(8,128)(2,1)S(1)} %get-tuple-element.789), channel_id=1, source_target_pairs={{0,2},{1,3},{2,0},{3,1},{4,6},{5,7},{6,4},{7,5},{8,10},{9,11},{10,... | collective-permute-start | bytes 7372808 | tf_op jit(solution)/shard_map/ppermute | solution.py:32
  376.0 17.1 %collective-permute-start.78 = (bf16[4,120,640]{2,1,0:T(8,128)(2,1)S(1)}, bf16[4,120,640]{2,1,0:T(8,128)(2,1)S(1)}, u32[]{:S(2)}, u32[]{:S(2)}) collective-permute-start(bf16[4,120,640]{2,1,0:T(8,128)(2,1)S(1)} %get-tuple-element.784), channel_id=1, source_target_pairs={{0,1},{1,0},{2,3},{3,2},{4,5},{5,4},{6,7},{7,6},{8,9},{9,8},{10,11... | collective-permute-start | bytes 1843208 | tf_op jit(solution)/shard_map/ppermute | solution.py:32
  376.2 16.9 %collective-permute-start.79 = (bf16[4,120,640]{2,1,0:T(8,128)(2,1)S(1)}, bf16[4,120,640]{2,1,0:T(8,128)(2,1)S(1)}, u32[]{:S(2)}, u32[]{:S(2)}) collective-permute-start(bf16[4,120,640]{2,1,0:T(8,128)(2,1)S(1)} %fusion.11), channel_id=1, source_target_pairs={{0,4},{1,5},{2,6},{3,7},{4,0},{5,1},{6,2},{7,3},{8,12},{9,13},{10,... | collective-permute-start | bytes 1843208 | tf_op jit(solution)/shard_map/ppermute | solution.py:32
  378.6 10.7 %collective-permute-start.81 = (bf16[80,960]{1,0:T(8,128)(2,1)S(1)}, bf16[80,960]{1,0:T(8,128)(2,1)S(1)}, u32[]{:S(2)}, u32[]{:S(2)}) collective-permute-start(bf16[80,960]{1,0:T(8,128)(2,1)S(1)} %fusion.14), channel_id=1, source_target_pairs={{0,16},{1,17},{2,18},{3,19},{4,20},{5,21},{6,22},{7,23},{8,24},{9,... | collective-permute-start | bytes 460808 | tf_op jit(solution)/shard_map/ppermute | solution.py:32
  381.6 11.6 %collective-permute-start.82 = (bf16[80,960]{1,0:T(8,128)(2,1)S(1)}, bf16[80,960]{1,0:T(8,128)(2,1)S(1)}, u32[]{:S(2)}, u32[]{:S(2)}) collective-permute-start(bf16[80,960]{1,0:T(8,128)(2,1)S(1)} %fusion.14), channel_id=1, source_target_pairs={{0,8},{1,9},{2,10},{3,11},{4,12},{5,13},{6,14},{7,15},{8,0},{9,1},... | collective-permute-start | bytes 460808 | tf_op jit(solution)/shard_map/ppermute | solution.py:32
  393.5 16.0 %collective-permute-start.84 = (bf16[4,120,640]{2,1,0:T(8,128)(2,1)S(1)}, bf16[4,120,640]{2,1,0:T(8,128)(2,1)S(1)}, u32[]{:S(2)}, u32[]{:S(2)}) collective-permute-start(bf16[4,120,640]{2,1,0:T(8,128)(2,1)S(1)} %get-tuple-element.800), channel_id=1, source_target_pairs={{0,1},{1,0},{2,3},{3,2},{4,5},{5,4},{6,7},{7,6},{8,9},{9,8},{10,11... | collective-permute-start | bytes 1843208 | tf_op jit(solution)/shard_map/ppermute | solution.py:32
  393.6 16.0 %collective-permute-start.88 = (bf16[4,80,960]{2,1,0:T(8,128)(2,1)S(1)}, bf16[4,80,960]{2,1,0:T(8,128)(2,1)S(1)}, u32[]{:S(2)}, u32[]{:S(2)}) collective-permute-start(bf16[4,80,960]{2,1,0:T(8,128)(2,1)S(1)} %get-tuple-element.804), channel_id=1, source_target_pairs={{0,4},{1,5},{2,6},{3,7},{4,0},{5,1},{6,2},{7,3},{8,12},{9,13},{10,... | collective-permute-start | bytes 1843208 | tf_op jit(solution)/shard_map/ppermute | solution.py:32
  396.1 13.5 %collective-permute-start.86 = (bf16[120,640]{1,0:T(8,128)(2,1)S(1)}, bf16[120,640]{1,0:T(8,128)(2,1)S(1)}, u32[]{:S(2)}, u32[]{:S(2)}) collective-permute-start(bf16[120,640]{1,0:T(8,128)(2,1)S(1)} %get-tuple-element.802), channel_id=1, source_target_pairs={{0,16},{1,17},{2,18},{3,19},{4,20},{5,21},{6,22},{7,23},{8,24},{9,... | collective-permute-start | bytes 460808 | tf_op jit(solution)/shard_map/ppermute | solution.py:32
  396.1 13.5 %collective-permute-start.87 = (bf16[120,640]{1,0:T(8,128)(2,1)S(1)}, bf16[120,640]{1,0:T(8,128)(2,1)S(1)}, u32[]{:S(2)}, u32[]{:S(2)}) collective-permute-start(bf16[120,640]{1,0:T(8,128)(2,1)S(1)} %get-tuple-element.803), channel_id=1, source_target_pairs={{0,8},{1,9},{2,10},{3,11},{4,12},{5,13},{6,14},{7,15},{8,0},{9,1},... | collective-permute-start | bytes 460808 | tf_op jit(solution)/shard_map/ppermute | solution.py:32
  410.0 18.8 %collective-permute-start.94 = (bf16[2,4,80,960]{3,2,1,0:T(8,128)(2,1)S(1)}, bf16[2,4,80,960]{3,2,1,0:T(8,128)(2,1)S(1)}, u32[]{:S(2)}, u32[]{:S(2)}) collective-permute-start(bf16[2,4,80,960]{3,2,1,0:T(8,128)(2,1)S(1)} %pad_maximum_fusion.near_ref), channel_id=1, source_target_pairs={{0,2},{1,3},{2,0},{3,1},{4,6},{5,7},{6,4},{7,5},{8,10},{9,11},{10,... | collective-permute-start | bytes 3686408 | tf_op jit(solution)/shard_map/ppermute | solution.py:32
  413.7 15.1 %collective-permute-start.89 = (bf16[4,120,640]{2,1,0:T(8,128)(2,1)S(1)}, bf16[4,120,640]{2,1,0:T(8,128)(2,1)S(1)}, u32[]{:S(2)}, u32[]{:S(2)}) collective-permute-start(bf16[4,120,640]{2,1,0:T(8,128)(2,1)S(1)} %get-tuple-element.812), channel_id=1, source_target_pairs={{0,1},{1,0},{2,3},{3,2},{4,5},{5,4},{6,7},{7,6},{8,9},{9,8},{10,11... | collective-permute-start | bytes 1843208 | tf_op jit(solution)/shard_map/ppermute | solution.py:32
  413.8 15.0 %collective-permute-start.90 = (bf16[4,120,640]{2,1,0:T(8,128)(2,1)S(1)}, bf16[4,120,640]{2,1,0:T(8,128)(2,1)S(1)}, u32[]{:S(2)}, u32[]{:S(2)}) collective-permute-start(bf16[4,120,640]{2,1,0:T(8,128)(2,1)S(1)} %fusion.5), channel_id=1, source_target_pairs={{0,4},{1,5},{2,6},{3,7},{4,0},{5,1},{6,2},{7,3},{8,12},{9,13},{10,... | collective-permute-start | bytes 1843208 | tf_op jit(solution)/shard_map/ppermute | solution.py:32
  415.2 10.7 %collective-permute-start.92 = (bf16[120,640]{1,0:T(8,128)(2,1)S(1)}, bf16[120,640]{1,0:T(8,128)(2,1)S(1)}, u32[]{:S(2)}, u32[]{:S(2)}) collective-permute-start(bf16[120,640]{1,0:T(8,128)(2,1)S(1)} %fusion.23), channel_id=1, source_target_pairs={{0,16},{1,17},{2,18},{3,19},{4,20},{5,21},{6,22},{7,23},{8,24},{9,... | collective-permute-start | bytes 460808 | tf_op jit(solution)/shard_map/ppermute | solution.py:32
  429.3 15.8 %collective-permute-start.95 = (bf16[4,120,640]{2,1,0:T(8,128)(2,1)S(1)}, bf16[4,120,640]{2,1,0:T(8,128)(2,1)S(1)}, u32[]{:S(2)}, u32[]{:S(2)}) collective-permute-start(bf16[4,120,640]{2,1,0:T(8,128)(2,1)S(1)} %get-tuple-element.826), channel_id=1, source_target_pairs={{0,1},{1,0},{2,3},{3,2},{4,5},{5,4},{6,7},{7,6},{8,9},{9,8},{10,11... | collective-permute-start | bytes 1843208 | tf_op jit(solution)/shard_map/ppermute | solution.py:32
  430.5 14.6 %collective-permute-start.99 = (bf16[4,120,640]{2,1,0:T(8,128)(2,1)S(1)}, bf16[4,120,640]{2,1,0:T(8,128)(2,1)S(1)}, u32[]{:S(2)}, u32[]{:S(2)}) collective-permute-start(bf16[4,120,640]{2,1,0:T(8,128)(2,1)S(1)} %get-tuple-element.830), channel_id=1, source_target_pairs={{0,4},{1,5},{2,6},{3,7},{4,0},{5,1},{6,2},{7,3},{8,12},{9,13},{10,... | collective-permute-start | bytes 1843208 | tf_op jit(solution)/shard_map/ppermute | solution.py:32
  433.6 11.4 %collective-permute-start.97 = (bf16[120,640]{1,0:T(8,128)(2,1)S(1)}, bf16[120,640]{1,0:T(8,128)(2,1)S(1)}, u32[]{:S(2)}, u32[]{:S(2)}) collective-permute-start(bf16[120,640]{1,0:T(8,128)(2,1)S(1)} %get-tuple-element.828), channel_id=1, source_target_pairs={{0,16},{1,17},{2,18},{3,19},{4,20},{5,21},{6,22},{7,23},{8,24},{9,... | collective-permute-start | bytes 460808 | tf_op jit(solution)/shard_map/ppermute | solution.py:32
  433.7 11.4 %collective-permute-start.98 = (bf16[120,640]{1,0:T(8,128)(2,1)S(1)}, bf16[120,640]{1,0:T(8,128)(2,1)S(1)}, u32[]{:S(2)}, u32[]{:S(2)}) collective-permute-start(bf16[120,640]{1,0:T(8,128)(2,1)S(1)} %get-tuple-element.829), channel_id=1, source_target_pairs={{0,8},{1,9},{2,10},{3,11},{4,12},{5,13},{6,14},{7,15},{8,0},{9,1},... | collective-permute-start | bytes 460808 | tf_op jit(solution)/shard_map/ppermute | solution.py:32
  445.5 18.0 %collective-permute-start.105 = (bf16[2,4,120,640]{3,2,1,0:T(8,128)(2,1)S(1)}, bf16[2,4,120,640]{3,2,1,0:T(8,128)(2,1)S(1)}, u32[]{:S(2)}, u32[]{:S(2)}) collective-permute-start(bf16[2,4,120,640]{3,2,1,0:T(8,128)(2,1)S(1)} %pad_maximum_fusion.1.near_ref), channel_id=1, source_target_pairs={{0,2},{1,3},{2,0},{3,1},{4,6},{5,7},{6,4},{7,5},{8,10},{9,11},{10,... | collective-permute-start | bytes 3686408 | tf_op jit(solution)/shard_map/ppermute | solution.py:32
  447.5 15.6 %collective-permute-start.100 = (bf16[4,120,640]{2,1,0:T(8,128)(2,1)S(1)}, bf16[4,120,640]{2,1,0:T(8,128)(2,1)S(1)}, u32[]{:S(2)}, u32[]{:S(2)}) collective-permute-start(bf16[4,120,640]{2,1,0:T(8,128)(2,1)S(1)} %get-tuple-element.847), channel_id=1, source_target_pairs={{0,1},{1,0},{2,3},{3,2},{4,5},{5,4},{6,7},{7,6},{8,9},{9,8},{10,11... | collective-permute-start | bytes 1843208 | tf_op jit(solution)/shard_map/ppermute | solution.py:32
  448.4 15.1 %collective-permute-start.101 = (bf16[4,120,640]{2,1,0:T(8,128)(2,1)S(1)}, bf16[4,120,640]{2,1,0:T(8,128)(2,1)S(1)}, u32[]{:S(2)}, u32[]{:S(2)}) collective-permute-start(bf16[4,120,640]{2,1,0:T(8,128)(2,1)S(1)} %fusion.8), channel_id=1, source_target_pairs={{0,4},{1,5},{2,6},{3,7},{4,0},{5,1},{6,2},{7,3},{8,12},{9,13},{10,... | collective-permute-start | bytes 1843208 | tf_op jit(solution)/shard_map/ppermute | solution.py:32
  452.6 10.4 %collective-permute-start.103 = (bf16[120,640]{1,0:T(8,128)(2,1)S(1)}, bf16[120,640]{1,0:T(8,128)(2,1)S(1)}, u32[]{:S(2)}, u32[]{:S(2)}) collective-permute-start(bf16[120,640]{1,0:T(8,128)(2,1)S(1)} %fusion.20), channel_id=1, source_target_pairs={{0,16},{1,17},{2,18},{3,19},{4,20},{5,21},{6,22},{7,23},{8,24},{9,... | collective-permute-start | bytes 460808 | tf_op jit(solution)/shard_map/ppermute | solution.py:32
  463.9 15.0 %collective-permute-start.110 = (bf16[4,120,640]{2,1,0:T(8,128)(2,1)S(1)}, bf16[4,120,640]{2,1,0:T(8,128)(2,1)S(1)}, u32[]{:S(2)}, u32[]{:S(2)}) collective-permute-start(bf16[4,120,640]{2,1,0:T(8,128)(2,1)S(1)} %get-tuple-element.865), channel_id=1, source_target_pairs={{0,4},{1,5},{2,6},{3,7},{4,0},{5,1},{6,2},{7,3},{8,12},{9,13},{10,... | collective-permute-start | bytes 1843208 | tf_op jit(solution)/shard_map/ppermute | solution.py:32
  466.5 12.4 %collective-permute-start.108 = (bf16[120,640]{1,0:T(8,128)(2,1)S(1)}, bf16[120,640]{1,0:T(8,128)(2,1)S(1)}, u32[]{:S(2)}, u32[]{:S(2)}) collective-permute-start(bf16[120,640]{1,0:T(8,128)(2,1)S(1)} %get-tuple-element.863), channel_id=1, source_target_pairs={{0,16},{1,17},{2,18},{3,19},{4,20},{5,21},{6,22},{7,23},{8,24},{9,... | collective-permute-start | bytes 460808 | tf_op jit(solution)/shard_map/ppermute | solution.py:32
  466.5 12.4 %collective-permute-start.109 = (bf16[120,640]{1,0:T(8,128)(2,1)S(1)}, bf16[120,640]{1,0:T(8,128)(2,1)S(1)}, u32[]{:S(2)}, u32[]{:S(2)}) collective-permute-start(bf16[120,640]{1,0:T(8,128)(2,1)S(1)} %get-tuple-element.864), channel_id=1, source_target_pairs={{0,8},{1,9},{2,10},{3,11},{4,12},{5,13},{6,14},{7,15},{8,0},{9,1},... | collective-permute-start | bytes 460808 | tf_op jit(solution)/shard_map/ppermute | solution.py:32
  479.1 16.9 %collective-permute-start.114 = (bf16[2,4,120,640]{3,2,1,0:T(8,128)(2,1)S(1)}, bf16[2,4,120,640]{3,2,1,0:T(8,128)(2,1)S(1)}, u32[]{:S(2)}, u32[]{:S(2)}) collective-permute-start(bf16[2,4,120,640]{3,2,1,0:T(8,128)(2,1)S(1)} %pad_maximum_fusion.2.near_ref), channel_id=1, source_target_pairs={{0,2},{1,3},{2,0},{3,1},{4,6},{5,7},{6,4},{7,5},{8,10},{9,11},{10,... | collective-permute-start | bytes 3686408 | tf_op jit(solution)/shard_map/ppermute | solution.py:32
  483.2 12.8 %collective-permute-start.112 = (bf16[120,640]{1,0:T(8,128)(2,1)S(1)}, bf16[120,640]{1,0:T(8,128)(2,1)S(1)}, u32[]{:S(2)}, u32[]{:S(2)}) collective-permute-start(bf16[120,640]{1,0:T(8,128)(2,1)S(1)} %fusion.17), channel_id=1, source_target_pairs={{0,16},{1,17},{2,18},{3,19},{4,20},{5,21},{6,22},{7,23},{8,24},{9,... | collective-permute-start | bytes 460808 | tf_op jit(solution)/shard_map/ppermute | solution.py:32
  483.2 12.8 %collective-permute-start.113 = (bf16[120,640]{1,0:T(8,128)(2,1)S(1)}, bf16[120,640]{1,0:T(8,128)(2,1)S(1)}, u32[]{:S(2)}, u32[]{:S(2)}) collective-permute-start(bf16[120,640]{1,0:T(8,128)(2,1)S(1)} %fusion.17), channel_id=1, source_target_pairs={{0,8},{1,9},{2,10},{3,11},{4,12},{5,13},{6,14},{7,15},{8,0},{9,1},... | collective-permute-start | bytes 460808 | tf_op jit(solution)/shard_map/ppermute | solution.py:32
  496.2 16.7 %collective-permute-start.116 = (bf16[4,120,640]{2,1,0:T(8,128)(2,1)S(1)}, bf16[4,120,640]{2,1,0:T(8,128)(2,1)S(1)}, u32[]{:S(2)}, u32[]{:S(2)}) collective-permute-start(bf16[4,120,640]{2,1,0:T(8,128)(2,1)S(1)} %get-tuple-element.889), channel_id=1, source_target_pairs={{0,4},{1,5},{2,6},{3,7},{4,0},{5,1},{6,2},{7,3},{8,12},{9,13},{10,... | collective-permute-start | bytes 1843208 | tf_op jit(solution)/shard_map/ppermute | solution.py:32
  496.9 16.0 %collective-permute-start.118 = (bf16[960,128]{1,0:T(8,128)(2,1)S(1)}, bf16[960,128]{1,0:T(8,128)(2,1)S(1)}, u32[]{:S(2)}, u32[]{:S(2)}) collective-permute-start(bf16[960,128]{1,0:T(8,128)(2,1)S(1)} %copy-done.50), channel_id=1, source_target_pairs={{0,0},{1,16},{2,2},{3,18},{4,4},{5,20},{6,6},{7,22},{8,8},{9,24},{... | collective-permute-start | bytes 737288 | tf_op jit(solution)/shard_map/ppermute | solution.py:41
  (109 other events, 855.4 us)

commit v4 on v3

--- a/solution.py
+++ b/solution.py
@@ -858,16 +858,21 @@
         at += ref.shape[0]
 
 
-def put_blocks(value, x_of, coords, ref, per_row):
-    y, _, x, z = coords
-    depth = ref.shape[-2]
+SPARE = 8
+
+
+def put_blocks(value, x_of, coords, ref, spare=None):
+    y, _, _, z = coords
+    depth = value.shape[0] // 8
     for ya in range(2):
-        for xa in range(2) if per_row else (None,):
-            for za in range(4):
-                row = (ya * (2 if per_row else 1) + (xa or 0)) * 4 + za
-                ref[y ^ ya, (x ^ xa) if per_row else x_of, z ^ za] = value[
-                    row * depth : (row + 1) * depth
-                ].astype(BF)
+        for za in range(4):
+            row = (ya * 4 + za) * depth
+            block = value[row : row + depth].astype(BF)
+            if spare is None:
+                ref[y ^ ya, x_of, z ^ za] = block
+            else:
+                ref[y ^ ya, x_of, z ^ za, :depth] = block
+                ref[y ^ ya, x_of, z ^ za, depth:] = spare(ya, za).astype(BF)
 
 
 def grad_cols_kernel(n_steps, coords_ref, *args):
@@ -884,7 +889,7 @@
         def body(rx, carry, far=far, ref=ref):
             start = pl.multiple_of(((c ^ far) * 2 + (x ^ rx)) * block, 128)
             value = mm(l_scr[...], r_scr[:, pl.ds(start, block)], TN)
-            put_blocks(value, rx, coords, ref, False)
+            put_blocks(value, rx, coords, ref)
             return carry
 
         lax.fori_loop(0, 2, body, 0)
@@ -914,7 +919,7 @@
         lax.fori_loop(0, 2, body, 0)
 
 
-def grad_mixed_kernel(n_steps, coords_ref, *args):
+def grad_mixed_kernel(n_steps, coords_ref, sums_ref, *args):
     groups = []
     for _ in range(4):
         groups.append(args[:n_steps])
@@ -942,16 +947,24 @@
                     axis=1,
                 )
 
+            def spare(ya, za, first=ca == 0 and xa == 0):
+                if not first or za:
+                    return jnp.zeros((SPARE, block), F32)
+                half = width // 2
+                rows = sums_ref[:, ya * half : (ya + 1) * half]
+                rows = jnp.concatenate([rows, jnp.zeros((2, block - half), F32)], axis=1)
+                return jnp.concatenate([rows, jnp.zeros((SPARE - 2, block), F32)], axis=0)
+
             @pl.when(c == ca)
-            def _(xa=xa):
-                put_blocks(val_scr[...], x ^ xa, coords, keep_ref, False)
+            def _(xa=xa, spare=spare):
+                put_blocks(val_scr[...], x ^ xa, coords, keep_ref, spare)
 
             @pl.when(c != ca)
-            def _(xa=xa):
-                put_blocks(val_scr[...], x ^ xa, coords, send_ref, False)
-
-
-def grad_call(kind, coords, groups):
+            def _(xa=xa, spare=spare):
+                put_blocks(val_scr[...], x ^ xa, coords, send_ref, spare)
+
+
+def grad_call(kind, coords, groups, sums=None):
     n_steps = len(groups[0])
     rows = sum(a.shape[0] for a in groups[0])
     width, cols = groups[0][0].shape[1], groups[1][0].shape[1]
@@ -962,10 +975,12 @@
         kernel, block = grad_cols_kernel, (width // 8, cols // 4)
     else:
         total = sum(g[0].shape[1] for g in groups[2:])
-        kernel, block = grad_mixed_kernel, (width // 8, total // 4)
+        kernel, block = grad_mixed_kernel, (width // 8 + SPARE, total // 4)
         scratch += [pltpu.VMEM((width, block[1]), F32)]
     out = shaped((2, 2, 4) + block, BF)
     ins = [a for g in groups for a in g]
+    if sums is not None:
+        ins = [sums, *ins]
     return pl.pallas_call(
         functools.partial(kernel, n_steps),
         name=f"grad_{kind}",
@@ -979,23 +994,29 @@
 
 
 def place_cols_kernel(coords_ref, near_ref, far_ref, *outs):
-    _, c, x, _ = read_coords(coords_ref)
+    _, c, x, z = read_coords(coords_ref)
     block = near_ref.shape[-1]
     mixed = len(outs) > 1
-    target = outs[4] if mixed else outs[0]
+    target = outs[5] if mixed else outs[0]
+    depth = target.shape[0]
     for far, ref in ((0, near_ref), (1, far_ref)):
         for rx in range(2):
             cols = pl.ds(pl.multiple_of(((c ^ far) * 2 + (x ^ rx)) * block, 128), block)
-            target[:, cols] = ref[rx, 0].astype(F32)
+            target[:, cols] = ref[rx, 0, :depth].astype(F32)
     if mixed:
-        q_ref, k_ref, o_ref, v_ref, _, k_scr, v_scr = outs
+        q_ref, k_ref, o_ref, v_ref, gains_ref, _, k_scr, v_scr = outs
         width, kv_width = q_ref.shape[1], k_ref.shape[0]
-        depth = q_ref.shape[0]
-        rows = pl.ds(pl.multiple_of((coords_ref[3] ^ pl.program_id(0)) * depth, 8), depth)
+        rows = pl.ds(pl.multiple_of((z ^ pl.program_id(0)) * depth, 8), depth)
         q_ref[...] = target[:, :width]
         k_scr[rows, :] = target[:, width : width + kv_width]
         o_ref[...] = target[:, width + kv_width : 2 * width + kv_width]
         v_scr[rows, :] = target[:, 2 * width + kv_width :]
+        for far, ref in ((0, near_ref), (1, far_ref)):
+
+            @pl.when((z == pl.program_id(0)) & (c == far))
+            def _(ref=ref):
+                spare = ref[x, 0, depth:].astype(F32)
+                gains_ref[...] = spare[:2, : gains_ref.shape[1]]
 
         @pl.when(pl.program_id(0) == 3)
         def _():
@@ -1035,7 +1056,9 @@
         scratch = [pltpu.VMEM((8 * depth, block), F32)]
     else:
         kernel, grid = place_cols_kernel, (4,)
-        source = pl.BlockSpec((2, 1, depth, block), lambda i, k: (0, i, 0, 0))
+        source = pl.BlockSpec((2, 1, *near.shape[-2:]), lambda i, k: (0, i, 0, 0))
+        if len(widths) > 1:
+            depth -= SPARE
         straight = lambda w: (
             stored((4 * depth, w), F32), pl.BlockSpec((depth, w), lambda i, k: (k[3] ^ i, 0))
         )
@@ -1046,6 +1069,8 @@
             *((turned if i % 2 else straight)(w) for i, w in enumerate(widths)), strict=True
         )
         if len(outs) > 1:
+            outs += (stored((2, 4 * depth), F32),)
+            targets += (pl.BlockSpec((2, 4 * depth), lambda i, k: (0, 0)),)
             scratch = [pltpu.VMEM((depth, 4 * block), F32)]
             scratch += [pltpu.VMEM((4 * depth, w), F32) for w in widths[1::2]]
     return pl.pallas_call(
@@ -1072,19 +1097,15 @@
     return values[:count], values[count:]
 
 
-def gather_keys(kv, order, near, beside=((), ()), meanwhile=([], [])):
+def gather_keys(kv, order, near, meanwhile=([], [])):
     if not near:
         whole = lax.all_gather(kv, "ctx", axis=0, tiled=True)
         half = whole.shape[0] // 2
         return whole[:half], whole[half:]
     kv = order.take(kv)
     hops = [hop(kv, m) for m in (X_BIT, Y_BIT, Z1_BIT, X_BIT | Y_BIT | Z1_BIT)]
-    for start in beside[0]:
-        start()
     (by_x, by_y, by_z, across), meanwhile[0][:] = split_list(order.all(*hops, *meanwhile[0]), 4)
     hops = [hop(by_x, Y_BIT), hop(by_y, Z1_BIT), hop(by_z, X_BIT)]
-    for start in beside[1]:
-        start()
     hops, meanwhile[1][:] = split_list(order.all(*hops, *meanwhile[1]), 3)
     part = stack_call([kv, by_x, by_y, by_z, across, *hops])
     return part, order.take(hop(part, C_BIT))
@@ -1134,8 +1155,16 @@
     return lax.dynamic_slice_in_dim(value, index * size, size, 1)
 
 
-def spread(mine):
-    return mine, hop(mine, X_BIT), hop(mine, Z1_BIT), hop(mine, X_BIT | Z1_BIT)
+class Share:
+    def __init__(self, mine):
+        self.mine = mine
+
+    def sends(self, turn):
+        return [(self.mine, mask) for mask in (X_BIT | Z1_BIT, X_BIT, Z1_BIT)]
+
+    def got(self, turn, values):
+        across, by_x, by_z = values
+        self.result = [self.mine, by_x, by_z, across]
 
 
 def pair_sum(keep, send, near):
@@ -1188,17 +1217,24 @@
             self.result = (self.total, *values)
 
 
-class RunningSum:
-    rounds = 5
-
-    def __init__(self, value):
-        self.result = value
-
+class BothWays(BlockSums):
     def sends(self, turn):
-        return [(self.result, (X_BIT, C_BIT, Y_BIT, Z1_BIT, Z2_BIT)[turn])]
+        if turn == 0:
+            return [(self.total[1, :, :2], Y_BIT), (self.total[:, 1, 2:], X_BIT)]
+        if turn == 1:
+            return [(self.first[1], X_BIT), (self.second[1], Y_BIT)]
+        return super().sends(turn)
 
     def got(self, turn, values):
-        self.result = self.result + values[0]
+        if turn == 0:
+            self.first = low_sum(self.total[0, :, :2], values[0])
+            self.second = low_sum(self.total[:, 0, 2:], values[1])
+        elif turn == 1:
+            self.total = jnp.concatenate(
+                [low_sum(self.first[0], values[0]), low_sum(self.second[0], values[1])]
+            )
+        else:
+            super().got(turn, values)
 
 
 class Move:
@@ -1273,15 +1309,14 @@
         beyond = hop(gains, Y_BIT)
         quad = x * 2 + (z & 1)
         own_down = w_down.T
-        fetched, cut_gate, cut_up, cut_out, cut_down = order.take(
+        fetched, cut_pair, cut_out, cut_down = order.take(
             fetched,
-            *(cut_cols(cut_rows(w, c, 2), quad, 4) for w in (w_gate, w_up)),
+            jnp.concatenate([cut_cols(cut_rows(w, c, 2), quad, 4) for w in (w_gate, w_up)], axis=0),
             cut_rows(w_out, c, 2),
             cut_rows(own_down, c, 2),
         )
         far = hop(fetched, C_BIT)
-        gate_mine, up_mine = hop(cut_gate, Y_BIT), hop(cut_up, Y_BIT)
-        out_mine, down_mine = hop(cut_out, Y_BIT), hop(cut_down, Y_BIT)
+        pair_mine, out_mine = hop(cut_pair, Y_BIT), hop(cut_out, Y_BIT)
         far, tok, beyond = order.take(far, tok, beyond)
         plan = tok[tok_local:, : plan.shape[1]].astype(jnp.int32)
         tok = tok[:tok_local]
@@ -1308,12 +1343,12 @@
                 ],
             )
 
-        def in_parts(own, mine, other):
+        def in_parts(own, mine, other, which):
             wide = mine.shape[1]
             groups = []
             for j in range(FF_CHUNKS):
                 column = lambda *k, j=j: part_of(j, k) * wide
-                block = lambda *k, j=j: (j * depth, 0)
+                block = lambda *k, j=j: ((2 * j + which) * depth, 0)
                 groups.append(
                     [
                         (0, half, wide,
@@ -1328,22 +1363,13 @@
             return Weight((2 * half, own.shape[1]), [own, mine, other], groups)
 
         (weight_qkv,) = join_call(coords, (in_rows(own_qkv, fetched, far),))
-        state, marks = {}, {}
-
-        def start_gate():
-            state["gate"] = spread(order.take(gate_mine))
-
-        def start_up():
-            state["up"] = spread(order.take(up_mine))
-
-        beside = ((start_gate,), (start_up,))
-
-        def fetch_rest():
-            gate = stack_call(order.take(*state["gate"]))
-            out, down = order.take(out_mine, down_mine)
-            fars = [hop(v, C_BIT) for v in (gate, out, down)]
-            up = stack_call(order.take(*state["up"]))
-            gate_far, out_far, down_far, up_far = order.take(*fars, hop(up, C_BIT))
+        marks = {}
+
+        def fetch_rest(pair, out, down):
+            pair = stack_call(pair)
+            shared = [Hop(v, C_BIT) for v in (pair, out, down)]
+            wave(order, [(s, 0) for s in shared])
+            pair_far, out_far, down_far = (s.result for s in shared)
             wide = own_down.shape[1]
             weight_d = Weight(
                 (width, 2 * wide),
@@ -1360,8 +1386,8 @@
                 coords,
                 (
                     in_rows(w_out, out, out_far),
-                    in_parts(w_gate, gate, gate_far),
-                    in_parts(w_up, up, up_far),
+                    in_parts(w_gate, pair, pair_far, 0),
+                    in_parts(w_up, pair, pair_far, 1),
                     weight_d,
                 ),
             )
@@ -1374,7 +1400,7 @@
             one_piece(whole(w_out)), in_columns(whole(w_gate)), in_columns(whole(w_up)),
             one_piece(whole(w_down).T),
         )
-        beside, fetch_rest = ((), ()), lambda: far_weights
+        fetch_rest = lambda: far_weights
     gain1, gain2 = (g.astype(F32) for g in gains)
 
     per_device = tok_local // BLK
@@ -1424,8 +1450,10 @@
     heights = []
     for step in range(3):
         if near and step == 0:
-            waits = (marks["places"], marks["tables"])
-            part_a, part_b = gather_keys(kv, order, near, beside, waits)
+            waits = ([*marks["places"], pair_mine], [*marks["tables"], out_mine])
+            part_a, part_b = gather_keys(kv, order, near, waits)
+            *marks["places"], pair_mine = waits[0]
+            *marks["tables"], out_mine = waits[1]
         else:
             part_a, part_b = gather_keys(kv, order, near)
         if near and step == 1:
@@ -1433,16 +1461,17 @@
         firsts.append(first_in)
         next_rows = (cap_mid, cap_last, tok_local)[step]
         attention = (query, part_a, part_b, key_places[step], key_live[step], query_places[step], prompt)
-        weights, mixed = attend_call(*attention)
-        if step == 0:
-            mixed = order.take(mixed)
+        if near and step == 0:
+            pair, down_mine = Share(pair_mine), Hop(cut_down, Y_BIT)
+            weights, mixed = wave(
+                order, [(down_mine, 0), (pair, 0)], lambda *a: attend_call(*a, prompt), attention[:-1]
+            )
+            dense_weights = fetch_rest(pair.result, out_mine, down_mine.result)
+            sel_own, live2_own, live3_own = marks["places"][6:]
+            tables[1:] = [marks["tables"][:2], marks["tables"][2:]]
+        elif step == 0:
+            weights, mixed = attend_call(*attention)
             dense_weights = fetch_rest()
-            if near:
-                sel_own, live2_own, live3_own = marks["places"][6:]
-                tables[1:] = [marks["tables"][:2], marks["tables"][2:]]
-        if step == 1:
-            mixed, cot = order.take(mixed, cotangent[0].T)
-            cot = relocate(cot)
         if step == 0:
             extra = (sel_own, *tables[1])
         elif step == 1:
@@ -1450,9 +1479,26 @@
         else:
             extra = (sel_own, live2_own, live3_own, heights[0], heights[1])
         mats = dense_weights + ((weight_qkv,) if step < 2 else ())
-        result = dense_call(
-            near, step, coords, xs[step], mixed, gain1, gain2, extra, mats, next_rows
-        )
+
+        def dense(mixed, step=step, extra=extra, mats=mats, next_rows=next_rows):
+            return dense_call(
+                near, step, coords, xs[step], mixed, gain1, gain2, extra, mats, next_rows
+            )
+
+        def both(*a):
+            made = attend_call(*a, prompt)
+            return *made, *dense(made[1])
+
+        if step == 0:
+            result = dense(mixed)
+        elif step == 1 and near:
+            there = Move(cotangent[0].T)
+            weights, mixed, *result = wave(order, [(there, 0)], both, attention[:-1])
+            cot = there.result
+        else:
+            weights, mixed, *result = both(*attention[:-1])
+            if step == 1:
+                cot = cotangent[0].T
         mixed_rows, middle, second, gate, up, hidden = result[:6]
         mixeds.append(mixed_rows)
         seconds.append(second)
@@ -1460,8 +1506,6 @@
         records.append((query, part_a, part_b, weights, middle, gate, up))
         if step < 2:
             height, following, first_in, query, kv = result[6:]
-            if step == 1:
-                following, cot = order.take(following, cot)
             heights.append(height)
             xs.append(following)
         else:
@@ -1492,7 +1536,10 @@
             extra, mats = (cot, sel_own, live2_own), (weight_qkv,) + mats
         else:
             extra, mats = (), (weight_qkv,)
-        result = list(back_call(near, phase, coords, before, parts, into, extra, mats, cap_mid))
+        last = lambda *parts: back_call(near, phase, coords, before, parts, into, extra, mats, cap_mid)
+        if near and phase == 3:
+            break
+        result = list(last(*parts))
         if phase > 0:
             d_firsts[step + 1], total = result[:2]
             sums_one.append(total)
@@ -1529,7 +1576,7 @@
             gate_grads_made = wave(
                 order, [(down, 0)], gate_grads, column(d_seconds, 1)
             )
-            down = BlockSums(low_sum(down_grads[0], down.result))
+            down = BothWays(low_sum(down_grads[0], down.result))
             gate = Hop(gate_grads_made[1], C_BIT)
             d_query, term_a, term_b = wave(order, [(down, 0), (gate, 0)], attend_last, (d_mixed,))
             gate = BlockSums(low_sum(gate_grads_made[0], gate.result))
@@ -1543,8 +1590,16 @@
 
     kv_width = key_weight.shape[1]
     hidden_width = w_gate.shape[1]
-    mixed_grads = lambda *d: grads("mixed", [firsts, mixeds, list(d), column(d_seconds, 3)])
-    sums = jnp.concatenate([sum(sums_one), sum(sums_two)], axis=0)
+
+    def mixed_grads(*d):
+        sums = jnp.concatenate([sum(sums_one), sum(sums_two)], axis=0)
+        return grad_call("mixed", block_coords, [firsts, mixeds, list(d), column(d_seconds, 3)], sums)
+
+    def last_grads(*parts):
+        d_firsts[0], total, grad_tokens = last(*parts)
+        sums_one.append(total)
+        return *mixed_grads(*d_firsts), grad_tokens
+
     placed = {}
 
     if near:
@@ -1552,33 +1607,33 @@
             return lambda near_blocks, far_blocks, at: place_call(kind, at, near_blocks, far_blocks, widths)
 
         placing = lambda chain: (*chain.result, coords)
-        rest_made = wave(order, [(gate, 0), (down, 2)], mixed_grads, d_firsts)
-        rest, gains_sum = Hop(rest_made[1], C_BIT), RunningSum(sums)
+        *rest_made, grad_tokens = wave(order, [(gate, 0), (down, 2)], last_grads, parts)
+        rest = Hop(rest_made[1], C_BIT)
         wave(order, [(gate, 1), (down, 3), (rest, 0)])
         rest = BlockSums(low_sum(rest_made[0], rest.result))
         wave(order, [(up, 0), (gate, 2), (down, 4)])
-        wave(order, [(up, 1), (gate, 3), (down, 5)])
+        wave(order, [(up, 1), (gate, 3)])
+        wave(order, [(rest, 0), (up, 2), (gate, 4)])
+        wave(order, [(rest, 1), (up, 3)])
+        wave(order, [(rest, 2), (up, 4), (down, 5)])
         placed["down"] = wave(
-            order, [(rest, 0), (up, 2), (gate, 4)], place("rows", None), placing(down)
-        )
-        wave(order, [(rest, 1), (up, 3), (gate, 5), (gains_sum, 1)])
-        placed["gate"] = wave(
-            order, [(rest, 2), (up, 4)], place("cols", (hidden_width,)), placing(gate)
+            order, [(rest, 3), (up, 5), (gate, 5)], place("rows", None), placing(down)
         )
         tokens_back = Move(grad_tokens)
-        wave(order, [(rest, 3), (up, 5), (gains_sum, 0)])
-        placed["up"] = wave(
-            order, [(rest, 4), (gains_sum, 2), (tokens_back, 0)], place("cols", (hidden_width,)), placing(up)
+
+        def place_two(*arrays):
+            cols = place("cols", (hidden_width,))
+            return *cols(*arrays[:3]), *cols(*arrays[3:])
+
+        placed["gate"], placed["up"] = wave(
+            order, [(rest, 4), (tokens_back, 0)], place_two, (*placing(gate), *placing(up))
         )
         grad_tokens = tokens_back.result.astype(F32)
-        wave(order, [(rest, 5), (gains_sum, 3)])
-        wave(order, [(gains_sum, 4)])
+        wave(order, [(rest, 5)])
         placed["rest"] = order.all(
             *place("cols", (width, kv_width, width, kv_width))(*rest.result, order.token)
         )
-        for name in ("down", "gate", "up"):
-            (placed[name],) = placed[name]
-        gain_sums = gains_sum.result
+        (placed["down"],) = placed["down"]
     else:
         sums_of.append(pair_sum(*mixed_grads(*d_firsts), near))
         for name, kind, widths, total in zip(
@@ -1592,12 +1647,10 @@
             placed[name] = place_call(kind, block_coords, mine[0], mine[1], widths)
         for name in ("down", "gate", "up"):
             (placed[name],) = placed[name]
-        gain_sums = lax.psum(sums, AXES)
         grad_tokens = grad_tokens.astype(F32)
     grad_down, grad_gate, grad_up = placed["down"].T, placed["gate"], placed["up"]
-    grad_query, grad_key, grad_out, grad_value = placed["rest"]
+    grad_query, grad_key, grad_out, grad_value, gain_sums = placed["rest"]
     grad_key, grad_value = grad_key.T, grad_value.T
-    gain_sums = lax.dynamic_slice_in_dim(gain_sums, y * half, half, 1)
     return (
         output.T[None],
         grad_tokens.T[None],

time: 535 us -> 516 us (0.964)
  waiting for transfers between devices: 182 us -> 169 us
  starting transfers between devices: 138 us -> 130 us
    ppermute x4, waiting for transfers between devices: 15.8 us -> 6.99 us  [move(): return lax.ppermute(value, AXES, [(i, swap_place(i)) for i in range(32)])]
    ppermute x118 -> x109, starting transfers between devices: 122 us -> 116 us  [hop(): return lax.ppermute(value, AXES, [(i, i ^ mask) for i in range(32)])]
    ppermute x118 -> x109, waiting for transfers between devices: 166 us -> 162 us  [hop(): return lax.ppermute(value, AXES, [(i, i ^ mask) for i in range(32)])]
  transfers between devices with their start and end apart: 122 -> 113, of which waited for: 58 -> 53; matrix products, arithmetic and copies ran while one was open for 6% -> 7% of each run, Pallas kernels for 15% -> 18%
where the time goes in v4:
time: 516 us; the launch traced here: 508 us
  waiting for transfers between devices  169 us (33%)
  Pallas kernels  160 us (31%)
  starting transfers between devices  130 us (25%)
  local copies, waits for them, and re-layouts  27.2 us (5%)
  other arithmetic  19.7 us (4%)
    ppermute x109, waiting for transfers between devices, hop(): return lax.ppermute(value, AXES, [(i, i ^ mask) for i in range(32)])  162 us
    ppermute x109, starting transfers between devices, hop(): return lax.ppermute(value, AXES, [(i, i ^ mask) for i in range(32)])  116 us
    pallas_call x3, Pallas kernels, attend_call(): pl.pallas_call(functools.partial(attend_kernel, prompt), name='attend', g...  30.8 us
    pallas_call x4, Pallas kernels, back_call(): pl.pallas_call(functools.partial(back_kernel, near, phase, weights, len(p...  26.5 us
    pallas_call x3, Pallas kernels, attend_back_call(): pl.pallas_call(attend_back_kernel, name='attend_back', grid=(heads,), out...  26.4 us
    pallas_call x4, Pallas kernels, grad_call(): pl.pallas_call(functools.partial(kernel, n_steps), name=f'grad_{kind}', o...  22.7 us
    pallas_call x3, Pallas kernels, dense_call(): pl.pallas_call(functools.partial(dense_kernel, near, step, weights), name...  19.3 us
    pallas_call x4, Pallas kernels, place_call(): pl.pallas_call(kernel, name=f'place_{kind}', grid_spec=pltpu.PrefetchScal...  15 us
  transfers between devices with their start and end apart: 113, of which 53 were waited for; matrix products, arithmetic and copies ran while one was open for 7% of the time, Pallas kernels for 18%

profile of v4, /device:TPU:7, one launch (start us, length us, event | category | flops | bytes accessed | tf_op | source)
XLA Modules:
  0.0 508.3 jit_solution(9853301825809421010)
XLA Ops:
  0.7 3.5 pack.1
  13.0 4.3 collective-permute-start.2
  39.2 2.4 join_weights.2.rest_0_.args_11_.args_22_.args_15_
  41.7 2.4 first_projection.1
  44.8 4.5 collective-permute-start.7
  54.2 5.8 %collective-permute-done.8.refs_0_ = bf16[480,640]{1,0:T(8,128)(2,1)} collective-permute-done((bf16[480,640]{1,0:T(8,128)(2,1)}, bf16[480,640]{1,0:T(8,128)(2,1)}, u32[]{:S(2)}, u32[]{:S(2)}) %collective-permute-start.8) | collective-permute-done | bytes 614432 | tf_op jit(solution)/shard_map/ppermute | solution.py:32
  61.0 2.4 collective-permute-done.5.refs_2_
  65.3 4.7 collective-permute-start.10
  76.0 3.1 collective-permute-start.13
  79.1 2.7 collective-permute-done.13.b_ref
  86.3 15.0 %attend.3 = (bf16[5,384,2048]{2,1,0:T(8,128)(2,1)}, bf16[5,128,192]{2,1,0:T(8,128)(2,1)S(1)}) custom-call(bf16[5,128,192]{2,1,0:T(8,128)(2,1)S(1)} %copy-done.2, bf16[1024,640]{1,0:T(8,128)(2,1)S(1)} %stack.152.a_ref, bf16[1024,640]{1,0:T(8,128)(2,1)S(1)} %collective-permute-done.13.b_ref, s32[1,2048]{1,0:T(1,128)S(1)} %add.171.kpos_ref, ...), custom_call_target="tpu_custom_call" | custom-call | bytes 14263717 | tf_op jit(solution)/shard_map/attend/pallas_call | solution.py:488
  101.3 10.0 %collective-permute-done.16.refs_1_ = bf16[480,640]{1,0:T(8,128)(2,1)S(1)} collective-permute-done((bf16[480,640]{1,0:T(8,128)(2,1)}, bf16[480,640]{1,0:T(8,128)(2,1)S(1)}, u32[]{:S(2)}, u32[]{:S(2)}) %collective-permute-start.16) | collective-permute-done | bytes 614432 | tf_op jit(solution)/shard_map/ppermute | solution.py:32
  115.0 5.4 %collective-permute-done.19.args_2_ = bf16[240,960]{1,0:T(8,128)(2,1)S(1)} collective-permute-done((bf16[240,960]{1,0:T(8,128)(2,1)}, bf16[240,960]{1,0:T(8,128)(2,1)S(1)}, u32[]{:S(2)}, u32[]{:S(2)}) %collective-permute-start.19) | collective-permute-done | bytes 460832 | tf_op jit(solution)/shard_map/ppermute | solution.py:32
  123.1 6.7 %join_weights.3 = (bf16[960,960]{1,0:T(8,128)(2,1)S(1)}, bf16[960,2560]{1,0:T(8,128)(2,1)S(1)}, bf16[960,2560]{1,0:T(8,128)(2,1)S(1)}, bf16[960,2560]{1,0:T(8,128)(2,1)S(1)}) custom-call(s32[4]{0:T(128)S(1)} %pad_add_fusion.1.coords_ref.args_0_, bf16[480,960]{1,0:T(8,128)(2,1)} %args_0_.4, bf16[240,960]{1,0:T(8,128)(2,1)} %collective-permute-done.12.args_1_, ...), custom_call_target="tpu_custom_call" | custom-call | bytes 925000 | tf_op jit(solution)/shard_map/join_weights/pallas_call | solution.py:218
  129.8 6.9 %dense_0.1 = (bf16[128,960]{1,0:T(8,128)(2,1)}, f32[128,960]{1,0:T(8,128)}, bf16[128,960]{1,0:T(8,128)(2,1)}, bf16[128,2560]{1,0:T(8,128)(2,1)}, bf16[128,2560]{...) custom-call(bf16[5,128,192]{2,1,0:T(8,128)(2,1)S(1)} %get-tuple-elem, ...), custom_call_target="tpu_custom_call" | custom-call | bytes 5550000 | tf_op jit(solution)/shard_map/dense_0/pallas_call | solution.py:691
  140.5 2.5 collective-permute-done.24.refs_4_
  147.8 3.0 collective-permute-done.25.refs_5_
  151.1 2.3 collective-permute-start.28
  155.6 3.7 collective-permute-start.29
  159.3 10.4 %attend.4 = (bf16[5,288,1536]{2,1,0:T(8,128)(2,1)}, bf16[5,96,192]{2,1,0:T(8,128)(2,1)S(1)}) custom-call(bf16[5,96,192]{2,1,0:T(8,128)(2,1)S(1)} %get-tuple-element.567.q_ref, bf16[768,640]{1,0:T(8,128)(2,1)S(1)} %stack.154.a_ref, bf16[768,640]{1,0:T(8,128)(2,1)S(1)} %collective-permute-done.28.b_ref, s32[1,1536]{1,0:T(1,128)S(1)} %reshape.149.kpos_ref, ...), custom_call_target="tpu_custom_call" | custom-call | bytes 8023341 | tf_op jit(solution)/shard_map/attend/pallas_call | solution.py:488
  169.7 6.9 %dense_1.1 = (bf16[96,960]{1,0:T(8,128)(2,1)}, f32[96,960]{1,0:T(8,128)}, bf16[96,960]{1,0:T(8,128)(2,1)}, bf16[96,2560]{1,0:T(8,128)(2,1)}, bf16[96,2560]{1,0:T...) custom-call(bf16[5,96,192]{2,1,0:T(8,128)(2,1)S(1)} %get-tuple-eleme, ...), custom_call_target="tpu_custom_call" | custom-call | bytes 5550000 | tf_op jit(solution)/shard_map/dense_1/pallas_call | solution.py:691
  177.4 2.8 collective-permute-start.31
  181.9 2.3 collective-permute-done.31.refs_2_
  187.9 3.3 collective-permute-start.37
  192.9 5.4 %attend.5 = (bf16[5,192,1024]{2,1,0:T(8,128)(2,1)}, bf16[5,64,192]{2,1,0:T(8,128)(2,1)S(1)}) custom-call(bf16[5,64,192]{2,1,0:T(8,128)(2,1)S(1)} %get-tuple-element.591.q_ref, bf16[512,640]{1,0:T(8,128)(2,1)S(1)} %stack.155.a_ref, bf16[512,640]{1,0:T(8,128)(2,1)S(1)} %collective-permute-done.37.b_ref, s32[1,1024]{1,0:T(1,128)S(1)} %copy-done.12, ...), custom_call_target="tpu_custom_call" | custom-call | bytes 3565929 | tf_op jit(solution)/shard_map/attend/pallas_call | solution.py:488
  198.3 5.5 %dense_2.1 = (bf16[64,960]{1,0:T(8,128)(2,1)}, f32[64,960]{1,0:T(8,128)}, bf16[64,960]{1,0:T(8,128)(2,1)}, bf16[64,2560]{1,0:T(8,128)(2,1)}, bf16[64,2560]{1,0:T...) custom-call(bf16[5,64,192]{2,1,0:T(8,128)(2,1)S(1)} %get-tuple-element.609.ao_ref, ...), custom_call_target="tpu_custom_call" | custom-call | bytes 5550000 | tf_op jit(solution)/shard_map/dense_2/pallas_call | solution.py:691
  203.8 4.5 collective-permute-start.38
  208.3 6.5 %back_0.1 = (bf16[64,960]{1,0:T(8,128)(2,1)}, bf16[64,2560]{1,0:T(8,128)(2,1)}, bf16[64,2560]{1,0:T(8,128)(2,1)}, f32[64,960]{1,0:T(8,128)}, bf16[64,960]{1,0:T(...) custom-call(s32[4]{0:T(128)S(1)} %pad_add_fusion.1.coords_ref.args_0_, ...), custom_call_target="tpu_custom_call" | custom-call | bytes 5550000 | tf_op jit(solution)/shard_map/back_0/pallas_call | solution.py:842
  214.8 5.8 %attend_back.3 = (f32[5,64,192]{2,1,0:T(8,128)S(1)}, f32[512,640]{1,0:T(8,128)S(1)}, bf16[512,640]{1,0:T(8,128)(2,1)S(1)}) custom-call(bf16[5,64,192]{2,1,0:T(8,128)(2,1)S(1)} %get-tuple-element.591.q_ref, bf16[5,64,192]{2,1,0:T(8,128)(2,1)S(1)} %get-tuple-element.623.do_ref, bf16[512,640]{1,0:T(8,128)(2,1)S(1)} %stack.155.a_ref, ...), custom_call_target="tpu_custom_call" | custom-call | bytes 2755490 | tf_op jit(solution)/shard_map/attend_back/pallas_call | solution.py:538
  224.2 2.9 collective-permute-start.43
  230.7 2.4 collective-permute-done.44.args_12_
  233.7 8.1 %back_1.1 = (bf16[64,1600]{1,0:T(8,128)(2,1)}, f32[1,960]{1,0:T(1,128)}, bf16[96,960]{1,0:T(8,128)(2,1)}, bf16[96,2560]{1,0:T(8,128)(2,1)}, bf16[96,2560]{1,0:T(...) custom-call(s32[4]{0:T(128)S(1)} %pad_add_fusion.1.coords_ref.args_0, ...), custom_call_target="tpu_custom_call" | custom-call | bytes 5550000 | tf_op jit(solution)/shard_map/back_1/pallas_call | solution.py:842
  241.8 8.6 %attend_back.4 = (f32[5,96,192]{2,1,0:T(8,128)S(1)}, f32[768,640]{1,0:T(8,128)S(1)}, bf16[768,640]{1,0:T(8,128)(2,1)S(1)}) custom-call(bf16[5,96,192]{2,1,0:T(8,128)(2,1)S(1)} %get-tuple-element.567.q_ref, bf16[5,96,192]{2,1,0:T(8,128)(2,1)S(1)} %get-tuple-element.672.do_ref, bf16[768,640]{1,0:T(8,128)(2,1)S(1)} %stack.154.a_ref, ...), custom_call_target="tpu_custom_call" | custom-call | bytes 6199854 | tf_op jit(solution)/shard_map/attend_back/pallas_call | solution.py:538
  250.5 2.7 collective-permute-start.47
  260.2 2.2 collective-permute-start.53
  264.9 3.6 collective-permute-done.52.args_12_
  269.6 8.9 %back_2.1 = (bf16[96,1600]{1,0:T(8,128)(2,1)}, f32[1,960]{1,0:T(1,128)}, bf16[128,960]{1,0:T(8,128)(2,1)}, bf16[128,2560]{1,0:T(8,128)(2,1)}, bf16[128,2560]{1,0...) custom-call(s32[4]{0:T(128)S(1)} %pad_add_fusion.1.coords_ref.args_0, ...), custom_call_target="tpu_custom_call" | custom-call | bytes 5550000 | tf_op jit(solution)/shard_map/back_2/pallas_call | solution.py:842
  278.5 5.2 %grad_rows.1 = (bf16[2,2,4,80,960]{4,3,2,1,0:T(8,128)(2,1)S(1)}, bf16[2,2,4,80,960]{4,3,2,1,0:T(8,128)(2,1)S(1)}) custom-call(s32[4]{0:T(128)S(1)} %pad_add_fusion.1.coords_ref.args_0_, bf16[128,2560]{1,0:T(8,128)(2,1)} %get-tuple-element.628.args_0_, bf16[96,2560]{1,0:T(8,128)(2,1)} %get-tuple-element.629.args_1_, ...), custom_call_target="tpu_custom_call" | custom-call | bytes 5550000 | tf_op jit(solution)/shard_map/grad_rows/pallas_call | solution.py:984
  285.5 5.4 %grad_cols.2 = (bf16[2,2,4,120,640]{4,3,2,1,0:T(8,128)(2,1)S(1)}, bf16[2,2,4,120,640]{4,3,2,1,0:T(8,128)(2,1)S(1)}) custom-call(s32[4]{0:T(128)S(1)} %pad_add_fusion.1.coords_ref.args_0_, bf16[128,960]{1,0:T(8,128)(2,1)} %get-tuple-element.719.args_0_, bf16[96,960]{1,0:T(8,128)(2,1)} %get-tuple-element.720.args_1_, ...), custom_call_target="tpu_custom_call" | custom-call | bytes 5550000 | tf_op jit(solution)/shard_map/grad_cols/pallas_call | solution.py:984
  293.9 12.0 %attend_back.5 = (f32[5,128,192]{2,1,0:T(8,128)S(1)}, f32[1024,640]{1,0:T(8,128)S(1)}, bf16[1024,640]{1,0:T(8,128)(2,1)S(1)}) custom-call(bf16[5,128,192]{2,1,0:T(8,128)(2,1)S(1)} %copy-done.2, bf16[5,128,192]{2,1,0:T(8,128)(2,1)S(1)} %get-tuple-element.737.do_ref, bf16[1024,640]{1,0:T(8,128)(2,1)S(1)} %stack.152.a_ref, ...), custom_call_target="tpu_custom_call" | custom-call | bytes 11021963 | tf_op jit(solution)/shard_map/attend_back/pallas_call | solution.py:538
  305.9 2.4 collective-permute-done.56
  312.4 5.4 %grad_cols.3 = (bf16[2,2,4,120,640]{4,3,2,1,0:T(8,128)(2,1)S(1)}, bf16[2,2,4,120,640]{4,3,2,1,0:T(8,128)(2,1)S(1)}) custom-call(s32[4]{0:T(128)S(1)} %pad_add_fusion.1.coords_ref.args_0_, bf16[128,960]{1,0:T(8,128)(2,1)} %get-tuple-element.719.args_0_, bf16[96,960]{1,0:T(8,128)(2,1)} %get-tuple-element.720.args_1_, ...), custom_call_target="tpu_custom_call" | custom-call | bytes 5550000 | tf_op jit(solution)/shard_map/grad_cols/pallas_call | solution.py:984
  317.8 2.7 collective-permute-done.59
  334.2 9.4 %collective-permute-done.66.args_12_ = bf16[128,640]{1,0:T(8,128)(2,1)S(1)} collective-permute-done((bf16[128,640]{1,0:T(8,128)(2,1)S(1)}, bf16[128,640]{1,0:T(8,128)(2,1)S(1)}, u32[]{:S(2)}, u32[]{:S(2)}) %collective-permute-start.66) | collective-permute-done | bytes 163872 | tf_op jit(solution)/shard_map/ppermute | solution.py:32
  348.1 3.0 back_3.1
  352.4 6.8 %grad_mixed.1 = (bf16[2,2,4,128,640]{4,3,2,1,0:T(8,128)(2,1)S(1)}, bf16[2,2,4,128,640]{4,3,2,1,0:T(8,128)(2,1)S(1)}) custom-call(s32[4]{0:T(128)S(1)} %pad_add_fusion.1.coords_ref.args_0_, f32[2,960]{1,0:T(2,128)} %pad_maximum_fusion.13.sums_ref, bf16[128,960]{1,0:T(8,128)(2,1)} %get-tuple-element.811.args_0_, bf16[96,960]{1,0:T(8,128)(2,1)} %get-tuple-element.812.args_1_, ...), custom_call_target="tpu_custom_call" | custom-call | bytes 5550000 | tf_op jit(solution)/shard_map/grad_mixed/pallas_call | solution.py:984
  366.6 3.9 collective-permute-done.76
  370.7 7.5 %collective-permute-done.77 = bf16[80,960]{1,0:T(8,128)(2,1)S(1)} collective-permute-done((bf16[80,960]{1,0:T(8,128)(2,1)S(1)}, bf16[80,960]{1,0:T(8,128)(2,1)S(1)}, u32[]{:S(2)}, u32[]{:S(2)}) %collective-permute-start.77) | collective-permute-done | bytes 153632 | tf_op jit(solution)/shard_map/ppermute | solution.py:32
  385.6 2.5 collective-permute-done.81
  388.2 8.5 %collective-permute-done.82 = bf16[120,640]{1,0:T(8,128)(2,1)S(1)} collective-permute-done((bf16[120,640]{1,0:T(8,128)(2,1)S(1)}, bf16[120,640]{1,0:T(8,128)(2,1)S(1)}, u32[]{:S(2)}, u32[]{:S(2)}) %collective-permute-start.82) | collective-permute-done | bytes 153632 | tf_op jit(solution)/shard_map/ppermute | solution.py:32
  402.9 2.4 collective-permute-done.87
  405.3 8.5 %collective-permute-done.88 = bf16[120,640]{1,0:T(8,128)(2,1)S(1)} collective-permute-done((bf16[120,640]{1,0:T(8,128)(2,1)S(1)}, bf16[120,640]{1,0:T(8,128)(2,1)S(1)}, u32[]{:S(2)}, u32[]{:S(2)}) %collective-permute-start.88) | collective-permute-done | bytes 153632 | tf_op jit(solution)/shard_map/ppermute | solution.py:32
  419.3 2.5 collective-permute-done.91
  421.8 8.5 %collective-permute-done.92 = bf16[120,640]{1,0:T(8,128)(2,1)S(1)} collective-permute-done((bf16[120,640]{1,0:T(8,128)(2,1)S(1)}, bf16[120,640]{1,0:T(8,128)(2,1)S(1)}, u32[]{:S(2)}, u32[]{:S(2)}) %collective-permute-start.92) | collective-permute-done | bytes 153632 | tf_op jit(solution)/shard_map/ppermute | solution.py:32
  435.8 2.4 collective-permute-done.97
  438.1 8.5 %collective-permute-done.98 = bf16[120,640]{1,0:T(8,128)(2,1)S(1)} collective-permute-done((bf16[120,640]{1,0:T(8,128)(2,1)S(1)}, bf16[120,640]{1,0:T(8,128)(2,1)S(1)}, u32[]{:S(2)}, u32[]{:S(2)}) %collective-permute-start.98) | collective-permute-done | bytes 153632 | tf_op jit(solution)/shard_map/ppermute | solution.py:32
  453.4 3.6 collective-permute-done.100
  457.0 7.9 %collective-permute-done.101 = bf16[128,640]{1,0:T(8,128)(2,1)S(1)} collective-permute-done((bf16[128,640]{1,0:T(8,128)(2,1)S(1)}, bf16[128,640]{1,0:T(8,128)(2,1)S(1)}, u32[]{:S(2)}, u32[]{:S(2)}) %collective-permute-start.101) | collective-permute-done | bytes 163872 | tf_op jit(solution)/shard_map/ppermute | solution.py:32
  469.5 3.8 place_rows.1
  473.3 7.9 %collective-permute-done.106 = bf16[128,640]{1,0:T(8,128)(2,1)S(1)} collective-permute-done((bf16[128,640]{1,0:T(8,128)(2,1)S(1)}, bf16[128,640]{1,0:T(8,128)(2,1)S(1)}, u32[]{:S(2)}, u32[]{:S(2)}) %collective-permute-start.106) | collective-permute-done | bytes 163872 | tf_op jit(solution)/shard_map/ppermute | solution.py:32
  484.0 3.4 place_cols.3
  487.4 3.4 place_cols.4
  490.7 7.0 %collective-permute-done.111 = bf16[960,128]{1,0:T(8,128)(2,1)S(1)} collective-permute-done((bf16[960,128]{1,0:T(8,128)(2,1)S(1)}, bf16[960,128]{1,0:T(8,128)(2,1)S(1)}, u32[]{:S(2)}, u32[]{:S(2)}) %collective-permute-start.111) | collective-permute-done | bytes 245792 | tf_op jit(solution)/shard_map/ppermute | solution.py:41
  501.4 4.4 place_cols.5
  (376 shorter events, 173.4 us)
Async XLA Ops:
  4.3 21.8 %collective-permute-start = (bf16[240,1664]{1,0:T(8,128)(2,1)S(1)}, bf16[240,1664]{1,0:T(8,128)(2,1)}, u32[]{:S(2)}, u32[]{:S(2)}) collective-permute-start(bf16[240,1664]{1,0:T(8,128)(2,1)S(1)} %get-tuple-element.483), channel_id=1, source_target_pairs={{0,1},{1,0},{2,3},{3,2},{4,5},{5,4},{6,7},{7,6},{8,9},{9,8},{10,11... | collective-permute-start | bytes 2396168 | tf_op jit(solution)/shard_map/ppermute | solution.py:32
  6.7 24.9 %collective-permute-start.3 = (bf16[2,480]{1,0:T(2,128)(2,1)}, bf16[2,480]{1,0:T(2,128)(2,1)}, u32[]{:S(2)}, u32[]{:S(2)}) collective-permute-start(bf16[2,480]{1,0:T(2,128)(2,1)} %pad_maximum_fusion.14), channel_id=1, source_target_pairs={{0,1},{1,0},{2,3},{3,2},{4,5},{5,4},{6,7},{7,6},{8,9},{9,8},{10,11... | collective-permute-start | bytes 5768 | tf_op jit(solution)/shard_map/ppermute | solution.py:32
  13.0 18.5 %collective-permute-start.2 = (bf16[144,960]{1,0:T(8,128)(2,1)S(1)}, bf16[144,960]{1,0:T(8,128)(2,1)}, u32[]{:S(2)}, u32[]{:S(2)}) collective-permute-start(bf16[144,960]{1,0:T(8,128)(2,1)S(1)} %pack_rows.1), channel_id=1, source_target_pairs={{0,0},{1,16},{2,2},{3,18},{4,4},{5,20},{6,6},{7,22},{8,8},{9,24},{... | collective-permute-start | bytes 829448 | tf_op jit(solution)/shard_map/ppermute | solution.py:41
  30.1 42.9 %collective-permute-start.12 = (bf16[240,960]{1,0:T(8,128)(2,1)}, bf16[240,960]{1,0:T(8,128)(2,1)}, u32[]{:S(2)}, u32[]{:S(2)}) collective-permute-start(bf16[240,960]{1,0:T(8,128)(2,1)} %constant_dynamic-slice_fusion), channel_id=1, source_target_pairs={{0,1},{1,0},{2,3},{3,2},{4,5},{5,4},{6,7},{7,6},{8,9},{9,8},{10,11... | collective-permute-start | bytes 1382408 | tf_op jit(solution)/shard_map/ppermute | solution.py:32
  30.1 29.9 %collective-permute-start.8 = (bf16[480,640]{1,0:T(8,128)(2,1)}, bf16[480,640]{1,0:T(8,128)(2,1)}, u32[]{:S(2)}, u32[]{:S(2)}) collective-permute-start(bf16[480,640]{1,0:T(8,128)(2,1)} %pad_maximum_fusion.6), channel_id=1, source_target_pairs={{0,1},{1,0},{2,3},{3,2},{4,5},{5,4},{6,7},{7,6},{8,9},{9,8},{10,11... | collective-permute-start | bytes 1843208 | tf_op jit(solution)/shard_map/ppermute | solution.py:32
  44.8 16.2 %collective-permute-start.7 = (bf16[128,640]{1,0:T(8,128)(2,1)}, bf16[128,640]{1,0:T(8,128)(2,1)}, u32[]{:S(2)}, u32[]{:S(2)}) collective-permute-start(bf16[128,640]{1,0:T(8,128)(2,1)} %get-tuple-element.494.refs_0_), channel_id=1, source_target_pairs={{0,13},{1,12},{2,15},{3,14},{4,9},{5,8},{6,11},{7,10},{8,5},{9,4},... | collective-permute-start | bytes 491528 | tf_op jit(solution)/shard_map/ppermute | solution.py:32
  49.3 11.7 %collective-permute-start.6 = (bf16[128,640]{1,0:T(8,128)(2,1)}, bf16[128,640]{1,0:T(8,128)(2,1)}, u32[]{:S(2)}, u32[]{:S(2)}) collective-permute-start(bf16[128,640]{1,0:T(8,128)(2,1)} %get-tuple-element.494.refs_0_), channel_id=1, source_target_pairs={{0,8},{1,9},{2,10},{3,11},{4,12},{5,13},{6,14},{7,15},{8,0},{9,1},... | collective-permute-start | bytes 491528 | tf_op jit(solution)/shard_map/ppermute | solution.py:32
  49.5 13.9 %collective-permute-start.5 = (bf16[128,640]{1,0:T(8,128)(2,1)}, bf16[128,640]{1,0:T(8,128)(2,1)}, u32[]{:S(2)}, u32[]{:S(2)}) collective-permute-start(bf16[128,640]{1,0:T(8,128)(2,1)} %get-tuple-element.494.refs_0_), channel_id=1, source_target_pairs={{0,1},{1,0},{2,3},{3,2},{4,5},{5,4},{6,7},{7,6},{8,9},{9,8},{10,11... | collective-permute-start | bytes 491528 | tf_op jit(solution)/shard_map/ppermute | solution.py:32
  64.7 8.3 %collective-permute-start.9 = (bf16[128,640]{1,0:T(8,128)(2,1)S(1)}, bf16[128,640]{1,0:T(8,128)(2,1)S(1)}, u32[]{:S(2)}, u32[]{:S(2)}) collective-permute-start(bf16[128,640]{1,0:T(8,128)(2,1)S(1)} %collective-permute-done.4.refs_1_), channel_id=1, source_target_pairs={{0,1},{1,0},{2,3},{3,2},{4,5},{5,4},{6,7},{7,6},{8,9},{9,8},{10,11... | collective-permute-start | bytes 491528 | tf_op jit(solution)/shard_map/ppermute | solution.py:32
  81.8 29.5 %collective-permute-start.14 = (bf16[480,1280]{1,0:T(8,128)(2,1)S(1)}, bf16[480,1280]{1,0:T(8,128)(2,1)S(1)}, u32[]{:S(2)}, u32[]{:S(2)}) collective-permute-start(bf16[480,1280]{1,0:T(8,128)(2,1)S(1)} %copy-done.21), channel_id=1, source_target_pairs={{0,1},{1,0},{2,3},{3,2},{4,5},{5,4},{6,7},{7,6},{8,9},{9,8},{10,11... | collective-permute-start | bytes 3686408 | tf_op jit(solution)/shard_map/ppermute | solution.py:32
  83.1 18.3 %collective-permute-start.15 = (bf16[480,640]{1,0:T(8,128)(2,1)}, bf16[480,640]{1,0:T(8,128)(2,1)S(1)}, u32[]{:S(2)}, u32[]{:S(2)}) collective-permute-start(bf16[480,640]{1,0:T(8,128)(2,1)} %collective-permute-done.8.refs_0_), channel_id=1, source_target_pairs={{0,12},{1,13},{2,14},{3,15},{4,8},{5,9},{6,10},{7,11},{8,4},{9,5},... | collective-permute-start | bytes 1843208 | tf_op jit(solution)/shard_map/ppermute | solution.py:32
  83.1 28.2 %collective-permute-start.16 = (bf16[480,640]{1,0:T(8,128)(2,1)}, bf16[480,640]{1,0:T(8,128)(2,1)S(1)}, u32[]{:S(2)}, u32[]{:S(2)}) collective-permute-start(bf16[480,640]{1,0:T(8,128)(2,1)} %collective-permute-done.8.refs_0_), channel_id=1, source_target_pairs={{0,4},{1,5},{2,6},{3,7},{4,0},{5,1},{6,2},{7,3},{8,12},{9,13},{10,... | collective-permute-start | bytes 1843208 | tf_op jit(solution)/shard_map/ppermute | solution.py:32
  84.0 27.3 %collective-permute-start.17 = (bf16[480,640]{1,0:T(8,128)(2,1)}, bf16[480,640]{1,0:T(8,128)(2,1)S(1)}, u32[]{:S(2)}, u32[]{:S(2)}) collective-permute-start(bf16[480,640]{1,0:T(8,128)(2,1)} %collective-permute-done.8.refs_0_), channel_id=1, source_target_pairs={{0,8},{1,9},{2,10},{3,11},{4,12},{5,13},{6,14},{7,15},{8,0},{9,1},... | collective-permute-start | bytes 1843208 | tf_op jit(solution)/shard_map/ppermute | solution.py:32
  113.0 8.2 %collective-permute-start.18 = (bf16[1920,640]{1,0:T(8,128)(2,1)S(1)}, bf16[1920,640]{1,0:T(8,128)(2,1)S(1)}, u32[]{:S(2)}, u32[]{:S(2)}) collective-permute-start(bf16[1920,640]{1,0:T(8,128)(2,1)S(1)} %stack.153.args_4_.args_7_), channel_id=1, source_target_pairs={{0,2},{1,3},{2,0},{3,1},{4,6},{5,7},{6,4},{7,5},{8,10},{9,11},{10,... | collective-permute-start | bytes 7372808 | tf_op jit(solution)/shard_map/ppermute | solution.py:32
  155.6 21.0 %collective-permute-start.29 = (bf16[960,128]{1,0:T(8,128)(2,1)S(1)}, bf16[960,128]{1,0:T(8,128)(2,1)S(1)}, u32[]{:S(2)}, u32[]{:S(2)}) collective-permute-start(bf16[960,128]{1,0:T(8,128)(2,1)S(1)} %bitcast.205), channel_id=1, source_target_pairs={{0,0},{1,16},{2,2},{3,18},{4,4},{5,20},{6,6},{7,22},{8,8},{9,24},{... | collective-permute-start | bytes 737288 | tf_op jit(solution)/shard_map/ppermute | solution.py:41
  203.8 16.9 %collective-permute-start.38 = (bf16[960,128]{1,0:T(8,128)(2,1)}, bf16[960,128]{1,0:T(8,128)(2,1)S(1)}, u32[]{:S(2)}, u32[]{:S(2)}) collective-permute-start(bf16[960,128]{1,0:T(8,128)(2,1)} %get-tuple-element.616), channel_id=1, source_target_pairs={{0,0},{1,16},{2,2},{3,18},{4,4},{5,20},{6,6},{7,22},{8,8},{9,24},{... | collective-permute-start | bytes 737288 | tf_op jit(solution)/shard_map/ppermute | solution.py:41
  259.5 9.0 %collective-permute-start.52 = (bf16[96,640]{1,0:T(8,128)(2,1)S(1)}, bf16[96,640]{1,0:T(8,128)(2,1)S(1)}, u32[]{:S(2)}, u32[]{:S(2)}) collective-permute-start(bf16[96,640]{1,0:T(8,128)(2,1)S(1)} %get-tuple-element.696), channel_id=1, source_target_pairs={{0,5},{1,4},{2,7},{3,6},{4,1},{5,0},{6,3},{7,2},{8,13},{9,12},{10,... | collective-permute-start | bytes 368648 | tf_op jit(solution)/shard_map/ppermute | solution.py:32
  260.2 8.3 %collective-permute-start.53 = (bf16[96,640]{1,0:T(8,128)(2,1)S(1)}, bf16[96,640]{1,0:T(8,128)(2,1)S(1)}, u32[]{:S(2)}, u32[]{:S(2)}) collective-permute-start(bf16[96,640]{1,0:T(8,128)(2,1)S(1)} %get-tuple-element.697), channel_id=1, source_target_pairs={{0,9},{1,8},{2,11},{3,10},{4,13},{5,12},{6,15},{7,14},{8,1},{9,0},... | collective-permute-start | bytes 368648 | tf_op jit(solution)/shard_map/ppermute | solution.py:32
  292.3 16.6 %collective-permute-start.58 = (bf16[2,2,4,120,640]{4,3,2,1,0:T(8,128)(2,1)S(1)}, bf16[2,2,4,120,640]{4,3,2,1,0:T(8,128)(2,1)S(1)}, u32[]{:S(2)}, u32[]{:S(2)}) collective-permute-start(bf16[2,2,4,120,640]{4,3,2,1,0:T(8,128)(2,1)S(1)} %get-tuple-element.736), channel_id=1, source_target_pairs={{0,2},{1,3},{2,0},{3,1},{4,6},{5,7},{6,4},{7,5},{8,10},{9,11},{10,... | collective-permute-start | bytes 7372808 | tf_op jit(solution)/shard_map/ppermute | solution.py:32
  292.3 15.9 %collective-permute-start.56 = (bf16[2,2,80,960]{3,2,1,0:T(8,128)(2,1)S(1)}, bf16[2,2,80,960]{3,2,1,0:T(8,128)(2,1)S(1)}, u32[]{:S(2)}, u32[]{:S(2)}) collective-permute-start(bf16[2,2,80,960]{3,2,1,0:T(8,128)(2,1)S(1)} %slice_bitcast_fusion.7), channel_id=1, source_target_pairs={{0,1},{1,0},{2,3},{3,2},{4,5},{5,4},{6,7},{7,6},{8,9},{9,8},{10,11... | collective-permute-start | bytes 1843208 | tf_op jit(solution)/shard_map/ppermute | solution.py:32
  293.3 15.6 %collective-permute-start.57 = (bf16[2,2,80,960]{3,2,1,0:T(8,128)(2,1)S(1)}, bf16[2,2,80,960]{3,2,1,0:T(8,128)(2,1)S(1)}, u32[]{:S(2)}, u32[]{:S(2)}) collective-permute-start(bf16[2,2,80,960]{3,2,1,0:T(8,128)(2,1)S(1)} %slice_bitcast_fusion.6), channel_id=1, source_target_pairs={{0,4},{1,5},{2,6},{3,7},{4,0},{5,1},{6,2},{7,3},{8,12},{9,13},{10,... | collective-permute-start | bytes 1843208 | tf_op jit(solution)/shard_map/ppermute | solution.py:32
  309.5 11.3 %collective-permute-start.61 = (bf16[1024,640]{1,0:T(8,128)(2,1)S(1)}, bf16[1024,640]{1,0:T(8,128)(2,1)S(1)}, u32[]{:S(2)}, u32[]{:S(2)}) collective-permute-start(bf16[1024,640]{1,0:T(8,128)(2,1)S(1)} %get-tuple-element.753), channel_id=1, source_target_pairs={{0,2},{1,3},{2,0},{3,1},{4,6},{5,7},{6,4},{7,5},{8,10},{9,11},{10,... | collective-permute-start | bytes 3932168 | tf_op jit(solution)/shard_map/ppermute | solution.py:32
  311.1 9.3 %collective-permute-start.59 = (bf16[2,80,960]{2,1,0:T(8,128)(2,1)S(1)}, bf16[2,80,960]{2,1,0:T(8,128)(2,1)S(1)}, u32[]{:S(2)}, u32[]{:S(2)}) collective-permute-start(bf16[2,80,960]{2,1,0:T(8,128)(2,1)S(1)} %slice_bitcast_fusion.18), channel_id=1, source_target_pairs={{0,4},{1,5},{2,6},{3,7},{4,0},{5,1},{6,2},{7,3},{8,12},{9,13},{10,... | collective-permute-start | bytes 921608 | tf_op jit(solution)/shard_map/ppermute | solution.py:32
  311.8 9.0 %collective-permute-start.60 = (bf16[2,80,960]{2,1,0:T(8,128)(2,1)S(1)}, bf16[2,80,960]{2,1,0:T(8,128)(2,1)S(1)}, u32[]{:S(2)}, u32[]{:S(2)}) collective-permute-start(bf16[2,80,960]{2,1,0:T(8,128)(2,1)S(1)} %slice_bitcast_fusion.17), channel_id=1, source_target_pairs={{0,1},{1,0},{2,3},{3,2},{4,5},{5,4},{6,7},{7,6},{8,9},{9,8},{10,11... | collective-permute-start | bytes 921608 | tf_op jit(solution)/shard_map/ppermute | solution.py:32
  321.0 22.6 %collective-permute-start.69 = (bf16[2,2,4,120,640]{4,3,2,1,0:T(8,128)(2,1)S(1)}, bf16[2,2,4,120,640]{4,3,2,1,0:T(8,128)(2,1)S(1)}, u32[]{:S(2)}, u32[]{:S(2)}) collective-permute-start(bf16[2,2,4,120,640]{4,3,2,1,0:T(8,128)(2,1)S(1)} %get-tuple-element.781), channel_id=1, source_target_pairs={{0,2},{1,3},{2,0},{3,1},{4,6},{5,7},{6,4},{7,5},{8,10},{9,11},{10,... | collective-permute-start | bytes 7372808 | tf_op jit(solution)/shard_map/ppermute | solution.py:32
  325.5 8.7 %collective-permute-start.65 = (bf16[128,640]{1,0:T(8,128)(2,1)S(1)}, bf16[128,640]{1,0:T(8,128)(2,1)S(1)}, u32[]{:S(2)}, u32[]{:S(2)}) collective-permute-start(bf16[128,640]{1,0:T(8,128)(2,1)S(1)} %get-tuple-element.777), channel_id=1, source_target_pairs={{0,13},{1,12},{2,15},{3,14},{4,9},{5,8},{6,11},{7,10},{8,5},{9,4},... | collective-permute-start | bytes 491528 | tf_op jit(solution)/shard_map/ppermute | solution.py:32
  328.9 14.7 %collective-permute-start.66 = (bf16[128,640]{1,0:T(8,128)(2,1)S(1)}, bf16[128,640]{1,0:T(8,128)(2,1)S(1)}, u32[]{:S(2)}, u32[]{:S(2)}) collective-permute-start(bf16[128,640]{1,0:T(8,128)(2,1)S(1)} %get-tuple-element.778), channel_id=1, source_target_pairs={{0,5},{1,4},{2,7},{3,6},{4,1},{5,0},{6,3},{7,2},{8,13},{9,12},{10,... | collective-permute-start | bytes 491528 | tf_op jit(solution)/shard_map/ppermute | solution.py:32
  330.1 13.6 %collective-permute-start.67 = (bf16[128,640]{1,0:T(8,128)(2,1)S(1)}, bf16[128,640]{1,0:T(8,128)(2,1)S(1)}, u32[]{:S(2)}, u32[]{:S(2)}) collective-permute-start(bf16[128,640]{1,0:T(8,128)(2,1)S(1)} %get-tuple-element.779), channel_id=1, source_target_pairs={{0,9},{1,8},{2,11},{3,10},{4,13},{5,12},{6,15},{7,14},{8,1},{9,0},... | collective-permute-start | bytes 491528 | tf_op jit(solution)/shard_map/ppermute | solution.py:32
  331.8 11.8 %collective-permute-start.68 = (bf16[128,640]{1,0:T(8,128)(2,1)S(1)}, bf16[128,640]{1,0:T(8,128)(2,1)S(1)}, u32[]{:S(2)}, u32[]{:S(2)}) collective-permute-start(bf16[128,640]{1,0:T(8,128)(2,1)S(1)} %get-tuple-element.780), channel_id=1, source_target_pairs={{0,12},{1,13},{2,14},{3,15},{4,8},{5,9},{6,10},{7,11},{8,4},{9,5},... | collective-permute-start | bytes 491528 | tf_op jit(solution)/shard_map/ppermute | solution.py:32
  343.7 17.5 %collective-permute-start.70 = (bf16[4,120,640]{2,1,0:T(8,128)(2,1)S(1)}, bf16[4,120,640]{2,1,0:T(8,128)(2,1)S(1)}, u32[]{:S(2)}, u32[]{:S(2)}) collective-permute-start(bf16[4,120,640]{2,1,0:T(8,128)(2,1)S(1)} %get-tuple-element.791), channel_id=1, source_target_pairs={{0,1},{1,0},{2,3},{3,2},{4,5},{5,4},{6,7},{7,6},{8,9},{9,8},{10,11... | collective-permute-start | bytes 1843208 | tf_op jit(solution)/shard_map/ppermute | solution.py:32
  344.5 14.7 %collective-permute-start.71 = (bf16[80,960]{1,0:T(8,128)(2,1)S(1)}, bf16[80,960]{1,0:T(8,128)(2,1)S(1)}, u32[]{:S(2)}, u32[]{:S(2)}) collective-permute-start(bf16[80,960]{1,0:T(8,128)(2,1)S(1)} %get-tuple-element.792), channel_id=1, source_target_pairs={{0,24},{1,25},{2,26},{3,27},{4,28},{5,29},{6,30},{7,31},{8,16},{9,... | collective-permute-start | bytes 460808 | tf_op jit(solution)/shard_map/ppermute | solution.py:32
  346.2 14.9 %collective-permute-start.72 = (bf16[80,960]{1,0:T(8,128)(2,1)S(1)}, bf16[80,960]{1,0:T(8,128)(2,1)S(1)}, u32[]{:S(2)}, u32[]{:S(2)}) collective-permute-start(bf16[80,960]{1,0:T(8,128)(2,1)S(1)} %get-tuple-element.793), channel_id=1, source_target_pairs={{0,16},{1,17},{2,18},{3,19},{4,20},{5,21},{6,22},{7,23},{8,24},{9,... | collective-permute-start | bytes 460808 | tf_op jit(solution)/shard_map/ppermute | solution.py:32
  346.9 14.2 %collective-permute-start.73 = (bf16[80,960]{1,0:T(8,128)(2,1)S(1)}, bf16[80,960]{1,0:T(8,128)(2,1)S(1)}, u32[]{:S(2)}, u32[]{:S(2)}) collective-permute-start(bf16[80,960]{1,0:T(8,128)(2,1)S(1)} %slice_bitcast_fusion.25), channel_id=1, source_target_pairs={{0,8},{1,9},{2,10},{3,11},{4,12},{5,13},{6,14},{7,15},{8,0},{9,1},... | collective-permute-start | bytes 460808 | tf_op jit(solution)/shard_map/ppermute | solution.py:32
  361.4 18.7 %collective-permute-start.79 = (bf16[2,2,4,128,640]{4,3,2,1,0:T(8,128)(2,1)S(1)}, bf16[2,2,4,128,640]{4,3,2,1,0:T(8,128)(2,1)S(1)}, u32[]{:S(2)}, u32[]{:S(2)}) collective-permute-start(bf16[2,2,4,128,640]{4,3,2,1,0:T(8,128)(2,1)S(1)} %get-tuple-element.839), channel_id=1, source_target_pairs={{0,2},{1,3},{2,0},{3,1},{4,6},{5,7},{6,4},{7,5},{8,10},{9,11},{10,... | collective-permute-start | bytes 7864328 | tf_op jit(solution)/shard_map/ppermute | solution.py:32
  364.7 15.1 %collective-permute-start.74 = (bf16[4,120,640]{2,1,0:T(8,128)(2,1)S(1)}, bf16[4,120,640]{2,1,0:T(8,128)(2,1)S(1)}, u32[]{:S(2)}, u32[]{:S(2)}) collective-permute-start(bf16[4,120,640]{2,1,0:T(8,128)(2,1)S(1)} %get-tuple-element.834), channel_id=1, source_target_pairs={{0,1},{1,0},{2,3},{3,2},{4,5},{5,4},{6,7},{7,6},{8,9},{9,8},{10,11... | collective-permute-start | bytes 1843208 | tf_op jit(solution)/shard_map/ppermute | solution.py:32
  365.4 14.8 %collective-permute-start.75 = (bf16[4,120,640]{2,1,0:T(8,128)(2,1)S(1)}, bf16[4,120,640]{2,1,0:T(8,128)(2,1)S(1)}, u32[]{:S(2)}, u32[]{:S(2)}) collective-permute-start(bf16[4,120,640]{2,1,0:T(8,128)(2,1)S(1)} %fusion.10), channel_id=1, source_target_pairs={{0,4},{1,5},{2,6},{3,7},{4,0},{5,1},{6,2},{7,3},{8,12},{9,13},{10,... | collective-permute-start | bytes 1843208 | tf_op jit(solution)/shard_map/ppermute | solution.py:32
  366.6 11.6 %collective-permute-start.77 = (bf16[80,960]{1,0:T(8,128)(2,1)S(1)}, bf16[80,960]{1,0:T(8,128)(2,1)S(1)}, u32[]{:S(2)}, u32[]{:S(2)}) collective-permute-start(bf16[80,960]{1,0:T(8,128)(2,1)S(1)} %fusion.18), channel_id=1, source_target_pairs={{0,16},{1,17},{2,18},{3,19},{4,20},{5,21},{6,22},{7,23},{8,24},{9,... | collective-permute-start | bytes 460808 | tf_op jit(solution)/shard_map/ppermute | solution.py:32
  370.6 8.0 %collective-permute-start.78 = (bf16[80,960]{1,0:T(8,128)(2,1)S(1)}, bf16[80,960]{1,0:T(8,128)(2,1)S(1)}, u32[]{:S(2)}, u32[]{:S(2)}) collective-permute-start(bf16[80,960]{1,0:T(8,128)(2,1)S(1)} %fusion.18), channel_id=1, source_target_pairs={{0,8},{1,9},{2,10},{3,11},{4,12},{5,13},{6,14},{7,15},{8,0},{9,1},... | collective-permute-start | bytes 460808 | tf_op jit(solution)/shard_map/ppermute | solution.py:32
  380.6 16.1 %collective-permute-start.80 = (bf16[4,120,640]{2,1,0:T(8,128)(2,1)S(1)}, bf16[4,120,640]{2,1,0:T(8,128)(2,1)S(1)}, u32[]{:S(2)}, u32[]{:S(2)}) collective-permute-start(bf16[4,120,640]{2,1,0:T(8,128)(2,1)S(1)} %get-tuple-element.850), channel_id=1, source_target_pairs={{0,1},{1,0},{2,3},{3,2},{4,5},{5,4},{6,7},{7,6},{8,9},{9,8},{10,11... | collective-permute-start | bytes 1843208 | tf_op jit(solution)/shard_map/ppermute | solution.py:32
  381.5 15.2 %collective-permute-start.84 = (bf16[4,80,960]{2,1,0:T(8,128)(2,1)S(1)}, bf16[4,80,960]{2,1,0:T(8,128)(2,1)S(1)}, u32[]{:S(2)}, u32[]{:S(2)}) collective-permute-start(bf16[4,80,960]{2,1,0:T(8,128)(2,1)S(1)} %get-tuple-element.854), channel_id=1, source_target_pairs={{0,4},{1,5},{2,6},{3,7},{4,0},{5,1},{6,2},{7,3},{8,12},{9,13},{10,... | collective-permute-start | bytes 1843208 | tf_op jit(solution)/shard_map/ppermute | solution.py:32
  383.6 13.0 %collective-permute-start.82 = (bf16[120,640]{1,0:T(8,128)(2,1)S(1)}, bf16[120,640]{1,0:T(8,128)(2,1)S(1)}, u32[]{:S(2)}, u32[]{:S(2)}) collective-permute-start(bf16[120,640]{1,0:T(8,128)(2,1)S(1)} %get-tuple-element.852), channel_id=1, source_target_pairs={{0,16},{1,17},{2,18},{3,19},{4,20},{5,21},{6,22},{7,23},{8,24},{9,... | collective-permute-start | bytes 460808 | tf_op jit(solution)/shard_map/ppermute | solution.py:32
  383.6 13.0 %collective-permute-start.83 = (bf16[120,640]{1,0:T(8,128)(2,1)S(1)}, bf16[120,640]{1,0:T(8,128)(2,1)S(1)}, u32[]{:S(2)}, u32[]{:S(2)}) collective-permute-start(bf16[120,640]{1,0:T(8,128)(2,1)S(1)} %get-tuple-element.853), channel_id=1, source_target_pairs={{0,8},{1,9},{2,10},{3,11},{4,12},{5,13},{6,14},{7,15},{8,0},{9,1},... | collective-permute-start | bytes 460808 | tf_op jit(solution)/shard_map/ppermute | solution.py:32
  396.9 16.9 %collective-permute-start.85 = (bf16[4,120,640]{2,1,0:T(8,128)(2,1)S(1)}, bf16[4,120,640]{2,1,0:T(8,128)(2,1)S(1)}, u32[]{:S(2)}, u32[]{:S(2)}) collective-permute-start(bf16[4,120,640]{2,1,0:T(8,128)(2,1)S(1)} %get-tuple-element.861), channel_id=1, source_target_pairs={{0,1},{1,0},{2,3},{3,2},{4,5},{5,4},{6,7},{7,6},{8,9},{9,8},{10,11... | collective-permute-start | bytes 1843208 | tf_op jit(solution)/shard_map/ppermute | solution.py:32
  397.5 16.3 %collective-permute-start.86 = (bf16[4,120,640]{2,1,0:T(8,128)(2,1)S(1)}, bf16[4,120,640]{2,1,0:T(8,128)(2,1)S(1)}, u32[]{:S(2)}, u32[]{:S(2)}) collective-permute-start(bf16[4,120,640]{2,1,0:T(8,128)(2,1)S(1)} %fusion.7), channel_id=1, source_target_pairs={{0,4},{1,5},{2,6},{3,7},{4,0},{5,1},{6,2},{7,3},{8,12},{9,13},{10,... | collective-permute-start | bytes 1843208 | tf_op jit(solution)/shard_map/ppermute | solution.py:32
  401.0 12.8 %collective-permute-start.88 = (bf16[120,640]{1,0:T(8,128)(2,1)S(1)}, bf16[120,640]{1,0:T(8,128)(2,1)S(1)}, u32[]{:S(2)}, u32[]{:S(2)}) collective-permute-start(bf16[120,640]{1,0:T(8,128)(2,1)S(1)} %fusion.24), channel_id=1, source_target_pairs={{0,16},{1,17},{2,18},{3,19},{4,20},{5,21},{6,22},{7,23},{8,24},{9,... | collective-permute-start | bytes 460808 | tf_op jit(solution)/shard_map/ppermute | solution.py:32
  401.0 12.8 %collective-permute-start.89 = (bf16[120,640]{1,0:T(8,128)(2,1)S(1)}, bf16[120,640]{1,0:T(8,128)(2,1)S(1)}, u32[]{:S(2)}, u32[]{:S(2)}) collective-permute-start(bf16[120,640]{1,0:T(8,128)(2,1)S(1)} %fusion.24), channel_id=1, source_target_pairs={{0,8},{1,9},{2,10},{3,11},{4,12},{5,13},{6,14},{7,15},{8,0},{9,1},... | collective-permute-start | bytes 460808 | tf_op jit(solution)/shard_map/ppermute | solution.py:32
  414.2 16.1 %collective-permute-start.90 = (bf16[4,128,640]{2,1,0:T(8,128)(2,1)S(1)}, bf16[4,128,640]{2,1,0:T(8,128)(2,1)S(1)}, u32[]{:S(2)}, u32[]{:S(2)}) collective-permute-start(bf16[4,128,640]{2,1,0:T(8,128)(2,1)S(1)} %get-tuple-element.873), channel_id=1, source_target_pairs={{0,1},{1,0},{2,3},{3,2},{4,5},{5,4},{6,7},{7,6},{8,9},{9,8},{10,11... | collective-permute-start | bytes 1966088 | tf_op jit(solution)/shard_map/ppermute | solution.py:32
  415.1 15.2 %collective-permute-start.94 = (bf16[4,120,640]{2,1,0:T(8,128)(2,1)S(1)}, bf16[4,120,640]{2,1,0:T(8,128)(2,1)S(1)}, u32[]{:S(2)}, u32[]{:S(2)}) collective-permute-start(bf16[4,120,640]{2,1,0:T(8,128)(2,1)S(1)} %get-tuple-element.877), channel_id=1, source_target_pairs={{0,4},{1,5},{2,6},{3,7},{4,0},{5,1},{6,2},{7,3},{8,12},{9,13},{10,... | collective-permute-start | bytes 1843208 | tf_op jit(solution)/shard_map/ppermute | solution.py:32
  417.2 13.1 %collective-permute-start.92 = (bf16[120,640]{1,0:T(8,128)(2,1)S(1)}, bf16[120,640]{1,0:T(8,128)(2,1)S(1)}, u32[]{:S(2)}, u32[]{:S(2)}) collective-permute-start(bf16[120,640]{1,0:T(8,128)(2,1)S(1)} %get-tuple-element.875), channel_id=1, source_target_pairs={{0,16},{1,17},{2,18},{3,19},{4,20},{5,21},{6,22},{7,23},{8,24},{9,... | collective-permute-start | bytes 460808 | tf_op jit(solution)/shard_map/ppermute | solution.py:32
  417.3 13.1 %collective-permute-start.93 = (bf16[120,640]{1,0:T(8,128)(2,1)S(1)}, bf16[120,640]{1,0:T(8,128)(2,1)S(1)}, u32[]{:S(2)}, u32[]{:S(2)}) collective-permute-start(bf16[120,640]{1,0:T(8,128)(2,1)S(1)} %get-tuple-element.876), channel_id=1, source_target_pairs={{0,8},{1,9},{2,10},{3,11},{4,12},{5,13},{6,14},{7,15},{8,0},{9,1},... | collective-permute-start | bytes 460808 | tf_op jit(solution)/shard_map/ppermute | solution.py:32
  430.6 16.0 %collective-permute-start.95 = (bf16[4,128,640]{2,1,0:T(8,128)(2,1)S(1)}, bf16[4,128,640]{2,1,0:T(8,128)(2,1)S(1)}, u32[]{:S(2)}, u32[]{:S(2)}) collective-permute-start(bf16[4,128,640]{2,1,0:T(8,128)(2,1)S(1)} %get-tuple-element.884), channel_id=1, source_target_pairs={{0,1},{1,0},{2,3},{3,2},{4,5},{5,4},{6,7},{7,6},{8,9},{9,8},{10,11... | collective-permute-start | bytes 1966088 | tf_op jit(solution)/shard_map/ppermute | solution.py:32
  431.2 15.4 %collective-permute-start.96 = (bf16[4,128,640]{2,1,0:T(8,128)(2,1)S(1)}, bf16[4,128,640]{2,1,0:T(8,128)(2,1)S(1)}, u32[]{:S(2)}, u32[]{:S(2)}) collective-permute-start(bf16[4,128,640]{2,1,0:T(8,128)(2,1)S(1)} %fusion), channel_id=1, source_target_pairs={{0,4},{1,5},{2,6},{3,7},{4,0},{5,1},{6,2},{7,3},{8,12},{9,13},{10,... | collective-permute-start | bytes 1966088 | tf_op jit(solution)/shard_map/ppermute | solution.py:32
  433.8 12.8 %collective-permute-start.98 = (bf16[120,640]{1,0:T(8,128)(2,1)S(1)}, bf16[120,640]{1,0:T(8,128)(2,1)S(1)}, u32[]{:S(2)}, u32[]{:S(2)}) collective-permute-start(bf16[120,640]{1,0:T(8,128)(2,1)S(1)} %fusion.21), channel_id=1, source_target_pairs={{0,16},{1,17},{2,18},{3,19},{4,20},{5,21},{6,22},{7,23},{8,24},{9,... | collective-permute-start | bytes 460808 | tf_op jit(solution)/shard_map/ppermute | solution.py:32
  433.8 12.8 %collective-permute-start.99 = (bf16[120,640]{1,0:T(8,128)(2,1)S(1)}, bf16[120,640]{1,0:T(8,128)(2,1)S(1)}, u32[]{:S(2)}, u32[]{:S(2)}) collective-permute-start(bf16[120,640]{1,0:T(8,128)(2,1)S(1)} %fusion.21), channel_id=1, source_target_pairs={{0,8},{1,9},{2,10},{3,11},{4,12},{5,13},{6,14},{7,15},{8,0},{9,1},... | collective-permute-start | bytes 460808 | tf_op jit(solution)/shard_map/ppermute | solution.py:32
  447.1 17.9 %collective-permute-start.104 = (bf16[2,4,80,960]{3,2,1,0:T(8,128)(2,1)S(1)}, bf16[2,4,80,960]{3,2,1,0:T(8,128)(2,1)S(1)}, u32[]{:S(2)}, u32[]{:S(2)}) collective-permute-start(bf16[2,4,80,960]{3,2,1,0:T(8,128)(2,1)S(1)} %pad_maximum_fusion.near_ref), channel_id=1, source_target_pairs={{0,2},{1,3},{2,0},{3,1},{4,6},{5,7},{6,4},{7,5},{8,10},{9,11},{10,... | collective-permute-start | bytes 3686408 | tf_op jit(solution)/shard_map/ppermute | solution.py:32
  448.9 16.1 %collective-permute-start.103 = (bf16[4,120,640]{2,1,0:T(8,128)(2,1)S(1)}, bf16[4,120,640]{2,1,0:T(8,128)(2,1)S(1)}, u32[]{:S(2)}, u32[]{:S(2)}) collective-permute-start(bf16[4,120,640]{2,1,0:T(8,128)(2,1)S(1)} %get-tuple-element.900), channel_id=1, source_target_pairs={{0,4},{1,5},{2,6},{3,7},{4,0},{5,1},{6,2},{7,3},{8,12},{9,13},{10,... | collective-permute-start | bytes 1843208 | tf_op jit(solution)/shard_map/ppermute | solution.py:32
  451.5 13.5 %collective-permute-start.101 = (bf16[128,640]{1,0:T(8,128)(2,1)S(1)}, bf16[128,640]{1,0:T(8,128)(2,1)S(1)}, u32[]{:S(2)}, u32[]{:S(2)}) collective-permute-start(bf16[128,640]{1,0:T(8,128)(2,1)S(1)} %get-tuple-element.898), channel_id=1, source_target_pairs={{0,16},{1,17},{2,18},{3,19},{4,20},{5,21},{6,22},{7,23},{8,24},{9,... | collective-permute-start | bytes 491528 | tf_op jit(solution)/shard_map/ppermute | solution.py:32
  451.5 13.5 %collective-permute-start.102 = (bf16[128,640]{1,0:T(8,128)(2,1)S(1)}, bf16[128,640]{1,0:T(8,128)(2,1)S(1)}, u32[]{:S(2)}, u32[]{:S(2)}) collective-permute-start(bf16[128,640]{1,0:T(8,128)(2,1)S(1)} %get-tuple-element.899), channel_id=1, source_target_pairs={{0,8},{1,9},{2,10},{3,11},{4,12},{5,13},{6,14},{7,15},{8,0},{9,1},... | collective-permute-start | bytes 491528 | tf_op jit(solution)/shard_map/ppermute | solution.py:32
  465.2 16.0 %collective-permute-start.108 = (bf16[2,4,120,640]{3,2,1,0:T(8,128)(2,1)S(1)}, bf16[2,4,120,640]{3,2,1,0:T(8,128)(2,1)S(1)}, u32[]{:S(2)}, u32[]{:S(2)}) collective-permute-start(bf16[2,4,120,640]{3,2,1,0:T(8,128)(2,1)S(1)} %pad_maximum_fusion.2.near_ref), channel_id=1, source_target_pairs={{0,2},{1,3},{2,0},{3,1},{4,6},{5,7},{6,4},{7,5},{8,10},{9,11},{10,... | collective-permute-start | bytes 3686408 | tf_op jit(solution)/shard_map/ppermute | solution.py:32
  465.9 15.3 %collective-permute-start.109 = (bf16[2,4,120,640]{3,2,1,0:T(8,128)(2,1)S(1)}, bf16[2,4,120,640]{3,2,1,0:T(8,128)(2,1)S(1)}, u32[]{:S(2)}, u32[]{:S(2)}) collective-permute-start(bf16[2,4,120,640]{3,2,1,0:T(8,128)(2,1)S(1)} %pad_maximum_fusion.3.near_ref), channel_id=1, source_target_pairs={{0,2},{1,3},{2,0},{3,1},{4,6},{5,7},{6,4},{7,5},{8,10},{9,11},{10,... | collective-permute-start | bytes 3686408 | tf_op jit(solution)/shard_map/ppermute | solution.py:32
  467.5 13.7 %collective-permute-start.106 = (bf16[128,640]{1,0:T(8,128)(2,1)S(1)}, bf16[128,640]{1,0:T(8,128)(2,1)S(1)}, u32[]{:S(2)}, u32[]{:S(2)}) collective-permute-start(bf16[128,640]{1,0:T(8,128)(2,1)S(1)} %fusion.15), channel_id=1, source_target_pairs={{0,16},{1,17},{2,18},{3,19},{4,20},{5,21},{6,22},{7,23},{8,24},{9,... | collective-permute-start | bytes 491528 | tf_op jit(solution)/shard_map/ppermute | solution.py:32
  467.5 13.7 %collective-permute-start.107 = (bf16[128,640]{1,0:T(8,128)(2,1)S(1)}, bf16[128,640]{1,0:T(8,128)(2,1)S(1)}, u32[]{:S(2)}, u32[]{:S(2)}) collective-permute-start(bf16[128,640]{1,0:T(8,128)(2,1)S(1)} %fusion.15), channel_id=1, source_target_pairs={{0,8},{1,9},{2,10},{3,11},{4,12},{5,13},{6,14},{7,15},{8,0},{9,1},... | collective-permute-start | bytes 491528 | tf_op jit(solution)/shard_map/ppermute | solution.py:32
  481.3 16.4 %collective-permute-start.110 = (bf16[4,128,640]{2,1,0:T(8,128)(2,1)S(1)}, bf16[4,128,640]{2,1,0:T(8,128)(2,1)S(1)}, u32[]{:S(2)}, u32[]{:S(2)}) collective-permute-start(bf16[4,128,640]{2,1,0:T(8,128)(2,1)S(1)} %get-tuple-element.926), channel_id=1, source_target_pairs={{0,4},{1,5},{2,6},{3,7},{4,0},{5,1},{6,2},{7,3},{8,12},{9,13},{10,... | collective-permute-start | bytes 1966088 | tf_op jit(solution)/shard_map/ppermute | solution.py:32
  482.1 15.7 %collective-permute-start.111 = (bf16[960,128]{1,0:T(8,128)(2,1)S(1)}, bf16[960,128]{1,0:T(8,128)(2,1)S(1)}, u32[]{:S(2)}, u32[]{:S(2)}) collective-permute-start(bf16[960,128]{1,0:T(8,128)(2,1)S(1)} %copy-done.41), channel_id=1, source_target_pairs={{0,0},{1,16},{2,2},{3,18},{4,4},{5,20},{6,6},{7,22},{8,8},{9,24},{... | collective-permute-start | bytes 737288 | tf_op jit(solution)/shard_map/ppermute | solution.py:41
  (91 other events, 796.2 us)

commit v5 on v4

--- a/solution.py
+++ b/solution.py
@@ -204,8 +204,9 @@
     return buffers, bring(weights, refs, buffers, sems, read_coords(coords_ref), turns)
 
 
-def join_kernel(weights, coords_ref, *args):
+def join_kernel(weights, n_bases, coords_ref, *args):
     count = len(arrays_of(weights))
+    args = args[n_bases:]
     refs, outs, sems = args[:count], args[count:-1], args[-1]
     turns = [(i, g) for i, w in enumerate(weights) for g in range(len(w.groups))]
     wait = bring(weights, refs, outs, sems, read_coords(coords_ref), turns, len(turns))
@@ -213,19 +214,28 @@
         wait(*turn)
 
 
-def join_call(coords, weights):
+def join_call(coords, weights, bases=()):
     arrays = arrays_of(weights)
-    joined = pl.pallas_call(
-        functools.partial(join_kernel, weights),
+    return pl.pallas_call(
+        functools.partial(join_kernel, weights, len(bases)),
         name="join_weights",
         out_shape=tuple(pltpu.VMEM(w.shape, BF) for w in weights),
-        in_specs=[sm()] + [hbm()] * len(arrays),
+        in_specs=[sm()] + [vm()] * len(bases) + [hbm()] * len(arrays),
         out_specs=tuple(vm() for _ in weights),
         scratch_shapes=scratch_of(weights)[-1:],
+        input_output_aliases={1 + i: i for i in range(len(bases))},
         compiler_params=params(24),
         cost_estimate=estimate(),
-    )(coords, *apart(arrays))
-    return tuple(one_piece(w) for w in joined)
+    )(coords, *bases, *apart(arrays))
+
+
+def part_of_weight(weight, own):
+    shift = 0 if own else 1
+    groups = [
+        [(copy[0] - shift, *copy[1:]) for copy in group if (copy[0] == 0) == own]
+        for group in weight.groups
+    ]
+    return Weight(weight.shape, weight.arrays[:1] if own else weight.arrays[1:], groups)
 
 
 def scratch_of(weights):
@@ -1113,13 +1123,22 @@
 
 class KeySums:
     def __init__(self, own, others):
-        self.own, self.others = own, others
+        self.own = own
+        self.near, self.across, self.beyond = others[:3], others[3], others[4:]
 
     def sends(self, turn):
-        return list(zip(self.others, NEAR[1:], strict=True))
+        if turn == 0:
+            return list(zip(self.beyond, (Y_BIT, Z1_BIT, X_BIT), strict=True))
+        return [
+            (self.across, X_BIT | Y_BIT | Z1_BIT),
+            *zip(self.near, (X_BIT, Y_BIT, Z1_BIT), strict=True),
+        ]
 
     def got(self, turn, values):
-        self.result = [self.own, *values]
+        if turn == 0:
+            self.near = [low_sum(a, b) for a, b in zip(self.near, values, strict=True)]
+        else:
+            self.result = [self.own, *values]
 
 
 class Hop:
@@ -1142,6 +1161,7 @@
     own, *others = split_call(part_a, far.result)
     sums = KeySums(own, others)
     wave(order, [(sums, 0)])
+    wave(order, [(sums, 1)])
     return sums.result
 
 
@@ -1362,35 +1382,38 @@
                 )
             return Weight((2 * half, own.shape[1]), [own, mine, other], groups)
 
-        (weight_qkv,) = join_call(coords, (in_rows(own_qkv, fetched, far),))
+        weight_qkv = one_piece(join_call(coords, (in_rows(own_qkv, fetched, far),))[0])
         marks = {}
 
         def fetch_rest(pair, out, down):
             pair = stack_call(pair)
             shared = [Hop(v, C_BIT) for v in (pair, out, down)]
-            wave(order, [(s, 0) for s in shared])
-            pair_far, out_far, down_far = (s.result for s in shared)
             wide = own_down.shape[1]
-            weight_d = Weight(
-                (width, 2 * wide),
-                [own_down, down, down_far],
-                [
+
+            def whole_weights(pair_far, out_far, down_far):
+                weight_d = Weight(
+                    (width, 2 * wide),
+                    [own_down, down, down_far],
                     [
-                        (0, width, wide, origin, lambda ky, kc, kx, kz: (0, ky * wide)),
-                        (1, width // 2, wide, origin, lambda ky, kc, kx, kz: (kc * (width // 2), (1 - ky) * wide)),
-                        (2, width // 2, wide, origin, lambda ky, kc, kx, kz: ((1 - kc) * (width // 2), (1 - ky) * wide)),
-                    ]
-                ],
-            )
-            return join_call(
-                coords,
-                (
+                        [
+                            (0, width, wide, origin, lambda ky, kc, kx, kz: (0, ky * wide)),
+                            (1, width // 2, wide, origin, lambda ky, kc, kx, kz: (kc * (width // 2), (1 - ky) * wide)),
+                            (2, width // 2, wide, origin, lambda ky, kc, kx, kz: ((1 - kc) * (width // 2), (1 - ky) * wide)),
+                        ]
+                    ],
+                )
+                return (
                     in_rows(w_out, out, out_far),
                     in_parts(w_gate, pair, pair_far, 0),
                     in_parts(w_up, pair, pair_far, 1),
                     weight_d,
-                ),
-            )
+                )
+
+            begun = [part_of_weight(w, True) for w in whole_weights(pair, out, down)]
+            bases = wave(order, [(s, 0) for s in shared], lambda k: join_call(k, begun), (coords,))
+            rest = whole_weights(*(s.result for s in shared))
+            joined = join_call(coords, [part_of_weight(w, False) for w in rest], bases)
+            return tuple(one_piece(w) for w in joined)
     else:
         tok = tokens[0]
         whole = lambda w: lax.all_gather(w, "ws", axis=0, tiled=True)
@@ -1585,6 +1608,7 @@
             own, *others = split_call(term_a, far.result)
             keys, up = KeySums(own, others), Hop(up_made[1], C_BIT)
             wave(order, [(keys, 0), (up, 0)])
+            wave(order, [(keys, 1)])
             up = BlockSums(low_sum(up_made[0], up.result))
             parts = keys.result
 

time: 516 us -> 511 us (level)
    pallas_call x2 -> x3, Pallas kernels: 9.08 us -> 10.7 us  [join_call(): pl.pallas_call(functools.partial(join_kernel, weights, len(bases)), name=...]
  transfers between devices with their start and end apart: 113 -> 113, of which waited for: 53 -> 60; matrix products, arithmetic and copies ran while one was open for 7% -> 6% of each run, Pallas kernels for 18% -> 19%
where the time goes in v5:
time: 511 us; the launch traced here: 504 us
  waiting for transfers between devices  173 us (34%)
  Pallas kernels  162 us (32%)
  starting transfers between devices  126 us (25%)
  local copies, waits for them, and re-layouts  24 us (5%)
  other arithmetic  16.5 us (3%)
    ppermute x109, waiting for transfers between devices, hop(): return lax.ppermute(value, AXES, [(i, i ^ mask) for i in range(32)])  164 us
    ppermute x109, starting transfers between devices, hop(): return lax.ppermute(value, AXES, [(i, i ^ mask) for i in range(32)])  112 us
    pallas_call x3, Pallas kernels, attend_call(): pl.pallas_call(functools.partial(attend_kernel, prompt), name='attend', g...  30.8 us
    pallas_call x4, Pallas kernels, back_call(): pl.pallas_call(functools.partial(back_kernel, near, phase, weights, len(p...  26.8 us
    pallas_call x3, Pallas kernels, attend_back_call(): pl.pallas_call(attend_back_kernel, name='attend_back', grid=(heads,), out...  26.5 us
    pallas_call x4, Pallas kernels, grad_call(): pl.pallas_call(functools.partial(kernel, n_steps), name=f'grad_{kind}', o...  22.6 us
    pallas_call x3, Pallas kernels, dense_call(): pl.pallas_call(functools.partial(dense_kernel, near, step, weights), name...  19.2 us
    pallas_call x4, Pallas kernels, place_call(): pl.pallas_call(kernel, name=f'place_{kind}', grid_spec=pltpu.PrefetchScal...  15 us
  transfers between devices with their start and end apart: 113, of which 60 were waited for; matrix products, arithmetic and copies ran while one was open for 6% of the time, Pallas kernels for 19%

profile of v5, /device:TPU:7, one launch (start us, length us, event | category | flops | bytes accessed | tf_op | source)
XLA Modules:
  0.0 504.1 jit_solution(6203834779171311180)
XLA Ops:
  0.7 3.5 pack.1
  12.5 4.2 collective-permute-start.2
  20.8 2.4 dynamic-slice_bitcast_fusion
  35.3 2.4 join_weights.3.rest_0_.args_11_.args_19_.args_12_
  37.7 2.4 first_projection.1
  40.8 4.4 collective-permute-start.7
  50.2 8.6 %collective-permute-done.8.refs_0_ = bf16[480,640]{1,0:T(8,128)(2,1)} collective-permute-done((bf16[480,640]{1,0:T(8,128)(2,1)}, bf16[480,640]{1,0:T(8,128)(2,1)}, u32[]{:S(2)}, u32[]{:S(2)}) %collective-permute-start.8) | collective-permute-done | bytes 614432 | tf_op jit(solution)/shard_map/ppermute | solution.py:32
  59.9 2.4 collective-permute-done.5.refs_2_
  64.3 4.4 collective-permute-start.10
  74.7 3.1 collective-permute-start.13
  77.8 2.7 collective-permute-done.13.b_ref
  85.1 15.1 %attend.3 = (bf16[5,384,2048]{2,1,0:T(8,128)(2,1)}, bf16[5,128,192]{2,1,0:T(8,128)(2,1)S(1)}) custom-call(bf16[5,128,192]{2,1,0:T(8,128)(2,1)S(1)} %copy-done.2, bf16[1024,640]{1,0:T(8,128)(2,1)S(1)} %stack.152.a_ref, bf16[1024,640]{1,0:T(8,128)(2,1)S(1)} %collective-permute-done.13.b_ref, s32[1,2048]{1,0:T(1,128)S(1)} %add.198.kpos_ref, ...), custom_call_target="tpu_custom_call" | custom-call | bytes 14263717 | tf_op jit(solution)/shard_map/attend/pallas_call | solution.py:498
  100.2 9.9 %collective-permute-done.16.refs_1_ = bf16[480,640]{1,0:T(8,128)(2,1)S(1)} collective-permute-done((bf16[480,640]{1,0:T(8,128)(2,1)}, bf16[480,640]{1,0:T(8,128)(2,1)S(1)}, u32[]{:S(2)}, u32[]{:S(2)}) %collective-permute-start.16) | collective-permute-done | bytes 614432 | tf_op jit(solution)/shard_map/ppermute | solution.py:32
  113.7 4.2 join_weights.4
  121.8 4.1 join_weights.5
  126.0 6.8 %dense_0.1 = (bf16[128,960]{1,0:T(8,128)(2,1)}, f32[128,960]{1,0:T(8,128)}, bf16[128,960]{1,0:T(8,128)(2,1)}, bf16[128,2560]{1,0:T(8,128)(2,1)}, bf16[128,2560]{...) custom-call(bf16[5,128,192]{2,1,0:T(8,128)(2,1)S(1)} %get-tuple-elem, ...), custom_call_target="tpu_custom_call" | custom-call | bytes 5550000 | tf_op jit(solution)/shard_map/dense_0/pallas_call | solution.py:701
  136.7 2.5 collective-permute-done.24.refs_4_
  143.9 3.0 collective-permute-done.25.refs_5_
  151.7 3.7 collective-permute-start.29
  155.4 10.3 %attend.4 = (bf16[5,288,1536]{2,1,0:T(8,128)(2,1)}, bf16[5,96,192]{2,1,0:T(8,128)(2,1)S(1)}) custom-call(bf16[5,96,192]{2,1,0:T(8,128)(2,1)S(1)} %get-tuple-element.588.q_ref, bf16[768,640]{1,0:T(8,128)(2,1)S(1)} %stack.154.a_ref, bf16[768,640]{1,0:T(8,128)(2,1)S(1)} %collective-permute-done.28.b_ref, s32[1,1536]{1,0:T(1,128)S(1)} %reshape.149.kpos_ref, ...), custom_call_target="tpu_custom_call" | custom-call | bytes 8023341 | tf_op jit(solution)/shard_map/attend/pallas_call | solution.py:498
  165.8 6.9 %dense_1.1 = (bf16[96,960]{1,0:T(8,128)(2,1)}, f32[96,960]{1,0:T(8,128)}, bf16[96,960]{1,0:T(8,128)(2,1)}, bf16[96,2560]{1,0:T(8,128)(2,1)}, bf16[96,2560]{1,0:T...) custom-call(bf16[5,96,192]{2,1,0:T(8,128)(2,1)S(1)} %get-tuple-eleme, ...), custom_call_target="tpu_custom_call" | custom-call | bytes 5550000 | tf_op jit(solution)/shard_map/dense_1/pallas_call | solution.py:701
  173.5 2.8 collective-permute-start.31
  184.0 3.2 collective-permute-start.37
  188.9 5.4 %attend.5 = (bf16[5,192,1024]{2,1,0:T(8,128)(2,1)}, bf16[5,64,192]{2,1,0:T(8,128)(2,1)S(1)}) custom-call(bf16[5,64,192]{2,1,0:T(8,128)(2,1)S(1)} %get-tuple-element.612.q_ref, bf16[512,640]{1,0:T(8,128)(2,1)S(1)} %stack.155.a_ref, bf16[512,640]{1,0:T(8,128)(2,1)S(1)} %collective-permute-done.37.b_ref, s32[1,1024]{1,0:T(1,128)S(1)} %copy-done.12, ...), custom_call_target="tpu_custom_call" | custom-call | bytes 3565929 | tf_op jit(solution)/shard_map/attend/pallas_call | solution.py:498
  194.4 5.4 %dense_2.1 = (bf16[64,960]{1,0:T(8,128)(2,1)}, f32[64,960]{1,0:T(8,128)}, bf16[64,960]{1,0:T(8,128)(2,1)}, bf16[64,2560]{1,0:T(8,128)(2,1)}, bf16[64,2560]{1,0:T...) custom-call(bf16[5,64,192]{2,1,0:T(8,128)(2,1)S(1)} %get-tuple-element.630.ao_ref, ...), custom_call_target="tpu_custom_call" | custom-call | bytes 5550000 | tf_op jit(solution)/shard_map/dense_2/pallas_call | solution.py:701
  199.8 4.5 collective-permute-start.38
  204.4 6.5 %back_0.1 = (bf16[64,960]{1,0:T(8,128)(2,1)}, bf16[64,2560]{1,0:T(8,128)(2,1)}, bf16[64,2560]{1,0:T(8,128)(2,1)}, f32[64,960]{1,0:T(8,128)}, bf16[64,960]{1,0:T(...) custom-call(s32[4]{0:T(128)S(1)} %pad_add_fusion.1.coords_ref.args_0_, ...), custom_call_target="tpu_custom_call" | custom-call | bytes 5550000 | tf_op jit(solution)/shard_map/back_0/pallas_call | solution.py:852
  210.9 5.8 %attend_back.3 = (f32[5,64,192]{2,1,0:T(8,128)S(1)}, f32[512,640]{1,0:T(8,128)S(1)}, bf16[512,640]{1,0:T(8,128)(2,1)S(1)}) custom-call(bf16[5,64,192]{2,1,0:T(8,128)(2,1)S(1)} %get-tuple-element.612.q_ref, bf16[5,64,192]{2,1,0:T(8,128)(2,1)S(1)} %get-tuple-element.644.do_ref, bf16[512,640]{1,0:T(8,128)(2,1)S(1)} %stack.155.a_ref, ...), custom_call_target="tpu_custom_call" | custom-call | bytes 2755490 | tf_op jit(solution)/shard_map/attend_back/pallas_call | solution.py:548
  220.4 2.7 collective-permute-done.40
  223.3 2.7 collective-permute-start.43
  231.1 8.3 %back_1.1 = (bf16[64,1600]{1,0:T(8,128)(2,1)}, f32[1,960]{1,0:T(1,128)}, bf16[96,960]{1,0:T(8,128)(2,1)}, bf16[96,2560]{1,0:T(8,128)(2,1)}, bf16[96,2560]{1,0:T(...) custom-call(s32[4]{0:T(128)S(1)} %pad_add_fusion.1.coords_ref.args_0, ...), custom_call_target="tpu_custom_call" | custom-call | bytes 5550000 | tf_op jit(solution)/shard_map/back_1/pallas_call | solution.py:852
  239.3 8.6 %attend_back.4 = (f32[5,96,192]{2,1,0:T(8,128)S(1)}, f32[768,640]{1,0:T(8,128)S(1)}, bf16[768,640]{1,0:T(8,128)(2,1)S(1)}) custom-call(bf16[5,96,192]{2,1,0:T(8,128)(2,1)S(1)} %get-tuple-element.588.q_ref, bf16[5,96,192]{2,1,0:T(8,128)(2,1)S(1)} %get-tuple-element.695.do_ref, bf16[768,640]{1,0:T(8,128)(2,1)S(1)} %stack.154.a_ref, ...), custom_call_target="tpu_custom_call" | custom-call | bytes 6199854 | tf_op jit(solution)/shard_map/attend_back/pallas_call | solution.py:548
  247.9 2.8 collective-permute-start.47
  255.7 2.4 collective-permute-done.48
  264.8 2.6 collective-permute-done.52.args_9_
  267.4 9.0 %back_2.1 = (bf16[96,1600]{1,0:T(8,128)(2,1)}, f32[1,960]{1,0:T(1,128)}, bf16[128,960]{1,0:T(8,128)(2,1)}, bf16[128,2560]{1,0:T(8,128)(2,1)}, bf16[128,2560]{1,0...) custom-call(s32[4]{0:T(128)S(1)} %pad_add_fusion.1.coords_ref.args_0, ...), custom_call_target="tpu_custom_call" | custom-call | bytes 5550000 | tf_op jit(solution)/shard_map/back_2/pallas_call | solution.py:852
  276.4 5.2 %grad_rows.1 = (bf16[2,2,4,80,960]{4,3,2,1,0:T(8,128)(2,1)S(1)}, bf16[2,2,4,80,960]{4,3,2,1,0:T(8,128)(2,1)S(1)}) custom-call(s32[4]{0:T(128)S(1)} %pad_add_fusion.1.coords_ref.args_0_, bf16[128,2560]{1,0:T(8,128)(2,1)} %get-tuple-element.649.args_0_, bf16[96,2560]{1,0:T(8,128)(2,1)} %get-tuple-element.650.args_1_, ...), custom_call_target="tpu_custom_call" | custom-call | bytes 5550000 | tf_op jit(solution)/shard_map/grad_rows/pallas_call | solution.py:994
  281.8 3.0 collective-permute-start.55
  284.8 5.3 %grad_cols.2 = (bf16[2,2,4,120,640]{4,3,2,1,0:T(8,128)(2,1)S(1)}, bf16[2,2,4,120,640]{4,3,2,1,0:T(8,128)(2,1)S(1)}) custom-call(s32[4]{0:T(128)S(1)} %pad_add_fusion.1.coords_ref.args_0_, bf16[128,960]{1,0:T(8,128)(2,1)} %get-tuple-element.744.args_0_, bf16[96,960]{1,0:T(8,128)(2,1)} %get-tuple-element.745.args_1_, ...), custom_call_target="tpu_custom_call" | custom-call | bytes 5550000 | tf_op jit(solution)/shard_map/grad_cols/pallas_call | solution.py:994
  292.5 12.0 %attend_back.5 = (f32[5,128,192]{2,1,0:T(8,128)S(1)}, f32[1024,640]{1,0:T(8,128)S(1)}, bf16[1024,640]{1,0:T(8,128)(2,1)S(1)}) custom-call(bf16[5,128,192]{2,1,0:T(8,128)(2,1)S(1)} %copy-done.2, bf16[5,128,192]{2,1,0:T(8,128)(2,1)S(1)} %get-tuple-element.762.do_ref, bf16[1024,640]{1,0:T(8,128)(2,1)S(1)} %stack.152.a_ref, ...), custom_call_target="tpu_custom_call" | custom-call | bytes 11021963 | tf_op jit(solution)/shard_map/attend_back/pallas_call | solution.py:548
  304.5 3.1 collective-permute-done.56
  311.7 5.3 %grad_cols.3 = (bf16[2,2,4,120,640]{4,3,2,1,0:T(8,128)(2,1)S(1)}, bf16[2,2,4,120,640]{4,3,2,1,0:T(8,128)(2,1)S(1)}) custom-call(s32[4]{0:T(128)S(1)} %pad_add_fusion.1.coords_ref.args_0_, bf16[128,960]{1,0:T(8,128)(2,1)} %get-tuple-element.744.args_0_, bf16[96,960]{1,0:T(8,128)(2,1)} %get-tuple-element.745.args_1_, ...), custom_call_target="tpu_custom_call" | custom-call | bytes 5550000 | tf_op jit(solution)/shard_map/grad_cols/pallas_call | solution.py:994
  324.2 3.3 collective-permute-done.62
  334.9 4.4 collective-permute-done.67.args_9_
  343.9 3.0 back_3.1
  348.2 6.8 %grad_mixed.1 = (bf16[2,2,4,128,640]{4,3,2,1,0:T(8,128)(2,1)S(1)}, bf16[2,2,4,128,640]{4,3,2,1,0:T(8,128)(2,1)S(1)}) custom-call(s32[4]{0:T(128)S(1)} %pad_add_fusion.1.coords_ref.args_0_, f32[2,960]{1,0:T(2,128)} %pad_maximum_fusion.13.sums_ref, bf16[128,960]{1,0:T(8,128)(2,1)} %get-tuple-element.835.args_0_, bf16[96,960]{1,0:T(8,128)(2,1)} %get-tuple-element.836.args_1_, ...), custom_call_target="tpu_custom_call" | custom-call | bytes 5550000 | tf_op jit(solution)/shard_map/grad_mixed/pallas_call | solution.py:994
  362.5 3.9 collective-permute-done.76
  366.5 7.5 %collective-permute-done.77 = bf16[80,960]{1,0:T(8,128)(2,1)S(1)} collective-permute-done((bf16[80,960]{1,0:T(8,128)(2,1)S(1)}, bf16[80,960]{1,0:T(8,128)(2,1)S(1)}, u32[]{:S(2)}, u32[]{:S(2)}) %collective-permute-start.77) | collective-permute-done | bytes 153632 | tf_op jit(solution)/shard_map/ppermute | solution.py:32
  381.4 2.5 collective-permute-done.81
  383.8 8.5 %collective-permute-done.82 = bf16[120,640]{1,0:T(8,128)(2,1)S(1)} collective-permute-done((bf16[120,640]{1,0:T(8,128)(2,1)S(1)}, bf16[120,640]{1,0:T(8,128)(2,1)S(1)}, u32[]{:S(2)}, u32[]{:S(2)}) %collective-permute-start.82) | collective-permute-done | bytes 153632 | tf_op jit(solution)/shard_map/ppermute | solution.py:32
  395.1 2.9 collective-permute-start.87
  401.2 8.5 %collective-permute-done.88 = bf16[120,640]{1,0:T(8,128)(2,1)S(1)} collective-permute-done((bf16[120,640]{1,0:T(8,128)(2,1)S(1)}, bf16[120,640]{1,0:T(8,128)(2,1)S(1)}, u32[]{:S(2)}, u32[]{:S(2)}) %collective-permute-start.88) | collective-permute-done | bytes 153632 | tf_op jit(solution)/shard_map/ppermute | solution.py:32
  415.0 2.5 collective-permute-done.91
  417.4 8.1 %collective-permute-done.92 = bf16[120,640]{1,0:T(8,128)(2,1)S(1)} collective-permute-done((bf16[120,640]{1,0:T(8,128)(2,1)S(1)}, bf16[120,640]{1,0:T(8,128)(2,1)S(1)}, u32[]{:S(2)}, u32[]{:S(2)}) %collective-permute-start.92) | collective-permute-done | bytes 153632 | tf_op jit(solution)/shard_map/ppermute | solution.py:32
  431.6 2.4 collective-permute-done.97
  433.9 8.4 %collective-permute-done.98 = bf16[120,640]{1,0:T(8,128)(2,1)S(1)} collective-permute-done((bf16[120,640]{1,0:T(8,128)(2,1)S(1)}, bf16[120,640]{1,0:T(8,128)(2,1)S(1)}, u32[]{:S(2)}, u32[]{:S(2)}) %collective-permute-start.98) | collective-permute-done | bytes 153632 | tf_op jit(solution)/shard_map/ppermute | solution.py:32
  449.2 3.6 collective-permute-done.100
  452.8 7.9 %collective-permute-done.101 = bf16[128,640]{1,0:T(8,128)(2,1)S(1)} collective-permute-done((bf16[128,640]{1,0:T(8,128)(2,1)S(1)}, bf16[128,640]{1,0:T(8,128)(2,1)S(1)}, u32[]{:S(2)}, u32[]{:S(2)}) %collective-permute-start.101) | collective-permute-done | bytes 163872 | tf_op jit(solution)/shard_map/ppermute | solution.py:32
  465.3 3.8 place_rows.1
  469.1 7.9 %collective-permute-done.106 = bf16[128,640]{1,0:T(8,128)(2,1)S(1)} collective-permute-done((bf16[128,640]{1,0:T(8,128)(2,1)S(1)}, bf16[128,640]{1,0:T(8,128)(2,1)S(1)}, u32[]{:S(2)}, u32[]{:S(2)}) %collective-permute-start.106) | collective-permute-done | bytes 163872 | tf_op jit(solution)/shard_map/ppermute | solution.py:32
  479.7 3.4 place_cols.3
  483.1 3.4 place_cols.4
  486.5 7.1 %collective-permute-done.111 = bf16[960,128]{1,0:T(8,128)(2,1)S(1)} collective-permute-done((bf16[960,128]{1,0:T(8,128)(2,1)S(1)}, bf16[960,128]{1,0:T(8,128)(2,1)S(1)}, u32[]{:S(2)}, u32[]{:S(2)}) %collective-permute-start.111) | collective-permute-done | bytes 245792 | tf_op jit(solution)/shard_map/ppermute | solution.py:41
  497.2 4.4 place_cols.5
  (386 shorter events, 174.2 us)
Async XLA Ops:
  4.3 20.0 %collective-permute-start = (bf16[240,1664]{1,0:T(8,128)(2,1)S(1)}, bf16[240,1664]{1,0:T(8,128)(2,1)}, u32[]{:S(2)}, u32[]{:S(2)}) collective-permute-start(bf16[240,1664]{1,0:T(8,128)(2,1)S(1)} %get-tuple-element.495), channel_id=1, source_target_pairs={{0,1},{1,0},{2,3},{3,2},{4,5},{5,4},{6,7},{7,6},{8,9},{9,8},{10,11... | collective-permute-start | bytes 2396168 | tf_op jit(solution)/shard_map/ppermute | solution.py:32
  5.9 22.6 %collective-permute-start.3 = (bf16[2,480]{1,0:T(2,128)(2,1)S(1)}, bf16[2,480]{1,0:T(2,128)(2,1)S(1)}, u32[]{:S(2)}, u32[]{:S(2)}) collective-permute-start(bf16[2,480]{1,0:T(2,128)(2,1)S(1)} %pad_maximum_fusion.14), channel_id=1, source_target_pairs={{0,1},{1,0},{2,3},{3,2},{4,5},{5,4},{6,7},{7,6},{8,9},{9,8},{10,11... | collective-permute-start | bytes 5768 | tf_op jit(solution)/shard_map/ppermute | solution.py:32
  12.5 17.9 %collective-permute-start.2 = (bf16[144,960]{1,0:T(8,128)(2,1)S(1)}, bf16[144,960]{1,0:T(8,128)(2,1)S(1)}, u32[]{:S(2)}, u32[]{:S(2)}) collective-permute-start(bf16[144,960]{1,0:T(8,128)(2,1)S(1)} %pack_rows.1), channel_id=1, source_target_pairs={{0,0},{1,16},{2,2},{3,18},{4,4},{5,20},{6,6},{7,22},{8,8},{9,24},{... | collective-permute-start | bytes 829448 | tf_op jit(solution)/shard_map/ppermute | solution.py:41
  27.0 44.7 %collective-permute-start.12 = (bf16[240,960]{1,0:T(8,128)(2,1)}, bf16[240,960]{1,0:T(8,128)(2,1)}, u32[]{:S(2)}, u32[]{:S(2)}) collective-permute-start(bf16[240,960]{1,0:T(8,128)(2,1)} %constant_dynamic-slice_fusion), channel_id=1, source_target_pairs={{0,1},{1,0},{2,3},{3,2},{4,5},{5,4},{6,7},{7,6},{8,9},{9,8},{10,11... | collective-permute-start | bytes 1382408 | tf_op jit(solution)/shard_map/ppermute | solution.py:32
  27.0 31.8 %collective-permute-start.8 = (bf16[480,640]{1,0:T(8,128)(2,1)}, bf16[480,640]{1,0:T(8,128)(2,1)}, u32[]{:S(2)}, u32[]{:S(2)}) collective-permute-start(bf16[480,640]{1,0:T(8,128)(2,1)} %pad_maximum_fusion.6), channel_id=1, source_target_pairs={{0,1},{1,0},{2,3},{3,2},{4,5},{5,4},{6,7},{7,6},{8,9},{9,8},{10,11... | collective-permute-start | bytes 1843208 | tf_op jit(solution)/shard_map/ppermute | solution.py:32
  40.8 19.0 %collective-permute-start.7 = (bf16[128,640]{1,0:T(8,128)(2,1)}, bf16[128,640]{1,0:T(8,128)(2,1)}, u32[]{:S(2)}, u32[]{:S(2)}) collective-permute-start(bf16[128,640]{1,0:T(8,128)(2,1)} %get-tuple-element.506.refs_0_), channel_id=1, source_target_pairs={{0,13},{1,12},{2,15},{3,14},{4,9},{5,8},{6,11},{7,10},{8,5},{9,4},... | collective-permute-start | bytes 491528 | tf_op jit(solution)/shard_map/ppermute | solution.py:32
  45.3 14.6 %collective-permute-start.6 = (bf16[128,640]{1,0:T(8,128)(2,1)}, bf16[128,640]{1,0:T(8,128)(2,1)}, u32[]{:S(2)}, u32[]{:S(2)}) collective-permute-start(bf16[128,640]{1,0:T(8,128)(2,1)} %get-tuple-element.506.refs_0_), channel_id=1, source_target_pairs={{0,8},{1,9},{2,10},{3,11},{4,12},{5,13},{6,14},{7,15},{8,0},{9,1},... | collective-permute-start | bytes 491528 | tf_op jit(solution)/shard_map/ppermute | solution.py:32
  45.5 16.8 %collective-permute-start.5 = (bf16[128,640]{1,0:T(8,128)(2,1)}, bf16[128,640]{1,0:T(8,128)(2,1)}, u32[]{:S(2)}, u32[]{:S(2)}) collective-permute-start(bf16[128,640]{1,0:T(8,128)(2,1)} %get-tuple-element.506.refs_0_), channel_id=1, source_target_pairs={{0,1},{1,0},{2,3},{3,2},{4,5},{5,4},{6,7},{7,6},{8,9},{9,8},{10,11... | collective-permute-start | bytes 491528 | tf_op jit(solution)/shard_map/ppermute | solution.py:32
  64.3 7.4 %collective-permute-start.10 = (bf16[128,640]{1,0:T(8,128)(2,1)}, bf16[128,640]{1,0:T(8,128)(2,1)S(1)}, u32[]{:S(2)}, u32[]{:S(2)}) collective-permute-start(bf16[128,640]{1,0:T(8,128)(2,1)} %collective-permute-done.5.refs_2_), channel_id=1, source_target_pairs={{0,8},{1,9},{2,10},{3,11},{4,12},{5,13},{6,14},{7,15},{8,0},{9,1},... | collective-permute-start | bytes 491528 | tf_op jit(solution)/shard_map/ppermute | solution.py:32
  80.5 29.5 %collective-permute-start.14 = (bf16[480,1280]{1,0:T(8,128)(2,1)S(1)}, bf16[480,1280]{1,0:T(8,128)(2,1)S(1)}, u32[]{:S(2)}, u32[]{:S(2)}) collective-permute-start(bf16[480,1280]{1,0:T(8,128)(2,1)S(1)} %copy-done.23), channel_id=1, source_target_pairs={{0,1},{1,0},{2,3},{3,2},{4,5},{5,4},{6,7},{7,6},{8,9},{9,8},{10,11... | collective-permute-start | bytes 3686408 | tf_op jit(solution)/shard_map/ppermute | solution.py:32
  81.8 18.4 %collective-permute-start.15 = (bf16[480,640]{1,0:T(8,128)(2,1)}, bf16[480,640]{1,0:T(8,128)(2,1)S(1)}, u32[]{:S(2)}, u32[]{:S(2)}) collective-permute-start(bf16[480,640]{1,0:T(8,128)(2,1)} %collective-permute-done.8.refs_0_), channel_id=1, source_target_pairs={{0,12},{1,13},{2,14},{3,15},{4,8},{5,9},{6,10},{7,11},{8,4},{9,5},... | collective-permute-start | bytes 1843208 | tf_op jit(solution)/shard_map/ppermute | solution.py:32
  81.8 28.2 %collective-permute-start.16 = (bf16[480,640]{1,0:T(8,128)(2,1)}, bf16[480,640]{1,0:T(8,128)(2,1)S(1)}, u32[]{:S(2)}, u32[]{:S(2)}) collective-permute-start(bf16[480,640]{1,0:T(8,128)(2,1)} %collective-permute-done.8.refs_0_), channel_id=1, source_target_pairs={{0,4},{1,5},{2,6},{3,7},{4,0},{5,1},{6,2},{7,3},{8,12},{9,13},{10,... | collective-permute-start | bytes 1843208 | tf_op jit(solution)/shard_map/ppermute | solution.py:32
  82.7 27.3 %collective-permute-start.17 = (bf16[480,640]{1,0:T(8,128)(2,1)}, bf16[480,640]{1,0:T(8,128)(2,1)S(1)}, u32[]{:S(2)}, u32[]{:S(2)}) collective-permute-start(bf16[480,640]{1,0:T(8,128)(2,1)} %collective-permute-done.8.refs_0_), channel_id=1, source_target_pairs={{0,8},{1,9},{2,10},{3,11},{4,12},{5,13},{6,14},{7,15},{8,0},{9,1},... | collective-permute-start | bytes 1843208 | tf_op jit(solution)/shard_map/ppermute | solution.py:32
  111.7 8.2 %collective-permute-start.18 = (bf16[1920,640]{1,0:T(8,128)(2,1)S(1)}, bf16[1920,640]{1,0:T(8,128)(2,1)S(1)}, u32[]{:S(2)}, u32[]{:S(2)}) collective-permute-start(bf16[1920,640]{1,0:T(8,128)(2,1)S(1)} %stack.153.args_6_.args_8_), channel_id=1, source_target_pairs={{0,2},{1,3},{2,0},{3,1},{4,6},{5,7},{6,4},{7,5},{8,10},{9,11},{10,... | collective-permute-start | bytes 7372808 | tf_op jit(solution)/shard_map/ppermute | solution.py:32
  151.7 21.0 %collective-permute-start.29 = (bf16[960,128]{1,0:T(8,128)(2,1)S(1)}, bf16[960,128]{1,0:T(8,128)(2,1)S(1)}, u32[]{:S(2)}, u32[]{:S(2)}) collective-permute-start(bf16[960,128]{1,0:T(8,128)(2,1)S(1)} %bitcast.205), channel_id=1, source_target_pairs={{0,0},{1,16},{2,2},{3,18},{4,4},{5,20},{6,6},{7,22},{8,8},{9,24},{... | collective-permute-start | bytes 737288 | tf_op jit(solution)/shard_map/ppermute | solution.py:41
  199.8 16.9 %collective-permute-start.38 = (bf16[960,128]{1,0:T(8,128)(2,1)}, bf16[960,128]{1,0:T(8,128)(2,1)S(1)}, u32[]{:S(2)}, u32[]{:S(2)}) collective-permute-start(bf16[960,128]{1,0:T(8,128)(2,1)} %get-tuple-element.637), channel_id=1, source_target_pairs={{0,0},{1,16},{2,2},{3,18},{4,4},{5,20},{6,6},{7,22},{8,8},{9,24},{... | collective-permute-start | bytes 737288 | tf_op jit(solution)/shard_map/ppermute | solution.py:41
  281.8 8.3 %collective-permute-start.55 = (bf16[2,2,4,80,960]{4,3,2,0,1:T(8,128)(2,1)S(1)}, bf16[2,2,4,80,960]{4,3,2,0,1:T(8,128)(2,1)S(1)}, u32[]{:S(2)}, u32[]{:S(2)}) collective-permute-start(bf16[2,2,4,80,960]{4,3,2,0,1:T(8,128)(2,1)S(1)} %copy.38), channel_id=1, source_target_pairs={{0,2},{1,3},{2,0},{3,1},{4,6},{5,7},{6,4},{7,5},{8,10},{9,11},{10,... | collective-permute-start | bytes 7372808 | tf_op jit(solution)/shard_map/ppermute | solution.py:32
  291.6 16.0 %collective-permute-start.58 = (bf16[2,2,4,120,640]{4,3,2,1,0:T(8,128)(2,1)S(1)}, bf16[2,2,4,120,640]{4,3,2,1,0:T(8,128)(2,1)S(1)}, u32[]{:S(2)}, u32[]{:S(2)}) collective-permute-start(bf16[2,2,4,120,640]{4,3,2,1,0:T(8,128)(2,1)S(1)} %get-tuple-element.761), channel_id=1, source_target_pairs={{0,2},{1,3},{2,0},{3,1},{4,6},{5,7},{6,4},{7,5},{8,10},{9,11},{10,... | collective-permute-start | bytes 7372808 | tf_op jit(solution)/shard_map/ppermute | solution.py:32
  291.7 15.9 %collective-permute-start.56 = (bf16[2,2,80,960]{3,2,1,0:T(8,128)(2,1)S(1)}, bf16[2,2,80,960]{3,2,1,0:T(8,128)(2,1)S(1)}, u32[]{:S(2)}, u32[]{:S(2)}) collective-permute-start(bf16[2,2,80,960]{3,2,1,0:T(8,128)(2,1)S(1)} %slice_bitcast_fusion.7), channel_id=1, source_target_pairs={{0,1},{1,0},{2,3},{3,2},{4,5},{5,4},{6,7},{7,6},{8,9},{9,8},{10,11... | collective-permute-start | bytes 1843208 | tf_op jit(solution)/shard_map/ppermute | solution.py:32
  291.7 15.9 %collective-permute-start.57 = (bf16[2,2,80,960]{3,2,1,0:T(8,128)(2,1)S(1)}, bf16[2,2,80,960]{3,2,1,0:T(8,128)(2,1)S(1)}, u32[]{:S(2)}, u32[]{:S(2)}) collective-permute-start(bf16[2,2,80,960]{3,2,1,0:T(8,128)(2,1)S(1)} %slice_bitcast_fusion.6), channel_id=1, source_target_pairs={{0,4},{1,5},{2,6},{3,7},{4,0},{5,1},{6,2},{7,3},{8,12},{9,13},{10,... | collective-permute-start | bytes 1843208 | tf_op jit(solution)/shard_map/ppermute | solution.py:32
  308.2 11.1 %collective-permute-start.61 = (bf16[1024,640]{1,0:T(8,128)(2,1)S(1)}, bf16[1024,640]{1,0:T(8,128)(2,1)S(1)}, u32[]{:S(2)}, u32[]{:S(2)}) collective-permute-start(bf16[1024,640]{1,0:T(8,128)(2,1)S(1)} %get-tuple-element.778), channel_id=1, source_target_pairs={{0,2},{1,3},{2,0},{3,1},{4,6},{5,7},{6,4},{7,5},{8,10},{9,11},{10,... | collective-permute-start | bytes 3932168 | tf_op jit(solution)/shard_map/ppermute | solution.py:32
  309.6 9.3 %collective-permute-start.59 = (bf16[2,80,960]{2,1,0:T(8,128)(2,1)S(1)}, bf16[2,80,960]{2,1,0:T(8,128)(2,1)S(1)}, u32[]{:S(2)}, u32[]{:S(2)}) collective-permute-start(bf16[2,80,960]{2,1,0:T(8,128)(2,1)S(1)} %slice_bitcast_fusion.18), channel_id=1, source_target_pairs={{0,4},{1,5},{2,6},{3,7},{4,0},{5,1},{6,2},{7,3},{8,12},{9,13},{10,... | collective-permute-start | bytes 921608 | tf_op jit(solution)/shard_map/ppermute | solution.py:32
  310.3 9.0 %collective-permute-start.60 = (bf16[2,80,960]{2,1,0:T(8,128)(2,1)S(1)}, bf16[2,80,960]{2,1,0:T(8,128)(2,1)S(1)}, u32[]{:S(2)}, u32[]{:S(2)}) collective-permute-start(bf16[2,80,960]{2,1,0:T(8,128)(2,1)S(1)} %slice_bitcast_fusion.17), channel_id=1, source_target_pairs={{0,1},{1,0},{2,3},{3,2},{4,5},{5,4},{6,7},{7,6},{8,9},{9,8},{10,11... | collective-permute-start | bytes 921608 | tf_op jit(solution)/shard_map/ppermute | solution.py:32
  319.5 9.0 %collective-permute-start.65 = (bf16[2,2,4,120,640]{4,3,2,1,0:T(8,128)(2,1)S(1)}, bf16[2,2,4,120,640]{4,3,2,1,0:T(8,128)(2,1)S(1)}, u32[]{:S(2)}, u32[]{:S(2)}) collective-permute-start(bf16[2,2,4,120,640]{4,3,2,1,0:T(8,128)(2,1)S(1)} %get-tuple-element.800), channel_id=1, source_target_pairs={{0,2},{1,3},{2,0},{3,1},{4,6},{5,7},{6,4},{7,5},{8,10},{9,11},{10,... | collective-permute-start | bytes 7372808 | tf_op jit(solution)/shard_map/ppermute | solution.py:32
  330.2 9.1 %collective-permute-start.67 = (bf16[128,640]{1,0:T(8,128)(2,1)S(1)}, bf16[128,640]{1,0:T(8,128)(2,1)S(1)}, u32[]{:S(2)}, u32[]{:S(2)}) collective-permute-start(bf16[128,640]{1,0:T(8,128)(2,1)S(1)} %add_convert_fusion.6), channel_id=1, source_target_pairs={{0,4},{1,5},{2,6},{3,7},{4,0},{5,1},{6,2},{7,3},{8,12},{9,13},{10,... | collective-permute-start | bytes 491528 | tf_op jit(solution)/shard_map/ppermute | solution.py:32
  330.9 8.9 %collective-permute-start.68 = (bf16[128,640]{1,0:T(8,128)(2,1)S(1)}, bf16[128,640]{1,0:T(8,128)(2,1)S(1)}, u32[]{:S(2)}, u32[]{:S(2)}) collective-permute-start(bf16[128,640]{1,0:T(8,128)(2,1)S(1)} %add_convert_fusion.5), channel_id=1, source_target_pairs={{0,1},{1,0},{2,3},{3,2},{4,5},{5,4},{6,7},{7,6},{8,9},{9,8},{10,11... | collective-permute-start | bytes 491528 | tf_op jit(solution)/shard_map/ppermute | solution.py:32
  332.3 7.5 %collective-permute-start.69 = (bf16[128,640]{1,0:T(8,128)(2,1)S(1)}, bf16[128,640]{1,0:T(8,128)(2,1)S(1)}, u32[]{:S(2)}, u32[]{:S(2)}) collective-permute-start(bf16[128,640]{1,0:T(8,128)(2,1)S(1)} %add_convert_fusion.4), channel_id=1, source_target_pairs={{0,8},{1,9},{2,10},{3,11},{4,12},{5,13},{6,14},{7,15},{8,0},{9,1},... | collective-permute-start | bytes 491528 | tf_op jit(solution)/shard_map/ppermute | solution.py:32
  339.8 17.2 %collective-permute-start.70 = (bf16[4,120,640]{2,1,0:T(8,128)(2,1)S(1)}, bf16[4,120,640]{2,1,0:T(8,128)(2,1)S(1)}, u32[]{:S(2)}, u32[]{:S(2)}) collective-permute-start(bf16[4,120,640]{2,1,0:T(8,128)(2,1)S(1)} %get-tuple-element.818), channel_id=1, source_target_pairs={{0,1},{1,0},{2,3},{3,2},{4,5},{5,4},{6,7},{7,6},{8,9},{9,8},{10,11... | collective-permute-start | bytes 1843208 | tf_op jit(solution)/shard_map/ppermute | solution.py:32
  340.3 14.8 %collective-permute-start.71 = (bf16[80,960]{1,0:T(8,128)(2,1)S(1)}, bf16[80,960]{1,0:T(8,128)(2,1)S(1)}, u32[]{:S(2)}, u32[]{:S(2)}) collective-permute-start(bf16[80,960]{1,0:T(8,128)(2,1)S(1)} %get-tuple-element.819), channel_id=1, source_target_pairs={{0,24},{1,25},{2,26},{3,27},{4,28},{5,29},{6,30},{7,31},{8,16},{9,... | collective-permute-start | bytes 460808 | tf_op jit(solution)/shard_map/ppermute | solution.py:32
  342.3 14.7 %collective-permute-start.72 = (bf16[80,960]{1,0:T(8,128)(2,1)S(1)}, bf16[80,960]{1,0:T(8,128)(2,1)S(1)}, u32[]{:S(2)}, u32[]{:S(2)}) collective-permute-start(bf16[80,960]{1,0:T(8,128)(2,1)S(1)} %get-tuple-element.820), channel_id=1, source_target_pairs={{0,16},{1,17},{2,18},{3,19},{4,20},{5,21},{6,22},{7,23},{8,24},{9,... | collective-permute-start | bytes 460808 | tf_op jit(solution)/shard_map/ppermute | solution.py:32
  342.7 14.3 %collective-permute-start.73 = (bf16[80,960]{1,0:T(8,128)(2,1)S(1)}, bf16[80,960]{1,0:T(8,128)(2,1)S(1)}, u32[]{:S(2)}, u32[]{:S(2)}) collective-permute-start(bf16[80,960]{1,0:T(8,128)(2,1)S(1)} %slice_bitcast_fusion.25), channel_id=1, source_target_pairs={{0,8},{1,9},{2,10},{3,11},{4,12},{5,13},{6,14},{7,15},{8,0},{9,1},... | collective-permute-start | bytes 460808 | tf_op jit(solution)/shard_map/ppermute | solution.py:32
  357.2 18.7 %collective-permute-start.79 = (bf16[2,2,4,128,640]{4,3,2,1,0:T(8,128)(2,1)S(1)}, bf16[2,2,4,128,640]{4,3,2,1,0:T(8,128)(2,1)S(1)}, u32[]{:S(2)}, u32[]{:S(2)}) collective-permute-start(bf16[2,2,4,128,640]{4,3,2,1,0:T(8,128)(2,1)S(1)} %get-tuple-element.863), channel_id=1, source_target_pairs={{0,2},{1,3},{2,0},{3,1},{4,6},{5,7},{6,4},{7,5},{8,10},{9,11},{10,... | collective-permute-start | bytes 7864328 | tf_op jit(solution)/shard_map/ppermute | solution.py:32
  358.7 7.6 %collective-permute-start.76 = (bf16[80,960]{1,0:T(8,128)(2,1)S(1)}, bf16[80,960]{1,0:T(8,128)(2,1)S(1)}, u32[]{:S(2)}, u32[]{:S(2)}) collective-permute-start(bf16[80,960]{1,0:T(8,128)(2,1)S(1)} %fusion.18), channel_id=1, source_target_pairs={{0,24},{1,25},{2,26},{3,27},{4,28},{5,29},{6,30},{7,31},{8,16},{9,... | collective-permute-start | bytes 460808 | tf_op jit(solution)/shard_map/ppermute | solution.py:32
  360.3 15.1 %collective-permute-start.74 = (bf16[4,120,640]{2,1,0:T(8,128)(2,1)S(1)}, bf16[4,120,640]{2,1,0:T(8,128)(2,1)S(1)}, u32[]{:S(2)}, u32[]{:S(2)}) collective-permute-start(bf16[4,120,640]{2,1,0:T(8,128)(2,1)S(1)} %get-tuple-element.858), channel_id=1, source_target_pairs={{0,1},{1,0},{2,3},{3,2},{4,5},{5,4},{6,7},{7,6},{8,9},{9,8},{10,11... | collective-permute-start | bytes 1843208 | tf_op jit(solution)/shard_map/ppermute | solution.py:32
  361.2 14.8 %collective-permute-start.75 = (bf16[4,120,640]{2,1,0:T(8,128)(2,1)S(1)}, bf16[4,120,640]{2,1,0:T(8,128)(2,1)S(1)}, u32[]{:S(2)}, u32[]{:S(2)}) collective-permute-start(bf16[4,120,640]{2,1,0:T(8,128)(2,1)S(1)} %fusion.10), channel_id=1, source_target_pairs={{0,4},{1,5},{2,6},{3,7},{4,0},{5,1},{6,2},{7,3},{8,12},{9,13},{10,... | collective-permute-start | bytes 1843208 | tf_op jit(solution)/shard_map/ppermute | solution.py:32
  362.4 11.6 %collective-permute-start.77 = (bf16[80,960]{1,0:T(8,128)(2,1)S(1)}, bf16[80,960]{1,0:T(8,128)(2,1)S(1)}, u32[]{:S(2)}, u32[]{:S(2)}) collective-permute-start(bf16[80,960]{1,0:T(8,128)(2,1)S(1)} %fusion.18), channel_id=1, source_target_pairs={{0,16},{1,17},{2,18},{3,19},{4,20},{5,21},{6,22},{7,23},{8,24},{9,... | collective-permute-start | bytes 460808 | tf_op jit(solution)/shard_map/ppermute | solution.py:32
  366.3 8.2 %collective-permute-start.78 = (bf16[80,960]{1,0:T(8,128)(2,1)S(1)}, bf16[80,960]{1,0:T(8,128)(2,1)S(1)}, u32[]{:S(2)}, u32[]{:S(2)}) collective-permute-start(bf16[80,960]{1,0:T(8,128)(2,1)S(1)} %fusion.18), channel_id=1, source_target_pairs={{0,8},{1,9},{2,10},{3,11},{4,12},{5,13},{6,14},{7,15},{8,0},{9,1},... | collective-permute-start | bytes 460808 | tf_op jit(solution)/shard_map/ppermute | solution.py:32
  376.4 15.9 %collective-permute-start.80 = (bf16[4,120,640]{2,1,0:T(8,128)(2,1)S(1)}, bf16[4,120,640]{2,1,0:T(8,128)(2,1)S(1)}, u32[]{:S(2)}, u32[]{:S(2)}) collective-permute-start(bf16[4,120,640]{2,1,0:T(8,128)(2,1)S(1)} %get-tuple-element.874), channel_id=1, source_target_pairs={{0,1},{1,0},{2,3},{3,2},{4,5},{5,4},{6,7},{7,6},{8,9},{9,8},{10,11... | collective-permute-start | bytes 1843208 | tf_op jit(solution)/shard_map/ppermute | solution.py:32
  377.0 15.3 %collective-permute-start.84 = (bf16[4,80,960]{2,1,0:T(8,128)(2,1)S(1)}, bf16[4,80,960]{2,1,0:T(8,128)(2,1)S(1)}, u32[]{:S(2)}, u32[]{:S(2)}) collective-permute-start(bf16[4,80,960]{2,1,0:T(8,128)(2,1)S(1)} %get-tuple-element.878), channel_id=1, source_target_pairs={{0,4},{1,5},{2,6},{3,7},{4,0},{5,1},{6,2},{7,3},{8,12},{9,13},{10,... | collective-permute-start | bytes 1843208 | tf_op jit(solution)/shard_map/ppermute | solution.py:32
  379.9 12.4 %collective-permute-start.82 = (bf16[120,640]{1,0:T(8,128)(2,1)S(1)}, bf16[120,640]{1,0:T(8,128)(2,1)S(1)}, u32[]{:S(2)}, u32[]{:S(2)}) collective-permute-start(bf16[120,640]{1,0:T(8,128)(2,1)S(1)} %get-tuple-element.876), channel_id=1, source_target_pairs={{0,16},{1,17},{2,18},{3,19},{4,20},{5,21},{6,22},{7,23},{8,24},{9,... | collective-permute-start | bytes 460808 | tf_op jit(solution)/shard_map/ppermute | solution.py:32
  379.9 12.4 %collective-permute-start.83 = (bf16[120,640]{1,0:T(8,128)(2,1)S(1)}, bf16[120,640]{1,0:T(8,128)(2,1)S(1)}, u32[]{:S(2)}, u32[]{:S(2)}) collective-permute-start(bf16[120,640]{1,0:T(8,128)(2,1)S(1)} %get-tuple-element.877), channel_id=1, source_target_pairs={{0,8},{1,9},{2,10},{3,11},{4,12},{5,13},{6,14},{7,15},{8,0},{9,1},... | collective-permute-start | bytes 460808 | tf_op jit(solution)/shard_map/ppermute | solution.py:32
  392.5 17.1 %collective-permute-start.85 = (bf16[4,120,640]{2,1,0:T(8,128)(2,1)S(1)}, bf16[4,120,640]{2,1,0:T(8,128)(2,1)S(1)}, u32[]{:S(2)}, u32[]{:S(2)}) collective-permute-start(bf16[4,120,640]{2,1,0:T(8,128)(2,1)S(1)} %get-tuple-element.885), channel_id=1, source_target_pairs={{0,1},{1,0},{2,3},{3,2},{4,5},{5,4},{6,7},{7,6},{8,9},{9,8},{10,11... | collective-permute-start | bytes 1843208 | tf_op jit(solution)/shard_map/ppermute | solution.py:32
  393.2 16.4 %collective-permute-start.86 = (bf16[4,120,640]{2,1,0:T(8,128)(2,1)S(1)}, bf16[4,120,640]{2,1,0:T(8,128)(2,1)S(1)}, u32[]{:S(2)}, u32[]{:S(2)}) collective-permute-start(bf16[4,120,640]{2,1,0:T(8,128)(2,1)S(1)} %fusion.7), channel_id=1, source_target_pairs={{0,4},{1,5},{2,6},{3,7},{4,0},{5,1},{6,2},{7,3},{8,12},{9,13},{10,... | collective-permute-start | bytes 1843208 | tf_op jit(solution)/shard_map/ppermute | solution.py:32
  398.1 11.6 %collective-permute-start.88 = (bf16[120,640]{1,0:T(8,128)(2,1)S(1)}, bf16[120,640]{1,0:T(8,128)(2,1)S(1)}, u32[]{:S(2)}, u32[]{:S(2)}) collective-permute-start(bf16[120,640]{1,0:T(8,128)(2,1)S(1)} %fusion.24), channel_id=1, source_target_pairs={{0,16},{1,17},{2,18},{3,19},{4,20},{5,21},{6,22},{7,23},{8,24},{9,... | collective-permute-start | bytes 460808 | tf_op jit(solution)/shard_map/ppermute | solution.py:32
  398.1 11.6 %collective-permute-start.89 = (bf16[120,640]{1,0:T(8,128)(2,1)S(1)}, bf16[120,640]{1,0:T(8,128)(2,1)S(1)}, u32[]{:S(2)}, u32[]{:S(2)}) collective-permute-start(bf16[120,640]{1,0:T(8,128)(2,1)S(1)} %fusion.24), channel_id=1, source_target_pairs={{0,8},{1,9},{2,10},{3,11},{4,12},{5,13},{6,14},{7,15},{8,0},{9,1},... | collective-permute-start | bytes 460808 | tf_op jit(solution)/shard_map/ppermute | solution.py:32
  410.1 15.4 %collective-permute-start.90 = (bf16[4,128,640]{2,1,0:T(8,128)(2,1)S(1)}, bf16[4,128,640]{2,1,0:T(8,128)(2,1)S(1)}, u32[]{:S(2)}, u32[]{:S(2)}) collective-permute-start(bf16[4,128,640]{2,1,0:T(8,128)(2,1)S(1)} %get-tuple-element.897), channel_id=1, source_target_pairs={{0,1},{1,0},{2,3},{3,2},{4,5},{5,4},{6,7},{7,6},{8,9},{9,8},{10,11... | collective-permute-start | bytes 1966088 | tf_op jit(solution)/shard_map/ppermute | solution.py:32
  410.6 14.9 %collective-permute-start.94 = (bf16[4,120,640]{2,1,0:T(8,128)(2,1)S(1)}, bf16[4,120,640]{2,1,0:T(8,128)(2,1)S(1)}, u32[]{:S(2)}, u32[]{:S(2)}) collective-permute-start(bf16[4,120,640]{2,1,0:T(8,128)(2,1)S(1)} %get-tuple-element.901), channel_id=1, source_target_pairs={{0,4},{1,5},{2,6},{3,7},{4,0},{5,1},{6,2},{7,3},{8,12},{9,13},{10,... | collective-permute-start | bytes 1843208 | tf_op jit(solution)/shard_map/ppermute | solution.py:32
  412.9 12.6 %collective-permute-start.92 = (bf16[120,640]{1,0:T(8,128)(2,1)S(1)}, bf16[120,640]{1,0:T(8,128)(2,1)S(1)}, u32[]{:S(2)}, u32[]{:S(2)}) collective-permute-start(bf16[120,640]{1,0:T(8,128)(2,1)S(1)} %get-tuple-element.899), channel_id=1, source_target_pairs={{0,16},{1,17},{2,18},{3,19},{4,20},{5,21},{6,22},{7,23},{8,24},{9,... | collective-permute-start | bytes 460808 | tf_op jit(solution)/shard_map/ppermute | solution.py:32
  412.9 12.6 %collective-permute-start.93 = (bf16[120,640]{1,0:T(8,128)(2,1)S(1)}, bf16[120,640]{1,0:T(8,128)(2,1)S(1)}, u32[]{:S(2)}, u32[]{:S(2)}) collective-permute-start(bf16[120,640]{1,0:T(8,128)(2,1)S(1)} %get-tuple-element.900), channel_id=1, source_target_pairs={{0,8},{1,9},{2,10},{3,11},{4,12},{5,13},{6,14},{7,15},{8,0},{9,1},... | collective-permute-start | bytes 460808 | tf_op jit(solution)/shard_map/ppermute | solution.py:32
  425.8 16.6 %collective-permute-start.95 = (bf16[4,128,640]{2,1,0:T(8,128)(2,1)S(1)}, bf16[4,128,640]{2,1,0:T(8,128)(2,1)S(1)}, u32[]{:S(2)}, u32[]{:S(2)}) collective-permute-start(bf16[4,128,640]{2,1,0:T(8,128)(2,1)S(1)} %get-tuple-element.908), channel_id=1, source_target_pairs={{0,1},{1,0},{2,3},{3,2},{4,5},{5,4},{6,7},{7,6},{8,9},{9,8},{10,11... | collective-permute-start | bytes 1966088 | tf_op jit(solution)/shard_map/ppermute | solution.py:32
  427.0 15.4 %collective-permute-start.96 = (bf16[4,128,640]{2,1,0:T(8,128)(2,1)S(1)}, bf16[4,128,640]{2,1,0:T(8,128)(2,1)S(1)}, u32[]{:S(2)}, u32[]{:S(2)}) collective-permute-start(bf16[4,128,640]{2,1,0:T(8,128)(2,1)S(1)} %fusion), channel_id=1, source_target_pairs={{0,4},{1,5},{2,6},{3,7},{4,0},{5,1},{6,2},{7,3},{8,12},{9,13},{10,... | collective-permute-start | bytes 1966088 | tf_op jit(solution)/shard_map/ppermute | solution.py:32
  429.6 12.7 %collective-permute-start.98 = (bf16[120,640]{1,0:T(8,128)(2,1)S(1)}, bf16[120,640]{1,0:T(8,128)(2,1)S(1)}, u32[]{:S(2)}, u32[]{:S(2)}) collective-permute-start(bf16[120,640]{1,0:T(8,128)(2,1)S(1)} %fusion.21), channel_id=1, source_target_pairs={{0,16},{1,17},{2,18},{3,19},{4,20},{5,21},{6,22},{7,23},{8,24},{9,... | collective-permute-start | bytes 460808 | tf_op jit(solution)/shard_map/ppermute | solution.py:32
  429.6 12.7 %collective-permute-start.99 = (bf16[120,640]{1,0:T(8,128)(2,1)S(1)}, bf16[120,640]{1,0:T(8,128)(2,1)S(1)}, u32[]{:S(2)}, u32[]{:S(2)}) collective-permute-start(bf16[120,640]{1,0:T(8,128)(2,1)S(1)} %fusion.21), channel_id=1, source_target_pairs={{0,8},{1,9},{2,10},{3,11},{4,12},{5,13},{6,14},{7,15},{8,0},{9,1},... | collective-permute-start | bytes 460808 | tf_op jit(solution)/shard_map/ppermute | solution.py:32
  442.8 17.9 %collective-permute-start.104 = (bf16[2,4,80,960]{3,2,1,0:T(8,128)(2,1)S(1)}, bf16[2,4,80,960]{3,2,1,0:T(8,128)(2,1)S(1)}, u32[]{:S(2)}, u32[]{:S(2)}) collective-permute-start(bf16[2,4,80,960]{3,2,1,0:T(8,128)(2,1)S(1)} %pad_maximum_fusion.near_ref), channel_id=1, source_target_pairs={{0,2},{1,3},{2,0},{3,1},{4,6},{5,7},{6,4},{7,5},{8,10},{9,11},{10,... | collective-permute-start | bytes 3686408 | tf_op jit(solution)/shard_map/ppermute | solution.py:32
  444.7 16.1 %collective-permute-start.103 = (bf16[4,120,640]{2,1,0:T(8,128)(2,1)S(1)}, bf16[4,120,640]{2,1,0:T(8,128)(2,1)S(1)}, u32[]{:S(2)}, u32[]{:S(2)}) collective-permute-start(bf16[4,120,640]{2,1,0:T(8,128)(2,1)S(1)} %get-tuple-element.924), channel_id=1, source_target_pairs={{0,4},{1,5},{2,6},{3,7},{4,0},{5,1},{6,2},{7,3},{8,12},{9,13},{10,... | collective-permute-start | bytes 1843208 | tf_op jit(solution)/shard_map/ppermute | solution.py:32
  447.3 13.4 %collective-permute-start.101 = (bf16[128,640]{1,0:T(8,128)(2,1)S(1)}, bf16[128,640]{1,0:T(8,128)(2,1)S(1)}, u32[]{:S(2)}, u32[]{:S(2)}) collective-permute-start(bf16[128,640]{1,0:T(8,128)(2,1)S(1)} %get-tuple-element.922), channel_id=1, source_target_pairs={{0,16},{1,17},{2,18},{3,19},{4,20},{5,21},{6,22},{7,23},{8,24},{9,... | collective-permute-start | bytes 491528 | tf_op jit(solution)/shard_map/ppermute | solution.py:32
  447.3 13.4 %collective-permute-start.102 = (bf16[128,640]{1,0:T(8,128)(2,1)S(1)}, bf16[128,640]{1,0:T(8,128)(2,1)S(1)}, u32[]{:S(2)}, u32[]{:S(2)}) collective-permute-start(bf16[128,640]{1,0:T(8,128)(2,1)S(1)} %get-tuple-element.923), channel_id=1, source_target_pairs={{0,8},{1,9},{2,10},{3,11},{4,12},{5,13},{6,14},{7,15},{8,0},{9,1},... | collective-permute-start | bytes 491528 | tf_op jit(solution)/shard_map/ppermute | solution.py:32
  461.0 16.0 %collective-permute-start.108 = (bf16[2,4,120,640]{3,2,1,0:T(8,128)(2,1)S(1)}, bf16[2,4,120,640]{3,2,1,0:T(8,128)(2,1)S(1)}, u32[]{:S(2)}, u32[]{:S(2)}) collective-permute-start(bf16[2,4,120,640]{3,2,1,0:T(8,128)(2,1)S(1)} %pad_maximum_fusion.2.near_ref), channel_id=1, source_target_pairs={{0,2},{1,3},{2,0},{3,1},{4,6},{5,7},{6,4},{7,5},{8,10},{9,11},{10,... | collective-permute-start | bytes 3686408 | tf_op jit(solution)/shard_map/ppermute | solution.py:32
  461.7 15.3 %collective-permute-start.109 = (bf16[2,4,120,640]{3,2,1,0:T(8,128)(2,1)S(1)}, bf16[2,4,120,640]{3,2,1,0:T(8,128)(2,1)S(1)}, u32[]{:S(2)}, u32[]{:S(2)}) collective-permute-start(bf16[2,4,120,640]{3,2,1,0:T(8,128)(2,1)S(1)} %pad_maximum_fusion.3.near_ref), channel_id=1, source_target_pairs={{0,2},{1,3},{2,0},{3,1},{4,6},{5,7},{6,4},{7,5},{8,10},{9,11},{10,... | collective-permute-start | bytes 3686408 | tf_op jit(solution)/shard_map/ppermute | solution.py:32
  461.7 7.4 %collective-permute-start.105 = (bf16[128,640]{1,0:T(8,128)(2,1)S(1)}, bf16[128,640]{1,0:T(8,128)(2,1)S(1)}, u32[]{:S(2)}, u32[]{:S(2)}) collective-permute-start(bf16[128,640]{1,0:T(8,128)(2,1)S(1)} %fusion.15), channel_id=1, source_target_pairs={{0,24},{1,25},{2,26},{3,27},{4,28},{5,29},{6,30},{7,31},{8,16},{9,... | collective-permute-start | bytes 491528 | tf_op jit(solution)/shard_map/ppermute | solution.py:32
  463.3 13.7 %collective-permute-start.106 = (bf16[128,640]{1,0:T(8,128)(2,1)S(1)}, bf16[128,640]{1,0:T(8,128)(2,1)S(1)}, u32[]{:S(2)}, u32[]{:S(2)}) collective-permute-start(bf16[128,640]{1,0:T(8,128)(2,1)S(1)} %fusion.15), channel_id=1, source_target_pairs={{0,16},{1,17},{2,18},{3,19},{4,20},{5,21},{6,22},{7,23},{8,24},{9,... | collective-permute-start | bytes 491528 | tf_op jit(solution)/shard_map/ppermute | solution.py:32
  463.3 13.7 %collective-permute-start.107 = (bf16[128,640]{1,0:T(8,128)(2,1)S(1)}, bf16[128,640]{1,0:T(8,128)(2,1)S(1)}, u32[]{:S(2)}, u32[]{:S(2)}) collective-permute-start(bf16[128,640]{1,0:T(8,128)(2,1)S(1)} %fusion.15), channel_id=1, source_target_pairs={{0,8},{1,9},{2,10},{3,11},{4,12},{5,13},{6,14},{7,15},{8,0},{9,1},... | collective-permute-start | bytes 491528 | tf_op jit(solution)/shard_map/ppermute | solution.py:32
  477.2 16.4 %collective-permute-start.110 = (bf16[4,128,640]{2,1,0:T(8,128)(2,1)S(1)}, bf16[4,128,640]{2,1,0:T(8,128)(2,1)S(1)}, u32[]{:S(2)}, u32[]{:S(2)}) collective-permute-start(bf16[4,128,640]{2,1,0:T(8,128)(2,1)S(1)} %get-tuple-element.950), channel_id=1, source_target_pairs={{0,4},{1,5},{2,6},{3,7},{4,0},{5,1},{6,2},{7,3},{8,12},{9,13},{10,... | collective-permute-start | bytes 1966088 | tf_op jit(solution)/shard_map/ppermute | solution.py:32
  477.8 15.8 %collective-permute-start.111 = (bf16[960,128]{1,0:T(8,128)(2,1)S(1)}, bf16[960,128]{1,0:T(8,128)(2,1)S(1)}, u32[]{:S(2)}, u32[]{:S(2)}) collective-permute-start(bf16[960,128]{1,0:T(8,128)(2,1)S(1)} %copy-done.41), channel_id=1, source_target_pairs={{0,0},{1,16},{2,2},{3,18},{4,4},{5,20},{6,6},{7,22},{8,8},{9,24},{... | collective-permute-start | bytes 737288 | tf_op jit(solution)/shard_map/ppermute | solution.py:41
  (91 other events, 767.9 us)

commit v6 on v5

--- a/solution.py
+++ b/solution.py
@@ -215,18 +215,20 @@
 
 
 def join_call(coords, weights, bases=()):
-    arrays = arrays_of(weights)
+    arrays, place = arrays_of(weights), pl.BlockSpec(memory_space=pl.ANY)
+    if not bases:
+        arrays, place = apart(arrays), hbm()
     return pl.pallas_call(
         functools.partial(join_kernel, weights, len(bases)),
         name="join_weights",
         out_shape=tuple(pltpu.VMEM(w.shape, BF) for w in weights),
-        in_specs=[sm()] + [vm()] * len(bases) + [hbm()] * len(arrays),
+        in_specs=[sm()] + [vm()] * len(bases) + [place] * len(arrays),
         out_specs=tuple(vm() for _ in weights),
         scratch_shapes=scratch_of(weights)[-1:],
         input_output_aliases={1 + i: i for i in range(len(bases))},
         compiler_params=params(24),
         cost_estimate=estimate(),
-    )(coords, *bases, *apart(arrays))
+    )(coords, *bases, *arrays)
 
 
 def part_of_weight(weight, own):

time: 511 us -> 507 us (level)
  transfers between devices with their start and end apart: 113 -> 113, of which waited for: 60 -> 61; matrix products, arithmetic and copies ran while one was open for 6% -> 6% of each run, Pallas kernels for 19% -> 20%
where the time goes in v6:
time: 507 us; the launch traced here: 499 us
  waiting for transfers between devices  174 us (34%)
  Pallas kernels  159 us (31%)
  starting transfers between devices  126 us (25%)
  local copies, waits for them, and re-layouts  22.2 us (4%)
  other arithmetic  16.4 us (3%)
    ppermute x109, waiting for transfers between devices, hop(): return lax.ppermute(value, AXES, [(i, i ^ mask) for i in range(32)])  165 us
    ppermute x109, starting transfers between devices, hop(): return lax.ppermute(value, AXES, [(i, i ^ mask) for i in range(32)])  111 us
    pallas_call x3, Pallas kernels, attend_call(): pl.pallas_call(functools.partial(attend_kernel, prompt), name='attend', g...  30.8 us
    pallas_call x4, Pallas kernels, back_call(): pl.pallas_call(functools.partial(back_kernel, near, phase, weights, len(p...  26.7 us
    pallas_call x3, Pallas kernels, attend_back_call(): pl.pallas_call(attend_back_kernel, name='attend_back', grid=(heads,), out...  26.5 us
    pallas_call x4, Pallas kernels, grad_call(): pl.pallas_call(functools.partial(kernel, n_steps), name=f'grad_{kind}', o...  22.6 us
    pallas_call x3, Pallas kernels, dense_call(): pl.pallas_call(functools.partial(dense_kernel, near, step, weights), name...  19.2 us
    pallas_call x4, Pallas kernels, place_call(): pl.pallas_call(kernel, name=f'place_{kind}', grid_spec=pltpu.PrefetchScal...  15 us
  transfers between devices with their start and end apart: 113, of which 61 were waited for; matrix products, arithmetic and copies ran while one was open for 6% of the time, Pallas kernels for 20%

profile of v6, /device:TPU:7, one launch (start us, length us, event | category | flops | bytes accessed | tf_op | source)
XLA Modules:
  0.0 499.3 jit_solution(1064780040707374541)
XLA Ops:
  0.7 3.5 pack.1
  12.5 4.2 collective-permute-start.2
  35.3 2.4 join_weights.3.rest_0_.args_11_.args_19_.args_12_
  37.7 2.4 first_projection.1
  40.9 4.4 collective-permute-start.7
  50.2 8.6 %collective-permute-done.8.refs_0_ = bf16[480,640]{1,0:T(8,128)(2,1)} collective-permute-done((bf16[480,640]{1,0:T(8,128)(2,1)}, bf16[480,640]{1,0:T(8,128)(2,1)}, u32[]{:S(2)}, u32[]{:S(2)}) %collective-permute-start.8) | collective-permute-done | bytes 614432 | tf_op jit(solution)/shard_map/ppermute | solution.py:32
  59.9 2.4 collective-permute-done.5.refs_2_
  64.3 4.4 collective-permute-start.10
  74.7 3.1 collective-permute-start.13
  77.8 2.7 collective-permute-done.13.b_ref
  85.1 15.1 %attend.3 = (bf16[5,384,2048]{2,1,0:T(8,128)(2,1)}, bf16[5,128,192]{2,1,0:T(8,128)(2,1)S(1)}) custom-call(bf16[5,128,192]{2,1,0:T(8,128)(2,1)S(1)} %copy-done.1, bf16[1024,640]{1,0:T(8,128)(2,1)S(1)} %stack.152.a_ref, bf16[1024,640]{1,0:T(8,128)(2,1)S(1)} %collective-permute-done.13.b_ref, s32[1,2048]{1,0:T(1,128)S(1)} %add.198.kpos_ref, ...), custom_call_target="tpu_custom_call" | custom-call | bytes 14263717 | tf_op jit(solution)/shard_map/attend/pallas_call | solution.py:500
  100.2 9.8 %collective-permute-done.16.refs_1_ = bf16[480,640]{1,0:T(8,128)(2,1)S(1)} collective-permute-done((bf16[480,640]{1,0:T(8,128)(2,1)}, bf16[480,640]{1,0:T(8,128)(2,1)S(1)}, u32[]{:S(2)}, u32[]{:S(2)}) %collective-permute-start.16) | collective-permute-done | bytes 614432 | tf_op jit(solution)/shard_map/ppermute | solution.py:32
  113.3 4.2 join_weights.4
  121.4 6.8 %dense_0.1 = (bf16[128,960]{1,0:T(8,128)(2,1)}, f32[128,960]{1,0:T(8,128)}, bf16[128,960]{1,0:T(8,128)(2,1)}, bf16[128,2560]{1,0:T(8,128)(2,1)}, bf16[128,2560]{...) custom-call(bf16[5,128,192]{2,1,0:T(8,128)(2,1)S(1)} %get-tuple-elem, ...), custom_call_target="tpu_custom_call" | custom-call | bytes 5550000 | tf_op jit(solution)/shard_map/dense_0/pallas_call | solution.py:703
  132.0 2.5 collective-permute-done.24.refs_4_
  139.3 3.0 collective-permute-done.25.refs_5_
  147.1 3.7 collective-permute-start.29
  150.8 10.3 %attend.4 = (bf16[5,288,1536]{2,1,0:T(8,128)(2,1)}, bf16[5,96,192]{2,1,0:T(8,128)(2,1)S(1)}) custom-call(bf16[5,96,192]{2,1,0:T(8,128)(2,1)S(1)} %get-tuple-element.588.q_ref, bf16[768,640]{1,0:T(8,128)(2,1)S(1)} %stack.154.a_ref, bf16[768,640]{1,0:T(8,128)(2,1)S(1)} %collective-permute-done.28.b_ref, s32[1,1536]{1,0:T(1,128)S(1)} %reshape.149.kpos_ref, ...), custom_call_target="tpu_custom_call" | custom-call | bytes 8023341 | tf_op jit(solution)/shard_map/attend/pallas_call | solution.py:500
  161.2 6.9 %dense_1.1 = (bf16[96,960]{1,0:T(8,128)(2,1)}, f32[96,960]{1,0:T(8,128)}, bf16[96,960]{1,0:T(8,128)(2,1)}, bf16[96,2560]{1,0:T(8,128)(2,1)}, bf16[96,2560]{1,0:T...) custom-call(bf16[5,96,192]{2,1,0:T(8,128)(2,1)S(1)} %get-tuple-eleme, ...), custom_call_target="tpu_custom_call" | custom-call | bytes 5550000 | tf_op jit(solution)/shard_map/dense_1/pallas_call | solution.py:703
  168.8 2.8 collective-permute-start.31
  179.3 3.2 collective-permute-start.37
  184.3 5.4 %attend.5 = (bf16[5,192,1024]{2,1,0:T(8,128)(2,1)}, bf16[5,64,192]{2,1,0:T(8,128)(2,1)S(1)}) custom-call(bf16[5,64,192]{2,1,0:T(8,128)(2,1)S(1)} %get-tuple-element.612.q_ref, bf16[512,640]{1,0:T(8,128)(2,1)S(1)} %stack.155.a_ref, bf16[512,640]{1,0:T(8,128)(2,1)S(1)} %collective-permute-done.37.b_ref, s32[1,1024]{1,0:T(1,128)S(1)} %copy-done.11, ...), custom_call_target="tpu_custom_call" | custom-call | bytes 3565929 | tf_op jit(solution)/shard_map/attend/pallas_call | solution.py:500
  189.7 5.5 %dense_2.1 = (bf16[64,960]{1,0:T(8,128)(2,1)}, f32[64,960]{1,0:T(8,128)}, bf16[64,960]{1,0:T(8,128)(2,1)}, bf16[64,2560]{1,0:T(8,128)(2,1)}, bf16[64,2560]{1,0:T...) custom-call(bf16[5,64,192]{2,1,0:T(8,128)(2,1)S(1)} %get-tuple-element.630.ao_ref, ...), custom_call_target="tpu_custom_call" | custom-call | bytes 5550000 | tf_op jit(solution)/shard_map/dense_2/pallas_call | solution.py:703
  195.2 4.5 collective-permute-start.38
  199.7 6.5 %back_0.1 = (bf16[64,960]{1,0:T(8,128)(2,1)}, bf16[64,2560]{1,0:T(8,128)(2,1)}, bf16[64,2560]{1,0:T(8,128)(2,1)}, f32[64,960]{1,0:T(8,128)}, bf16[64,960]{1,0:T(...) custom-call(s32[4]{0:T(128)S(1)} %pad_add_fusion.1.coords_ref.args_0_, ...), custom_call_target="tpu_custom_call" | custom-call | bytes 5550000 | tf_op jit(solution)/shard_map/back_0/pallas_call | solution.py:854
  206.3 5.8 %attend_back.3 = (f32[5,64,192]{2,1,0:T(8,128)S(1)}, f32[512,640]{1,0:T(8,128)S(1)}, bf16[512,640]{1,0:T(8,128)(2,1)S(1)}) custom-call(bf16[5,64,192]{2,1,0:T(8,128)(2,1)S(1)} %get-tuple-element.612.q_ref, bf16[5,64,192]{2,1,0:T(8,128)(2,1)S(1)} %get-tuple-element.644.do_ref, bf16[512,640]{1,0:T(8,128)(2,1)S(1)} %stack.155.a_ref, ...), custom_call_target="tpu_custom_call" | custom-call | bytes 2755490 | tf_op jit(solution)/shard_map/attend_back/pallas_call | solution.py:550
  215.7 2.7 collective-permute-done.40
  218.7 2.7 collective-permute-start.43
  226.4 8.3 %back_1.1 = (bf16[64,1600]{1,0:T(8,128)(2,1)}, f32[1,960]{1,0:T(1,128)}, bf16[96,960]{1,0:T(8,128)(2,1)}, bf16[96,2560]{1,0:T(8,128)(2,1)}, bf16[96,2560]{1,0:T(...) custom-call(s32[4]{0:T(128)S(1)} %pad_add_fusion.1.coords_ref.args_0, ...), custom_call_target="tpu_custom_call" | custom-call | bytes 5550000 | tf_op jit(solution)/shard_map/back_1/pallas_call | solution.py:854
  234.7 8.6 %attend_back.4 = (f32[5,96,192]{2,1,0:T(8,128)S(1)}, f32[768,640]{1,0:T(8,128)S(1)}, bf16[768,640]{1,0:T(8,128)(2,1)S(1)}) custom-call(bf16[5,96,192]{2,1,0:T(8,128)(2,1)S(1)} %get-tuple-element.588.q_ref, bf16[5,96,192]{2,1,0:T(8,128)(2,1)S(1)} %get-tuple-element.695.do_ref, bf16[768,640]{1,0:T(8,128)(2,1)S(1)} %stack.154.a_ref, ...), custom_call_target="tpu_custom_call" | custom-call | bytes 6199854 | tf_op jit(solution)/shard_map/attend_back/pallas_call | solution.py:550
  243.3 2.8 collective-permute-start.47
  260.2 2.6 collective-permute-done.52.args_9_
  262.8 9.0 %back_2.1 = (bf16[96,1600]{1,0:T(8,128)(2,1)}, f32[1,960]{1,0:T(1,128)}, bf16[128,960]{1,0:T(8,128)(2,1)}, bf16[128,2560]{1,0:T(8,128)(2,1)}, bf16[128,2560]{1,0...) custom-call(s32[4]{0:T(128)S(1)} %pad_add_fusion.1.coords_ref.args_0, ...), custom_call_target="tpu_custom_call" | custom-call | bytes 5550000 | tf_op jit(solution)/shard_map/back_2/pallas_call | solution.py:854
  271.8 5.2 %grad_rows.1 = (bf16[2,2,4,80,960]{4,3,2,1,0:T(8,128)(2,1)S(1)}, bf16[2,2,4,80,960]{4,3,2,1,0:T(8,128)(2,1)S(1)}) custom-call(s32[4]{0:T(128)S(1)} %pad_add_fusion.1.coords_ref.args_0_, bf16[128,2560]{1,0:T(8,128)(2,1)} %get-tuple-element.649.args_0_, bf16[96,2560]{1,0:T(8,128)(2,1)} %get-tuple-element.650.args_1_, ...), custom_call_target="tpu_custom_call" | custom-call | bytes 5550000 | tf_op jit(solution)/shard_map/grad_rows/pallas_call | solution.py:996
  277.2 3.0 collective-permute-start.55
  280.2 5.3 %grad_cols.2 = (bf16[2,2,4,120,640]{4,3,2,1,0:T(8,128)(2,1)S(1)}, bf16[2,2,4,120,640]{4,3,2,1,0:T(8,128)(2,1)S(1)}) custom-call(s32[4]{0:T(128)S(1)} %pad_add_fusion.1.coords_ref.args_0_, bf16[128,960]{1,0:T(8,128)(2,1)} %get-tuple-element.744.args_0_, bf16[96,960]{1,0:T(8,128)(2,1)} %get-tuple-element.745.args_1_, ...), custom_call_target="tpu_custom_call" | custom-call | bytes 5550000 | tf_op jit(solution)/shard_map/grad_cols/pallas_call | solution.py:996
  287.9 12.0 %attend_back.5 = (f32[5,128,192]{2,1,0:T(8,128)S(1)}, f32[1024,640]{1,0:T(8,128)S(1)}, bf16[1024,640]{1,0:T(8,128)(2,1)S(1)}) custom-call(bf16[5,128,192]{2,1,0:T(8,128)(2,1)S(1)} %copy-done.1, bf16[5,128,192]{2,1,0:T(8,128)(2,1)S(1)} %get-tuple-element.762.do_ref, bf16[1024,640]{1,0:T(8,128)(2,1)S(1)} %stack.152.a_ref, ...), custom_call_target="tpu_custom_call" | custom-call | bytes 11021963 | tf_op jit(solution)/shard_map/attend_back/pallas_call | solution.py:550
  299.9 3.1 collective-permute-done.56
  307.1 5.3 %grad_cols.3 = (bf16[2,2,4,120,640]{4,3,2,1,0:T(8,128)(2,1)S(1)}, bf16[2,2,4,120,640]{4,3,2,1,0:T(8,128)(2,1)S(1)}) custom-call(s32[4]{0:T(128)S(1)} %pad_add_fusion.1.coords_ref.args_0_, bf16[128,960]{1,0:T(8,128)(2,1)} %get-tuple-element.744.args_0_, bf16[96,960]{1,0:T(8,128)(2,1)} %get-tuple-element.745.args_1_, ...), custom_call_target="tpu_custom_call" | custom-call | bytes 5550000 | tf_op jit(solution)/shard_map/grad_cols/pallas_call | solution.py:996
  319.5 3.3 collective-permute-done.62
  330.3 4.4 collective-permute-done.67.args_9_
  339.2 3.0 back_3.1
  343.6 6.8 %grad_mixed.1 = (bf16[2,2,4,128,640]{4,3,2,1,0:T(8,128)(2,1)S(1)}, bf16[2,2,4,128,640]{4,3,2,1,0:T(8,128)(2,1)S(1)}) custom-call(s32[4]{0:T(128)S(1)} %pad_add_fusion.1.coords_ref.args_0_, f32[2,960]{1,0:T(2,128)} %pad_maximum_fusion.13.sums_ref, bf16[128,960]{1,0:T(8,128)(2,1)} %get-tuple-element.835.args_0_, bf16[96,960]{1,0:T(8,128)(2,1)} %get-tuple-element.836.args_1_, ...), custom_call_target="tpu_custom_call" | custom-call | bytes 5550000 | tf_op jit(solution)/shard_map/grad_mixed/pallas_call | solution.py:996
  357.8 3.9 collective-permute-done.76
  361.8 7.5 %collective-permute-done.77 = bf16[80,960]{1,0:T(8,128)(2,1)S(1)} collective-permute-done((bf16[80,960]{1,0:T(8,128)(2,1)S(1)}, bf16[80,960]{1,0:T(8,128)(2,1)S(1)}, u32[]{:S(2)}, u32[]{:S(2)}) %collective-permute-start.77) | collective-permute-done | bytes 153632 | tf_op jit(solution)/shard_map/ppermute | solution.py:32
  371.7 2.5 collective-permute-start.80
  374.7 3.1 collective-permute-start.83
  377.8 2.8 collective-permute-done.81
  380.6 7.5 %collective-permute-done.82 = bf16[120,640]{1,0:T(8,128)(2,1)S(1)} collective-permute-done((bf16[120,640]{1,0:T(8,128)(2,1)S(1)}, bf16[120,640]{1,0:T(8,128)(2,1)S(1)}, u32[]{:S(2)}, u32[]{:S(2)}) %collective-permute-start.82) | collective-permute-done | bytes 153632 | tf_op jit(solution)/shard_map/ppermute | solution.py:32
  391.9 2.7 collective-permute-start.89
  397.1 8.2 %collective-permute-done.88 = bf16[120,640]{1,0:T(8,128)(2,1)S(1)} collective-permute-done((bf16[120,640]{1,0:T(8,128)(2,1)S(1)}, bf16[120,640]{1,0:T(8,128)(2,1)S(1)}, u32[]{:S(2)}, u32[]{:S(2)}) %collective-permute-start.88) | collective-permute-done | bytes 153632 | tf_op jit(solution)/shard_map/ppermute | solution.py:32
  410.5 2.5 collective-permute-done.91
  413.0 8.4 %collective-permute-done.92 = bf16[120,640]{1,0:T(8,128)(2,1)S(1)} collective-permute-done((bf16[120,640]{1,0:T(8,128)(2,1)S(1)}, bf16[120,640]{1,0:T(8,128)(2,1)S(1)}, u32[]{:S(2)}, u32[]{:S(2)}) %collective-permute-start.92) | collective-permute-done | bytes 153632 | tf_op jit(solution)/shard_map/ppermute | solution.py:32
  424.6 2.5 collective-permute-start.99
  429.6 8.4 %collective-permute-done.98 = bf16[120,640]{1,0:T(8,128)(2,1)S(1)} collective-permute-done((bf16[120,640]{1,0:T(8,128)(2,1)S(1)}, bf16[120,640]{1,0:T(8,128)(2,1)S(1)}, u32[]{:S(2)}, u32[]{:S(2)}) %collective-permute-start.98) | collective-permute-done | bytes 153632 | tf_op jit(solution)/shard_map/ppermute | solution.py:32
  442.2 2.5 collective-permute-start.102
  444.9 3.6 collective-permute-done.100
  448.5 7.7 %collective-permute-done.101 = bf16[128,640]{1,0:T(8,128)(2,1)S(1)} collective-permute-done((bf16[128,640]{1,0:T(8,128)(2,1)S(1)}, bf16[128,640]{1,0:T(8,128)(2,1)S(1)}, u32[]{:S(2)}, u32[]{:S(2)}) %collective-permute-start.101) | collective-permute-done | bytes 163872 | tf_op jit(solution)/shard_map/ppermute | solution.py:32
  460.6 3.8 place_rows.1
  464.5 7.8 %collective-permute-done.106 = bf16[128,640]{1,0:T(8,128)(2,1)S(1)} collective-permute-done((bf16[128,640]{1,0:T(8,128)(2,1)S(1)}, bf16[128,640]{1,0:T(8,128)(2,1)S(1)}, u32[]{:S(2)}, u32[]{:S(2)}) %collective-permute-start.106) | collective-permute-done | bytes 163872 | tf_op jit(solution)/shard_map/ppermute | solution.py:32
  475.2 3.4 place_cols.3
  478.6 3.4 place_cols.4
  481.9 6.9 %collective-permute-done.111 = bf16[960,128]{1,0:T(8,128)(2,1)S(1)} collective-permute-done((bf16[960,128]{1,0:T(8,128)(2,1)S(1)}, bf16[960,128]{1,0:T(8,128)(2,1)S(1)}, u32[]{:S(2)}, u32[]{:S(2)}) %collective-permute-start.111) | collective-permute-done | bytes 245792 | tf_op jit(solution)/shard_map/ppermute | solution.py:41
  492.5 4.4 place_cols.5
  (376 shorter events, 171.4 us)
Async XLA Ops:
  4.3 20.0 %collective-permute-start = (bf16[240,1664]{1,0:T(8,128)(2,1)S(1)}, bf16[240,1664]{1,0:T(8,128)(2,1)}, u32[]{:S(2)}, u32[]{:S(2)}) collective-permute-start(bf16[240,1664]{1,0:T(8,128)(2,1)S(1)} %get-tuple-element.495), channel_id=1, source_target_pairs={{0,1},{1,0},{2,3},{3,2},{4,5},{5,4},{6,7},{7,6},{8,9},{9,8},{10,11... | collective-permute-start | bytes 2396168 | tf_op jit(solution)/shard_map/ppermute | solution.py:32
  5.9 22.6 %collective-permute-start.3 = (bf16[2,480]{1,0:T(2,128)(2,1)S(1)}, bf16[2,480]{1,0:T(2,128)(2,1)S(1)}, u32[]{:S(2)}, u32[]{:S(2)}) collective-permute-start(bf16[2,480]{1,0:T(2,128)(2,1)S(1)} %pad_maximum_fusion.14), channel_id=1, source_target_pairs={{0,1},{1,0},{2,3},{3,2},{4,5},{5,4},{6,7},{7,6},{8,9},{9,8},{10,11... | collective-permute-start | bytes 5768 | tf_op jit(solution)/shard_map/ppermute | solution.py:32
  12.5 17.9 %collective-permute-start.2 = (bf16[144,960]{1,0:T(8,128)(2,1)S(1)}, bf16[144,960]{1,0:T(8,128)(2,1)S(1)}, u32[]{:S(2)}, u32[]{:S(2)}) collective-permute-start(bf16[144,960]{1,0:T(8,128)(2,1)S(1)} %pack_rows.1), channel_id=1, source_target_pairs={{0,0},{1,16},{2,2},{3,18},{4,4},{5,20},{6,6},{7,22},{8,8},{9,24},{... | collective-permute-start | bytes 829448 | tf_op jit(solution)/shard_map/ppermute | solution.py:41
  27.0 44.7 %collective-permute-start.12 = (bf16[240,960]{1,0:T(8,128)(2,1)}, bf16[240,960]{1,0:T(8,128)(2,1)}, u32[]{:S(2)}, u32[]{:S(2)}) collective-permute-start(bf16[240,960]{1,0:T(8,128)(2,1)} %constant_dynamic-slice_fusion), channel_id=1, source_target_pairs={{0,1},{1,0},{2,3},{3,2},{4,5},{5,4},{6,7},{7,6},{8,9},{9,8},{10,11... | collective-permute-start | bytes 1382408 | tf_op jit(solution)/shard_map/ppermute | solution.py:32
  27.0 31.8 %collective-permute-start.8 = (bf16[480,640]{1,0:T(8,128)(2,1)}, bf16[480,640]{1,0:T(8,128)(2,1)}, u32[]{:S(2)}, u32[]{:S(2)}) collective-permute-start(bf16[480,640]{1,0:T(8,128)(2,1)} %pad_maximum_fusion.6), channel_id=1, source_target_pairs={{0,1},{1,0},{2,3},{3,2},{4,5},{5,4},{6,7},{7,6},{8,9},{9,8},{10,11... | collective-permute-start | bytes 1843208 | tf_op jit(solution)/shard_map/ppermute | solution.py:32
  40.9 19.0 %collective-permute-start.7 = (bf16[128,640]{1,0:T(8,128)(2,1)}, bf16[128,640]{1,0:T(8,128)(2,1)}, u32[]{:S(2)}, u32[]{:S(2)}) collective-permute-start(bf16[128,640]{1,0:T(8,128)(2,1)} %get-tuple-element.506.refs_0_), channel_id=1, source_target_pairs={{0,13},{1,12},{2,15},{3,14},{4,9},{5,8},{6,11},{7,10},{8,5},{9,4},... | collective-permute-start | bytes 491528 | tf_op jit(solution)/shard_map/ppermute | solution.py:32
  45.3 14.6 %collective-permute-start.6 = (bf16[128,640]{1,0:T(8,128)(2,1)}, bf16[128,640]{1,0:T(8,128)(2,1)}, u32[]{:S(2)}, u32[]{:S(2)}) collective-permute-start(bf16[128,640]{1,0:T(8,128)(2,1)} %get-tuple-element.506.refs_0_), channel_id=1, source_target_pairs={{0,8},{1,9},{2,10},{3,11},{4,12},{5,13},{6,14},{7,15},{8,0},{9,1},... | collective-permute-start | bytes 491528 | tf_op jit(solution)/shard_map/ppermute | solution.py:32
  45.5 16.8 %collective-permute-start.5 = (bf16[128,640]{1,0:T(8,128)(2,1)}, bf16[128,640]{1,0:T(8,128)(2,1)}, u32[]{:S(2)}, u32[]{:S(2)}) collective-permute-start(bf16[128,640]{1,0:T(8,128)(2,1)} %get-tuple-element.506.refs_0_), channel_id=1, source_target_pairs={{0,1},{1,0},{2,3},{3,2},{4,5},{5,4},{6,7},{7,6},{8,9},{9,8},{10,11... | collective-permute-start | bytes 491528 | tf_op jit(solution)/shard_map/ppermute | solution.py:32
  80.5 29.5 %collective-permute-start.14 = (bf16[480,1280]{1,0:T(8,128)(2,1)S(1)}, bf16[480,1280]{1,0:T(8,128)(2,1)S(1)}, u32[]{:S(2)}, u32[]{:S(2)}) collective-permute-start(bf16[480,1280]{1,0:T(8,128)(2,1)S(1)} %copy-done.19), channel_id=1, source_target_pairs={{0,1},{1,0},{2,3},{3,2},{4,5},{5,4},{6,7},{7,6},{8,9},{9,8},{10,11... | collective-permute-start | bytes 3686408 | tf_op jit(solution)/shard_map/ppermute | solution.py:32
  81.8 18.4 %collective-permute-start.15 = (bf16[480,640]{1,0:T(8,128)(2,1)}, bf16[480,640]{1,0:T(8,128)(2,1)S(1)}, u32[]{:S(2)}, u32[]{:S(2)}) collective-permute-start(bf16[480,640]{1,0:T(8,128)(2,1)} %collective-permute-done.8.refs_0_), channel_id=1, source_target_pairs={{0,12},{1,13},{2,14},{3,15},{4,8},{5,9},{6,10},{7,11},{8,4},{9,5},... | collective-permute-start | bytes 1843208 | tf_op jit(solution)/shard_map/ppermute | solution.py:32
  81.8 28.2 %collective-permute-start.16 = (bf16[480,640]{1,0:T(8,128)(2,1)}, bf16[480,640]{1,0:T(8,128)(2,1)S(1)}, u32[]{:S(2)}, u32[]{:S(2)}) collective-permute-start(bf16[480,640]{1,0:T(8,128)(2,1)} %collective-permute-done.8.refs_0_), channel_id=1, source_target_pairs={{0,4},{1,5},{2,6},{3,7},{4,0},{5,1},{6,2},{7,3},{8,12},{9,13},{10,... | collective-permute-start | bytes 1843208 | tf_op jit(solution)/shard_map/ppermute | solution.py:32
  82.7 27.3 %collective-permute-start.17 = (bf16[480,640]{1,0:T(8,128)(2,1)}, bf16[480,640]{1,0:T(8,128)(2,1)S(1)}, u32[]{:S(2)}, u32[]{:S(2)}) collective-permute-start(bf16[480,640]{1,0:T(8,128)(2,1)} %collective-permute-done.8.refs_0_), channel_id=1, source_target_pairs={{0,8},{1,9},{2,10},{3,11},{4,12},{5,13},{6,14},{7,15},{8,0},{9,1},... | collective-permute-start | bytes 1843208 | tf_op jit(solution)/shard_map/ppermute | solution.py:32
  111.3 8.2 %collective-permute-start.18 = (bf16[1920,640]{1,0:T(8,128)(2,1)S(1)}, bf16[1920,640]{1,0:T(8,128)(2,1)S(1)}, u32[]{:S(2)}, u32[]{:S(2)}) collective-permute-start(bf16[1920,640]{1,0:T(8,128)(2,1)S(1)} %stack.153.args_6_.args_8_), channel_id=1, source_target_pairs={{0,2},{1,3},{2,0},{3,1},{4,6},{5,7},{6,4},{7,5},{8,10},{9,11},{10,... | collective-permute-start | bytes 7372808 | tf_op jit(solution)/shard_map/ppermute | solution.py:32
  130.5 7.4 %collective-permute-start.22 = (bf16[96,640]{1,0:T(8,128)(2,1)S(1)}, bf16[96,640]{1,0:T(8,128)(2,1)S(1)}, u32[]{:S(2)}, u32[]{:S(2)}) collective-permute-start(bf16[96,640]{1,0:T(8,128)(2,1)S(1)} %get-tuple-element.571.refs_0_), channel_id=1, source_target_pairs={{0,1},{1,0},{2,3},{3,2},{4,5},{5,4},{6,7},{7,6},{8,9},{9,8},{10,11... | collective-permute-start | bytes 368648 | tf_op jit(solution)/shard_map/ppermute | solution.py:32
  147.1 21.0 %collective-permute-start.29 = (bf16[960,128]{1,0:T(8,128)(2,1)S(1)}, bf16[960,128]{1,0:T(8,128)(2,1)S(1)}, u32[]{:S(2)}, u32[]{:S(2)}) collective-permute-start(bf16[960,128]{1,0:T(8,128)(2,1)S(1)} %bitcast.205), channel_id=1, source_target_pairs={{0,0},{1,16},{2,2},{3,18},{4,4},{5,20},{6,6},{7,22},{8,8},{9,24},{... | collective-permute-start | bytes 737288 | tf_op jit(solution)/shard_map/ppermute | solution.py:41
  195.2 16.9 %collective-permute-start.38 = (bf16[960,128]{1,0:T(8,128)(2,1)}, bf16[960,128]{1,0:T(8,128)(2,1)S(1)}, u32[]{:S(2)}, u32[]{:S(2)}) collective-permute-start(bf16[960,128]{1,0:T(8,128)(2,1)} %get-tuple-element.637), channel_id=1, source_target_pairs={{0,0},{1,16},{2,2},{3,18},{4,4},{5,20},{6,6},{7,22},{8,8},{9,24},{... | collective-permute-start | bytes 737288 | tf_op jit(solution)/shard_map/ppermute | solution.py:41
  277.2 8.3 %collective-permute-start.55 = (bf16[2,2,4,80,960]{4,3,2,0,1:T(8,128)(2,1)S(1)}, bf16[2,2,4,80,960]{4,3,2,0,1:T(8,128)(2,1)S(1)}, u32[]{:S(2)}, u32[]{:S(2)}) collective-permute-start(bf16[2,2,4,80,960]{4,3,2,0,1:T(8,128)(2,1)S(1)} %copy.38), channel_id=1, source_target_pairs={{0,2},{1,3},{2,0},{3,1},{4,6},{5,7},{6,4},{7,5},{8,10},{9,11},{10,... | collective-permute-start | bytes 7372808 | tf_op jit(solution)/shard_map/ppermute | solution.py:32
  286.9 16.0 %collective-permute-start.58 = (bf16[2,2,4,120,640]{4,3,2,1,0:T(8,128)(2,1)S(1)}, bf16[2,2,4,120,640]{4,3,2,1,0:T(8,128)(2,1)S(1)}, u32[]{:S(2)}, u32[]{:S(2)}) collective-permute-start(bf16[2,2,4,120,640]{4,3,2,1,0:T(8,128)(2,1)S(1)} %get-tuple-element.761), channel_id=1, source_target_pairs={{0,2},{1,3},{2,0},{3,1},{4,6},{5,7},{6,4},{7,5},{8,10},{9,11},{10,... | collective-permute-start | bytes 7372808 | tf_op jit(solution)/shard_map/ppermute | solution.py:32
  287.0 15.9 %collective-permute-start.56 = (bf16[2,2,80,960]{3,2,1,0:T(8,128)(2,1)S(1)}, bf16[2,2,80,960]{3,2,1,0:T(8,128)(2,1)S(1)}, u32[]{:S(2)}, u32[]{:S(2)}) collective-permute-start(bf16[2,2,80,960]{3,2,1,0:T(8,128)(2,1)S(1)} %slice_bitcast_fusion.7), channel_id=1, source_target_pairs={{0,1},{1,0},{2,3},{3,2},{4,5},{5,4},{6,7},{7,6},{8,9},{9,8},{10,11... | collective-permute-start | bytes 1843208 | tf_op jit(solution)/shard_map/ppermute | solution.py:32
  287.1 15.9 %collective-permute-start.57 = (bf16[2,2,80,960]{3,2,1,0:T(8,128)(2,1)S(1)}, bf16[2,2,80,960]{3,2,1,0:T(8,128)(2,1)S(1)}, u32[]{:S(2)}, u32[]{:S(2)}) collective-permute-start(bf16[2,2,80,960]{3,2,1,0:T(8,128)(2,1)S(1)} %slice_bitcast_fusion.6), channel_id=1, source_target_pairs={{0,4},{1,5},{2,6},{3,7},{4,0},{5,1},{6,2},{7,3},{8,12},{9,13},{10,... | collective-permute-start | bytes 1843208 | tf_op jit(solution)/shard_map/ppermute | solution.py:32
  303.6 11.1 %collective-permute-start.61 = (bf16[1024,640]{1,0:T(8,128)(2,1)S(1)}, bf16[1024,640]{1,0:T(8,128)(2,1)S(1)}, u32[]{:S(2)}, u32[]{:S(2)}) collective-permute-start(bf16[1024,640]{1,0:T(8,128)(2,1)S(1)} %get-tuple-element.778), channel_id=1, source_target_pairs={{0,2},{1,3},{2,0},{3,1},{4,6},{5,7},{6,4},{7,5},{8,10},{9,11},{10,... | collective-permute-start | bytes 3932168 | tf_op jit(solution)/shard_map/ppermute | solution.py:32
  305.0 9.3 %collective-permute-start.59 = (bf16[2,80,960]{2,1,0:T(8,128)(2,1)S(1)}, bf16[2,80,960]{2,1,0:T(8,128)(2,1)S(1)}, u32[]{:S(2)}, u32[]{:S(2)}) collective-permute-start(bf16[2,80,960]{2,1,0:T(8,128)(2,1)S(1)} %slice_bitcast_fusion.18), channel_id=1, source_target_pairs={{0,4},{1,5},{2,6},{3,7},{4,0},{5,1},{6,2},{7,3},{8,12},{9,13},{10,... | collective-permute-start | bytes 921608 | tf_op jit(solution)/shard_map/ppermute | solution.py:32
  305.7 9.0 %collective-permute-start.60 = (bf16[2,80,960]{2,1,0:T(8,128)(2,1)S(1)}, bf16[2,80,960]{2,1,0:T(8,128)(2,1)S(1)}, u32[]{:S(2)}, u32[]{:S(2)}) collective-permute-start(bf16[2,80,960]{2,1,0:T(8,128)(2,1)S(1)} %slice_bitcast_fusion.17), channel_id=1, source_target_pairs={{0,1},{1,0},{2,3},{3,2},{4,5},{5,4},{6,7},{7,6},{8,9},{9,8},{10,11... | collective-permute-start | bytes 921608 | tf_op jit(solution)/shard_map/ppermute | solution.py:32
  314.9 9.0 %collective-permute-start.65 = (bf16[2,2,4,120,640]{4,3,2,1,0:T(8,128)(2,1)S(1)}, bf16[2,2,4,120,640]{4,3,2,1,0:T(8,128)(2,1)S(1)}, u32[]{:S(2)}, u32[]{:S(2)}) collective-permute-start(bf16[2,2,4,120,640]{4,3,2,1,0:T(8,128)(2,1)S(1)} %get-tuple-element.800), channel_id=1, source_target_pairs={{0,2},{1,3},{2,0},{3,1},{4,6},{5,7},{6,4},{7,5},{8,10},{9,11},{10,... | collective-permute-start | bytes 7372808 | tf_op jit(solution)/shard_map/ppermute | solution.py:32
  325.6 9.1 %collective-permute-start.67 = (bf16[128,640]{1,0:T(8,128)(2,1)S(1)}, bf16[128,640]{1,0:T(8,128)(2,1)S(1)}, u32[]{:S(2)}, u32[]{:S(2)}) collective-permute-start(bf16[128,640]{1,0:T(8,128)(2,1)S(1)} %add_convert_fusion.6), channel_id=1, source_target_pairs={{0,4},{1,5},{2,6},{3,7},{4,0},{5,1},{6,2},{7,3},{8,12},{9,13},{10,... | collective-permute-start | bytes 491528 | tf_op jit(solution)/shard_map/ppermute | solution.py:32
  326.3 8.9 %collective-permute-start.68 = (bf16[128,640]{1,0:T(8,128)(2,1)S(1)}, bf16[128,640]{1,0:T(8,128)(2,1)S(1)}, u32[]{:S(2)}, u32[]{:S(2)}) collective-permute-start(bf16[128,640]{1,0:T(8,128)(2,1)S(1)} %add_convert_fusion.5), channel_id=1, source_target_pairs={{0,1},{1,0},{2,3},{3,2},{4,5},{5,4},{6,7},{7,6},{8,9},{9,8},{10,11... | collective-permute-start | bytes 491528 | tf_op jit(solution)/shard_map/ppermute | solution.py:32
  327.7 7.5 %collective-permute-start.69 = (bf16[128,640]{1,0:T(8,128)(2,1)S(1)}, bf16[128,640]{1,0:T(8,128)(2,1)S(1)}, u32[]{:S(2)}, u32[]{:S(2)}) collective-permute-start(bf16[128,640]{1,0:T(8,128)(2,1)S(1)} %add_convert_fusion.4), channel_id=1, source_target_pairs={{0,8},{1,9},{2,10},{3,11},{4,12},{5,13},{6,14},{7,15},{8,0},{9,1},... | collective-permute-start | bytes 491528 | tf_op jit(solution)/shard_map/ppermute | solution.py:32
  335.2 17.2 %collective-permute-start.70 = (bf16[4,120,640]{2,1,0:T(8,128)(2,1)S(1)}, bf16[4,120,640]{2,1,0:T(8,128)(2,1)S(1)}, u32[]{:S(2)}, u32[]{:S(2)}) collective-permute-start(bf16[4,120,640]{2,1,0:T(8,128)(2,1)S(1)} %get-tuple-element.818), channel_id=1, source_target_pairs={{0,1},{1,0},{2,3},{3,2},{4,5},{5,4},{6,7},{7,6},{8,9},{9,8},{10,11... | collective-permute-start | bytes 1843208 | tf_op jit(solution)/shard_map/ppermute | solution.py:32
  335.6 14.8 %collective-permute-start.71 = (bf16[80,960]{1,0:T(8,128)(2,1)S(1)}, bf16[80,960]{1,0:T(8,128)(2,1)S(1)}, u32[]{:S(2)}, u32[]{:S(2)}) collective-permute-start(bf16[80,960]{1,0:T(8,128)(2,1)S(1)} %get-tuple-element.819), channel_id=1, source_target_pairs={{0,24},{1,25},{2,26},{3,27},{4,28},{5,29},{6,30},{7,31},{8,16},{9,... | collective-permute-start | bytes 460808 | tf_op jit(solution)/shard_map/ppermute | solution.py:32
  337.7 14.7 %collective-permute-start.72 = (bf16[80,960]{1,0:T(8,128)(2,1)S(1)}, bf16[80,960]{1,0:T(8,128)(2,1)S(1)}, u32[]{:S(2)}, u32[]{:S(2)}) collective-permute-start(bf16[80,960]{1,0:T(8,128)(2,1)S(1)} %get-tuple-element.820), channel_id=1, source_target_pairs={{0,16},{1,17},{2,18},{3,19},{4,20},{5,21},{6,22},{7,23},{8,24},{9,... | collective-permute-start | bytes 460808 | tf_op jit(solution)/shard_map/ppermute | solution.py:32
  338.1 14.3 %collective-permute-start.73 = (bf16[80,960]{1,0:T(8,128)(2,1)S(1)}, bf16[80,960]{1,0:T(8,128)(2,1)S(1)}, u32[]{:S(2)}, u32[]{:S(2)}) collective-permute-start(bf16[80,960]{1,0:T(8,128)(2,1)S(1)} %slice_bitcast_fusion.25), channel_id=1, source_target_pairs={{0,8},{1,9},{2,10},{3,11},{4,12},{5,13},{6,14},{7,15},{8,0},{9,1},... | collective-permute-start | bytes 460808 | tf_op jit(solution)/shard_map/ppermute | solution.py:32
  352.6 18.7 %collective-permute-start.79 = (bf16[2,2,4,128,640]{4,3,2,1,0:T(8,128)(2,1)S(1)}, bf16[2,2,4,128,640]{4,3,2,1,0:T(8,128)(2,1)S(1)}, u32[]{:S(2)}, u32[]{:S(2)}) collective-permute-start(bf16[2,2,4,128,640]{4,3,2,1,0:T(8,128)(2,1)S(1)} %get-tuple-element.863), channel_id=1, source_target_pairs={{0,2},{1,3},{2,0},{3,1},{4,6},{5,7},{6,4},{7,5},{8,10},{9,11},{10,... | collective-permute-start | bytes 7864328 | tf_op jit(solution)/shard_map/ppermute | solution.py:32
  354.1 7.6 %collective-permute-start.76 = (bf16[80,960]{1,0:T(8,128)(2,1)S(1)}, bf16[80,960]{1,0:T(8,128)(2,1)S(1)}, u32[]{:S(2)}, u32[]{:S(2)}) collective-permute-start(bf16[80,960]{1,0:T(8,128)(2,1)S(1)} %fusion.18), channel_id=1, source_target_pairs={{0,24},{1,25},{2,26},{3,27},{4,28},{5,29},{6,30},{7,31},{8,16},{9,... | collective-permute-start | bytes 460808 | tf_op jit(solution)/shard_map/ppermute | solution.py:32
  355.7 15.1 %collective-permute-start.74 = (bf16[4,120,640]{2,1,0:T(8,128)(2,1)S(1)}, bf16[4,120,640]{2,1,0:T(8,128)(2,1)S(1)}, u32[]{:S(2)}, u32[]{:S(2)}) collective-permute-start(bf16[4,120,640]{2,1,0:T(8,128)(2,1)S(1)} %get-tuple-element.858), channel_id=1, source_target_pairs={{0,1},{1,0},{2,3},{3,2},{4,5},{5,4},{6,7},{7,6},{8,9},{9,8},{10,11... | collective-permute-start | bytes 1843208 | tf_op jit(solution)/shard_map/ppermute | solution.py:32
  356.5 14.8 %collective-permute-start.75 = (bf16[4,120,640]{2,1,0:T(8,128)(2,1)S(1)}, bf16[4,120,640]{2,1,0:T(8,128)(2,1)S(1)}, u32[]{:S(2)}, u32[]{:S(2)}) collective-permute-start(bf16[4,120,640]{2,1,0:T(8,128)(2,1)S(1)} %fusion.10), channel_id=1, source_target_pairs={{0,4},{1,5},{2,6},{3,7},{4,0},{5,1},{6,2},{7,3},{8,12},{9,13},{10,... | collective-permute-start | bytes 1843208 | tf_op jit(solution)/shard_map/ppermute | solution.py:32
  357.7 11.6 %collective-permute-start.77 = (bf16[80,960]{1,0:T(8,128)(2,1)S(1)}, bf16[80,960]{1,0:T(8,128)(2,1)S(1)}, u32[]{:S(2)}, u32[]{:S(2)}) collective-permute-start(bf16[80,960]{1,0:T(8,128)(2,1)S(1)} %fusion.18), channel_id=1, source_target_pairs={{0,16},{1,17},{2,18},{3,19},{4,20},{5,21},{6,22},{7,23},{8,24},{9,... | collective-permute-start | bytes 460808 | tf_op jit(solution)/shard_map/ppermute | solution.py:32
  361.7 8.2 %collective-permute-start.78 = (bf16[80,960]{1,0:T(8,128)(2,1)S(1)}, bf16[80,960]{1,0:T(8,128)(2,1)S(1)}, u32[]{:S(2)}, u32[]{:S(2)}) collective-permute-start(bf16[80,960]{1,0:T(8,128)(2,1)S(1)} %fusion.18), channel_id=1, source_target_pairs={{0,8},{1,9},{2,10},{3,11},{4,12},{5,13},{6,14},{7,15},{8,0},{9,1},... | collective-permute-start | bytes 460808 | tf_op jit(solution)/shard_map/ppermute | solution.py:32
  371.7 16.4 %collective-permute-start.80 = (bf16[4,120,640]{2,1,0:T(8,128)(2,1)S(1)}, bf16[4,120,640]{2,1,0:T(8,128)(2,1)S(1)}, u32[]{:S(2)}, u32[]{:S(2)}) collective-permute-start(bf16[4,120,640]{2,1,0:T(8,128)(2,1)S(1)} %get-tuple-element.874), channel_id=1, source_target_pairs={{0,1},{1,0},{2,3},{3,2},{4,5},{5,4},{6,7},{7,6},{8,9},{9,8},{10,11... | collective-permute-start | bytes 1843208 | tf_op jit(solution)/shard_map/ppermute | solution.py:32
  374.2 15.5 %collective-permute-start.84 = (bf16[4,80,960]{2,1,0:T(8,128)(2,1)S(1)}, bf16[4,80,960]{2,1,0:T(8,128)(2,1)S(1)}, u32[]{:S(2)}, u32[]{:S(2)}) collective-permute-start(bf16[4,80,960]{2,1,0:T(8,128)(2,1)S(1)} %get-tuple-element.878), channel_id=1, source_target_pairs={{0,4},{1,5},{2,6},{3,7},{4,0},{5,1},{6,2},{7,3},{8,12},{9,13},{10,... | collective-permute-start | bytes 1843208 | tf_op jit(solution)/shard_map/ppermute | solution.py:32
  374.7 13.4 %collective-permute-start.82 = (bf16[120,640]{1,0:T(8,128)(2,1)S(1)}, bf16[120,640]{1,0:T(8,128)(2,1)S(1)}, u32[]{:S(2)}, u32[]{:S(2)}) collective-permute-start(bf16[120,640]{1,0:T(8,128)(2,1)S(1)} %get-tuple-element.876), channel_id=1, source_target_pairs={{0,16},{1,17},{2,18},{3,19},{4,20},{5,21},{6,22},{7,23},{8,24},{9,... | collective-permute-start | bytes 460808 | tf_op jit(solution)/shard_map/ppermute | solution.py:32
  374.7 13.4 %collective-permute-start.83 = (bf16[120,640]{1,0:T(8,128)(2,1)S(1)}, bf16[120,640]{1,0:T(8,128)(2,1)S(1)}, u32[]{:S(2)}, u32[]{:S(2)}) collective-permute-start(bf16[120,640]{1,0:T(8,128)(2,1)S(1)} %get-tuple-element.877), channel_id=1, source_target_pairs={{0,8},{1,9},{2,10},{3,11},{4,12},{5,13},{6,14},{7,15},{8,0},{9,1},... | collective-permute-start | bytes 460808 | tf_op jit(solution)/shard_map/ppermute | solution.py:32
  389.9 15.4 %collective-permute-start.85 = (bf16[4,120,640]{2,1,0:T(8,128)(2,1)S(1)}, bf16[4,120,640]{2,1,0:T(8,128)(2,1)S(1)}, u32[]{:S(2)}, u32[]{:S(2)}) collective-permute-start(bf16[4,120,640]{2,1,0:T(8,128)(2,1)S(1)} %get-tuple-element.885), channel_id=1, source_target_pairs={{0,1},{1,0},{2,3},{3,2},{4,5},{5,4},{6,7},{7,6},{8,9},{9,8},{10,11... | collective-permute-start | bytes 1843208 | tf_op jit(solution)/shard_map/ppermute | solution.py:32
  390.1 15.2 %collective-permute-start.86 = (bf16[4,120,640]{2,1,0:T(8,128)(2,1)S(1)}, bf16[4,120,640]{2,1,0:T(8,128)(2,1)S(1)}, u32[]{:S(2)}, u32[]{:S(2)}) collective-permute-start(bf16[4,120,640]{2,1,0:T(8,128)(2,1)S(1)} %fusion.7), channel_id=1, source_target_pairs={{0,4},{1,5},{2,6},{3,7},{4,0},{5,1},{6,2},{7,3},{8,12},{9,13},{10,... | collective-permute-start | bytes 1843208 | tf_op jit(solution)/shard_map/ppermute | solution.py:32
  391.9 13.5 %collective-permute-start.88 = (bf16[120,640]{1,0:T(8,128)(2,1)S(1)}, bf16[120,640]{1,0:T(8,128)(2,1)S(1)}, u32[]{:S(2)}, u32[]{:S(2)}) collective-permute-start(bf16[120,640]{1,0:T(8,128)(2,1)S(1)} %fusion.24), channel_id=1, source_target_pairs={{0,16},{1,17},{2,18},{3,19},{4,20},{5,21},{6,22},{7,23},{8,24},{9,... | collective-permute-start | bytes 460808 | tf_op jit(solution)/shard_map/ppermute | solution.py:32
  391.9 13.5 %collective-permute-start.89 = (bf16[120,640]{1,0:T(8,128)(2,1)S(1)}, bf16[120,640]{1,0:T(8,128)(2,1)S(1)}, u32[]{:S(2)}, u32[]{:S(2)}) collective-permute-start(bf16[120,640]{1,0:T(8,128)(2,1)S(1)} %fusion.24), channel_id=1, source_target_pairs={{0,8},{1,9},{2,10},{3,11},{4,12},{5,13},{6,14},{7,15},{8,0},{9,1},... | collective-permute-start | bytes 460808 | tf_op jit(solution)/shard_map/ppermute | solution.py:32
  405.8 15.6 %collective-permute-start.90 = (bf16[4,128,640]{2,1,0:T(8,128)(2,1)S(1)}, bf16[4,128,640]{2,1,0:T(8,128)(2,1)S(1)}, u32[]{:S(2)}, u32[]{:S(2)}) collective-permute-start(bf16[4,128,640]{2,1,0:T(8,128)(2,1)S(1)} %get-tuple-element.897), channel_id=1, source_target_pairs={{0,1},{1,0},{2,3},{3,2},{4,5},{5,4},{6,7},{7,6},{8,9},{9,8},{10,11... | collective-permute-start | bytes 1966088 | tf_op jit(solution)/shard_map/ppermute | solution.py:32
  406.4 15.0 %collective-permute-start.94 = (bf16[4,120,640]{2,1,0:T(8,128)(2,1)S(1)}, bf16[4,120,640]{2,1,0:T(8,128)(2,1)S(1)}, u32[]{:S(2)}, u32[]{:S(2)}) collective-permute-start(bf16[4,120,640]{2,1,0:T(8,128)(2,1)S(1)} %get-tuple-element.901), channel_id=1, source_target_pairs={{0,4},{1,5},{2,6},{3,7},{4,0},{5,1},{6,2},{7,3},{8,12},{9,13},{10,... | collective-permute-start | bytes 1843208 | tf_op jit(solution)/shard_map/ppermute | solution.py:32
  408.8 12.6 %collective-permute-start.92 = (bf16[120,640]{1,0:T(8,128)(2,1)S(1)}, bf16[120,640]{1,0:T(8,128)(2,1)S(1)}, u32[]{:S(2)}, u32[]{:S(2)}) collective-permute-start(bf16[120,640]{1,0:T(8,128)(2,1)S(1)} %get-tuple-element.899), channel_id=1, source_target_pairs={{0,16},{1,17},{2,18},{3,19},{4,20},{5,21},{6,22},{7,23},{8,24},{9,... | collective-permute-start | bytes 460808 | tf_op jit(solution)/shard_map/ppermute | solution.py:32
  408.8 12.6 %collective-permute-start.93 = (bf16[120,640]{1,0:T(8,128)(2,1)S(1)}, bf16[120,640]{1,0:T(8,128)(2,1)S(1)}, u32[]{:S(2)}, u32[]{:S(2)}) collective-permute-start(bf16[120,640]{1,0:T(8,128)(2,1)S(1)} %get-tuple-element.900), channel_id=1, source_target_pairs={{0,8},{1,9},{2,10},{3,11},{4,12},{5,13},{6,14},{7,15},{8,0},{9,1},... | collective-permute-start | bytes 460808 | tf_op jit(solution)/shard_map/ppermute | solution.py:32
  421.6 16.4 %collective-permute-start.95 = (bf16[4,128,640]{2,1,0:T(8,128)(2,1)S(1)}, bf16[4,128,640]{2,1,0:T(8,128)(2,1)S(1)}, u32[]{:S(2)}, u32[]{:S(2)}) collective-permute-start(bf16[4,128,640]{2,1,0:T(8,128)(2,1)S(1)} %get-tuple-element.908), channel_id=1, source_target_pairs={{0,1},{1,0},{2,3},{3,2},{4,5},{5,4},{6,7},{7,6},{8,9},{9,8},{10,11... | collective-permute-start | bytes 1966088 | tf_op jit(solution)/shard_map/ppermute | solution.py:32
  422.1 15.9 %collective-permute-start.96 = (bf16[4,128,640]{2,1,0:T(8,128)(2,1)S(1)}, bf16[4,128,640]{2,1,0:T(8,128)(2,1)S(1)}, u32[]{:S(2)}, u32[]{:S(2)}) collective-permute-start(bf16[4,128,640]{2,1,0:T(8,128)(2,1)S(1)} %fusion), channel_id=1, source_target_pairs={{0,4},{1,5},{2,6},{3,7},{4,0},{5,1},{6,2},{7,3},{8,12},{9,13},{10,... | collective-permute-start | bytes 1966088 | tf_op jit(solution)/shard_map/ppermute | solution.py:32
  424.6 13.4 %collective-permute-start.98 = (bf16[120,640]{1,0:T(8,128)(2,1)S(1)}, bf16[120,640]{1,0:T(8,128)(2,1)S(1)}, u32[]{:S(2)}, u32[]{:S(2)}) collective-permute-start(bf16[120,640]{1,0:T(8,128)(2,1)S(1)} %fusion.21), channel_id=1, source_target_pairs={{0,16},{1,17},{2,18},{3,19},{4,20},{5,21},{6,22},{7,23},{8,24},{9,... | collective-permute-start | bytes 460808 | tf_op jit(solution)/shard_map/ppermute | solution.py:32
  424.6 13.4 %collective-permute-start.99 = (bf16[120,640]{1,0:T(8,128)(2,1)S(1)}, bf16[120,640]{1,0:T(8,128)(2,1)S(1)}, u32[]{:S(2)}, u32[]{:S(2)}) collective-permute-start(bf16[120,640]{1,0:T(8,128)(2,1)S(1)} %fusion.21), channel_id=1, source_target_pairs={{0,8},{1,9},{2,10},{3,11},{4,12},{5,13},{6,14},{7,15},{8,0},{9,1},... | collective-permute-start | bytes 460808 | tf_op jit(solution)/shard_map/ppermute | solution.py:32
  438.4 17.7 %collective-permute-start.104 = (bf16[2,4,80,960]{3,2,1,0:T(8,128)(2,1)S(1)}, bf16[2,4,80,960]{3,2,1,0:T(8,128)(2,1)S(1)}, u32[]{:S(2)}, u32[]{:S(2)}) collective-permute-start(bf16[2,4,80,960]{3,2,1,0:T(8,128)(2,1)S(1)} %pad_maximum_fusion.near_ref), channel_id=1, source_target_pairs={{0,2},{1,3},{2,0},{3,1},{4,6},{5,7},{6,4},{7,5},{8,10},{9,11},{10,... | collective-permute-start | bytes 3686408 | tf_op jit(solution)/shard_map/ppermute | solution.py:32
  439.7 16.4 %collective-permute-start.103 = (bf16[4,120,640]{2,1,0:T(8,128)(2,1)S(1)}, bf16[4,120,640]{2,1,0:T(8,128)(2,1)S(1)}, u32[]{:S(2)}, u32[]{:S(2)}) collective-permute-start(bf16[4,120,640]{2,1,0:T(8,128)(2,1)S(1)} %get-tuple-element.924), channel_id=1, source_target_pairs={{0,4},{1,5},{2,6},{3,7},{4,0},{5,1},{6,2},{7,3},{8,12},{9,13},{10,... | collective-permute-start | bytes 1843208 | tf_op jit(solution)/shard_map/ppermute | solution.py:32
  442.2 13.9 %collective-permute-start.101 = (bf16[128,640]{1,0:T(8,128)(2,1)S(1)}, bf16[128,640]{1,0:T(8,128)(2,1)S(1)}, u32[]{:S(2)}, u32[]{:S(2)}) collective-permute-start(bf16[128,640]{1,0:T(8,128)(2,1)S(1)} %get-tuple-element.922), channel_id=1, source_target_pairs={{0,16},{1,17},{2,18},{3,19},{4,20},{5,21},{6,22},{7,23},{8,24},{9,... | collective-permute-start | bytes 491528 | tf_op jit(solution)/shard_map/ppermute | solution.py:32
  442.2 13.9 %collective-permute-start.102 = (bf16[128,640]{1,0:T(8,128)(2,1)S(1)}, bf16[128,640]{1,0:T(8,128)(2,1)S(1)}, u32[]{:S(2)}, u32[]{:S(2)}) collective-permute-start(bf16[128,640]{1,0:T(8,128)(2,1)S(1)} %get-tuple-element.923), channel_id=1, source_target_pairs={{0,8},{1,9},{2,10},{3,11},{4,12},{5,13},{6,14},{7,15},{8,0},{9,1},... | collective-permute-start | bytes 491528 | tf_op jit(solution)/shard_map/ppermute | solution.py:32
  456.4 15.8 %collective-permute-start.108 = (bf16[2,4,120,640]{3,2,1,0:T(8,128)(2,1)S(1)}, bf16[2,4,120,640]{3,2,1,0:T(8,128)(2,1)S(1)}, u32[]{:S(2)}, u32[]{:S(2)}) collective-permute-start(bf16[2,4,120,640]{3,2,1,0:T(8,128)(2,1)S(1)} %pad_maximum_fusion.2.near_ref), channel_id=1, source_target_pairs={{0,2},{1,3},{2,0},{3,1},{4,6},{5,7},{6,4},{7,5},{8,10},{9,11},{10,... | collective-permute-start | bytes 3686408 | tf_op jit(solution)/shard_map/ppermute | solution.py:32
  457.0 15.3 %collective-permute-start.109 = (bf16[2,4,120,640]{3,2,1,0:T(8,128)(2,1)S(1)}, bf16[2,4,120,640]{3,2,1,0:T(8,128)(2,1)S(1)}, u32[]{:S(2)}, u32[]{:S(2)}) collective-permute-start(bf16[2,4,120,640]{3,2,1,0:T(8,128)(2,1)S(1)} %pad_maximum_fusion.3.near_ref), channel_id=1, source_target_pairs={{0,2},{1,3},{2,0},{3,1},{4,6},{5,7},{6,4},{7,5},{8,10},{9,11},{10,... | collective-permute-start | bytes 3686408 | tf_op jit(solution)/shard_map/ppermute | solution.py:32
  457.1 7.4 %collective-permute-start.105 = (bf16[128,640]{1,0:T(8,128)(2,1)S(1)}, bf16[128,640]{1,0:T(8,128)(2,1)S(1)}, u32[]{:S(2)}, u32[]{:S(2)}) collective-permute-start(bf16[128,640]{1,0:T(8,128)(2,1)S(1)} %fusion.15), channel_id=1, source_target_pairs={{0,24},{1,25},{2,26},{3,27},{4,28},{5,29},{6,30},{7,31},{8,16},{9,... | collective-permute-start | bytes 491528 | tf_op jit(solution)/shard_map/ppermute | solution.py:32
  458.9 13.4 %collective-permute-start.106 = (bf16[128,640]{1,0:T(8,128)(2,1)S(1)}, bf16[128,640]{1,0:T(8,128)(2,1)S(1)}, u32[]{:S(2)}, u32[]{:S(2)}) collective-permute-start(bf16[128,640]{1,0:T(8,128)(2,1)S(1)} %fusion.15), channel_id=1, source_target_pairs={{0,16},{1,17},{2,18},{3,19},{4,20},{5,21},{6,22},{7,23},{8,24},{9,... | collective-permute-start | bytes 491528 | tf_op jit(solution)/shard_map/ppermute | solution.py:32
  458.9 13.4 %collective-permute-start.107 = (bf16[128,640]{1,0:T(8,128)(2,1)S(1)}, bf16[128,640]{1,0:T(8,128)(2,1)S(1)}, u32[]{:S(2)}, u32[]{:S(2)}) collective-permute-start(bf16[128,640]{1,0:T(8,128)(2,1)S(1)} %fusion.15), channel_id=1, source_target_pairs={{0,8},{1,9},{2,10},{3,11},{4,12},{5,13},{6,14},{7,15},{8,0},{9,1},... | collective-permute-start | bytes 491528 | tf_op jit(solution)/shard_map/ppermute | solution.py:32
  472.4 16.4 %collective-permute-start.110 = (bf16[4,128,640]{2,1,0:T(8,128)(2,1)S(1)}, bf16[4,128,640]{2,1,0:T(8,128)(2,1)S(1)}, u32[]{:S(2)}, u32[]{:S(2)}) collective-permute-start(bf16[4,128,640]{2,1,0:T(8,128)(2,1)S(1)} %get-tuple-element.950), channel_id=1, source_target_pairs={{0,4},{1,5},{2,6},{3,7},{4,0},{5,1},{6,2},{7,3},{8,12},{9,13},{10,... | collective-permute-start | bytes 1966088 | tf_op jit(solution)/shard_map/ppermute | solution.py:32
  473.3 15.5 %collective-permute-start.111 = (bf16[960,128]{1,0:T(8,128)(2,1)S(1)}, bf16[960,128]{1,0:T(8,128)(2,1)S(1)}, u32[]{:S(2)}, u32[]{:S(2)}) collective-permute-start(bf16[960,128]{1,0:T(8,128)(2,1)S(1)} %copy-done.36), channel_id=1, source_target_pairs={{0,0},{1,16},{2,2},{3,18},{4,4},{5,20},{6,6},{7,22},{8,8},{9,24},{... | collective-permute-start | bytes 737288 | tf_op jit(solution)/shard_map/ppermute | solution.py:41
  (86 other events, 755.4 us)
